TPU v7x, 256 devices: a whole 4x4x8 slice. The times are simulated.
256 devices in a mesh: ens: 2 (over x_lo), sx: 16 (over x_hi, y, core), sy: 8 (over z).
Axes of the slice: x: 4 (x_hi: 2, x_lo: 2; x = x_hi * 2 + x_lo), y: 4, z: 8, core: 2. Of those that a mesh axis runs over, the one named last changes fastest.
Arguments:
- snapshots: bfloat16 [4, 4, 128, 512, 512], P('ens', None, 'sx', 'sy'), may hold values from -6 to 6
- coefficients: bfloat16 [4, 256, 512], P('ens'), may hold values from -0.125 to 0.125
- modes: bfloat16 [4, 128, 512, 256], P(None, 'sx', 'sy'), may hold values from -12 to 12
Outputs:
- new_modes: bfloat16 [4, 128, 512, 256], P(None, 'sx', 'sy')
- gram: float32 [256, 256], replicated
- proj: float32 [4, 256, 512], P('ens')
All inputs are finite; a program needn't handle non-finite values.
Results may differ from a plain program's by a relative error of at most 0.005.
Values may be sent and summed in bfloat16 or wider, within the bound.
No kernel may reach another device: no remote copies, remote signals or barrier semaphores. Data moves between devices by JAX's collectives and lax.ppermute only.
A program may use at most 64 MiB of HBM per device.

v0:
```python
import math

import jax
import jax.numpy as jnp
from jax import lax
from jax.sharding import PartitionSpec as P

ETA = 0.25
LAM = 0.5
TAU = 0.4


def padded_2(array, sides, width):
    for axis, dim in sides:
        size, length = (lax.axis_size(axis), array.shape[dim])
        up = [(i, (i + 1) % size) for i in range(size - 1)]
        down = [(j, i) for i, j in up]
        last = lax.slice_in_dim(array, length - width, length, axis=dim)
        leading = lax.slice_in_dim(array, 0, width, axis=dim)
        before = lax.ppermute(last, axis, up)
        after = lax.ppermute(leading, axis, down)
        array = jnp.concatenate([before, array, after], axis=dim)
    return array


def bend(field):
    padded = padded_2(field, (("sx", 1), ("sy", 2)), 1).astype(jnp.float32)
    centre = padded[:, 1:-1, 1:-1]
    beside_all = (
        padded[:, 2:, 1:-1] + padded[:, :-2, 1:-1] + padded[:, 1:-1, 2:] + padded[:, 1:-1, :-2]
    )
    return 4.0 * centre - beside_all


def local(snapshots, coefficients, modes):
    members, levels, rows_x, rows_y, frames = snapshots.shape
    width = modes.shape[3]
    local_cells = levels * rows_x * rows_y
    total_cells = local_cells * lax.axis_size("sx") * lax.axis_size("sy")
    flat_modes = modes.reshape(local_cells, width)
    series = snapshots.reshape(members, local_cells, frames)
    bent = bend(modes).reshape(local_cells, width)
    partial_grad = jnp.zeros((local_cells, width), jnp.float32)
    for member in range(members):
        fitted = jnp.dot(flat_modes, coefficients[member], preferred_element_type=jnp.float32)
        misfit = (fitted - series[member].astype(jnp.float32)).astype(jnp.bfloat16)
        partial_grad = partial_grad + jnp.einsum(
            "ct,rt->cr", misfit, coefficients[member], preferred_element_type=jnp.float32
        )
    grad_full = lax.psum(partial_grad, "ens")
    moved = (flat_modes.astype(jnp.float32) - ETA * (grad_full + LAM * bent)).astype(jnp.bfloat16)
    moved_f = moved.astype(jnp.float32)
    squares = lax.psum(jnp.sum(moved_f * moved_f, axis=0), ("sx", "sy"))
    raw_gram = jnp.einsum("cr,cs->rs", moved, moved, preferred_element_type=jnp.float32)
    raw_proj = jnp.einsum("cr,mct->mrt", moved, series, preferred_element_type=jnp.float32)
    gram_sum, proj_sum = lax.psum((raw_gram, raw_proj), ("sx", "sy"))
    shrink = jnp.maximum(0.0, 1.0 - TAU / jnp.sqrt(squares / total_cells + 1e-06))
    new_modes = (
        (moved_f * shrink[None, :]).astype(jnp.bfloat16).reshape(levels, rows_x, rows_y, width)
    )
    gram = shrink[:, None] * gram_sum * shrink[None, :] / total_cells
    projected = shrink[None, :, None] * proj_sum / math.sqrt(total_cells)
    return (new_modes, gram, projected)


def solution(mesh):
    in_specs = (P("ens", None, "sx", "sy", None), P("ens", None, None), P(None, "sx", "sy", None))
    out_specs = (P(None, "sx", "sy", None), P(), P("ens", None, None))
    return jax.shard_map(local, mesh=mesh, in_specs=in_specs, out_specs=out_specs, check_vma=False)
```

profile of v0, /device:TPU:1, one launch (start us, length us, event | category | flops | bytes accessed | tf_op | source)
XLA Modules:
  0.0 1315.3 jit_solution(10424352402243552512)
XLA Ops:
  7.2 0.0 copy-start.1
  7.2 0.0 all-reduce.4.cloned.1.call-start
  7.2 4.1 fusion.20
  11.3 0.0 copy-done.1
  11.3 4.2 fusion.9
  15.5 4.3 convolution_add_fusion
  19.9 0.0 all-reduce.4.cloned.1.call-update
  19.9 0.0 all-reduce.6.cloned.1.call-start
  20.0 4.6 collective-permute-start
  24.5 1.9 collective-permute-start.1
  26.5 0.0 collective-permute-done
  26.5 0.1 constant_dynamic-update-slice_fusion.1
  26.6 4.2 collective-permute-done.1
  30.8 0.1 fusion.21
  30.9 1.3 collective-permute-start.3
  32.2 4.2 collective-permute-start.2
  36.4 0.0 collective-permute-done.3
  36.4 1.1 collective-permute-done.2
  37.5 0.5 maximum_convert_fusion
  38.0 0.7 fusion.5
  38.8 59.7 %all-reduce.4.cloned.1.call-done = f32[2048,256]{1,0:T(8,128)} async-done(((f32[2048,256]{1,0:T(8,128)}), f32[2048,256]{1,0:T(8,128)}) %all-reduce.4.cloned.1.call-update) | async-done | bytes 2097168 | tf_op jit(solution)/shard_map/psum | solution.py:50
  98.5 0.0 copy-start
  98.5 2.5 fusion.2
  101.0 1.2 fusion.23
  102.1 0.0 copy-done
  102.1 2.2 convolution_bitcast_fusion
  104.4 0.0 all-reduce.6.cloned.1.call-update
  104.4 312.9 %psum.29 = f32[256]{0:T(256)S(1)} all-reduce(f32[256]{0:T(256)S(1)} %get-tuple-element.5), channel_id=1, replica_groups=mesh['ens'=2,'sx'=16,'sy'=8] {'sx','sy'}, use_global_device_ids=true, to_apply=%region_2.0 | all-reduce | flops 256 | bytes 2048 | tf_op jit(solution)/shard_map/psum | solution.py:53
  417.3 1.2 fusion.3
  418.5 885.9 %all-reduce.6.cloned.1.call-done = (f32[256,256]{1,0:T(8,128)}, f32[2,256,512]{2,1,0:T(8,128)}) async-done(((f32[256,256]{1,0:T(8,128)}, f32[2,256,512]{2,1,0:T(8,128)}), (f32[256,256]{1,0:T(8,128)}, f32[2,256,512]{2,1,0:T(8,128)})) %all-reduce.6.cloned.1.call-update) | async-done | bytes 1310736 | tf_op jit(solution)/shard_map/psum | solution.py:56
  1304.4 1.8 multiply_multiply_fusion.1
  1306.1 2.3 multiply_multiply_fusion
  (4 shorter events, 0.1 us)
Async XLA Ops:
  7.2 4.1 copy-start.1
  7.2 91.3 %all-reduce.4.cloned.1.call-start = ((), (), s32[]{:S(2)}) async-start(), calls=%async_computation | async-start | bytes 4194304 | tf_op jit(solution)/shard_map/psum | solution.py:50
  19.9 1284.5 %all-reduce.6.cloned.1.call-start = ((), (), s32[]{:S(2)}) async-start(), calls=%async_computation.1 | async-start | bytes 2621440 | tf_op jit(solution)/shard_map/psum | solution.py:56
  20.0 6.5 collective-permute-start
  24.5 6.3 collective-permute-start.1
  30.9 5.5 collective-permute-start.3
  32.2 5.3 collective-permute-start.2
  98.5 3.7 copy-start
Sparse Core Ops, SparseCore 0:
  20.0 78.4 all-reduce.3
  104.5 1199.8 all-reduce.5
where the time goes:
time: 1320 us
  waiting for transfers between devices  951 us (72%)
  blocking collectives  313 us (24%)
  between operations  14.1 us (1%)
    psum x1, waiting for transfers between devices, local(): gram_sum, proj_sum = lax.psum((raw_gram, raw_proj), ('sx', 'sy'))  886 us
    psum x1, blocking collectives, local(): squares = lax.psum(jnp.sum(moved_f * moved_f, axis=0), ('sx', 'sy'))  313 us
    psum x1, waiting for transfers between devices, local(): grad_full = lax.psum(partial_grad, 'ens')  59.7 us
  transfers between devices with their start and end apart: 6, of which 4 were waited for; matrix products, arithmetic and copies ran while one was open for 0% of the time, Pallas kernels for 0%

commit v1 on v0

v1 whole, which is shorter than its diff:
```python
import functools
import math

import jax
import jax.numpy as jnp
from jax import lax
from jax.experimental import pallas as pl
from jax.experimental.pallas import tpu as pltpu
from jax.sharding import Mesh, PartitionSpec as P

ETA = 0.25
LAM = 0.5
TAU = 0.4

F32 = jnp.float32
BF16 = jnp.bfloat16
VMEM_LIMIT = 48 * 1024 * 1024
PARAMS = pltpu.CompilerParams(vmem_limit_bytes=VMEM_LIMIT)

GROUP = ("xh", "y", "z")
SHARES = 64
PROJ_ROWS = 16
SHARE_ROWS = 24


def dot_t(a, b):
    return lax.dot_general(a, b, (((0,), (0,)), ((), ())), preferred_element_type=F32)


def grad_kernel(m_ref, c_ref, x_ref, g_ref):
    members = c_ref.shape[0]
    acc = None
    for e in range(members):
        fitted = jnp.dot(m_ref[...], c_ref[e], preferred_element_type=F32)
        misfit = (fitted - x_ref[e].astype(F32)).astype(BF16)
        term = lax.dot_general(misfit, c_ref[e], (((1,), (1,)), ((), ())), preferred_element_type=F32)
        acc = term if acc is None else acc + term
    g_ref[...] = acc.astype(BF16)


def grad_level(flat_modes, coefficients, series, level, cells):
    members, _, frames = series.shape
    width = flat_modes.shape[1]
    return pl.pallas_call(
        grad_kernel,
        grid=(1,),
        in_specs=[
            pl.BlockSpec((cells, width), lambda i: (level, 0)),
            pl.BlockSpec(coefficients.shape, lambda i: (0, 0, 0)),
            pl.BlockSpec((members, cells, frames), lambda i: (0, level, 0)),
        ],
        out_specs=pl.BlockSpec((cells, width), lambda i: (0, 0)),
        out_shape=jax.ShapeDtypeStruct((cells, width), BF16),
        compiler_params=PARAMS,
        cost_estimate=pl.CostEstimate(
            flops=4 * members * cells * frames * width,
            bytes_accessed=2 * cells * (2 * width + members * frames) + 2 * members * width * frames,
            transcendentals=0,
        ),
    )(flat_modes, coefficients, series)


def moved_of(level, m_ref, xlo_ref, xhi_ref, zlo_ref, zhi_ref, own_ref, got_ref):
    rows_x, rows_y, width = m_ref.shape
    f = m_ref[...].astype(F32)
    up = jnp.concatenate([xlo_ref[...].astype(F32), f[:-1]], axis=0)
    down = jnp.concatenate([f[1:], xhi_ref[...].astype(F32)], axis=0)
    at = lax.broadcasted_iota(jnp.int32, (rows_x, rows_y, width), 1)
    zlo = zlo_ref[level * rows_x : (level + 1) * rows_x, :].astype(F32)
    zhi = zhi_ref[level * rows_x : (level + 1) * rows_x, :].astype(F32)
    left = jnp.where(at == 0, jnp.broadcast_to(zlo[:, None, :], f.shape), pltpu.roll(f, 1, 1))
    right = jnp.where(
        at == rows_y - 1, jnp.broadcast_to(zhi[:, None, :], f.shape), pltpu.roll(f, rows_y - 1, 1)
    )
    bent = 4.0 * f - (down + up + right + left)
    cells = rows_x * rows_y
    grad = own_ref[...].astype(F32) + got_ref[...].astype(F32)
    return (f.reshape(cells, width) - ETA * (grad + LAM * bent.reshape(cells, width))).astype(BF16)


def emit_share(out_ref, half, proj_ref, gram_ref, squares_ref, tmp_ref):
    members, width, frames = proj_ref.shape
    per = width // PROJ_ROWS
    for tb in range(frames // 256):
        for m in range(members):
            at = pl.multiple_of((half * (frames // 256) + tb) * 128, 128)
            block = proj_ref[m, :, pl.ds(at, 128)]
            first = (tb * members + m) * per
            out_ref[first : first + per, 0:PROJ_ROWS, :] = block.reshape(per, PROJ_ROWS, 128).astype(BF16)
    gram = gram_ref[:, pl.ds(pl.multiple_of(half * 128, 128), 128)]
    for q in range(4):
        tmp_ref[:, q, :] = gram[q * SHARES : (q + 1) * SHARES, :]
    for k in range(2):
        part = squares_ref[0:1, k * 128 : (k + 1) * 128]
        high = part.astype(BF16).astype(F32)
        tmp_ref[:, 4 + k, :] = jnp.broadcast_to(high, (SHARES, 128))
        tmp_ref[:, 6 + k, :] = jnp.broadcast_to(part - high, (SHARES, 128))
    out_ref[:, PROJ_ROWS:SHARE_ROWS, :] = tmp_ref[...].astype(BF16)


def step_kernel(level, first, last, *refs):
    (core_ref, m_ref, xlo_ref, xhi_ref, zlo_ref, zhi_ref, own_ref, got_ref, x_ref), refs = refs[:9], refs[9:]
    if not first:
        (proj_in, gram_in, squares_in), refs = refs[:3], refs[3:]
    if last:
        moved_ref, keep_ref, send_ref, proj_ref, gram_ref, squares_ref, tmp_ref = refs
    else:
        moved_ref, proj_ref, gram_ref, squares_ref = refs
    moved = moved_of(level, m_ref, xlo_ref, xhi_ref, zlo_ref, zhi_ref, own_ref, got_ref)
    moved_ref[...] = moved
    members = x_ref.shape[0]
    wide = moved.astype(F32)
    squares = jnp.sum(wide * wide, axis=0, keepdims=True)
    gram = dot_t(moved, moved)
    squares_ref[...] = squares if first else squares_in[...] + squares
    gram_ref[...] = gram if first else gram_in[...] + gram
    for e in range(members):
        proj = dot_t(moved, x_ref[e])
        proj_ref[e] = proj if first else proj_in[e] + proj
    if last:
        core = core_ref[0]
        emit_share(keep_ref, core, proj_ref, gram_ref, squares_ref, tmp_ref)
        emit_share(send_ref, 1 - core, proj_ref, gram_ref, squares_ref, tmp_ref)


def step_level(level, levels, core, modes, halos, own, got, series, carry):
    members, total, frames = series.shape
    _, rows_x, rows_y, width = modes.shape
    cells = rows_x * rows_y
    first, last = level == 0, level == levels - 1
    xlo, xhi, zlo, zhi = halos
    whole = lambda a: pl.BlockSpec(a.shape, lambda i, c: (0,) * len(a.shape))
    in_specs = [
        pl.BlockSpec((None, rows_x, rows_y, width), lambda i, c: (level, 0, 0, 0)),
        pl.BlockSpec((None, 1, rows_y, width), lambda i, c: (level, 0, 0, 0)),
        pl.BlockSpec((None, 1, rows_y, width), lambda i, c: (level, 0, 0, 0)),
        whole(zlo),
        whole(zhi),
        whole(own),
        whole(got),
        pl.BlockSpec((members, cells, frames), lambda i, c: (0, level, 0)),
    ]
    args = [modes, xlo, xhi, zlo, zhi, own, got, series]
    if not first:
        in_specs += [whole(a) for a in carry]
        args += list(carry)
    sums = [
        jax.ShapeDtypeStruct((members, width, frames), F32),
        jax.ShapeDtypeStruct((width, width), F32),
        jax.ShapeDtypeStruct((1, width), F32),
    ]
    outs = [jax.ShapeDtypeStruct((cells, width), BF16)]
    scratch = []
    if last:
        share = jax.ShapeDtypeStruct((SHARES, SHARE_ROWS, 128), BF16)
        outs += [share, share]
        scratch = [pltpu.VMEM(s.shape, F32) for s in sums] + [pltpu.VMEM((SHARES, 8, 128), F32)]
    else:
        outs += sums
    return pl.pallas_call(
        functools.partial(step_kernel, level, first, last),
        grid_spec=pltpu.PrefetchScalarGridSpec(
            num_scalar_prefetch=1,
            grid=(1,),
            in_specs=in_specs,
            out_specs=[whole(o) for o in outs],
            scratch_shapes=scratch,
        ),
        out_shape=outs,
        compiler_params=PARAMS,
        cost_estimate=pl.CostEstimate(
            flops=2 * cells * width * (width + members * frames),
            bytes_accessed=2 * cells * (4 * width + members * frames),
            transcendentals=0,
        ),
    )(core, *args)


def join_kernel(keep_ref, got_ref, out_ref):
    out_ref[:, 0:PROJ_ROWS, :] = (
        keep_ref[:, 0:PROJ_ROWS, :].astype(F32) + got_ref[:, 0:PROJ_ROWS, :].astype(F32)
    ).astype(BF16)
    tail = keep_ref[:, PROJ_ROWS:SHARE_ROWS, :].astype(F32) + got_ref[:, PROJ_ROWS:SHARE_ROWS, :].astype(F32)
    row = lax.broadcasted_iota(jnp.int32, tail.shape, 1)
    total = tail + pltpu.roll(tail, 6, 1)
    high = total.astype(BF16).astype(F32)
    low = pltpu.roll(total - high, 2, 1)
    out_ref[:, PROJ_ROWS:SHARE_ROWS, :] = jnp.where(
        row < 4, tail, jnp.where(row < 6, high, low)
    ).astype(BF16)


def reduce_kernel(total_cells, at_ref, in_ref, out_ref, shrink_ref, column_ref):
    core, share = at_ref[0], at_ref[1]
    total = jnp.sum(in_ref[...].astype(F32), axis=0)
    squares = total[20:22, :] + total[22:24, :]
    shrink = jnp.maximum(0.0, 1.0 - TAU / jnp.sqrt(squares / total_cells + 1e-06))
    shrink_ref[...] = shrink
    for k in range(2):
        column_ref[k * 128 : (k + 1) * 128, :] = jnp.broadcast_to(shrink[k : k + 1, :], (128, 128)).T
    per = column_ref.shape[0] // PROJ_ROWS
    at = pl.multiple_of(lax.rem(share, per) * PROJ_ROWS, PROJ_ROWS)
    proj = column_ref[pl.ds(at, PROJ_ROWS), :] * total[0:PROJ_ROWS, :] / math.sqrt(total_cells)
    rows = jnp.concatenate([column_ref[pl.ds(share + q * SHARES, 1), :] for q in range(4)], axis=0)
    lanes = jnp.where(core == 0, shrink[0:1, :], shrink[1:2, :])
    gram = rows * total[16:20, :] * lanes / total_cells
    tail = jnp.concatenate([gram, jnp.zeros((4, 128), F32)], axis=0)
    mine = jnp.concatenate([proj, tail], axis=0).astype(BF16)
    out_ref[...] = jnp.broadcast_to(mine[None], out_ref.shape)


def scale_kernel(shrink_ref, *refs):
    out_ref = refs[-1]
    for level, m_ref in enumerate(refs[:-1]):
        for k in range(2):
            lanes = slice(k * 128, (k + 1) * 128)
            out_ref[level, :, lanes] = (m_ref[:, lanes].astype(F32) * shrink_ref[k : k + 1, :]).astype(BF16)


def final_kernel(core_ref, own_ref, got_ref, proj_ref, gram_ref, tmp_ref):
    core = core_ref[0]
    members, width, frames = proj_ref.shape
    per = width // PROJ_ROWS
    for ref, half in ((own_ref, core), (got_ref, 1 - core)):
        for tb in range(frames // 256):
            for m in range(members):
                at = pl.multiple_of((half * (frames // 256) + tb) * 128, 128)
                first = (tb * members + m) * per
                proj_ref[m, :, pl.ds(at, 128)] = (
                    ref[first : first + per, 0:PROJ_ROWS, :].astype(F32).reshape(width, 128)
                )
        tmp_ref[...] = ref[:, PROJ_ROWS:SHARE_ROWS, :].astype(F32)
        for q in range(4):
            gram_ref[q * SHARES : (q + 1) * SHARES, pl.ds(pl.multiple_of(half * 128, 128), 128)] = tmp_ref[:, q, :]


VM = pl.BlockSpec(memory_space=pltpu.VMEM)
SM = pl.BlockSpec(memory_space=pltpu.SMEM)


def local(snapshots, coefficients, modes):
    members, levels, rows_x, rows_y, frames = snapshots.shape
    width = modes.shape[3]
    cells = rows_x * rows_y
    local_cells = levels * cells
    sx_axes = ("xh", "y", "c")
    n_sx, n_z = lax.axis_size(sx_axes), lax.axis_size("z")
    total_cells = local_cells * n_sx * n_z
    core = lax.axis_index("c").astype(jnp.int32)
    share = lax.axis_index(GROUP).astype(jnp.int32)
    flat_modes = modes.reshape(local_cells, width)
    series = snapshots.reshape(members, local_cells, frames)

    swap = [(0, 1), (1, 0)]
    own, got = [], []
    for level in range(levels):
        g = grad_level(flat_modes, coefficients, series, level, cells)
        own.append(g)
        got.append(lax.ppermute(g, "ens", swap))

    def shifts(n):
        up = [(i, i + 1) for i in range(n - 1)]
        return up, [(j, i) for i, j in up]

    up, down = shifts(n_sx)
    xlo = lax.ppermute(modes[:, rows_x - 1 :], sx_axes, up)
    xhi = lax.ppermute(modes[:, :1], sx_axes, down)
    up, down = shifts(n_z)
    zlo = lax.ppermute(modes[:, :, rows_y - 1].reshape(levels * rows_x, width), "z", up)
    zhi = lax.ppermute(modes[:, :, 0].reshape(levels * rows_x, width), "z", down)
    halos = (xlo, xhi, zlo, zhi)

    moved, carry = [], None
    for level in range(levels):
        m, *carry = step_level(
            level, levels, core.reshape(1), modes, halos, own[level], got[level], series, carry
        )
        moved.append(m)
    keep, send = carry

    share_shape = jax.ShapeDtypeStruct((SHARES, SHARE_ROWS, 128), BF16)
    other = lax.ppermute(send, "c", swap)
    joined = pl.pallas_call(
        join_kernel, in_specs=[VM, VM], out_specs=VM, out_shape=share_shape, compiler_params=PARAMS
    )(keep, other)
    parts = lax.all_to_all(joined, GROUP, 0, 0)
    spread, shrink = pl.pallas_call(
        functools.partial(reduce_kernel, total_cells),
        in_specs=[SM, VM],
        out_specs=[VM, VM],
        out_shape=[share_shape, jax.ShapeDtypeStruct((2, 128), F32)],
        scratch_shapes=[pltpu.VMEM((width, 128), F32)],
        compiler_params=PARAMS,
    )(jnp.stack([core, share]), parts)
    half = lax.all_to_all(spread, GROUP, 0, 0)
    new_modes = pl.pallas_call(
        scale_kernel,
        in_specs=[VM] * (1 + levels),
        out_specs=VM,
        out_shape=jax.ShapeDtypeStruct((levels, cells, width), BF16),
        compiler_params=PARAMS,
    )(shrink, *moved).reshape(modes.shape)
    other_half = lax.ppermute(half, "c", swap)
    projected, gram = pl.pallas_call(
        final_kernel,
        in_specs=[SM, VM, VM],
        out_specs=[VM, VM],
        out_shape=[
            jax.ShapeDtypeStruct((members, width, frames), F32),
            jax.ShapeDtypeStruct((width, width), F32),
        ],
        scratch_shapes=[pltpu.VMEM((SHARES, 8, 128), F32)],
        compiler_params=PARAMS,
    )(core.reshape(1), half, other_half)
    return (new_modes, gram, projected)


def solution(mesh):
    ens, n_sx, n_sy = (mesh.shape[a] for a in ("ens", "sx", "sy"))
    fine = Mesh(mesh.devices.reshape(ens, 2, n_sx // 4, 2, n_sy), ("ens", "xh", "y", "c", "z"))
    sx = ("xh", "y", "c")
    in_specs = (P("ens", None, sx, "z", None), P("ens", None, None), P(None, sx, "z", None))
    out_specs = (P(None, sx, "z", None), P(), P("ens", None, None))
    return jax.shard_map(local, mesh=fine, in_specs=in_specs, out_specs=out_specs, check_vma=False)
```

time: 1320 us -> 110 us (0.08)
  waiting for transfers between devices: 951 us -> 23.8 us
  blocking collectives: 313 us -> 20.5 us
  starting transfers between devices: 12.1 us -> 42 us
  Pallas kernels: 0 us -> 16.9 us
  between operations: 14.1 us -> 0.85 us
    psum x2 -> x0, waiting for transfers between devices: 946 us -> none  [the longest x1 886 us: local(): gram_sum, proj_sum = lax.psum((raw_gram, raw_proj), ('sx', 'sy'))]
    psum x1 -> x0, blocking collectives: 313 us -> none  [local(): squares = lax.psum(jnp.sum(moved_f * moved_f, axis=0), ('sx', 'sy'))]
    all_to_all x0 -> x1, starting transfers between devices: none -> 23.1 us  [local(): parts = lax.all_to_all(joined, GROUP, 0, 0)]
    all_to_all x0 -> x1, blocking collectives: none -> 20.5 us  [local(): half = lax.all_to_all(spread, GROUP, 0, 0)]
    pallas_call x0 -> x12, Pallas kernels: none -> 16.9 us  [the longest x4 8.99 us: step_level(): pl.pallas_call(functools.partial(step_kernel, level, first, last), grid_s...]
    all_to_all x0 -> x1, waiting for transfers between devices: none -> 15.7 us  [local(): parts = lax.all_to_all(joined, GROUP, 0, 0)]
  transfers between devices with their start and end apart: 6 -> 11, of which waited for: 4 -> 5; matrix products, arithmetic and copies ran while one was open for 0% -> 1% of each run, Pallas kernels for 0% -> 10%
where the time goes in v1:
time: 110 us; the launch traced here: 109 us
  starting transfers between devices  42 us (38%)
  waiting for transfers between devices  23.8 us (22%)
  blocking collectives  20.5 us (19%)
  Pallas kernels  16.9 us (15%)
  local copies, waits for them, and re-layouts  5.2 us (5%)
    all_to_all x1, starting transfers between devices, local(): parts = lax.all_to_all(joined, GROUP, 0, 0)  23.1 us
    all_to_all x1, blocking collectives, local(): half = lax.all_to_all(spread, GROUP, 0, 0)  20.5 us
    all_to_all x1, waiting for transfers between devices, local(): parts = lax.all_to_all(joined, GROUP, 0, 0)  15.7 us
    pallas_call x4, Pallas kernels, step_level(): pl.pallas_call(functools.partial(step_kernel, level, first, last), grid_s...  8.99 us
    ppermute x1, waiting for transfers between devices, local(): xhi = lax.ppermute(modes[:, :1], sx_axes, down)  4.86 us
    unnamed x14, local copies, waits for them, and re-layouts  4.48 us
    ppermute x4, starting transfers between devices, local(): got.append(lax.ppermute(g, 'ens', swap))  4.11 us
    ppermute x1, starting transfers between devices, local(): xlo = lax.ppermute(modes[:, rows_x - 1:], sx_axes, up)  4.03 us
  transfers between devices with their start and end apart: 11, of which 5 were waited for; matrix products, arithmetic and copies ran while one was open for 1% of the time, Pallas kernels for 10%

profile of v1, /device:TPU:1, one launch (start us, length us, event | category | flops | bytes accessed | tf_op | source)
XLA Modules:
  0.0 109.3 jit_solution(2105850749303071343)
XLA Ops:
  0.6 0.0 copy-start
  0.6 2.2 %copy-done = bf16[2,4,8,64,512]{4,3,2,1,0:T(8,128)(2,1)S(1)} copy-done((bf16[2,4,8,64,512]{4,3,2,1,0:T(8,128)(2,1)S(1)}, bf16[2,4,8,64,512]{4,3,2,1,0:T(8,128)(2,1)}, u32[]{:S(2)}) %copy-start) | copy-done | bytes 4194328
  2.8 0.0 copy-start.1
  2.8 1.2 %copy-done.1 = bf16[4,8,64,256]{3,2,1,0:T(8,128)(2,1)S(1)} copy-done((bf16[4,8,64,256]{3,2,1,0:T(8,128)(2,1)S(1)}, bf16[4,8,64,256]{3,2,1,0:T(8,128)(2,1)}, u32[]{:S(2)}) %copy-start.1) | copy-done | bytes 1048600
  4.0 0.0 copy-start.3
  4.0 1.0 copy-done.3
  5.1 0.9 shard_map.61.refs_6_
  6.0 2.1 %collective-permute-start.7 = (bf16[512,256]{1,0:T(8,128)(2,1)S(1)}, bf16[512,256]{1,0:T(8,128)(2,1)S(1)}, u32[]{:S(2)}, u32[]{:S(2)}) collective-permute-start(bf16[512,256]{1,0:T(8,128)(2,1)S(1)} %shard_map.61.refs_6_), channel_id=1, source_target_pairs={{0,128},{128,0},{1,129},{129,1},{2,130},{130,2},{3,131},{131,3},{4... | collective-permute-start | bytes 786440 | tf_op jit(solution)/shard_map/ppermute | solution.py:259
  8.2 0.7 fusion.1
  8.8 4.0 %collective-permute-start = (bf16[4,1,64,256]{3,2,1,0:T(8,128)(2,1)S(1)}, bf16[4,1,64,256]{3,2,1,0:T(8,128)(2,1)S(1)}, u32[]{:S(2)}, u32[]{:S(2)}) collective-permute-start(bf16[4,1,64,256]{3,2,1,0:T(8,128)(2,1)S(1)} %get-tuple-element.44), channel_id=1, source_target_pairs={{0,8},{8,16},{16,24},{24,32},{32,40},{40,48},{48,56},{56,64},{64,7... | collective-permute-start | bytes 393224 | tf_op jit(solution)/shard_map/ppermute | solution.py:266
  12.9 0.1 fusion
  13.0 3.5 %collective-permute-start.2 = (bf16[32,256]{1,0:T(8,128)(2,1)S(1)}, bf16[32,256]{1,0:T(8,128)(2,1)S(1)}, u32[]{:S(2)}, u32[]{:S(2)}) collective-permute-start(bf16[32,256]{1,0:T(8,128)(2,1)S(1)} %bitcast.25), channel_id=1, source_target_pairs={{0,1},{1,2},{2,3},{3,4},{4,5},{5,6},{6,7},{8,9},{9,10},{10,11},{11... | collective-permute-start | bytes 49160 | tf_op jit(solution)/shard_map/ppermute | solution.py:269
  16.5 1.3 %collective-permute-start.3 = (bf16[32,256]{1,0:T(8,128)(2,1)S(1)}, bf16[32,256]{1,0:T(8,128)(2,1)S(1)}, u32[]{:S(2)}, u32[]{:S(2)}) collective-permute-start(bf16[32,256]{1,0:T(8,128)(2,1)S(1)} %bitcast.24), channel_id=1, source_target_pairs={{1,0},{2,1},{3,2},{4,3},{5,4},{6,5},{7,6},{9,8},{10,9},{11,10},{12... | collective-permute-start | bytes 49160 | tf_op jit(solution)/shard_map/ppermute | solution.py:270
  17.8 1.0 shard_map.60.refs_6_
  18.8 0.3 collective-permute-start.6
  19.1 0.9 shard_map.59.refs_6_
  20.1 0.0 copy-start.2
  20.1 0.0 collective-permute-done.2.refs_4_
  20.1 1.3 %collective-permute-start.5 = (bf16[512,256]{1,0:T(8,128)(2,1)S(1)}, bf16[512,256]{1,0:T(8,128)(2,1)S(1)}, u32[]{:S(2)}, u32[]{:S(2)}) collective-permute-start(bf16[512,256]{1,0:T(8,128)(2,1)S(1)} %shard_map.59.refs_6_), channel_id=1, source_target_pairs={{0,128},{128,0},{1,129},{129,1},{2,130},{130,2},{3,131},{131,3},{4... | collective-permute-start | bytes 786440 | tf_op jit(solution)/shard_map/ppermute | solution.py:259
  21.4 0.9 shard_map.58.refs_6_
  22.4 0.0 collective-permute-done.3.refs_5_
  22.4 0.3 collective-permute-start.4
  22.7 0.0 collective-permute-done.refs_2_
  22.7 1.9 %collective-permute-start.1 = (bf16[4,1,64,256]{3,2,1,0:T(8,128)(2,1)}, bf16[4,1,64,256]{3,2,1,0:T(8,128)(2,1)S(1)}, u32[]{:S(2)}, u32[]{:S(2)}) collective-permute-start(bf16[4,1,64,256]{3,2,1,0:T(8,128)(2,1)} %get-tuple-element.43), channel_id=1, source_target_pairs={{8,0},{16,8},{24,16},{32,24},{40,32},{48,40},{56,48},{64,56},{72,6... | collective-permute-start | bytes 393224 | tf_op jit(solution)/shard_map/ppermute | solution.py:267
  24.6 4.9 %collective-permute-done.1.refs_3_ = bf16[4,1,64,256]{3,2,1,0:T(8,128)(2,1)S(1)} collective-permute-done((bf16[4,1,64,256]{3,2,1,0:T(8,128)(2,1)}, bf16[4,1,64,256]{3,2,1,0:T(8,128)(2,1)S(1)}, u32[]{:S(2)}, u32[]{:S(2)}) %collective-permute-start.1) | collective-permute-done | bytes 131104 | tf_op jit(solution)/shard_map/ppermute | solution.py:267
  29.5 0.0 collective-permute-done.7.refs_7_
  29.5 0.0 copy-done.2
  29.5 2.1 %shard_map.62 = (bf16[512,256]{1,0:T(8,128)(2,1)S(1)}, f32[2,256,512]{2,1,0:T(8,128)S(1)}, f32[256,256]{1,0:T(8,128)S(1)}, f32[1,256]{1,0:T(1,128)S(1)}) custom-call(s32[1]{0:T(128)} %bitcast.refs_0_.core_ref, bf16[4,8,64,256]{3,2,1,0:T(8,128)(2,1)S(1)} %copy-done.2, bf16[4,1,64,256]{3,2,1,0:T(8,128)(2,1)S(1)} %collective-permute-done.refs_2_, ...), custom_call_target="tpu_custom_call" | custom-call | flops 335544320 | bytes 2097152 | tf_op jit(solution)/shard_map/pallas_call | solution.py:160
  31.6 0.0 copy-start.4
  31.6 0.0 collective-permute-done.6.refs_7_
  31.6 2.2 %shard_map.63 = (bf16[512,256]{1,0:T(8,128)(2,1)S(1)}, f32[2,256,512]{2,1,0:T(8,128)S(1)}, f32[256,256]{1,0:T(8,128)S(1)}, f32[1,256]{1,0:T(1,128)S(1)}) custom-call(s32[1]{0:T(128)} %bitcast.refs_0_.core_ref, bf16[4,8,64,256]{3,2,1,0:T(8,128)(2,1)S(1)} %copy-done.2, bf16[4,1,64,256]{3,2,1,0:T(8,128)(2,1)S(1)} %collective-permute-done.refs_2_, ...), custom_call_target="tpu_custom_call" | custom-call | flops 335544320 | bytes 2097152 | tf_op jit(solution)/shard_map/pallas_call | solution.py:160
  33.8 0.0 collective-permute-done.5.refs_7_
  33.8 2.1 %shard_map.64 = (bf16[512,256]{1,0:T(8,128)(2,1)S(1)}, f32[2,256,512]{2,1,0:T(8,128)S(1)}, f32[256,256]{1,0:T(8,128)S(1)}, f32[1,256]{1,0:T(1,128)S(1)}) custom-call(s32[1]{0:T(128)} %bitcast.refs_0_.core_ref, bf16[4,8,64,256]{3,2,1,0:T(8,128)(2,1)S(1)} %copy-done.2, bf16[4,1,64,256]{3,2,1,0:T(8,128)(2,1)S(1)} %collective-permute-done.refs_2_, ...), custom_call_target="tpu_custom_call" | custom-call | flops 335544320 | bytes 2097152 | tf_op jit(solution)/shard_map/pallas_call | solution.py:160
  35.9 0.0 copy-done.4
  35.9 1.3 %collective-permute-done.4.refs_7_ = bf16[512,256]{1,0:T(8,128)(2,1)S(1)} collective-permute-done((bf16[512,256]{1,0:T(8,128)(2,1)S(1)}, bf16[512,256]{1,0:T(8,128)(2,1)S(1)}, u32[]{:S(2)}, u32[]{:S(2)}) %collective-permute-start.4) | collective-permute-done | bytes 262176 | tf_op jit(solution)/shard_map/ppermute | solution.py:259
  37.3 0.0 copy-start.5
  37.3 2.6 %shard_map.65 = (bf16[512,256]{1,0:T(8,128)(2,1)S(1)}, bf16[64,24,128]{2,1,0:T(8,128)(2,1)S(1)}, bf16[64,24,128]{2,1,0:T(8,128)(2,1)S(1)}) custom-call(s32[1]{0:T(128)} %bitcast.refs_0_.core_ref, bf16[4,8,64,256]{3,2,1,0:T(8,128)(2,1)S(1)} %copy-done.2, bf16[4,1,64,256]{3,2,1,0:T(8,128)(2,1)S(1)} %collective-permute-done.refs_2_, ...), custom_call_target="tpu_custom_call" | custom-call | flops 335544320 | bytes 2097152 | tf_op jit(solution)/shard_map/pallas_call | solution.py:160
  39.9 0.1 collective-permute-start.8
  40.0 1.7 %collective-permute-done.8.got_ref = bf16[64,24,128]{2,1,0:T(8,128)(2,1)S(1)} collective-permute-done((bf16[64,24,128]{2,1,0:T(8,128)(2,1)S(1)}, bf16[64,24,128]{2,1,0:T(8,128)(2,1)S(1)}, u32[]{:S(2)}, u32[]{:S(2)}) %collective-permute-start.8) | collective-permute-done | bytes 393248 | tf_op jit(solution)/shard_map/ppermute | solution.py:282
  41.7 0.9 shard_map.66
  42.6 23.1 %all-to-all-start = ((bf16[64,24,128]{2,1,0:T(8,128)(2,1)}), bf16[64,24,128]{2,1,0:T(8,128)(2,1)S(1)}, u32[]{:S(2)}, u32[]{:S(2)}) async-start(bf16[64,24,128]{2,1,0:T(8,128)(2,1)} %shard_map.66), calls=%async_computation | async-start | bytes 786432 | tf_op jit(solution)/shard_map/all_to_all | solution.py:286
  65.7 0.1 pad_add_fusion.at_ref
  65.8 15.7 %all-to-all-done.in_ref = bf16[64,24,128]{2,1,0:T(8,128)(2,1)S(1)} async-done(((bf16[64,24,128]{2,1,0:T(8,128)(2,1)}), bf16[64,24,128]{2,1,0:T(8,128)(2,1)S(1)}, u32[]{:S(2)}, u32[]{:S(2)}) %all-to-all-start) | async-done | bytes 393248 | tf_op jit(solution)/shard_map/all_to_all | solution.py:286
  81.6 0.8 shard_map.67
  82.3 20.5 %all_to_all.10.own_ref = bf16[64,24,128]{2,1,0:T(8,128)(2,1)S(1)} all-to-all(bf16[64,24,128]{2,1,0:T(8,128)(2,1)S(1)} %get-tuple-element.38), channel_id=1, replica_groups=mesh['ens'=2,'xh'=2,'y'=4,'c'=2,'z'=8] {'xh','y','z'}, dimensions={0} | all-to-all | bytes 786432 | tf_op jit(solution)/shard_map/all_to_all | solution.py:295
  102.8 3.9 %collective-permute-start.9 = (bf16[64,24,128]{2,1,0:T(8,128)(2,1)S(1)}, bf16[64,24,128]{2,1,0:T(8,128)(2,1)S(1)}, u32[]{:S(2)}, u32[]{:S(2)}) collective-permute-start(bf16[64,24,128]{2,1,0:T(8,128)(2,1)S(1)} %all_to_all.10.own_ref), channel_id=1, source_target_pairs={{0,8},{8,0},{1,9},{9,1},{2,10},{10,2},{3,11},{11,3},{4,12},{12,4},... | collective-permute-start | bytes 1179656 | tf_op jit(solution)/shard_map/ppermute | solution.py:303
  106.7 0.0 copy-done.5
  106.7 1.2 %shard_map.68 = bf16[4,512,256]{2,1,0:T(8,128)(2,1)} custom-call(f32[2,128]{1,0:T(2,128)S(1)} %get-tuple-element.33.shrink_ref, bf16[512,256]{1,0:T(8,128)(2,1)S(1)} %copy-done.5, bf16[512,256]{1,0:T(8,128)(2,1)S(1)} %get-tuple-element.35.refs_1_, bf16[512,256]{1,0:T(8,128)(2,1)S(1)} %get-tuple-element.36.refs_2_, bf16[512,256]{1,0:T(8,128)(2,1)S(1)} %get-tuple-element.37.refs_3_), custom_call_target="tpu_custom_call" | custom-call | tf_op jit(solution)/shard_map/pallas_call | solution.py:296
  107.9 0.2 collective-permute-done.9.got_ref
  108.1 1.3 %shard_map.69 = (f32[2,256,512]{2,1,0:T(8,128)}, f32[256,256]{1,0:T(8,128)}) custom-call(s32[1]{0:T(128)} %bitcast.refs_0_.core_ref, bf16[64,24,128]{2,1,0:T(8,128)(2,1)S(1)} %all_to_all.10.own_ref, bf16[64,24,128]{2,1,0:T(8,128)(2,1)S(1)} %collective-permute-done.9.got_ref), custom_call_target="tpu_custom_call" | custom-call | tf_op jit(solution)/shard_map/pallas_call | solution.py:304
  (2 shorter events, 0.0 us)
Async XLA Ops:
  0.6 2.2 %copy-start = (bf16[2,4,8,64,512]{4,3,2,1,0:T(8,128)(2,1)S(1)}, bf16[2,4,8,64,512]{4,3,2,1,0:T(8,128)(2,1)}, u32[]{:S(2)}) copy-start(bf16[2,4,8,64,512]{4,3,2,1,0:T(8,128)(2,1)} %param.3) | copy-start | bytes 12582916
  2.8 1.2 %copy-start.1 = (bf16[4,8,64,256]{3,2,1,0:T(8,128)(2,1)S(1)}, bf16[4,8,64,256]{3,2,1,0:T(8,128)(2,1)}, u32[]{:S(2)}) copy-start(bf16[4,8,64,256]{3,2,1,0:T(8,128)(2,1)} %refs_1_.7) | copy-start | bytes 3145732
  4.0 1.0 copy-start.3
  6.0 23.5 %collective-permute-start.7 = (bf16[512,256]{1,0:T(8,128)(2,1)S(1)}, bf16[512,256]{1,0:T(8,128)(2,1)S(1)}, u32[]{:S(2)}, u32[]{:S(2)}) collective-permute-start(bf16[512,256]{1,0:T(8,128)(2,1)S(1)} %shard_map.61.refs_6_), channel_id=1, source_target_pairs={{0,128},{128,0},{1,129},{129,1},{2,130},{130,2},{3,131},{131,3},{4... | collective-permute-start | bytes 786440 | tf_op jit(solution)/shard_map/ppermute | solution.py:259
  8.8 13.9 %collective-permute-start = (bf16[4,1,64,256]{3,2,1,0:T(8,128)(2,1)S(1)}, bf16[4,1,64,256]{3,2,1,0:T(8,128)(2,1)S(1)}, u32[]{:S(2)}, u32[]{:S(2)}) collective-permute-start(bf16[4,1,64,256]{3,2,1,0:T(8,128)(2,1)S(1)} %get-tuple-element.44), channel_id=1, source_target_pairs={{0,8},{8,16},{16,24},{24,32},{32,40},{40,48},{48,56},{56,64},{64,7... | collective-permute-start | bytes 393224 | tf_op jit(solution)/shard_map/ppermute | solution.py:266
  13.0 7.1 %collective-permute-start.2 = (bf16[32,256]{1,0:T(8,128)(2,1)S(1)}, bf16[32,256]{1,0:T(8,128)(2,1)S(1)}, u32[]{:S(2)}, u32[]{:S(2)}) collective-permute-start(bf16[32,256]{1,0:T(8,128)(2,1)S(1)} %bitcast.25), channel_id=1, source_target_pairs={{0,1},{1,2},{2,3},{3,4},{4,5},{5,6},{6,7},{8,9},{9,10},{10,11},{11... | collective-permute-start | bytes 49160 | tf_op jit(solution)/shard_map/ppermute | solution.py:269
  16.5 5.8 %collective-permute-start.3 = (bf16[32,256]{1,0:T(8,128)(2,1)S(1)}, bf16[32,256]{1,0:T(8,128)(2,1)S(1)}, u32[]{:S(2)}, u32[]{:S(2)}) collective-permute-start(bf16[32,256]{1,0:T(8,128)(2,1)S(1)} %bitcast.24), channel_id=1, source_target_pairs={{1,0},{2,1},{3,2},{4,3},{5,4},{6,5},{7,6},{9,8},{10,9},{11,10},{12... | collective-permute-start | bytes 49160 | tf_op jit(solution)/shard_map/ppermute | solution.py:270
  18.8 12.8 %collective-permute-start.6 = (bf16[512,256]{1,0:T(8,128)(2,1)S(1)}, bf16[512,256]{1,0:T(8,128)(2,1)S(1)}, u32[]{:S(2)}, u32[]{:S(2)}) collective-permute-start(bf16[512,256]{1,0:T(8,128)(2,1)S(1)} %shard_map.60.refs_6_), channel_id=1, source_target_pairs={{0,128},{128,0},{1,129},{129,1},{2,130},{130,2},{3,131},{131,3},{4... | collective-permute-start | bytes 786440 | tf_op jit(solution)/shard_map/ppermute | solution.py:259
  20.1 9.4 %copy-start.2 = (bf16[4,8,64,256]{3,2,1,0:T(8,128)(2,1)S(1)}, bf16[4,8,64,256]{3,2,1,0:T(8,128)(2,1)}, u32[]{:S(2)}) copy-start(bf16[4,8,64,256]{3,2,1,0:T(8,128)(2,1)} %refs_1_.7) | copy-start | bytes 3145732
  20.1 13.7 %collective-permute-start.5 = (bf16[512,256]{1,0:T(8,128)(2,1)S(1)}, bf16[512,256]{1,0:T(8,128)(2,1)S(1)}, u32[]{:S(2)}, u32[]{:S(2)}) collective-permute-start(bf16[512,256]{1,0:T(8,128)(2,1)S(1)} %shard_map.59.refs_6_), channel_id=1, source_target_pairs={{0,128},{128,0},{1,129},{129,1},{2,130},{130,2},{3,131},{131,3},{4... | collective-permute-start | bytes 786440 | tf_op jit(solution)/shard_map/ppermute | solution.py:259
  22.4 14.9 %collective-permute-start.4 = (bf16[512,256]{1,0:T(8,128)(2,1)S(1)}, bf16[512,256]{1,0:T(8,128)(2,1)S(1)}, u32[]{:S(2)}, u32[]{:S(2)}) collective-permute-start(bf16[512,256]{1,0:T(8,128)(2,1)S(1)} %shard_map.58.refs_6_), channel_id=1, source_target_pairs={{0,128},{128,0},{1,129},{129,1},{2,130},{130,2},{3,131},{131,3},{4... | collective-permute-start | bytes 786440 | tf_op jit(solution)/shard_map/ppermute | solution.py:259
  22.7 6.8 %collective-permute-start.1 = (bf16[4,1,64,256]{3,2,1,0:T(8,128)(2,1)}, bf16[4,1,64,256]{3,2,1,0:T(8,128)(2,1)S(1)}, u32[]{:S(2)}, u32[]{:S(2)}) collective-permute-start(bf16[4,1,64,256]{3,2,1,0:T(8,128)(2,1)} %get-tuple-element.43), channel_id=1, source_target_pairs={{8,0},{16,8},{24,16},{32,24},{40,32},{48,40},{56,48},{64,56},{72,6... | collective-permute-start | bytes 393224 | tf_op jit(solution)/shard_map/ppermute | solution.py:267
  31.6 4.3 %copy-start.4 = (bf16[512,256]{1,0:T(8,128)(2,1)}, bf16[512,256]{1,0:T(8,128)(2,1)S(1)}, u32[]{:S(2)}) copy-start(bf16[512,256]{1,0:T(8,128)(2,1)S(1)} %get-tuple-element.34.refs_0_) | copy-start | bytes 786436
  37.3 69.5 %copy-start.5 = (bf16[512,256]{1,0:T(8,128)(2,1)S(1)}, bf16[512,256]{1,0:T(8,128)(2,1)}, u32[]{:S(2)}) copy-start(bf16[512,256]{1,0:T(8,128)(2,1)} %copy-done.4) | copy-start | bytes 786436
  39.9 1.8 %collective-permute-start.8 = (bf16[64,24,128]{2,1,0:T(8,128)(2,1)S(1)}, bf16[64,24,128]{2,1,0:T(8,128)(2,1)S(1)}, u32[]{:S(2)}, u32[]{:S(2)}) collective-permute-start(bf16[64,24,128]{2,1,0:T(8,128)(2,1)S(1)} %get-tuple-element.32), channel_id=1, source_target_pairs={{0,8},{8,0},{1,9},{9,1},{2,10},{10,2},{3,11},{11,3},{4,12},{12,4},... | collective-permute-start | bytes 1179656 | tf_op jit(solution)/shard_map/ppermute | solution.py:282
  42.6 38.9 %all-to-all-start = ((bf16[64,24,128]{2,1,0:T(8,128)(2,1)}), bf16[64,24,128]{2,1,0:T(8,128)(2,1)S(1)}, u32[]{:S(2)}, u32[]{:S(2)}) async-start(bf16[64,24,128]{2,1,0:T(8,128)(2,1)} %shard_map.66), calls=%async_computation | async-start | bytes 786432 | tf_op jit(solution)/shard_map/all_to_all | solution.py:286
  102.8 5.3 %collective-permute-start.9 = (bf16[64,24,128]{2,1,0:T(8,128)(2,1)S(1)}, bf16[64,24,128]{2,1,0:T(8,128)(2,1)S(1)}, u32[]{:S(2)}, u32[]{:S(2)}) collective-permute-start(bf16[64,24,128]{2,1,0:T(8,128)(2,1)S(1)} %all_to_all.10.own_ref), channel_id=1, source_target_pairs={{0,8},{8,0},{1,9},{9,1},{2,10},{10,2},{3,11},{11,3},{4,12},{12,4},... | collective-permute-start | bytes 1179656 | tf_op jit(solution)/shard_map/ppermute | solution.py:303

commit v2 on v1

v2 whole, which is shorter than its diff:
```python
import functools
import math

import jax
import jax.numpy as jnp
from jax import lax
from jax.experimental import pallas as pl
from jax.experimental.pallas import tpu as pltpu
from jax.sharding import Mesh, PartitionSpec as P

ETA = 0.25
LAM = 0.5
TAU = 0.4

F32 = jnp.float32
BF16 = jnp.bfloat16
VMEM_LIMIT = 40 * 1024 * 1024
PARAMS = pltpu.CompilerParams(vmem_limit_bytes=VMEM_LIMIT)

SX = ("xh", "y", "c")
PLANE = ("xh", "y")
PARTS = 8
PROJ_ROWS = 128
GRAM_ROWS = 32
SUM_ROWS = PROJ_ROWS + GRAM_ROWS
PART_ROWS = SUM_ROWS + 8

VM = pl.BlockSpec(memory_space=pltpu.VMEM)
SM = pl.BlockSpec(memory_space=pltpu.SMEM)
HBM = pl.BlockSpec(memory_space=pltpu.HBM)


def gradient(m, coefficients, series):
    acc = None
    for e in range(len(coefficients)):
        c = coefficients[e]()
        fitted = jnp.dot(m, c, preferred_element_type=F32)
        misfit = (fitted - series[e]().astype(F32)).astype(BF16)
        term = lax.dot_general(misfit, c, (((1,), (1,)), ((), ())), preferred_element_type=F32)
        acc = term if acc is None else acc + term
    return acc.astype(BF16)


def first_grad_kernel(cells, m_hbm, c_hbm, x_hbm, g_ref, m_ref, c_ref, x_ref, sems):
    members = c_ref.shape[0]
    rows = pl.ds(0, cells)
    copies = [pltpu.make_async_copy(m_hbm.at[rows], m_ref, sems.at[0])]
    for e in range(members):
        copies.append(pltpu.make_async_copy(c_hbm.at[e], c_ref.at[e], sems.at[1 + 2 * e]))
        copies.append(pltpu.make_async_copy(x_hbm.at[e, rows], x_ref.at[e], sems.at[2 + 2 * e]))
    for copy in copies:
        copy.start()
    copies[0].wait()

    def ready(copy, ref, e):
        def load():
            copy.wait()
            return ref[e]

        return load

    g_ref[...] = gradient(
        m_ref[...],
        [ready(copies[1 + 2 * e], c_ref, e) for e in range(members)],
        [ready(copies[2 + 2 * e], x_ref, e) for e in range(members)],
    )


def grad_kernel(level, m_ref, c_ref, x_ref, g_ref):
    cells = g_ref.shape[0]
    members = c_ref.shape[0]
    rows = slice(level * cells, (level + 1) * cells)

    def part(ref, *at):
        return lambda: ref[at]

    g_ref[...] = gradient(
        m_ref[rows, :],
        [part(c_ref, e) for e in range(members)],
        [part(x_ref, e, rows) for e in range(members)],
    )


def grad_level(flat_modes, coefficients, series, level, cells):
    members, _, frames = series.shape
    width = flat_modes.shape[1]
    if level == 0:
        kernel, specs = functools.partial(first_grad_kernel, cells), [HBM, HBM, HBM]
        scratch = [
            pltpu.VMEM((cells, width), BF16),
            pltpu.VMEM(coefficients.shape, BF16),
            pltpu.VMEM((members, cells, frames), BF16),
            pltpu.SemaphoreType.DMA((1 + 2 * members,)),
        ]
    else:
        kernel, specs, scratch = functools.partial(grad_kernel, level), [VM, VM, VM], []
    return pl.pallas_call(
        kernel,
        in_specs=specs,
        out_specs=VM,
        out_shape=jax.ShapeDtypeStruct((cells, width), BF16),
        scratch_shapes=scratch,
        compiler_params=PARAMS,
        cost_estimate=pl.CostEstimate(
            flops=4 * members * cells * frames * width,
            bytes_accessed=2 * cells * (2 * width + members * frames) + 2 * members * width * frames,
            transcendentals=0,
        ),
    )(flat_modes, coefficients, series)


def moved_of(level, at_ref, m_ref, xa_ref, xb_ref, za_ref, zb_ref, own_ref, got_ref):
    _, rows_x, rows_y, width = m_ref.shape
    f = m_ref[level].astype(F32)
    lower = at_ref[0] == 0
    even = at_ref[1] == 0
    xa, xb = xa_ref[level].astype(F32), xb_ref[level].astype(F32)
    rows = slice(level * rows_x, (level + 1) * rows_x)
    za, zb = za_ref[rows, :].astype(F32), zb_ref[rows, :].astype(F32)
    up = jnp.concatenate([jnp.where(lower, xb, xa), f[:-1]], axis=0)
    down = jnp.concatenate([f[1:], jnp.where(lower, xa, xb)], axis=0)
    at = lax.broadcasted_iota(jnp.int32, (rows_x, rows_y, width), 1)
    zlo = jnp.broadcast_to(jnp.where(even, zb, za)[:, None, :], f.shape)
    zhi = jnp.broadcast_to(jnp.where(even, za, zb)[:, None, :], f.shape)
    left = jnp.where(at == 0, zlo, pltpu.roll(f, 1, 1))
    right = jnp.where(at == rows_y - 1, zhi, pltpu.roll(f, rows_y - 1, 1))
    bent = 4.0 * f - (down + up + right + left)
    cells = rows_x * rows_y
    grad = own_ref[...].astype(F32) + got_ref[...].astype(F32)
    return (f.reshape(cells, width) - ETA * (grad + LAM * bent.reshape(cells, width))).astype(BF16)


def split_squares(squares, rows):
    high = squares.astype(BF16).astype(F32)
    return jnp.concatenate([high, squares - high, jnp.zeros((rows - 4, 128), F32)], axis=0)


def emit(out_ref, half, proj_ref, gram_ref, squares):
    members = proj_ref.shape[0]
    for j in range(PARTS):
        tb, m, r = j // 4, (j // 2) % members, j % 2
        at = pl.multiple_of((half * 2 + tb) * 128, 128)
        block = proj_ref[m, r * 128 : (r + 1) * 128, pl.ds(at, 128)]
        out_ref[j, 0:PROJ_ROWS, :] = block.astype(BF16)
        at = pl.multiple_of(half * 128, 128)
        block = gram_ref[j * GRAM_ROWS : (j + 1) * GRAM_ROWS, pl.ds(at, 128)]
        out_ref[j, PROJ_ROWS:SUM_ROWS, :] = block.astype(BF16)
        out_ref[j, SUM_ROWS:PART_ROWS, :] = squares


def step_kernel(level, first, last, *refs):
    inputs, refs = refs[:8], refs[8:]
    x_ref, refs = refs[0], refs[1:]
    if not first:
        (proj_in, gram_in, squares_in), refs = refs[:3], refs[3:]
    if last:
        moved_ref, keep_ref, send_ref, proj_ref, gram_ref = refs
    else:
        moved_ref, proj_ref, gram_ref, squares_ref = refs
    moved = moved_of(level, *inputs)
    moved_ref[...] = moved
    cells = moved.shape[0]
    rows = slice(level * cells, (level + 1) * cells)
    wide = moved.astype(F32)
    squares = jnp.sum(wide * wide, axis=0, keepdims=True)
    if not first:
        squares = squares + squares_in[...]
    turned = moved.T
    gram = jnp.dot(turned, moved, preferred_element_type=F32)
    gram_ref[...] = gram if first else gram_in[...] + gram
    for e in range(x_ref.shape[0]):
        proj = jnp.dot(turned, x_ref[e, rows, :], preferred_element_type=F32)
        proj_ref[e] = proj if first else proj_in[e] + proj
    if last:
        core = inputs[0][0]
        pair = jnp.concatenate([squares[:, 0:128], squares[:, 128:256]], axis=0)
        packed = split_squares(pair, 8).astype(BF16)
        emit(send_ref, 1 - core, proj_ref, gram_ref, packed)
        emit(keep_ref, core, proj_ref, gram_ref, packed)
    else:
        squares_ref[...] = squares


def step_level(level, levels, place, modes, halos, own, got, series, carry):
    members, _, frames = series.shape
    _, rows_x, rows_y, width = modes.shape
    cells = rows_x * rows_y
    first, last = level == 0, level == levels - 1
    args = [place, modes, *halos, own, got, series]
    if not first:
        args += list(carry)
    sums = [
        jax.ShapeDtypeStruct((members, width, frames), F32),
        jax.ShapeDtypeStruct((width, width), F32),
        jax.ShapeDtypeStruct((1, width), F32),
    ]
    outs = [jax.ShapeDtypeStruct((cells, width), BF16)]
    scratch, aliases = [], {}
    if last:
        outs += [jax.ShapeDtypeStruct((PARTS, PART_ROWS, 128), BF16)] * 2
        scratch = [pltpu.VMEM(s.shape, F32) for s in sums[:2]]
    else:
        outs += sums
        if not first:
            aliases = {9 + i: 1 + i for i in range(3)}
    return pl.pallas_call(
        functools.partial(step_kernel, level, first, last),
        in_specs=[SM] + [VM] * (len(args) - 1),
        out_specs=[VM] * len(outs),
        out_shape=outs,
        scratch_shapes=scratch,
        input_output_aliases=aliases,
        compiler_params=PARAMS,
        cost_estimate=pl.CostEstimate(
            flops=2 * cells * width * (width + members * frames),
            bytes_accessed=2 * cells * (4 * width + members * frames),
            transcendentals=0,
        ),
    )(*args)


def whole_squares(part):
    return part[SUM_ROWS : SUM_ROWS + 2, :] + part[SUM_ROWS + 2 : SUM_ROWS + 4, :]


def join_kernel(keep_ref, got_ref, out_ref):
    out_ref[:, 0:SUM_ROWS, :] = (
        keep_ref[:, 0:SUM_ROWS, :].astype(F32) + got_ref[:, 0:SUM_ROWS, :].astype(F32)
    ).astype(BF16)
    tail = keep_ref[0, SUM_ROWS:PART_ROWS, :].astype(F32) + got_ref[0, SUM_ROWS:PART_ROWS, :].astype(F32)
    packed = split_squares(tail[0:2, :] + tail[2:4, :], 8).astype(BF16)
    for j in range(PARTS):
        out_ref[j, SUM_ROWS:PART_ROWS, :] = packed


def gather_sum(in_ref):
    total = in_ref[0].astype(F32)
    for j in range(1, PARTS):
        total = total + in_ref[j].astype(F32)
    return total


def plane_kernel(in_ref, out_ref):
    total = gather_sum(in_ref)
    packed = split_squares(whole_squares(total), 8)
    mine = jnp.concatenate([total[0:SUM_ROWS, :], packed], axis=0).astype(BF16)
    for j in range(PARTS):
        out_ref[j] = mine


def reduce_kernel(total_cells, at_ref, in_ref, out_ref, shrink_ref, column_ref):
    core, part = at_ref[0], at_ref[2]
    total = gather_sum(in_ref)
    squares = whole_squares(total)
    shrink = jnp.maximum(0.0, 1.0 - TAU / jnp.sqrt(squares / total_cells + 1e-06))
    shrink_ref[...] = shrink
    for k in range(2):
        column_ref[k * 128 : (k + 1) * 128, :] = jnp.broadcast_to(shrink[k : k + 1, :], (128, 128)).T
    at = pl.multiple_of(lax.rem(part, 2) * 128, 128)
    proj = column_ref[pl.ds(at, 128), :] * total[0:PROJ_ROWS, :] * (1.0 / math.sqrt(total_cells))
    at = pl.multiple_of(part * GRAM_ROWS, GRAM_ROWS)
    lanes = jnp.where(core == 0, shrink[0:1, :], shrink[1:2, :])
    gram = column_ref[pl.ds(at, GRAM_ROWS), :] * total[PROJ_ROWS:SUM_ROWS, :] * lanes * (1.0 / total_cells)
    mine = jnp.concatenate([proj, gram], axis=0).astype(BF16)
    for j in range(PARTS):
        out_ref[j] = mine


def scale_kernel(shrink_ref, *refs):
    out_ref = refs[-1]
    for level, m_ref in enumerate(refs[:-1]):
        for k in range(2):
            lanes = slice(k * 128, (k + 1) * 128)
            out_ref[level, :, lanes] = (m_ref[:, lanes].astype(F32) * shrink_ref[k : k + 1, :]).astype(BF16)


def final_kernel(at_ref, own_ref, got_ref, proj_ref, gram_ref):
    core = at_ref[0]
    members = proj_ref.shape[0]
    for ref, half in ((own_ref, core), (got_ref, 1 - core)):
        for j in range(PARTS):
            tb, m, r = j // 4, (j // 2) % members, j % 2
            at = pl.multiple_of((half * 2 + tb) * 128, 128)
            proj_ref[m, r * 128 : (r + 1) * 128, pl.ds(at, 128)] = ref[j, 0:PROJ_ROWS, :].astype(F32)
            at = pl.multiple_of(half * 128, 128)
            gram_ref[j * GRAM_ROWS : (j + 1) * GRAM_ROWS, pl.ds(at, 128)] = (
                ref[j, PROJ_ROWS:SUM_ROWS, :].astype(F32)
            )


def both_ways(pairs):
    return [p for i, j in pairs for p in ((i, j), (j, i))]


def local(snapshots, coefficients, modes):
    members, levels, rows_x, rows_y, frames = snapshots.shape
    width = modes.shape[3]
    cells = rows_x * rows_y
    local_cells = levels * cells
    n_sx, n_z = lax.axis_size(SX), lax.axis_size("z")
    total_cells = local_cells * n_sx * n_z
    core = lax.axis_index("c").astype(jnp.int32)
    parity = lax.axis_index("z").astype(jnp.int32) % 2
    part = lax.axis_index(PLANE).astype(jnp.int32)
    place = jnp.stack([core, parity, part])
    flat_modes = modes.reshape(local_cells, width)
    series = snapshots.reshape(members, local_cells, frames)
    swap = [(0, 1), (1, 0)]

    own, got = [], []
    for level in range(levels):
        own.append(grad_level(flat_modes, coefficients, series, level, cells))
        got.append(lax.ppermute(own[level], "ens", swap))

    edge_modes, _ = lax.optimization_barrier((modes, own[1]))
    upper = (rows_x - 1) * (1 - core)
    edge_a = lax.dynamic_slice_in_dim(edge_modes, upper, 1, axis=1)
    edge_b = lax.dynamic_slice_in_dim(edge_modes, rows_x - 1 - upper, 1, axis=1)
    row_lo = edge_modes[:, :, 0].reshape(levels * rows_x, width)
    row_hi = edge_modes[:, :, rows_y - 1].reshape(levels * rows_x, width)
    xb = lax.ppermute(edge_b[:, 0], SX, both_ways([(i, i + 1) for i in range(1, n_sx - 1, 2)]))
    za = lax.ppermute(
        jnp.where(parity == 0, row_hi, row_lo), "z", both_ways([(i, i + 1) for i in range(0, n_z, 2)])
    )
    zb = lax.ppermute(
        jnp.where(parity == 0, row_lo, row_hi), "z", both_ways([(i, i + 1) for i in range(1, n_z - 1, 2)])
    )
    xa = lax.ppermute(edge_a[:, 0], "c", swap)
    halos = (xa[:, None], xb[:, None], za, zb)

    moved, carry = [], None
    for level in range(levels):
        m, *carry = step_level(
            level, levels, place, modes, halos, own[level], got[level], series, carry
        )
        moved.append(m)
    keep, send = carry

    part_shape = jax.ShapeDtypeStruct((PARTS, PART_ROWS, 128), BF16)
    other = lax.ppermute(send, "c", swap)
    joined = pl.pallas_call(
        join_kernel, in_specs=[VM, VM], out_specs=VM, out_shape=part_shape, compiler_params=PARAMS
    )(keep, other)
    parts = lax.all_to_all(joined, PLANE, 0, 0)
    planes = pl.pallas_call(
        plane_kernel, in_specs=[VM], out_specs=VM, out_shape=part_shape, compiler_params=PARAMS
    )(parts)
    planes = lax.all_to_all(planes, "z", 0, 0)
    spread, shrink = pl.pallas_call(
        functools.partial(reduce_kernel, total_cells),
        in_specs=[SM, VM],
        out_specs=[VM, VM],
        out_shape=[
            jax.ShapeDtypeStruct((PARTS, SUM_ROWS, 128), BF16),
            jax.ShapeDtypeStruct((2, 128), F32),
        ],
        scratch_shapes=[pltpu.VMEM((width, 128), F32)],
        compiler_params=PARAMS,
    )(place, planes)
    half = lax.all_to_all(spread, PLANE, 0, 0)
    new_modes = pl.pallas_call(
        scale_kernel,
        in_specs=[VM] * (1 + levels),
        out_specs=VM,
        out_shape=jax.ShapeDtypeStruct((levels, cells, width), BF16),
        compiler_params=PARAMS,
    )(shrink, *moved)
    half, new_modes = lax.optimization_barrier((half, new_modes))
    other_half = lax.ppermute(half, "c", swap)
    projected, gram = pl.pallas_call(
        final_kernel,
        in_specs=[SM, VM, VM],
        out_specs=[VM, VM],
        out_shape=[
            jax.ShapeDtypeStruct((members, width, frames), F32),
            jax.ShapeDtypeStruct((width, width), F32),
        ],
        compiler_params=PARAMS,
    )(place, half, other_half)
    return (new_modes.reshape(modes.shape), gram, projected)


def solution(mesh):
    ens, n_sx, n_sy = (mesh.shape[a] for a in ("ens", "sx", "sy"))
    fine = Mesh(mesh.devices.reshape(ens, 2, n_sx // 4, 2, n_sy), ("ens", "xh", "y", "c", "z"))
    in_specs = (P("ens", None, SX, "z", None), P("ens", None, None), P(None, SX, "z", None))
    out_specs = (P(None, SX, "z", None), P(), P("ens", None, None))
    return jax.shard_map(local, mesh=fine, in_specs=in_specs, out_specs=out_specs, check_vma=False)
```

time: 110 us -> 103 us (0.936)
  blocking collectives: 20.5 us -> 42.5 us
  starting transfers between devices: 42 us -> 20.8 us
  waiting for transfers between devices: 23.8 us -> 13.5 us
  local copies, waits for them, and re-layouts: 5.2 us -> 9.45 us
  Pallas kernels: 16.9 us -> 15.4 us
    all_to_all x1 -> x2, blocking collectives: 20.5 us -> 42.5 us  [the longest x1 22.7 us: local(): parts = lax.all_to_all(joined, PLANE, 0, 0)]
    all_to_all x1, starting transfers between devices: 23.1 us -> 4.05 us  [local(): half = lax.all_to_all(spread, PLANE, 0, 0)]
    all_to_all x1, waiting for transfers between devices: 15.7 us -> 6.71 us  [local(): half = lax.all_to_all(spread, PLANE, 0, 0)]
    unnamed x14 -> x18, local copies, waits for them, and re-layouts: 4.48 us -> 8.84 us
    ppermute x8, starting transfers between devices: 14.9 us -> 11.7 us  [the longest x4 4.11 us: local(): got.append(lax.ppermute(own[level], 'ens', swap))]
    pallas_call x9 -> x10, Pallas kernels: 13.7 us -> 11 us  [the longest x4 6.37 us: step_level(): pl.pallas_call(functools.partial(step_kernel, level, first, last), in_spe...]
    ppermute x8, waiting for transfers between devices: 6.2 us -> 4.23 us  [the longest x1 2.85 us: local(): lax.ppermute(edge_b[:, 0], SX, both_ways([(i, i + 1) for i in range(1, n_...]
  transfers between devices with their start and end apart: 11 -> 11, of which waited for: 5 -> 5; matrix products, arithmetic and copies ran while one was open for 1% -> 1% of each run, Pallas kernels for 10% -> 9%
where the time goes in v2:
time: 103 us
  blocking collectives  42.5 us (41%)
  starting transfers between devices  20.8 us (20%)
  Pallas kernels  15.4 us (15%)
  waiting for transfers between devices  13.5 us (13%)
  local copies, waits for them, and re-layouts  9.45 us (9%)
    all_to_all x1, blocking collectives, local(): parts = lax.all_to_all(joined, PLANE, 0, 0)  22.7 us
    all_to_all x1, blocking collectives, local(): planes = lax.all_to_all(planes, 'z', 0, 0)  19.7 us
    unnamed x18, local copies, waits for them, and re-layouts  8.84 us
    all_to_all x1, waiting for transfers between devices, local(): half = lax.all_to_all(spread, PLANE, 0, 0)  6.71 us
    pallas_call x4, Pallas kernels, step_level(): pl.pallas_call(functools.partial(step_kernel, level, first, last), in_spe...  6.37 us
    pallas_call x4, Pallas kernels, grad_level(): pl.pallas_call(kernel, in_specs=specs, out_specs=VM, out_shape=jax.ShapeD...  4.5 us
    ppermute x1, starting transfers between devices, local(): other_half = lax.ppermute(half, 'c', swap)  4.17 us
    ppermute x4, starting transfers between devices, local(): got.append(lax.ppermute(own[level], 'ens', swap))  4.11 us
  transfers between devices with their start and end apart: 11, of which 5 were waited for; matrix products, arithmetic and copies ran while one was open for 1% of the time, Pallas kernels for 9%

profile of v2, /device:TPU:1, one launch (start us, length us, event | category | flops | bytes accessed | tf_op | source)
XLA Modules:
  0.0 102.5 jit_solution(8727002200748316591)
XLA Ops:
  0.6 0.0 copy-start
  0.6 2.2 %copy-done = bf16[2,4,8,64,512]{4,3,2,1,0:T(8,128)(2,1)S(1)} copy-done((bf16[2,4,8,64,512]{4,3,2,1,0:T(8,128)(2,1)S(1)}, bf16[2,4,8,64,512]{4,3,2,1,0:T(8,128)(2,1)}, u32[]{:S(2)}) %copy-start) | copy-done | bytes 4194328
  2.8 0.0 copy-start.3
  2.8 1.2 %copy-done.3 = bf16[4,8,64,256]{3,2,1,0:T(8,128)(2,1)S(1)} copy-done((bf16[4,8,64,256]{3,2,1,0:T(8,128)(2,1)S(1)}, bf16[4,8,64,256]{3,2,1,0:T(8,128)(2,1)}, u32[]{:S(2)}) %copy-start.3) | copy-done | bytes 1048600
  4.0 0.0 copy-start.5
  4.0 1.0 %copy-done.5 = bf16[2,256,512]{2,1,0:T(8,128)(2,1)S(1)} copy-done((bf16[2,256,512]{2,1,0:T(8,128)(2,1)S(1)}, bf16[2,256,512]{2,1,0:T(8,128)(2,1)}, u32[]{:S(2)}) %copy-start.5) | copy-done | bytes 524312
  5.1 0.0 copy-start.4
  5.1 0.0 copy-start.6
  5.1 1.0 shard_map.58.refs_6_
  6.0 2.1 %collective-permute-start.6 = (bf16[512,256]{1,0:T(8,128)(2,1)S(1)}, bf16[512,256]{1,0:T(8,128)(2,1)S(1)}, u32[]{:S(2)}, u32[]{:S(2)}) collective-permute-start(bf16[512,256]{1,0:T(8,128)(2,1)S(1)} %shard_map.58.refs_6_), channel_id=1, source_target_pairs={{0,128},{128,0},{1,129},{129,1},{2,130},{130,2},{3,131},{131,3},{4... | collective-permute-start | bytes 786440 | tf_op jit(solution)/shard_map/ppermute | solution.py:313
  8.2 0.0 copy-done.4
  8.2 0.6 copy.12
  8.8 1.7 %collective-permute-start.2 = (bf16[32,256]{1,0:T(8,128)(2,1)S(1)}, bf16[32,256]{1,0:T(8,128)(2,1)S(1)}, u32[]{:S(2)}, u32[]{:S(2)}) collective-permute-start(bf16[32,256]{1,0:T(8,128)(2,1)S(1)} %get-tuple-element.48), channel_id=1, source_target_pairs={{0,1},{1,0},{2,3},{3,2},{4,5},{5,4},{6,7},{7,6},{8,9},{9,8},{10,11... | collective-permute-start | bytes 49160 | tf_op jit(solution)/shard_map/ppermute | solution.py:322
  10.5 0.7 collective-permute-start.3
  11.2 1.3 %collective-permute-start = (bf16[4,64,256]{2,1,0:T(8,128)(2,1)S(1)}, bf16[4,64,256]{2,1,0:T(8,128)(2,1)S(1)}, u32[]{:S(2)}, u32[]{:S(2)}) collective-permute-start(bf16[4,64,256]{2,1,0:T(8,128)(2,1)S(1)} %get-tuple-element.50), channel_id=1, source_target_pairs={{0,8},{8,0},{1,9},{9,1},{2,10},{10,2},{3,11},{11,3},{4,12},{12,4},... | collective-permute-start | bytes 393224 | tf_op jit(solution)/shard_map/ppermute | solution.py:328
  12.5 0.0 copy-done.6
  12.5 0.0 copy-start.1
  12.5 2.2 %copy-done.1 = bf16[2,4,8,64,512]{4,3,2,1,0:T(8,128)(2,1)S(1)} copy-done((bf16[2,4,8,64,512]{4,3,2,1,0:T(8,128)(2,1)S(1)}, bf16[2,4,8,64,512]{4,3,2,1,0:T(8,128)(2,1)}, u32[]{:S(2)}) %copy-start.1) | copy-done | bytes 4194328
  14.7 1.6 %shard_map.61.refs_6_ = bf16[512,256]{1,0:T(8,128)(2,1)S(1)} custom-call(bf16[2048,256]{1,0:T(8,128)(2,1)S(1)} %bitcast.25, bf16[2,256,512]{2,1,0:T(8,128)(2,1)S(1)} %copy-done.6, bf16[2,2048,512]{2,1,0:T(8,128)(2,1)S(1)} %bitcast.17), custom_call_target="tpu_custom_call" | custom-call | flops 536870912 | bytes 2097152 | tf_op jit(solution)/shard_map/pallas_call | solution.py:97
  16.4 0.3 collective-permute-start.7
  16.7 0.9 shard_map.60.refs_6_
  17.7 0.0 collective-permute-done.2.refs_4_
  17.7 1.3 %collective-permute-start.5 = (bf16[512,256]{1,0:T(8,128)(2,1)S(1)}, bf16[512,256]{1,0:T(8,128)(2,1)S(1)}, u32[]{:S(2)}, u32[]{:S(2)}) collective-permute-start(bf16[512,256]{1,0:T(8,128)(2,1)S(1)} %shard_map.60.refs_6_), channel_id=1, source_target_pairs={{0,128},{128,0},{1,129},{129,1},{2,130},{130,2},{3,131},{131,3},{4... | collective-permute-start | bytes 786440 | tf_op jit(solution)/shard_map/ppermute | solution.py:313
  19.0 1.0 shard_map.59.refs_6_
  19.9 0.0 collective-permute-done.3.refs_5_
  19.9 0.3 collective-permute-start.4
  20.3 0.0 collective-permute-done
  20.3 3.9 %collective-permute-start.1 = (bf16[4,64,256]{2,1,0:T(8,128)(2,1)S(1)}, bf16[4,64,256]{2,1,0:T(8,128)(2,1)S(1)}, u32[]{:S(2)}, u32[]{:S(2)}) collective-permute-start(bf16[4,64,256]{2,1,0:T(8,128)(2,1)S(1)} %get-tuple-element.49), channel_id=1, source_target_pairs={{8,16},{16,8},{24,32},{32,24},{40,48},{48,40},{56,64},{64,56},{72,... | collective-permute-start | bytes 393224 | tf_op jit(solution)/shard_map/ppermute | solution.py:321
  24.2 0.1 pad_add_fusion.refs_0_.at_ref
  24.3 2.8 %collective-permute-done.1 = bf16[4,64,256]{2,1,0:T(8,128)(2,1)S(1)} collective-permute-done((bf16[4,64,256]{2,1,0:T(8,128)(2,1)S(1)}, bf16[4,64,256]{2,1,0:T(8,128)(2,1)S(1)}, u32[]{:S(2)}, u32[]{:S(2)}) %collective-permute-start.1) | collective-permute-done | bytes 131104 | tf_op jit(solution)/shard_map/ppermute | solution.py:321
  27.2 0.0 collective-permute-done.7.refs_7_
  27.2 0.0 copy-start.2
  27.2 2.2 %copy-done.2 = bf16[2,4,8,64,512]{4,3,2,1,0:T(8,128)(2,1)S(1)} copy-done((bf16[2,4,8,64,512]{4,3,2,1,0:T(8,128)(2,1)S(1)}, bf16[2,4,8,64,512]{4,3,2,1,0:T(8,128)(2,1)}, u32[]{:S(2)}) %copy-start.2) | copy-done | bytes 4194328
  29.4 1.8 %shard_map.62 = (bf16[512,256]{1,0:T(8,128)(2,1)S(1)}, f32[2,256,512]{2,1,0:T(8,128)S(1)}, f32[256,256]{1,0:T(8,128)S(1)}, f32[1,256]{1,0:T(1,128)S(1)}) custom-call(s32[3]{0:T(128)S(1)} %pad_add_fusion.refs_0_.at_ref, bf16[4,8,64,256]{3,2,1,0:T(8,128)(2,1)S(1)} %copy-done.4, bf16[4,1,64,256]{3,2,1,0:T(8,128)(2,1)S(1)} %bitcast.28, ...), custom_call_target="tpu_custom_call" | custom-call | flops 335544320 | bytes 2097152 | tf_op jit(solution)/shard_map/pallas_call | solution.py:206
  31.2 0.0 copy-start.7
  31.2 0.0 collective-permute-done.6.refs_7_
  31.2 1.5 %shard_map.63 = (bf16[512,256]{1,0:T(8,128)(2,1)S(1)}, f32[2,256,512]{2,1,0:T(8,128)S(1)}, f32[256,256]{1,0:T(8,128)S(1)}, f32[1,256]{1,0:T(1,128)S(1)}) custom-call(s32[3]{0:T(128)S(1)} %pad_add_fusion.refs_0_.at_ref, bf16[4,8,64,256]{3,2,1,0:T(8,128)(2,1)S(1)} %copy-done.4, ...), custom_call_target="tpu_custom_call", output_to_operand_aliasing={{1}: (9, {}), {2}: (10, {}), {3}: (11, {})} | custom-call | flops 335544320 | bytes 2097152 | tf_op jit(solution)/shard_map/pallas_call | solution.py:206
  32.7 0.0 collective-permute-done.5.refs_7_
  32.7 1.5 %shard_map.64 = (bf16[512,256]{1,0:T(8,128)(2,1)S(1)}, f32[2,256,512]{2,1,0:T(8,128)S(1)}, f32[256,256]{1,0:T(8,128)S(1)}, f32[1,256]{1,0:T(1,128)S(1)}) custom-call(s32[3]{0:T(128)S(1)} %pad_add_fusion.refs_0_.at_ref, bf16[4,8,64,256]{3,2,1,0:T(8,128)(2,1)S(1)} %copy-done.4, ...), custom_call_target="tpu_custom_call", output_to_operand_aliasing={{1}: (9, {}), {2}: (10, {}), {3}: (11, {})} | custom-call | flops 335544320 | bytes 2097152 | tf_op jit(solution)/shard_map/pallas_call | solution.py:206
  34.2 0.0 copy-done.7
  34.2 1.4 %collective-permute-done.4.refs_7_ = bf16[512,256]{1,0:T(8,128)(2,1)S(1)} collective-permute-done((bf16[512,256]{1,0:T(8,128)(2,1)S(1)}, bf16[512,256]{1,0:T(8,128)(2,1)S(1)}, u32[]{:S(2)}, u32[]{:S(2)}) %collective-permute-start.4) | collective-permute-done | bytes 262176 | tf_op jit(solution)/shard_map/ppermute | solution.py:313
  35.6 0.0 copy-start.8
  35.6 1.6 %shard_map.65 = (bf16[512,256]{1,0:T(8,128)(2,1)S(1)}, bf16[8,168,128]{2,1,0:T(8,128)(2,1)S(1)}, bf16[8,168,128]{2,1,0:T(8,128)(2,1)S(1)}) custom-call(s32[3]{0:T(128)S(1)} %pad_add_fusion.refs_0_.at_ref, bf16[4,8,64,256]{3,2,1,0:T(8,128)(2,1)S(1)} %copy-done.4, bf16[4,1,64,256]{3,2,1,0:T(8,128)(2,1)S(1)} %bitcast.31, bf16[4,1,64,256]{3,2,1,0:T(8,128)(2,1)S(1)} %bitcast.35, ...), custom_call_target="tpu_custom_call" | custom-call | flops 335544320 | bytes 2097152 | tf_op jit(solution)/shard_map/pallas_call | solution.py:206
  37.2 0.9 collective-permute-start.8
  38.1 1.3 %collective-permute-done.8.got_ref = bf16[8,168,128]{2,1,0:T(8,128)(2,1)S(1)} collective-permute-done((bf16[8,168,128]{2,1,0:T(8,128)(2,1)S(1)}, bf16[8,168,128]{2,1,0:T(8,128)(2,1)S(1)}, u32[]{:S(2)}, u32[]{:S(2)}) %collective-permute-start.8) | collective-permute-done | bytes 344096 | tf_op jit(solution)/shard_map/ppermute | solution.py:340
  39.3 0.1 shard_map.66
  39.4 22.7 %all_to_all.15.in_ref = bf16[8,168,128]{2,1,0:T(8,128)(2,1)S(1)} all-to-all(bf16[8,168,128]{2,1,0:T(8,128)(2,1)S(1)} %shard_map.66), channel_id=1, replica_groups=mesh['ens'=2,'xh'=2,'y'=4,'c'=2,'z'=8] {'xh','y'}, dimensions={0} | all-to-all | bytes 688128 | tf_op jit(solution)/shard_map/all_to_all | solution.py:344
  62.2 0.1 shard_map.67
  62.2 19.7 %all_to_all.16.in_ref = bf16[8,168,128]{2,1,0:T(8,128)(2,1)S(1)} all-to-all(bf16[8,168,128]{2,1,0:T(8,128)(2,1)S(1)} %shard_map.67), channel_id=1, replica_groups=mesh['ens'=2,'xh'=2,'y'=4,'c'=2,'z'=8] {'z'}, dimensions={0} | all-to-all | bytes 688128 | tf_op jit(solution)/shard_map/all_to_all | solution.py:348
  82.0 1.4 %shard_map.68 = (bf16[8,160,128]{2,1,0:T(8,128)(2,1)}, f32[2,128]{1,0:T(2,128)S(1)}) custom-call(s32[3]{0:T(128)S(1)} %pad_add_fusion.refs_0_.at_ref, bf16[8,168,128]{2,1,0:T(8,128)(2,1)S(1)} %all_to_all.16.in_ref), custom_call_target="tpu_custom_call" | custom-call | tf_op jit(solution)/shard_map/pallas_call | solution.py:349
  83.4 4.0 %all-to-all-start.2 = ((bf16[8,160,128]{2,1,0:T(8,128)(2,1)}), bf16[8,160,128]{2,1,0:T(8,128)(2,1)S(1)}, u32[]{:S(2)}, u32[]{:S(2)}) async-start(bf16[8,160,128]{2,1,0:T(8,128)(2,1)} %get-tuple-element.37), calls=%async_computation.2 | async-start | bytes 655360 | tf_op jit(solution)/shard_map/all_to_all | solution.py:360
  87.4 0.0 copy-done.8
  87.4 1.2 %shard_map.69 = bf16[4,512,256]{2,1,0:T(8,128)(2,1)} custom-call(f32[2,128]{1,0:T(2,128)S(1)} %get-tuple-element.38.shrink_ref, bf16[512,256]{1,0:T(8,128)(2,1)S(1)} %copy-done.8, bf16[512,256]{1,0:T(8,128)(2,1)S(1)} %get-tuple-element.40.refs_1_, bf16[512,256]{1,0:T(8,128)(2,1)S(1)} %get-tuple-element.41.refs_2_, bf16[512,256]{1,0:T(8,128)(2,1)S(1)} %get-tuple-element.42.refs_3_), custom_call_target="tpu_custom_call" | custom-call | tf_op jit(solution)/shard_map/pallas_call | solution.py:361
  88.6 6.7 %all-to-all-done.2.own_ref = bf16[8,160,128]{2,1,0:T(8,128)(2,1)S(1)} async-done(((bf16[8,160,128]{2,1,0:T(8,128)(2,1)}), bf16[8,160,128]{2,1,0:T(8,128)(2,1)S(1)}, u32[]{:S(2)}, u32[]{:S(2)}) %all-to-all-start.2) | async-done | bytes 327712 | tf_op jit(solution)/shard_map/all_to_all | solution.py:360
  95.3 4.2 %collective-permute-start.9 = (bf16[8,160,128]{2,1,0:T(8,128)(2,1)S(1)}, bf16[8,160,128]{2,1,0:T(8,128)(2,1)S(1)}, u32[]{:S(2)}, u32[]{:S(2)}) collective-permute-start(bf16[8,160,128]{2,1,0:T(8,128)(2,1)S(1)} %all-to-all-done.2.own_ref), channel_id=1, source_target_pairs={{0,8},{8,0},{1,9},{9,1},{2,10},{10,2},{3,11},{11,3},{4,12},{12,4},... | collective-permute-start | bytes 983048 | tf_op jit(solution)/shard_map/ppermute | solution.py:369
  99.5 1.3 %collective-permute-done.9.got_ref = bf16[8,160,128]{2,1,0:T(8,128)(2,1)S(1)} collective-permute-done((bf16[8,160,128]{2,1,0:T(8,128)(2,1)S(1)}, bf16[8,160,128]{2,1,0:T(8,128)(2,1)S(1)}, u32[]{:S(2)}, u32[]{:S(2)}) %collective-permute-start.9) | collective-permute-done | bytes 327712 | tf_op jit(solution)/shard_map/ppermute | solution.py:369
  100.8 1.7 %shard_map.70 = (f32[2,256,512]{2,1,0:T(8,128)}, f32[256,256]{1,0:T(8,128)}) custom-call(s32[3]{0:T(128)S(1)} %pad_add_fusion.refs_0_.at_ref, bf16[8,160,128]{2,1,0:T(8,128)(2,1)S(1)} %all-to-all-done.2.own_ref, bf16[8,160,128]{2,1,0:T(8,128)(2,1)S(1)} %collective-permute-done.9.got_ref), custom_call_target="tpu_custom_call" | custom-call | tf_op jit(solution)/shard_map/pallas_call | solution.py:370
  (2 shorter events, 0.0 us)
Async XLA Ops:
  0.6 2.2 %copy-start = (bf16[2,4,8,64,512]{4,3,2,1,0:T(8,128)(2,1)S(1)}, bf16[2,4,8,64,512]{4,3,2,1,0:T(8,128)(2,1)}, u32[]{:S(2)}) copy-start(bf16[2,4,8,64,512]{4,3,2,1,0:T(8,128)(2,1)} %param.3) | copy-start | bytes 12582916
  2.8 1.2 %copy-start.3 = (bf16[4,8,64,256]{3,2,1,0:T(8,128)(2,1)S(1)}, bf16[4,8,64,256]{3,2,1,0:T(8,128)(2,1)}, u32[]{:S(2)}) copy-start(bf16[4,8,64,256]{3,2,1,0:T(8,128)(2,1)} %refs_1_.7) | copy-start | bytes 3145732
  4.0 1.0 %copy-start.5 = (bf16[2,256,512]{2,1,0:T(8,128)(2,1)S(1)}, bf16[2,256,512]{2,1,0:T(8,128)(2,1)}, u32[]{:S(2)}) copy-start(bf16[2,256,512]{2,1,0:T(8,128)(2,1)} %c_hbm.1) | copy-start | bytes 1572868
  5.1 3.1 %copy-start.4 = (bf16[4,8,64,256]{3,2,1,0:T(8,128)(2,1)S(1)}, bf16[4,8,64,256]{3,2,1,0:T(8,128)(2,1)}, u32[]{:S(2)}) copy-start(bf16[4,8,64,256]{3,2,1,0:T(8,128)(2,1)} %refs_1_.7) | copy-start | bytes 3145732
  5.1 7.4 %copy-start.6 = (bf16[2,256,512]{2,1,0:T(8,128)(2,1)S(1)}, bf16[2,256,512]{2,1,0:T(8,128)(2,1)}, u32[]{:S(2)}) copy-start(bf16[2,256,512]{2,1,0:T(8,128)(2,1)} %c_hbm.1) | copy-start | bytes 1572868
  6.0 25.2 %collective-permute-start.6 = (bf16[512,256]{1,0:T(8,128)(2,1)S(1)}, bf16[512,256]{1,0:T(8,128)(2,1)S(1)}, u32[]{:S(2)}, u32[]{:S(2)}) collective-permute-start(bf16[512,256]{1,0:T(8,128)(2,1)S(1)} %shard_map.58.refs_6_), channel_id=1, source_target_pairs={{0,128},{128,0},{1,129},{129,1},{2,130},{130,2},{3,131},{131,3},{4... | collective-permute-start | bytes 786440 | tf_op jit(solution)/shard_map/ppermute | solution.py:313
  8.8 8.9 %collective-permute-start.2 = (bf16[32,256]{1,0:T(8,128)(2,1)S(1)}, bf16[32,256]{1,0:T(8,128)(2,1)S(1)}, u32[]{:S(2)}, u32[]{:S(2)}) collective-permute-start(bf16[32,256]{1,0:T(8,128)(2,1)S(1)} %get-tuple-element.48), channel_id=1, source_target_pairs={{0,1},{1,0},{2,3},{3,2},{4,5},{5,4},{6,7},{7,6},{8,9},{9,8},{10,11... | collective-permute-start | bytes 49160 | tf_op jit(solution)/shard_map/ppermute | solution.py:322
  10.5 9.4 %collective-permute-start.3 = (bf16[32,256]{1,0:T(8,128)(2,1)S(1)}, bf16[32,256]{1,0:T(8,128)(2,1)S(1)}, u32[]{:S(2)}, u32[]{:S(2)}) collective-permute-start(bf16[32,256]{1,0:T(8,128)(2,1)S(1)} %get-tuple-element.47), channel_id=1, source_target_pairs={{1,2},{2,1},{3,4},{4,3},{5,6},{6,5},{9,10},{10,9},{11,12},{12,11},... | collective-permute-start | bytes 49160 | tf_op jit(solution)/shard_map/ppermute | solution.py:325
  11.2 9.1 %collective-permute-start = (bf16[4,64,256]{2,1,0:T(8,128)(2,1)S(1)}, bf16[4,64,256]{2,1,0:T(8,128)(2,1)S(1)}, u32[]{:S(2)}, u32[]{:S(2)}) collective-permute-start(bf16[4,64,256]{2,1,0:T(8,128)(2,1)S(1)} %get-tuple-element.50), channel_id=1, source_target_pairs={{0,8},{8,0},{1,9},{9,1},{2,10},{10,2},{3,11},{11,3},{4,12},{12,4},... | collective-permute-start | bytes 393224 | tf_op jit(solution)/shard_map/ppermute | solution.py:328
  12.5 2.2 %copy-start.1 = (bf16[2,4,8,64,512]{4,3,2,1,0:T(8,128)(2,1)S(1)}, bf16[2,4,8,64,512]{4,3,2,1,0:T(8,128)(2,1)}, u32[]{:S(2)}) copy-start(bf16[2,4,8,64,512]{4,3,2,1,0:T(8,128)(2,1)} %param.3) | copy-start | bytes 12582916
  16.4 10.8 %collective-permute-start.7 = (bf16[512,256]{1,0:T(8,128)(2,1)S(1)}, bf16[512,256]{1,0:T(8,128)(2,1)}, u32[]{:S(2)}, u32[]{:S(2)}) collective-permute-start(bf16[512,256]{1,0:T(8,128)(2,1)S(1)} %shard_map.61.refs_6_), channel_id=1, source_target_pairs={{0,128},{128,0},{1,129},{129,1},{2,130},{130,2},{3,131},{131,3},{4... | collective-permute-start | bytes 786440 | tf_op jit(solution)/shard_map/ppermute | solution.py:313
  17.7 15.0 %collective-permute-start.5 = (bf16[512,256]{1,0:T(8,128)(2,1)S(1)}, bf16[512,256]{1,0:T(8,128)(2,1)S(1)}, u32[]{:S(2)}, u32[]{:S(2)}) collective-permute-start(bf16[512,256]{1,0:T(8,128)(2,1)S(1)} %shard_map.60.refs_6_), channel_id=1, source_target_pairs={{0,128},{128,0},{1,129},{129,1},{2,130},{130,2},{3,131},{131,3},{4... | collective-permute-start | bytes 786440 | tf_op jit(solution)/shard_map/ppermute | solution.py:313
  19.9 15.7 %collective-permute-start.4 = (bf16[512,256]{1,0:T(8,128)(2,1)S(1)}, bf16[512,256]{1,0:T(8,128)(2,1)S(1)}, u32[]{:S(2)}, u32[]{:S(2)}) collective-permute-start(bf16[512,256]{1,0:T(8,128)(2,1)S(1)} %shard_map.59.refs_6_), channel_id=1, source_target_pairs={{0,128},{128,0},{1,129},{129,1},{2,130},{130,2},{3,131},{131,3},{4... | collective-permute-start | bytes 786440 | tf_op jit(solution)/shard_map/ppermute | solution.py:313
  20.3 6.9 %collective-permute-start.1 = (bf16[4,64,256]{2,1,0:T(8,128)(2,1)S(1)}, bf16[4,64,256]{2,1,0:T(8,128)(2,1)S(1)}, u32[]{:S(2)}, u32[]{:S(2)}) collective-permute-start(bf16[4,64,256]{2,1,0:T(8,128)(2,1)S(1)} %get-tuple-element.49), channel_id=1, source_target_pairs={{8,16},{16,8},{24,32},{32,24},{40,48},{48,40},{56,64},{64,56},{72,... | collective-permute-start | bytes 393224 | tf_op jit(solution)/shard_map/ppermute | solution.py:321
  27.2 2.2 %copy-start.2 = (bf16[2,4,8,64,512]{4,3,2,1,0:T(8,128)(2,1)S(1)}, bf16[2,4,8,64,512]{4,3,2,1,0:T(8,128)(2,1)}, u32[]{:S(2)}) copy-start(bf16[2,4,8,64,512]{4,3,2,1,0:T(8,128)(2,1)} %param.3) | copy-start | bytes 12582916
  31.2 3.0 %copy-start.7 = (bf16[512,256]{1,0:T(8,128)(2,1)}, bf16[512,256]{1,0:T(8,128)(2,1)S(1)}, u32[]{:S(2)}) copy-start(bf16[512,256]{1,0:T(8,128)(2,1)S(1)} %get-tuple-element.39.refs_0_) | copy-start | bytes 786436
  35.6 51.8 %copy-start.8 = (bf16[512,256]{1,0:T(8,128)(2,1)S(1)}, bf16[512,256]{1,0:T(8,128)(2,1)}, u32[]{:S(2)}) copy-start(bf16[512,256]{1,0:T(8,128)(2,1)} %copy-done.7) | copy-start | bytes 786436
  37.2 2.2 %collective-permute-start.8 = (bf16[8,168,128]{2,1,0:T(8,128)(2,1)S(1)}, bf16[8,168,128]{2,1,0:T(8,128)(2,1)S(1)}, u32[]{:S(2)}, u32[]{:S(2)}) collective-permute-start(bf16[8,168,128]{2,1,0:T(8,128)(2,1)S(1)} %get-tuple-element.36), channel_id=1, source_target_pairs={{0,8},{8,0},{1,9},{9,1},{2,10},{10,2},{3,11},{11,3},{4,12},{12,4},... | collective-permute-start | bytes 1032200 | tf_op jit(solution)/shard_map/ppermute | solution.py:340
  83.4 11.9 %all-to-all-start.2 = ((bf16[8,160,128]{2,1,0:T(8,128)(2,1)}), bf16[8,160,128]{2,1,0:T(8,128)(2,1)S(1)}, u32[]{:S(2)}, u32[]{:S(2)}) async-start(bf16[8,160,128]{2,1,0:T(8,128)(2,1)} %get-tuple-element.37), calls=%async_computation.2 | async-start | bytes 655360 | tf_op jit(solution)/shard_map/all_to_all | solution.py:360
  95.3 5.4 %collective-permute-start.9 = (bf16[8,160,128]{2,1,0:T(8,128)(2,1)S(1)}, bf16[8,160,128]{2,1,0:T(8,128)(2,1)S(1)}, u32[]{:S(2)}, u32[]{:S(2)}) collective-permute-start(bf16[8,160,128]{2,1,0:T(8,128)(2,1)S(1)} %all-to-all-done.2.own_ref), channel_id=1, source_target_pairs={{0,8},{8,0},{1,9},{9,1},{2,10},{10,2},{3,11},{11,3},{4,12},{12,4},... | collective-permute-start | bytes 983048 | tf_op jit(solution)/shard_map/ppermute | solution.py:369

commit v3 on v2

--- a/solution.py
+++ b/solution.py
@@ -28,6 +28,10 @@
 VM = pl.BlockSpec(memory_space=pltpu.VMEM)
 SM = pl.BlockSpec(memory_space=pltpu.SMEM)
 HBM = pl.BlockSpec(memory_space=pltpu.HBM)
+
+
+def in_hbm(array):
+    return pltpu.with_memory_space_constraint(array, pltpu.HBM)
 
 
 def gradient(m, coefficients, series):
@@ -41,9 +45,10 @@
     return acc.astype(BF16)
 
 
-def first_grad_kernel(cells, m_hbm, c_hbm, x_hbm, g_ref, m_ref, c_ref, x_ref, sems):
+def grad_kernel(level, m_hbm, c_hbm, x_hbm, g_ref, m_ref, c_ref, x_ref, sems):
     members = c_ref.shape[0]
-    rows = pl.ds(0, cells)
+    cells = m_ref.shape[0]
+    rows = pl.ds(level * cells, cells)
     copies = [pltpu.make_async_copy(m_hbm.at[rows], m_ref, sems.at[0])]
     for e in range(members):
         copies.append(pltpu.make_async_copy(c_hbm.at[e], c_ref.at[e], sems.at[1 + 2 * e]))
@@ -66,52 +71,32 @@
     )
 
 
-def grad_kernel(level, m_ref, c_ref, x_ref, g_ref):
-    cells = g_ref.shape[0]
-    members = c_ref.shape[0]
-    rows = slice(level * cells, (level + 1) * cells)
-
-    def part(ref, *at):
-        return lambda: ref[at]
-
-    g_ref[...] = gradient(
-        m_ref[rows, :],
-        [part(c_ref, e) for e in range(members)],
-        [part(x_ref, e, rows) for e in range(members)],
-    )
-
-
 def grad_level(flat_modes, coefficients, series, level, cells):
     members, _, frames = series.shape
     width = flat_modes.shape[1]
-    if level == 0:
-        kernel, specs = functools.partial(first_grad_kernel, cells), [HBM, HBM, HBM]
-        scratch = [
+    return pl.pallas_call(
+        functools.partial(grad_kernel, level),
+        in_specs=[HBM, HBM, HBM],
+        out_specs=VM,
+        out_shape=jax.ShapeDtypeStruct((cells, width), BF16),
+        scratch_shapes=[
             pltpu.VMEM((cells, width), BF16),
             pltpu.VMEM(coefficients.shape, BF16),
             pltpu.VMEM((members, cells, frames), BF16),
             pltpu.SemaphoreType.DMA((1 + 2 * members,)),
-        ]
-    else:
-        kernel, specs, scratch = functools.partial(grad_kernel, level), [VM, VM, VM], []
-    return pl.pallas_call(
-        kernel,
-        in_specs=specs,
-        out_specs=VM,
-        out_shape=jax.ShapeDtypeStruct((cells, width), BF16),
-        scratch_shapes=scratch,
+        ],
         compiler_params=PARAMS,
         cost_estimate=pl.CostEstimate(
             flops=4 * members * cells * frames * width,
             bytes_accessed=2 * cells * (2 * width + members * frames) + 2 * members * width * frames,
             transcendentals=0,
         ),
-    )(flat_modes, coefficients, series)
+    )(in_hbm(flat_modes), in_hbm(coefficients), in_hbm(series))
 
 
 def moved_of(level, at_ref, m_ref, xa_ref, xb_ref, za_ref, zb_ref, own_ref, got_ref):
-    _, rows_x, rows_y, width = m_ref.shape
-    f = m_ref[level].astype(F32)
+    rows_x, rows_y, width = m_ref.shape
+    f = m_ref[...].astype(F32)
     lower = at_ref[0] == 0
     even = at_ref[1] == 0
     xa, xb = xa_ref[level].astype(F32), xb_ref[level].astype(F32)
@@ -149,18 +134,25 @@
 
 
 def step_kernel(level, first, last, *refs):
-    inputs, refs = refs[:8], refs[8:]
-    x_ref, refs = refs[0], refs[1:]
+    (at_ref, m_hbm, *inputs), refs = refs[:8], refs[8:]
+    x_hbm, refs = refs[0], refs[1:]
+    *refs, m_ref, x_ref, sems = refs
+    cells = x_ref.shape[1]
+    copies = [pltpu.make_async_copy(m_hbm.at[level], m_ref, sems.at[0])]
+    for e in range(x_ref.shape[0]):
+        source = x_hbm.at[e, pl.ds(level * cells, cells)]
+        copies.append(pltpu.make_async_copy(source, x_ref.at[e], sems.at[1 + e]))
+    for copy in copies:
+        copy.start()
     if not first:
         (proj_in, gram_in, squares_in), refs = refs[:3], refs[3:]
     if last:
         moved_ref, keep_ref, send_ref, proj_ref, gram_ref = refs
     else:
         moved_ref, proj_ref, gram_ref, squares_ref = refs
-    moved = moved_of(level, *inputs)
+    copies[0].wait()
+    moved = moved_of(level, at_ref, m_ref, *inputs)
     moved_ref[...] = moved
-    cells = moved.shape[0]
-    rows = slice(level * cells, (level + 1) * cells)
     wide = moved.astype(F32)
     squares = jnp.sum(wide * wide, axis=0, keepdims=True)
     if not first:
@@ -169,10 +161,11 @@
     gram = jnp.dot(turned, moved, preferred_element_type=F32)
     gram_ref[...] = gram if first else gram_in[...] + gram
     for e in range(x_ref.shape[0]):
-        proj = jnp.dot(turned, x_ref[e, rows, :], preferred_element_type=F32)
+        copies[1 + e].wait()
+        proj = jnp.dot(turned, x_ref[e], preferred_element_type=F32)
         proj_ref[e] = proj if first else proj_in[e] + proj
     if last:
-        core = inputs[0][0]
+        core = at_ref[0]
         pair = jnp.concatenate([squares[:, 0:128], squares[:, 128:256]], axis=0)
         packed = split_squares(pair, 8).astype(BF16)
         emit(send_ref, 1 - core, proj_ref, gram_ref, packed)
@@ -186,7 +179,7 @@
     _, rows_x, rows_y, width = modes.shape
     cells = rows_x * rows_y
     first, last = level == 0, level == levels - 1
-    args = [place, modes, *halos, own, got, series]
+    args = [place, in_hbm(modes), *halos, own, got, in_hbm(series)]
     if not first:
         args += list(carry)
     sums = [
@@ -205,10 +198,15 @@
             aliases = {9 + i: 1 + i for i in range(3)}
     return pl.pallas_call(
         functools.partial(step_kernel, level, first, last),
-        in_specs=[SM] + [VM] * (len(args) - 1),
+        in_specs=[SM, HBM] + [VM] * 6 + [HBM] + [VM] * (len(args) - 9),
         out_specs=[VM] * len(outs),
         out_shape=outs,
-        scratch_shapes=scratch,
+        scratch_shapes=scratch
+        + [
+            pltpu.VMEM((rows_x, rows_y, width), BF16),
+            pltpu.VMEM((members, cells, frames), BF16),
+            pltpu.SemaphoreType.DMA((1 + members,)),
+        ],
         input_output_aliases=aliases,
         compiler_params=PARAMS,
         cost_estimate=pl.CostEstimate(
@@ -308,24 +306,29 @@
     swap = [(0, 1), (1, 0)]
 
     own, got = [], []
-    for level in range(levels):
-        own.append(grad_level(flat_modes, coefficients, series, level, cells))
+
+    def send_level(level, *after):
+        c, *_ = lax.optimization_barrier((coefficients, *after))
+        own.append(grad_level(flat_modes, c, series, level, cells))
         got.append(lax.ppermute(own[level], "ens", swap))
 
+    send_level(0)
+    edge_modes, _ = lax.optimization_barrier((modes, own[0]))
+    upper = (rows_x - 1) * (1 - core)
+    edge_a = lax.dynamic_slice_in_dim(edge_modes, upper, 1, axis=1)[:, 0]
+    edge_b = lax.dynamic_slice_in_dim(edge_modes, rows_x - 1 - upper, 1, axis=1)[:, 0]
+    xb = lax.ppermute(edge_b, SX, both_ways([(i, i + 1) for i in range(1, n_sx - 1, 2)]))
+    send_level(1, own[0], edge_a, edge_b)
     edge_modes, _ = lax.optimization_barrier((modes, own[1]))
-    upper = (rows_x - 1) * (1 - core)
-    edge_a = lax.dynamic_slice_in_dim(edge_modes, upper, 1, axis=1)
-    edge_b = lax.dynamic_slice_in_dim(edge_modes, rows_x - 1 - upper, 1, axis=1)
     row_lo = edge_modes[:, :, 0].reshape(levels * rows_x, width)
     row_hi = edge_modes[:, :, rows_y - 1].reshape(levels * rows_x, width)
-    xb = lax.ppermute(edge_b[:, 0], SX, both_ways([(i, i + 1) for i in range(1, n_sx - 1, 2)]))
-    za = lax.ppermute(
-        jnp.where(parity == 0, row_hi, row_lo), "z", both_ways([(i, i + 1) for i in range(0, n_z, 2)])
-    )
-    zb = lax.ppermute(
-        jnp.where(parity == 0, row_lo, row_hi), "z", both_ways([(i, i + 1) for i in range(1, n_z - 1, 2)])
-    )
-    xa = lax.ppermute(edge_a[:, 0], "c", swap)
+    row_a, row_b = jnp.where(parity == 0, row_hi, row_lo), jnp.where(parity == 0, row_lo, row_hi)
+    za = lax.ppermute(row_a, "z", both_ways([(i, i + 1) for i in range(0, n_z, 2)]))
+    zb = lax.ppermute(row_b, "z", both_ways([(i, i + 1) for i in range(1, n_z - 1, 2)]))
+    xa = lax.ppermute(edge_a, "c", swap)
+    send_level(2, own[1], row_a, row_b)
+    for level in range(3, levels):
+        send_level(level, own[level - 1])
     halos = (xa[:, None], xb[:, None], za, zb)
 
     moved, carry = [], None

time: 103 us -> 100 us (0.971)
  Pallas kernels: 15.4 us -> 25.8 us
  local copies, waits for them, and re-layouts: 9.45 us -> 1.58 us
  blocking collectives: 42.5 us -> 38.8 us
  waiting for transfers between devices: 13.5 us -> 12.3 us
    unnamed x18 -> x2, local copies, waits for them, and re-layouts: 8.84 us -> 0.01 us
    pallas_call x4, Pallas kernels: 4.5 us -> 10.1 us  [grad_level(): pl.pallas_call(functools.partial(grad_kernel, level), in_specs=[HBM, HBM,...]
    pallas_call x4, Pallas kernels: 6.37 us -> 11.1 us  [step_level(): pl.pallas_call(functools.partial(step_kernel, level, first, last), in_spe...]
    all_to_all x1, blocking collectives: 22.7 us -> 19.3 us  [local(): parts = lax.all_to_all(joined, PLANE, 0, 0)]
    ppermute x8, waiting for transfers between devices: 4.23 us -> 2.69 us  [the longest x1 2.67 us: local(): lax.ppermute(edge_b, SX, both_ways([(i, i + 1) for i in range(1, n_sx - 1...]
  transfers between devices with their start and end apart: 11 -> 11, of which waited for: 5 -> 4; matrix products, arithmetic and copies ran while one was open for 1% -> 2% of each run, Pallas kernels for 9% -> 17%
where the time goes in v3:
time: 100 us; the launch traced here: 99.6 us
  blocking collectives  38.8 us (39%)
  Pallas kernels  25.8 us (26%)
  starting transfers between devices  20.2 us (20%)
  waiting for transfers between devices  12.3 us (12%)
  local copies, waits for them, and re-layouts  1.58 us (2%)
    all_to_all x1, blocking collectives, local(): planes = lax.all_to_all(planes, 'z', 0, 0)  19.5 us
    all_to_all x1, blocking collectives, local(): parts = lax.all_to_all(joined, PLANE, 0, 0)  19.3 us
    pallas_call x4, Pallas kernels, step_level(): pl.pallas_call(functools.partial(step_kernel, level, first, last), in_spe...  11.1 us
    pallas_call x4, Pallas kernels, grad_level(): pl.pallas_call(functools.partial(grad_kernel, level), in_specs=[HBM, HBM,...  10.1 us
    all_to_all x1, waiting for transfers between devices, local(): half = lax.all_to_all(spread, PLANE, 0, 0)  6.72 us
    ppermute x4, starting transfers between devices, send_level(): got.append(lax.ppermute(own[level], 'ens', swap))  5.5 us
    ppermute x1, starting transfers between devices, local(): lax.ppermute(edge_b, SX, both_ways([(i, i + 1) for i in range(1, n_sx - 1...  4.27 us
    ppermute x1, starting transfers between devices, local(): other_half = lax.ppermute(half, 'c', swap)  4.17 us
  transfers between devices with their start and end apart: 11, of which 4 were waited for; matrix products, arithmetic and copies ran while one was open for 2% of the time, Pallas kernels for 17%

profile of v3, /device:TPU:1, one launch (start us, length us, event | category | flops | bytes accessed | tf_op | source)
XLA Modules:
  0.0 99.6 jit_solution(2581565547255761827)
XLA Ops:
  0.6 2.5 %shard_map.58.refs_6_ = bf16[512,256]{1,0:T(8,128)(2,1)S(1)} custom-call(bf16[2048,256]{1,0:T(8,128)(2,1)} %bitcast.32, bf16[2,256,512]{2,1,0:T(8,128)(2,1)} %c_hbm.3, bf16[2,2048,512]{2,1,0:T(8,128)(2,1)} %bitcast.24), custom_call_target="tpu_custom_call" | custom-call | flops 536870912 | bytes 2097152 | tf_op jit(solution)/shard_map/pallas_call | solution.py:77
  3.2 0.0 copy-start
  3.2 2.1 %collective-permute-start.7 = (bf16[512,256]{1,0:T(8,128)(2,1)S(1)}, bf16[512,256]{1,0:T(8,128)(2,1)S(1)}, u32[]{:S(2)}, u32[]{:S(2)}) collective-permute-start(bf16[512,256]{1,0:T(8,128)(2,1)S(1)} %shard_map.58.refs_6_), channel_id=1, source_target_pairs={{0,128},{128,0},{1,129},{129,1},{2,130},{130,2},{3,131},{131,3},{4... | collective-permute-start | bytes 786440 | tf_op jit(solution)/shard_map/ppermute | solution.py:313
  5.3 1.0 dynamic-slice_bitcast_fusion
  6.3 1.4 %collective-permute-start = (bf16[4,64,256]{2,1,0:T(8,128)(2,1)S(1)}, bf16[4,64,256]{2,1,0:T(8,128)(2,1)S(1)}, u32[]{:S(2)}, u32[]{:S(2)}) collective-permute-start(bf16[4,64,256]{2,1,0:T(8,128)(2,1)S(1)} %get-tuple-element.58), channel_id=1, source_target_pairs={{0,8},{8,0},{1,9},{9,1},{2,10},{10,2},{3,11},{11,3},{4,12},{12,4},... | collective-permute-start | bytes 393224 | tf_op jit(solution)/shard_map/ppermute | solution.py:328
  7.7 2.5 %shard_map.59.refs_6_ = bf16[512,256]{1,0:T(8,128)(2,1)S(1)} custom-call(bf16[2048,256]{1,0:T(8,128)(2,1)} %bitcast.33, bf16[2,256,512]{2,1,0:T(8,128)(2,1)} %c_hbm.3, bf16[2,2048,512]{2,1,0:T(8,128)(2,1)} %bitcast.25), custom_call_target="tpu_custom_call" | custom-call | flops 536870912 | bytes 2097152 | tf_op jit(solution)/shard_map/pallas_call | solution.py:77
  10.2 1.7 %collective-permute-start.6 = (bf16[512,256]{1,0:T(8,128)(2,1)S(1)}, bf16[512,256]{1,0:T(8,128)(2,1)S(1)}, u32[]{:S(2)}, u32[]{:S(2)}) collective-permute-start(bf16[512,256]{1,0:T(8,128)(2,1)S(1)} %shard_map.59.refs_6_), channel_id=1, source_target_pairs={{0,128},{128,0},{1,129},{129,1},{2,130},{130,2},{3,131},{131,3},{4... | collective-permute-start | bytes 786440 | tf_op jit(solution)/shard_map/ppermute | solution.py:313
  12.0 0.0 copy-done
  12.0 0.6 copy.12
  12.6 0.1 collective-permute-start.2
  12.7 0.7 collective-permute-start.3
  13.4 2.5 %shard_map.60.refs_6_ = bf16[512,256]{1,0:T(8,128)(2,1)S(1)} custom-call(bf16[2048,256]{1,0:T(8,128)(2,1)} %bitcast.34, bf16[2,256,512]{2,1,0:T(8,128)(2,1)} %c_hbm.3, bf16[2,2048,512]{2,1,0:T(8,128)(2,1)} %bitcast.26), custom_call_target="tpu_custom_call" | custom-call | flops 536870912 | bytes 2097152 | tf_op jit(solution)/shard_map/pallas_call | solution.py:77
  15.9 0.0 collective-permute-done.2.refs_4_
  15.9 1.2 %collective-permute-start.5 = (bf16[512,256]{1,0:T(8,128)(2,1)S(1)}, bf16[512,256]{1,0:T(8,128)(2,1)S(1)}, u32[]{:S(2)}, u32[]{:S(2)}) collective-permute-start(bf16[512,256]{1,0:T(8,128)(2,1)S(1)} %shard_map.60.refs_6_), channel_id=1, source_target_pairs={{0,128},{128,0},{1,129},{129,1},{2,130},{130,2},{3,131},{131,3},{4... | collective-permute-start | bytes 786440 | tf_op jit(solution)/shard_map/ppermute | solution.py:313
  17.1 2.5 %shard_map.61.refs_6_ = bf16[512,256]{1,0:T(8,128)(2,1)S(1)} custom-call(bf16[2048,256]{1,0:T(8,128)(2,1)} %bitcast.35, bf16[2,256,512]{2,1,0:T(8,128)(2,1)} %c_hbm.3, bf16[2,2048,512]{2,1,0:T(8,128)(2,1)} %bitcast.27), custom_call_target="tpu_custom_call" | custom-call | flops 536870912 | bytes 2097152 | tf_op jit(solution)/shard_map/pallas_call | solution.py:77
  19.6 0.0 collective-permute-done.3.refs_5_
  19.6 0.5 collective-permute-start.4
  20.1 0.0 collective-permute-done
  20.1 4.3 %collective-permute-start.1 = (bf16[4,64,256]{2,1,0:T(8,128)(2,1)S(1)}, bf16[4,64,256]{2,1,0:T(8,128)(2,1)S(1)}, u32[]{:S(2)}, u32[]{:S(2)}) collective-permute-start(bf16[4,64,256]{2,1,0:T(8,128)(2,1)S(1)} %get-tuple-element.57), channel_id=1, source_target_pairs={{8,16},{16,8},{24,32},{32,24},{40,48},{48,40},{56,64},{64,56},{72,... | collective-permute-start | bytes 393224 | tf_op jit(solution)/shard_map/ppermute | solution.py:320
  24.4 0.1 pad_add_fusion.refs_0_.at_ref
  24.5 2.7 %collective-permute-done.1 = bf16[4,64,256]{2,1,0:T(8,128)(2,1)S(1)} collective-permute-done((bf16[4,64,256]{2,1,0:T(8,128)(2,1)S(1)}, bf16[4,64,256]{2,1,0:T(8,128)(2,1)S(1)}, u32[]{:S(2)}, u32[]{:S(2)}) %collective-permute-start.1) | collective-permute-done | bytes 131104 | tf_op jit(solution)/shard_map/ppermute | solution.py:320
  27.1 0.0 collective-permute-done.7.refs_7_
  27.1 2.7 %shard_map.62 = (bf16[512,256]{1,0:T(8,128)(2,1)S(1)}, f32[2,256,512]{2,1,0:T(8,128)S(1)}, f32[256,256]{1,0:T(8,128)S(1)}, f32[1,256]{1,0:T(1,128)S(1)}) custom-call(s32[3]{0:T(128)S(1)} %pad_add_fusion.refs_0_.at_ref, bf16[4,8,64,256]{3,2,1,0:T(8,128)(2,1)} %refs_1_.7, bf16[4,1,64,256]{3,2,1,0:T(8,128)(2,1)S(1)} %bitcast.16, ...), custom_call_target="tpu_custom_call" | custom-call | flops 335544320 | bytes 2097152 | tf_op jit(solution)/shard_map/pallas_call | solution.py:199
  29.9 0.0 collective-permute-done.6.refs_7_
  29.9 2.7 %shard_map.63 = (bf16[512,256]{1,0:T(8,128)(2,1)S(1)}, f32[2,256,512]{2,1,0:T(8,128)S(1)}, f32[256,256]{1,0:T(8,128)S(1)}, f32[1,256]{1,0:T(1,128)S(1)}) custom-call(s32[3]{0:T(128)S(1)} %pad_add_fusion.refs_0_.at_ref, bf16[4,8,64,256]{3,2,1,0:T(8,128)(2,1)} %refs_1_.7, ...), custom_call_target="tpu_custom_call", output_to_operand_aliasing={{1}: (9, {}), {2}: (10, {}), {3}: (11, {})} | custom-call | flops 335544320 | bytes 2097152 | tf_op jit(solution)/shard_map/pallas_call | solution.py:199
  32.6 0.0 collective-permute-done.5.refs_7_
  32.7 2.8 %shard_map.64 = (bf16[512,256]{1,0:T(8,128)(2,1)S(1)}, f32[2,256,512]{2,1,0:T(8,128)S(1)}, f32[256,256]{1,0:T(8,128)S(1)}, f32[1,256]{1,0:T(1,128)S(1)}) custom-call(s32[3]{0:T(128)S(1)} %pad_add_fusion.refs_0_.at_ref, bf16[4,8,64,256]{3,2,1,0:T(8,128)(2,1)} %refs_1_.7, ...), custom_call_target="tpu_custom_call", output_to_operand_aliasing={{1}: (9, {}), {2}: (10, {}), {3}: (11, {})} | custom-call | flops 335544320 | bytes 2097152 | tf_op jit(solution)/shard_map/pallas_call | solution.py:199
  35.4 0.0 collective-permute-done.4.refs_7_
  35.4 2.9 %shard_map.65 = (bf16[512,256]{1,0:T(8,128)(2,1)S(1)}, bf16[8,168,128]{2,1,0:T(8,128)(2,1)S(1)}, bf16[8,168,128]{2,1,0:T(8,128)(2,1)S(1)}) custom-call(s32[3]{0:T(128)S(1)} %pad_add_fusion.refs_0_.at_ref, bf16[4,8,64,256]{3,2,1,0:T(8,128)(2,1)} %refs_1_.7, bf16[4,1,64,256]{3,2,1,0:T(8,128)(2,1)S(1)} %bitcast.19, bf16[4,1,64,256]{3,2,1,0:T(8,128)(2,1)S(1)} %bitcast.23, ...), custom_call_target="tpu_custom_call" | custom-call | flops 335544320 | bytes 2097152 | tf_op jit(solution)/shard_map/pallas_call | solution.py:199
  38.3 0.1 collective-permute-start.8
  38.4 1.6 %collective-permute-done.8.got_ref = bf16[8,168,128]{2,1,0:T(8,128)(2,1)S(1)} collective-permute-done((bf16[8,168,128]{2,1,0:T(8,128)(2,1)S(1)}, bf16[8,168,128]{2,1,0:T(8,128)(2,1)S(1)}, u32[]{:S(2)}, u32[]{:S(2)}) %collective-permute-start.8) | collective-permute-done | bytes 344096 | tf_op jit(solution)/shard_map/ppermute | solution.py:343
  40.1 0.1 shard_map.66
  40.2 19.3 %all_to_all.15.in_ref = bf16[8,168,128]{2,1,0:T(8,128)(2,1)S(1)} all-to-all(bf16[8,168,128]{2,1,0:T(8,128)(2,1)S(1)} %shard_map.66), channel_id=1, replica_groups=mesh['ens'=2,'xh'=2,'y'=4,'c'=2,'z'=8] {'xh','y'}, dimensions={0} | all-to-all | bytes 688128 | tf_op jit(solution)/shard_map/all_to_all | solution.py:347
  59.5 0.1 shard_map.67
  59.5 19.5 %all_to_all.16.in_ref = bf16[8,168,128]{2,1,0:T(8,128)(2,1)S(1)} all-to-all(bf16[8,168,128]{2,1,0:T(8,128)(2,1)S(1)} %shard_map.67), channel_id=1, replica_groups=mesh['ens'=2,'xh'=2,'y'=4,'c'=2,'z'=8] {'z'}, dimensions={0} | all-to-all | bytes 688128 | tf_op jit(solution)/shard_map/all_to_all | solution.py:351
  79.0 1.4 %shard_map.68 = (bf16[8,160,128]{2,1,0:T(8,128)(2,1)}, f32[2,128]{1,0:T(2,128)S(1)}) custom-call(s32[3]{0:T(128)S(1)} %pad_add_fusion.refs_0_.at_ref, bf16[8,168,128]{2,1,0:T(8,128)(2,1)S(1)} %all_to_all.16.in_ref), custom_call_target="tpu_custom_call" | custom-call | tf_op jit(solution)/shard_map/pallas_call | solution.py:352
  80.4 4.0 %all-to-all-start.2 = ((bf16[8,160,128]{2,1,0:T(8,128)(2,1)}), bf16[8,160,128]{2,1,0:T(8,128)(2,1)S(1)}, u32[]{:S(2)}, u32[]{:S(2)}) async-start(bf16[8,160,128]{2,1,0:T(8,128)(2,1)} %get-tuple-element.45), calls=%async_computation.2 | async-start | bytes 655360 | tf_op jit(solution)/shard_map/all_to_all | solution.py:363
  84.5 1.2 %shard_map.69 = bf16[4,512,256]{2,1,0:T(8,128)(2,1)} custom-call(f32[2,128]{1,0:T(2,128)S(1)} %get-tuple-element.46.shrink_ref, bf16[512,256]{1,0:T(8,128)(2,1)S(1)} %get-tuple-element.47.refs_0_, bf16[512,256]{1,0:T(8,128)(2,1)S(1)} %get-tuple-element.48.refs_1_, bf16[512,256]{1,0:T(8,128)(2,1)S(1)} %get-tuple-element.49.refs_2_, ...), custom_call_target="tpu_custom_call" | custom-call | tf_op jit(solution)/shard_map/pallas_call | solution.py:364
  85.7 6.7 %all-to-all-done.2.own_ref = bf16[8,160,128]{2,1,0:T(8,128)(2,1)S(1)} async-done(((bf16[8,160,128]{2,1,0:T(8,128)(2,1)}), bf16[8,160,128]{2,1,0:T(8,128)(2,1)S(1)}, u32[]{:S(2)}, u32[]{:S(2)}) %all-to-all-start.2) | async-done | bytes 327712 | tf_op jit(solution)/shard_map/all_to_all | solution.py:363
  92.4 4.2 %collective-permute-start.9 = (bf16[8,160,128]{2,1,0:T(8,128)(2,1)S(1)}, bf16[8,160,128]{2,1,0:T(8,128)(2,1)S(1)}, u32[]{:S(2)}, u32[]{:S(2)}) collective-permute-start(bf16[8,160,128]{2,1,0:T(8,128)(2,1)S(1)} %all-to-all-done.2.own_ref), channel_id=1, source_target_pairs={{0,8},{8,0},{1,9},{9,1},{2,10},{10,2},{3,11},{11,3},{4,12},{12,4},... | collective-permute-start | bytes 983048 | tf_op jit(solution)/shard_map/ppermute | solution.py:372
  96.6 1.3 %collective-permute-done.9.got_ref = bf16[8,160,128]{2,1,0:T(8,128)(2,1)S(1)} collective-permute-done((bf16[8,160,128]{2,1,0:T(8,128)(2,1)S(1)}, bf16[8,160,128]{2,1,0:T(8,128)(2,1)S(1)}, u32[]{:S(2)}, u32[]{:S(2)}) %collective-permute-start.9) | collective-permute-done | bytes 327712 | tf_op jit(solution)/shard_map/ppermute | solution.py:372
  97.8 1.7 %shard_map.70 = (f32[2,256,512]{2,1,0:T(8,128)}, f32[256,256]{1,0:T(8,128)}) custom-call(s32[3]{0:T(128)S(1)} %pad_add_fusion.refs_0_.at_ref, bf16[8,160,128]{2,1,0:T(8,128)(2,1)S(1)} %all-to-all-done.2.own_ref, bf16[8,160,128]{2,1,0:T(8,128)(2,1)S(1)} %collective-permute-done.9.got_ref), custom_call_target="tpu_custom_call" | custom-call | tf_op jit(solution)/shard_map/pallas_call | solution.py:373
  (1 shorter events, 0.0 us)
Async XLA Ops:
  3.2 8.8 %copy-start = (bf16[4,8,64,256]{3,2,1,0:T(8,128)(2,1)S(1)}, bf16[4,8,64,256]{3,2,1,0:T(8,128)(2,1)}, u32[]{:S(2)}) copy-start(bf16[4,8,64,256]{3,2,1,0:T(8,128)(2,1)} %refs_1_.7) | copy-start | bytes 3145732
  3.2 23.9 %collective-permute-start.7 = (bf16[512,256]{1,0:T(8,128)(2,1)S(1)}, bf16[512,256]{1,0:T(8,128)(2,1)S(1)}, u32[]{:S(2)}, u32[]{:S(2)}) collective-permute-start(bf16[512,256]{1,0:T(8,128)(2,1)S(1)} %shard_map.58.refs_6_), channel_id=1, source_target_pairs={{0,128},{128,0},{1,129},{129,1},{2,130},{130,2},{3,131},{131,3},{4... | collective-permute-start | bytes 786440 | tf_op jit(solution)/shard_map/ppermute | solution.py:313
  6.3 13.8 %collective-permute-start = (bf16[4,64,256]{2,1,0:T(8,128)(2,1)S(1)}, bf16[4,64,256]{2,1,0:T(8,128)(2,1)S(1)}, u32[]{:S(2)}, u32[]{:S(2)}) collective-permute-start(bf16[4,64,256]{2,1,0:T(8,128)(2,1)S(1)} %get-tuple-element.58), channel_id=1, source_target_pairs={{0,8},{8,0},{1,9},{9,1},{2,10},{10,2},{3,11},{11,3},{4,12},{12,4},... | collective-permute-start | bytes 393224 | tf_op jit(solution)/shard_map/ppermute | solution.py:328
  10.2 19.7 %collective-permute-start.6 = (bf16[512,256]{1,0:T(8,128)(2,1)S(1)}, bf16[512,256]{1,0:T(8,128)(2,1)S(1)}, u32[]{:S(2)}, u32[]{:S(2)}) collective-permute-start(bf16[512,256]{1,0:T(8,128)(2,1)S(1)} %shard_map.59.refs_6_), channel_id=1, source_target_pairs={{0,128},{128,0},{1,129},{129,1},{2,130},{130,2},{3,131},{131,3},{4... | collective-permute-start | bytes 786440 | tf_op jit(solution)/shard_map/ppermute | solution.py:313
  12.6 3.3 %collective-permute-start.2 = (bf16[32,256]{1,0:T(8,128)(2,1)S(1)}, bf16[32,256]{1,0:T(8,128)(2,1)S(1)}, u32[]{:S(2)}, u32[]{:S(2)}) collective-permute-start(bf16[32,256]{1,0:T(8,128)(2,1)S(1)} %get-tuple-element.56), channel_id=1, source_target_pairs={{0,1},{1,0},{2,3},{3,2},{4,5},{5,4},{6,7},{7,6},{8,9},{9,8},{10,11... | collective-permute-start | bytes 49160 | tf_op jit(solution)/shard_map/ppermute | solution.py:326
  12.7 6.9 %collective-permute-start.3 = (bf16[32,256]{1,0:T(8,128)(2,1)S(1)}, bf16[32,256]{1,0:T(8,128)(2,1)S(1)}, u32[]{:S(2)}, u32[]{:S(2)}) collective-permute-start(bf16[32,256]{1,0:T(8,128)(2,1)S(1)} %get-tuple-element.55), channel_id=1, source_target_pairs={{1,2},{2,1},{3,4},{4,3},{5,6},{6,5},{9,10},{10,9},{11,12},{12,11},... | collective-permute-start | bytes 49160 | tf_op jit(solution)/shard_map/ppermute | solution.py:327
  15.9 16.7 %collective-permute-start.5 = (bf16[512,256]{1,0:T(8,128)(2,1)S(1)}, bf16[512,256]{1,0:T(8,128)(2,1)S(1)}, u32[]{:S(2)}, u32[]{:S(2)}) collective-permute-start(bf16[512,256]{1,0:T(8,128)(2,1)S(1)} %shard_map.60.refs_6_), channel_id=1, source_target_pairs={{0,128},{128,0},{1,129},{129,1},{2,130},{130,2},{3,131},{131,3},{4... | collective-permute-start | bytes 786440 | tf_op jit(solution)/shard_map/ppermute | solution.py:313
  19.6 15.8 %collective-permute-start.4 = (bf16[512,256]{1,0:T(8,128)(2,1)S(1)}, bf16[512,256]{1,0:T(8,128)(2,1)S(1)}, u32[]{:S(2)}, u32[]{:S(2)}) collective-permute-start(bf16[512,256]{1,0:T(8,128)(2,1)S(1)} %shard_map.61.refs_6_), channel_id=1, source_target_pairs={{0,128},{128,0},{1,129},{129,1},{2,130},{130,2},{3,131},{131,3},{4... | collective-permute-start | bytes 786440 | tf_op jit(solution)/shard_map/ppermute | solution.py:313
  20.1 7.0 %collective-permute-start.1 = (bf16[4,64,256]{2,1,0:T(8,128)(2,1)S(1)}, bf16[4,64,256]{2,1,0:T(8,128)(2,1)S(1)}, u32[]{:S(2)}, u32[]{:S(2)}) collective-permute-start(bf16[4,64,256]{2,1,0:T(8,128)(2,1)S(1)} %get-tuple-element.57), channel_id=1, source_target_pairs={{8,16},{16,8},{24,32},{32,24},{40,48},{48,40},{56,64},{64,56},{72,... | collective-permute-start | bytes 393224 | tf_op jit(solution)/shard_map/ppermute | solution.py:320
  38.3 1.7 %collective-permute-start.8 = (bf16[8,168,128]{2,1,0:T(8,128)(2,1)S(1)}, bf16[8,168,128]{2,1,0:T(8,128)(2,1)S(1)}, u32[]{:S(2)}, u32[]{:S(2)}) collective-permute-start(bf16[8,168,128]{2,1,0:T(8,128)(2,1)S(1)} %get-tuple-element.44), channel_id=1, source_target_pairs={{0,8},{8,0},{1,9},{9,1},{2,10},{10,2},{3,11},{11,3},{4,12},{12,4},... | collective-permute-start | bytes 1032200 | tf_op jit(solution)/shard_map/ppermute | solution.py:343
  80.4 11.9 %all-to-all-start.2 = ((bf16[8,160,128]{2,1,0:T(8,128)(2,1)}), bf16[8,160,128]{2,1,0:T(8,128)(2,1)S(1)}, u32[]{:S(2)}, u32[]{:S(2)}) async-start(bf16[8,160,128]{2,1,0:T(8,128)(2,1)} %get-tuple-element.45), calls=%async_computation.2 | async-start | bytes 655360 | tf_op jit(solution)/shard_map/all_to_all | solution.py:363
  92.4 5.4 %collective-permute-start.9 = (bf16[8,160,128]{2,1,0:T(8,128)(2,1)S(1)}, bf16[8,160,128]{2,1,0:T(8,128)(2,1)S(1)}, u32[]{:S(2)}, u32[]{:S(2)}) collective-permute-start(bf16[8,160,128]{2,1,0:T(8,128)(2,1)S(1)} %all-to-all-done.2.own_ref), channel_id=1, source_target_pairs={{0,8},{8,0},{1,9},{9,1},{2,10},{10,2},{3,11},{11,3},{4,12},{12,4},... | collective-permute-start | bytes 983048 | tf_op jit(solution)/shard_map/ppermute | solution.py:372

commit v4 on v2

v4 whole, which is shorter than its diff:
```python
import functools
import math

import jax
import jax.numpy as jnp
from jax import lax
from jax.experimental import pallas as pl
from jax.experimental.pallas import tpu as pltpu
from jax.sharding import Mesh, PartitionSpec as P

ETA = 0.25
LAM = 0.5
TAU = 0.4

F32 = jnp.float32
BF16 = jnp.bfloat16
VMEM_LIMIT = 40 * 1024 * 1024
PARAMS = pltpu.CompilerParams(vmem_limit_bytes=VMEM_LIMIT)

SX = ("xh", "y", "c")
PLANE = ("xh", "y")
PARTS = 8
PROJ_ROWS = 128
GRAM_ROWS = 32
SUM_ROWS = PROJ_ROWS + GRAM_ROWS
PART_ROWS = SUM_ROWS + 8

VM = pl.BlockSpec(memory_space=pltpu.VMEM)
SM = pl.BlockSpec(memory_space=pltpu.SMEM)
HBM = pl.BlockSpec(memory_space=pltpu.HBM)


def core_of(place):
    return place & 1


def parity_of(place):
    return (place >> 1) & 1


def part_of(place):
    return place >> 2


def gradient(m, coefficients, series):
    acc = None
    for e in range(len(coefficients)):
        c = coefficients[e]()
        fitted = jnp.dot(m, c, preferred_element_type=F32)
        misfit = (fitted - series[e]().astype(F32)).astype(BF16)
        term = lax.dot_general(misfit, c, (((1,), (1,)), ((), ())), preferred_element_type=F32)
        acc = term if acc is None else acc + term
    return acc.astype(BF16)


def first_grad_kernel(count, at_ref, m_hbm, c_hbm, x_hbm, *refs):
    g_ref, m_ref, c_ref, x_ref, xa_ref, xb_ref, za_ref, zb_ref, tmp_ref, sems = refs
    members, levels, cells, _ = x_hbm.shape
    _, rows_x, rows_y, width = m_ref.shape
    head, rest = pl.ds(0, count), pl.ds(count, levels - count)
    copies = [(m_hbm, m_ref)]
    for e in range(members):
        copies.append((c_hbm.at[e], c_ref.at[e]))
        copies.append((x_hbm.at[e, head], x_ref.at[e, head]))
    for e in range(members):
        copies.append((x_hbm.at[e, rest], x_ref.at[e, rest]))
    copies = [pltpu.make_async_copy(s, d, sems.at[i]) for i, (s, d) in enumerate(copies)]
    for copy in copies:
        copy.start()
    copies[0].wait()

    def part(copy, ref, *at):
        def load():
            copy.wait()
            return ref[at].reshape(-1, ref.shape[-1])

        return load

    g_ref[...] = gradient(
        m_ref[0:count].reshape(count * cells, width),
        [part(copies[1 + 2 * e], c_ref, e) for e in range(members)],
        [part(copies[2 + 2 * e], x_ref, e, slice(0, count)) for e in range(members)],
    )
    core, even = core_of(at_ref[0]), parity_of(at_ref[0]) == 0
    xa_ref[...] = m_ref[:, (rows_x - 1) * (1 - core)]
    xb_ref[...] = m_ref[:, (rows_x - 1) * core]
    tmp_ref[0] = m_ref[:, :, 0:8, :].reshape(levels * rows_x, 8, width).astype(F32)
    tmp_ref[1] = m_ref[:, :, rows_y - 8 : rows_y, :].reshape(levels * rows_x, 8, width).astype(F32)
    lo, hi = tmp_ref[0, :, 0, :], tmp_ref[1, :, 7, :]
    za_ref[...] = jnp.where(even, hi, lo).astype(BF16)
    zb_ref[...] = jnp.where(even, lo, hi).astype(BF16)
    for copy in copies[1 + 2 * members :]:
        copy.wait()


def grad_kernel(level, m_ref, c_ref, x_ref, g_ref):
    members = c_ref.shape[0]

    def part(ref, *at):
        return lambda: ref[at]

    g_ref[...] = gradient(
        m_ref[level].reshape(g_ref.shape),
        [part(c_ref, e) for e in range(members)],
        [part(x_ref, e, level) for e in range(members)],
    )


def grad_cost(members, cells, frames, width):
    return pl.CostEstimate(
        flops=4 * members * cells * frames * width,
        bytes_accessed=2 * cells * (2 * width + members * frames) + 2 * members * width * frames,
        transcendentals=0,
    )


def first_grad(place, modes, coefficients, series, count):
    members, levels, cells, frames = series.shape
    _, rows_x, rows_y, width = modes.shape
    arrays = [modes, coefficients, series]
    outs = [jax.ShapeDtypeStruct((count * cells, width), BF16)]
    outs += [pltpu.VMEM(a.shape, a.dtype) for a in arrays]
    outs += [jax.ShapeDtypeStruct((levels, rows_y, width), BF16)] * 2
    outs += [jax.ShapeDtypeStruct((levels * rows_x, width), BF16)] * 2
    return pl.pallas_call(
        functools.partial(first_grad_kernel, count),
        in_specs=[SM] + [HBM] * 3,
        out_specs=[VM] * len(outs),
        out_shape=outs,
        scratch_shapes=[
            pltpu.VMEM((2, levels * rows_x, 8, width), F32),
            pltpu.SemaphoreType.DMA((1 + 3 * members,)),
        ],
        compiler_params=PARAMS,
        cost_estimate=grad_cost(members, count * cells, frames, width),
    )(place, *[pltpu.with_memory_space_constraint(a, pltpu.HBM) for a in arrays])


def grad_level(modes, coefficients, series, level):
    members, _, cells, frames = series.shape
    width = modes.shape[3]
    return pl.pallas_call(
        functools.partial(grad_kernel, level),
        in_specs=[VM] * 3,
        out_specs=VM,
        out_shape=jax.ShapeDtypeStruct((cells, width), BF16),
        compiler_params=PARAMS,
        cost_estimate=grad_cost(members, cells, frames, width),
    )(modes, coefficients, series)


def base_kernel(at_ref, m_ref, xa_ref, xb_ref, za_ref, zb_ref, base_ref):
    levels, rows_x, rows_y, width = m_ref.shape
    lower, even = core_of(at_ref[0]) == 0, parity_of(at_ref[0]) == 0
    shape = (rows_x, rows_y, width)
    at = lax.broadcasted_iota(jnp.int32, shape, 1)
    for level in range(levels):
        f = m_ref[level].astype(F32)
        xa, xb = xa_ref[level : level + 1].astype(F32), xb_ref[level : level + 1].astype(F32)
        rows = slice(level * rows_x, (level + 1) * rows_x)
        za, zb = za_ref[rows, :].astype(F32), zb_ref[rows, :].astype(F32)
        up = jnp.concatenate([jnp.where(lower, xb, xa), f[:-1]], axis=0)
        down = jnp.concatenate([f[1:], jnp.where(lower, xa, xb)], axis=0)
        zlo = jnp.broadcast_to(jnp.where(even, zb, za)[:, None, :], shape)
        zhi = jnp.broadcast_to(jnp.where(even, za, zb)[:, None, :], shape)
        left = jnp.where(at == 0, zlo, pltpu.roll(f, 1, 1))
        right = jnp.where(at == rows_y - 1, zhi, pltpu.roll(f, rows_y - 1, 1))
        bent = 4.0 * f - (down + up + right + left)
        base_ref[level] = (f - (ETA * LAM) * bent).reshape(rows_x * rows_y, width)


def split_squares(squares, rows):
    high = squares.astype(BF16).astype(F32)
    return jnp.concatenate([high, squares - high, jnp.zeros((rows - 4, 128), F32)], axis=0)


def emit(out_ref, half, proj_ref, gram_ref, squares):
    members = proj_ref.shape[0]
    for j in range(PARTS):
        tb, m, r = j // 4, (j // 2) % members, j % 2
        at = pl.multiple_of((half * 2 + tb) * 128, 128)
        block = proj_ref[m, r * 128 : (r + 1) * 128, pl.ds(at, 128)]
        out_ref[j, 0:PROJ_ROWS, :] = block.astype(BF16)
        at = pl.multiple_of(half * 128, 128)
        block = gram_ref[j * GRAM_ROWS : (j + 1) * GRAM_ROWS, pl.ds(at, 128)]
        out_ref[j, PROJ_ROWS:SUM_ROWS, :] = block.astype(BF16)
        out_ref[j, SUM_ROWS:PART_ROWS, :] = squares


def step_kernel(level, count, first, last, *refs):
    (at_ref, base_ref, own_ref, got_ref, x_ref), refs = refs[:5], refs[5:]
    if not first:
        (proj_in, gram_in, squares_in), refs = refs[:3], refs[3:]
    if last:
        moved_ref, keep_ref, send_ref, proj_ref, gram_ref = refs
    else:
        moved_ref, proj_ref, gram_ref, squares_ref = refs
    grad = own_ref[...].astype(F32) + got_ref[...].astype(F32)
    levels = slice(level, level + count)
    moved = (base_ref[levels].reshape(grad.shape) - ETA * grad).astype(BF16)
    moved_ref[...] = moved
    wide = moved.astype(F32)
    squares = jnp.sum(wide * wide, axis=0, keepdims=True)
    if not first:
        squares = squares + squares_in[...]
    turned = moved.T
    gram = jnp.dot(turned, moved, preferred_element_type=F32)
    gram_ref[...] = gram if first else gram_in[...] + gram
    for e in range(x_ref.shape[0]):
        x = x_ref[e, levels].reshape(grad.shape[0], -1)
        proj = jnp.dot(turned, x, preferred_element_type=F32)
        proj_ref[e] = proj if first else proj_in[e] + proj
    if last:
        core = core_of(at_ref[0])
        pair = jnp.concatenate([squares[:, 0:128], squares[:, 128:256]], axis=0)
        packed = split_squares(pair, 8).astype(BF16)
        emit(send_ref, 1 - core, proj_ref, gram_ref, packed)
        emit(keep_ref, core, proj_ref, gram_ref, packed)
    else:
        squares_ref[...] = squares


def step_levels(level, count, place, base, own, got, series, carry):
    members, levels, cells, frames = series.shape
    rows, width = own.shape
    first, last = carry is None, level + count == levels
    args = [place, base, own, got, series]
    if not first:
        args += list(carry)
    sums = [
        jax.ShapeDtypeStruct((members, width, frames), F32),
        jax.ShapeDtypeStruct((width, width), F32),
        jax.ShapeDtypeStruct((1, width), F32),
    ]
    outs = [jax.ShapeDtypeStruct((rows, width), BF16)]
    scratch, aliases = [], {}
    if last:
        outs += [jax.ShapeDtypeStruct((PARTS, PART_ROWS, 128), BF16)] * 2
        scratch = [pltpu.VMEM(s.shape, F32) for s in sums[:2]]
    else:
        outs += sums
        if not first:
            aliases = {5 + i: 1 + i for i in range(3)}
    return pl.pallas_call(
        functools.partial(step_kernel, level, count, first, last),
        in_specs=[SM] + [VM] * (len(args) - 1),
        out_specs=[VM] * len(outs),
        out_shape=outs,
        scratch_shapes=scratch,
        input_output_aliases=aliases,
        compiler_params=PARAMS,
        cost_estimate=pl.CostEstimate(
            flops=2 * rows * width * (width + members * frames),
            bytes_accessed=2 * rows * (4 * width + members * frames),
            transcendentals=0,
        ),
    )(*args)


def whole_squares(part):
    return part[SUM_ROWS : SUM_ROWS + 2, :] + part[SUM_ROWS + 2 : SUM_ROWS + 4, :]


def join_kernel(keep_ref, got_ref, out_ref):
    out_ref[:, 0:SUM_ROWS, :] = (
        keep_ref[:, 0:SUM_ROWS, :].astype(F32) + got_ref[:, 0:SUM_ROWS, :].astype(F32)
    ).astype(BF16)
    tail = keep_ref[0, SUM_ROWS:PART_ROWS, :].astype(F32) + got_ref[0, SUM_ROWS:PART_ROWS, :].astype(F32)
    packed = split_squares(tail[0:2, :] + tail[2:4, :], 8).astype(BF16)
    for j in range(PARTS):
        out_ref[j, SUM_ROWS:PART_ROWS, :] = packed


def gather_sum(in_ref):
    total = in_ref[0].astype(F32)
    for j in range(1, PARTS):
        total = total + in_ref[j].astype(F32)
    return total


def plane_kernel(in_ref, out_ref):
    total = gather_sum(in_ref)
    packed = split_squares(whole_squares(total), 8)
    mine = jnp.concatenate([total[0:SUM_ROWS, :], packed], axis=0).astype(BF16)
    for j in range(PARTS):
        out_ref[j] = mine


def reduce_kernel(total_cells, at_ref, in_ref, out_ref, shrink_ref, column_ref):
    core, part = core_of(at_ref[0]), part_of(at_ref[0])
    total = gather_sum(in_ref)
    squares = whole_squares(total)
    shrink = jnp.maximum(0.0, 1.0 - TAU / jnp.sqrt(squares / total_cells + 1e-06))
    shrink_ref[...] = shrink
    for k in range(2):
        column_ref[k * 128 : (k + 1) * 128, :] = jnp.broadcast_to(shrink[k : k + 1, :], (128, 128)).T
    at = pl.multiple_of(lax.rem(part, 2) * 128, 128)
    proj = column_ref[pl.ds(at, 128), :] * total[0:PROJ_ROWS, :] * (1.0 / math.sqrt(total_cells))
    at = pl.multiple_of(part * GRAM_ROWS, GRAM_ROWS)
    lanes = jnp.where(core == 0, shrink[0:1, :], shrink[1:2, :])
    gram = column_ref[pl.ds(at, GRAM_ROWS), :] * total[PROJ_ROWS:SUM_ROWS, :] * lanes * (1.0 / total_cells)
    mine = jnp.concatenate([proj, gram], axis=0).astype(BF16)
    for j in range(PARTS):
        out_ref[j] = mine


def scale_kernel(shrink_ref, *refs):
    out_ref = refs[-1]
    at = 0
    for m_ref in refs[:-1]:
        rows = slice(at, at + m_ref.shape[0])
        at = rows.stop
        for k in range(2):
            lanes = slice(k * 128, (k + 1) * 128)
            out_ref[rows, lanes] = (m_ref[:, lanes].astype(F32) * shrink_ref[k : k + 1, :]).astype(BF16)


def final_kernel(at_ref, own_ref, got_ref, proj_ref, gram_ref):
    core = core_of(at_ref[0])
    members = proj_ref.shape[0]
    for ref, half in ((own_ref, core), (got_ref, 1 - core)):
        for j in range(PARTS):
            tb, m, r = j // 4, (j // 2) % members, j % 2
            at = pl.multiple_of((half * 2 + tb) * 128, 128)
            proj_ref[m, r * 128 : (r + 1) * 128, pl.ds(at, 128)] = ref[j, 0:PROJ_ROWS, :].astype(F32)
            at = pl.multiple_of(half * 128, 128)
            gram_ref[j * GRAM_ROWS : (j + 1) * GRAM_ROWS, pl.ds(at, 128)] = (
                ref[j, PROJ_ROWS:SUM_ROWS, :].astype(F32)
            )


def both_ways(pairs):
    return [p for i, j in pairs for p in ((i, j), (j, i))]


def local(snapshots, coefficients, modes):
    members, levels, rows_x, rows_y, frames = snapshots.shape
    width = modes.shape[3]
    cells = rows_x * rows_y
    local_cells = levels * cells
    n_sx, n_z = lax.axis_size(SX), lax.axis_size("z")
    total_cells = local_cells * n_sx * n_z
    core = lax.axis_index("c").astype(jnp.int32)
    parity = lax.axis_index("z").astype(jnp.int32) & 1
    part = lax.axis_index(PLANE).astype(jnp.int32)
    place = (core + 2 * parity + 4 * part).reshape(1)
    series = snapshots.reshape(members, levels, cells, frames)
    swap = [(0, 1), (1, 0)]

    chunks = [(0, 2), (2, 1), (3, 1)]
    g, modes, coefficients, series, edge_a, edge_b, row_a, row_b = first_grad(
        place, modes, coefficients, series, chunks[0][1]
    )
    own, got = [g], [lax.ppermute(g, "ens", swap)]
    xb = lax.ppermute(edge_b, SX, both_ways([(i, i + 1) for i in range(1, n_sx - 1, 2)]))
    za = lax.ppermute(row_a, "z", both_ways([(i, i + 1) for i in range(0, n_z, 2)]))
    zb = lax.ppermute(row_b, "z", both_ways([(i, i + 1) for i in range(1, n_z - 1, 2)]))
    xa = lax.ppermute(edge_a, "c", swap)

    def send_level(level, *after):
        c, *_ = lax.optimization_barrier((coefficients, *after))
        g = grad_level(modes, c, series, level)
        own.append(g)
        got.append(lax.ppermute(g, "ens", swap))

    send_level(2, xa, xb, za, zb)
    base = pl.pallas_call(
        base_kernel,
        in_specs=[SM] + [VM] * 5,
        out_specs=VM,
        out_shape=jax.ShapeDtypeStruct((levels, cells, width), F32),
        compiler_params=PARAMS,
        cost_estimate=pl.CostEstimate(flops=12 * local_cells * width, bytes_accessed=6 * local_cells * width, transcendentals=0),
    )(place, modes, xa, xb, za, zb)
    send_level(3, own[1], base)

    moved, carry = [], None
    for i, (level, count) in enumerate(chunks):
        m, *carry = step_levels(level, count, place, base, own[i], got[i], series, carry)
        moved.append(m)
    keep, send = carry

    part_shape = jax.ShapeDtypeStruct((PARTS, PART_ROWS, 128), BF16)
    other = lax.ppermute(send, "c", swap)
    joined = pl.pallas_call(
        join_kernel, in_specs=[VM, VM], out_specs=VM, out_shape=part_shape, compiler_params=PARAMS
    )(keep, other)
    parts = lax.all_to_all(joined, PLANE, 0, 0)
    planes = pl.pallas_call(
        plane_kernel, in_specs=[VM], out_specs=VM, out_shape=part_shape, compiler_params=PARAMS
    )(parts)
    planes = lax.all_to_all(planes, "z", 0, 0)
    spread, shrink = pl.pallas_call(
        functools.partial(reduce_kernel, total_cells),
        in_specs=[SM, VM],
        out_specs=[VM, VM],
        out_shape=[
            jax.ShapeDtypeStruct((PARTS, SUM_ROWS, 128), BF16),
            jax.ShapeDtypeStruct((2, 128), F32),
        ],
        scratch_shapes=[pltpu.VMEM((width, 128), F32)],
        compiler_params=PARAMS,
    )(place, planes)
    half = lax.all_to_all(spread, PLANE, 0, 0)
    new_modes = pl.pallas_call(
        scale_kernel,
        in_specs=[VM] * (1 + len(moved)),
        out_specs=VM,
        out_shape=jax.ShapeDtypeStruct((local_cells, width), BF16),
        compiler_params=PARAMS,
    )(shrink, *moved)
    half, new_modes = lax.optimization_barrier((half, new_modes))
    other_half = lax.ppermute(half, "c", swap)
    projected, gram = pl.pallas_call(
        final_kernel,
        in_specs=[SM, VM, VM],
        out_specs=[VM, VM],
        out_shape=[
            jax.ShapeDtypeStruct((members, width, frames), F32),
            jax.ShapeDtypeStruct((width, width), F32),
        ],
        compiler_params=PARAMS,
    )(place, half, other_half)
    return (new_modes.reshape(levels, rows_x, rows_y, width), gram, projected)


def solution(mesh):
    ens, n_sx, n_sy = (mesh.shape[a] for a in ("ens", "sx", "sy"))
    fine = Mesh(mesh.devices.reshape(ens, 2, n_sx // 4, 2, n_sy), ("ens", "xh", "y", "c", "z"))
    in_specs = (P("ens", None, SX, "z", None), P("ens", None, None), P(None, SX, "z", None))
    out_specs = (P(None, SX, "z", None), P(), P("ens", None, None))
    return jax.shard_map(local, mesh=fine, in_specs=in_specs, out_specs=out_specs, check_vma=False)
```

time: 103 us -> 88.3 us (0.86)
  local copies, waits for them, and re-layouts: 9.45 us -> 0 us
  blocking collectives: 42.5 us -> 35.5 us
  waiting for transfers between devices: 13.5 us -> 19.3 us
  Pallas kernels: 15.4 us -> 12.9 us
  starting transfers between devices: 20.8 us -> 19.7 us
    unnamed x18 -> x0, local copies, waits for them, and re-layouts: 8.84 us -> none
    all_to_all x1, blocking collectives: 22.7 us -> 16.4 us  [local(): parts = lax.all_to_all(joined, PLANE, 0, 0)]
    ppermute x8 -> x7, waiting for transfers between devices: 4.23 us -> 10 us  [the longest x2 8.57 us: send_level(): got.append(lax.ppermute(g, 'ens', swap))]
    pallas_call x9 -> x8, Pallas kernels: 12 us -> 10.6 us  [the longest x1 3.82 us: first_grad(): pl.pallas_call(functools.partial(first_grad_kernel, count), in_specs=[SM]...]
    ppermute x8 -> x7, starting transfers between devices: 11.7 us -> 10.4 us  [the longest x1 2.74 us: local(): lax.ppermute(edge_b, SX, both_ways([(i, i + 1) for i in range(1, n_sx - 1...]
  transfers between devices with their start and end apart: 11 -> 10, of which waited for: 5 -> 7; matrix products, arithmetic and copies ran while one was open for 1% -> 0% of each run, Pallas kernels for 9% -> 7%
where the time goes in v4:
time: 88.3 us; the launch traced here: 88 us
  blocking collectives  35.5 us (40%)
  starting transfers between devices  19.7 us (22%)
  waiting for transfers between devices  19.3 us (22%)
  Pallas kernels  12.9 us (15%)
    all_to_all x1, blocking collectives, local(): planes = lax.all_to_all(planes, 'z', 0, 0)  19.1 us
    all_to_all x1, blocking collectives, local(): parts = lax.all_to_all(joined, PLANE, 0, 0)  16.4 us
    ppermute x2, waiting for transfers between devices, send_level(): got.append(lax.ppermute(g, 'ens', swap))  8.57 us
    all_to_all x1, waiting for transfers between devices, local(): half = lax.all_to_all(spread, PLANE, 0, 0)  6.72 us
    ppermute x1, starting transfers between devices, local(): other_half = lax.ppermute(half, 'c', swap)  4.17 us
    all_to_all x1, starting transfers between devices, local(): half = lax.all_to_all(spread, PLANE, 0, 0)  4.05 us
    pallas_call x1, Pallas kernels, first_grad(): pl.pallas_call(functools.partial(first_grad_kernel, count), in_specs=[SM]...  3.82 us
    pallas_call x3, Pallas kernels, step_levels(): pl.pallas_call(functools.partial(step_kernel, level, count, first, last),...  2.78 us
  transfers between devices with their start and end apart: 10, of which 7 were waited for; matrix products, arithmetic and copies ran while one was open for 0% of the time, Pallas kernels for 7%

profile of v4, /device:TPU:1, one launch (start us, length us, event | category | flops | bytes accessed | tf_op | source)
XLA Modules:
  0.0 88.0 jit_solution(2505598387131939447)
XLA Ops:
  0.6 3.8 %shard_map.58 = (bf16[1024,256]{1,0:T(8,128)(2,1)S(1)}, bf16[4,8,64,256]{3,2,1,0:T(8,128)(2,1)S(1)}, bf16[2,256,512]{2,1,0:T(8,128)(2,1)S(1)}, bf16[2,4,512,512]...) custom-call(s32[1]{0:T(128)} %bitcast.at_ref.refs_0_, ...), custom_call_target="tpu_custom_call" | custom-call | flops 1073741824 | bytes 3670016 | tf_op jit(solution)/shard_map/pallas_call | solution.py:125
  4.5 2.1 %collective-permute-start.6 = (bf16[1024,256]{1,0:T(8,128)(2,1)S(1)}, bf16[1024,256]{1,0:T(8,128)(2,1)S(1)}, u32[]{:S(2)}, u32[]{:S(2)}) collective-permute-start(bf16[1024,256]{1,0:T(8,128)(2,1)S(1)} %get-tuple-element.39.refs_2_), channel_id=1, source_target_pairs={{0,128},{128,0},{1,129},{129,1},{2,130},{130,2},{3,131},{131,3},{4... | collective-permute-start | bytes 1572872 | tf_op jit(solution)/shard_map/ppermute | solution.py:354
  6.6 1.3 %collective-permute-start = (bf16[4,64,256]{2,1,0:T(8,128)(2,1)S(1)}, bf16[4,64,256]{2,1,0:T(8,128)(2,1)S(1)}, u32[]{:S(2)}, u32[]{:S(2)}) collective-permute-start(bf16[4,64,256]{2,1,0:T(8,128)(2,1)S(1)} %get-tuple-element.31), channel_id=1, source_target_pairs={{0,8},{8,0},{1,9},{9,1},{2,10},{10,2},{3,11},{11,3},{4,12},{12,4},... | collective-permute-start | bytes 393224 | tf_op jit(solution)/shard_map/ppermute | solution.py:358
  7.9 2.7 %collective-permute-start.1 = (bf16[4,64,256]{2,1,0:T(8,128)(2,1)S(1)}, bf16[4,64,256]{2,1,0:T(8,128)(2,1)S(1)}, u32[]{:S(2)}, u32[]{:S(2)}) collective-permute-start(bf16[4,64,256]{2,1,0:T(8,128)(2,1)S(1)} %get-tuple-element.32), channel_id=1, source_target_pairs={{8,16},{16,8},{24,32},{32,24},{40,48},{48,40},{56,64},{64,56},{72,... | collective-permute-start | bytes 393224 | tf_op jit(solution)/shard_map/ppermute | solution.py:355
  10.6 1.7 %collective-permute-start.2 = (bf16[32,256]{1,0:T(8,128)(2,1)S(1)}, bf16[32,256]{1,0:T(8,128)(2,1)S(1)}, u32[]{:S(2)}, u32[]{:S(2)}) collective-permute-start(bf16[32,256]{1,0:T(8,128)(2,1)S(1)} %get-tuple-element.33), channel_id=1, source_target_pairs={{0,1},{1,0},{2,3},{3,2},{4,5},{5,4},{6,7},{7,6},{8,9},{9,8},{10,11... | collective-permute-start | bytes 49160 | tf_op jit(solution)/shard_map/ppermute | solution.py:356
  12.4 0.7 collective-permute-start.3
  13.0 0.8 collective-permute-done.2.za_ref
  13.8 0.0 collective-permute-done.3.zb_ref
  13.8 0.0 collective-permute-done.xa_ref
  13.8 0.7 collective-permute-done.1.xb_ref
  14.5 1.0 %shard_map.60.refs_2_ = bf16[512,256]{1,0:T(8,128)(2,1)S(1)} custom-call(bf16[4,8,64,256]{3,2,1,0:T(8,128)(2,1)S(1)} %get-tuple-element.30.m_ref, bf16[2,256,512]{2,1,0:T(8,128)(2,1)S(1)} %get-tuple-element.38.c_ref, bf16[2,4,512,512]{3,2,1,0:T(8,128)(2,1)S(1)} %get-tuple-element.37.x_ref.refs_4_), custom_call_target="tpu_custom_call" | custom-call | flops 536870912 | bytes 2097152 | tf_op jit(solution)/shard_map/pallas_call | solution.py:142
  15.4 1.7 %collective-permute-start.5 = (bf16[512,256]{1,0:T(8,128)(2,1)S(1)}, bf16[512,256]{1,0:T(8,128)(2,1)S(1)}, u32[]{:S(2)}, u32[]{:S(2)}) collective-permute-start(bf16[512,256]{1,0:T(8,128)(2,1)S(1)} %shard_map.60.refs_2_), channel_id=1, source_target_pairs={{0,128},{128,0},{1,129},{129,1},{2,130},{130,2},{3,131},{131,3},{4... | collective-permute-start | bytes 786440 | tf_op jit(solution)/shard_map/ppermute | solution.py:364
  17.2 0.9 %shard_map.59.refs_1_ = f32[4,512,256]{2,1,0:T(8,128)S(1)} custom-call(s32[1]{0:T(128)} %bitcast.at_ref.refs_0_, bf16[4,8,64,256]{3,2,1,0:T(8,128)(2,1)S(1)} %get-tuple-element.30.m_ref, bf16[4,64,256]{2,1,0:T(8,128)(2,1)S(1)} %collective-permute-done.xa_ref, bf16[4,64,256]{2,1,0:T(8,128)(2,1)S(1)} %collective-permute-done.1.xb_ref, ...), custom_call_target="tpu_custom_call" | custom-call | flops 6291456 | bytes 3145728 | tf_op jit(solution)/shard_map/pallas_call | solution.py:367
  18.1 1.0 %shard_map.61.refs_2_ = bf16[512,256]{1,0:T(8,128)(2,1)S(1)} custom-call(bf16[4,8,64,256]{3,2,1,0:T(8,128)(2,1)S(1)} %get-tuple-element.30.m_ref, bf16[2,256,512]{2,1,0:T(8,128)(2,1)S(1)} %get-tuple-element.38.c_ref, bf16[2,4,512,512]{3,2,1,0:T(8,128)(2,1)S(1)} %get-tuple-element.37.x_ref.refs_4_), custom_call_target="tpu_custom_call" | custom-call | flops 536870912 | bytes 2097152 | tf_op jit(solution)/shard_map/pallas_call | solution.py:142
  19.1 0.1 collective-permute-start.4
  19.2 0.0 collective-permute-done.6.refs_3_
  19.2 1.1 %shard_map.62 = (bf16[1024,256]{1,0:T(8,128)(2,1)S(1)}, f32[2,256,512]{2,1,0:T(8,128)S(1)}, f32[256,256]{1,0:T(8,128)S(1)}, f32[1,256]{1,0:T(1,128)S(1)}) custom-call(s32[1]{0:T(128)} %bitcast.at_ref.refs_0_, f32[4,512,256]{2,1,0:T(8,128)S(1)} %shard_map.59.refs_1_, bf16[1024,256]{1,0:T(8,128)(2,1)S(1)} %get-tuple-element.39.refs_2_, ...), custom_call_target="tpu_custom_call" | custom-call | flops 671088640 | bytes 4194304 | tf_op jit(solution)/shard_map/pallas_call | solution.py:244
  20.3 3.8 %collective-permute-done.5.refs_3_ = bf16[512,256]{1,0:T(8,128)(2,1)S(1)} collective-permute-done((bf16[512,256]{1,0:T(8,128)(2,1)S(1)}, bf16[512,256]{1,0:T(8,128)(2,1)S(1)}, u32[]{:S(2)}, u32[]{:S(2)}) %collective-permute-start.5) | collective-permute-done | bytes 262176 | tf_op jit(solution)/shard_map/ppermute | solution.py:364
  24.1 0.8 shard_map.63
  24.9 4.8 %collective-permute-done.4.refs_3_ = bf16[512,256]{1,0:T(8,128)(2,1)S(1)} collective-permute-done((bf16[512,256]{1,0:T(8,128)(2,1)S(1)}, bf16[512,256]{1,0:T(8,128)(2,1)S(1)}, u32[]{:S(2)}, u32[]{:S(2)}) %collective-permute-start.4) | collective-permute-done | bytes 262176 | tf_op jit(solution)/shard_map/ppermute | solution.py:364
  29.7 0.8 shard_map.64
  30.6 1.1 %collective-permute-start.7 = (bf16[8,168,128]{2,1,0:T(8,128)(2,1)S(1)}, bf16[8,168,128]{2,1,0:T(8,128)(2,1)S(1)}, u32[]{:S(2)}, u32[]{:S(2)}) collective-permute-start(bf16[8,168,128]{2,1,0:T(8,128)(2,1)S(1)} %get-tuple-element.47), channel_id=1, source_target_pairs={{0,8},{8,0},{1,9},{9,1},{2,10},{10,2},{3,11},{11,3},{4,12},{12,4},... | collective-permute-start | bytes 1032200 | tf_op jit(solution)/shard_map/ppermute | solution.py:384
  31.7 1.3 %collective-permute-done.7.got_ref = bf16[8,168,128]{2,1,0:T(8,128)(2,1)S(1)} collective-permute-done((bf16[8,168,128]{2,1,0:T(8,128)(2,1)S(1)}, bf16[8,168,128]{2,1,0:T(8,128)(2,1)S(1)}, u32[]{:S(2)}, u32[]{:S(2)}) %collective-permute-start.7) | collective-permute-done | bytes 344096 | tf_op jit(solution)/shard_map/ppermute | solution.py:384
  32.9 0.1 shard_map.65
  33.0 16.4 %all_to_all.15.in_ref = bf16[8,168,128]{2,1,0:T(8,128)(2,1)S(1)} all-to-all(bf16[8,168,128]{2,1,0:T(8,128)(2,1)S(1)} %shard_map.65), channel_id=1, replica_groups=mesh['ens'=2,'xh'=2,'y'=4,'c'=2,'z'=8] {'xh','y'}, dimensions={0} | all-to-all | bytes 688128 | tf_op jit(solution)/shard_map/all_to_all | solution.py:388
  49.4 0.1 shard_map.66
  49.5 19.1 %all_to_all.16.in_ref = bf16[8,168,128]{2,1,0:T(8,128)(2,1)S(1)} all-to-all(bf16[8,168,128]{2,1,0:T(8,128)(2,1)S(1)} %shard_map.66), channel_id=1, replica_groups=mesh['ens'=2,'xh'=2,'y'=4,'c'=2,'z'=8] {'z'}, dimensions={0} | all-to-all | bytes 688128 | tf_op jit(solution)/shard_map/all_to_all | solution.py:392
  68.5 0.9 %shard_map.67 = (bf16[8,160,128]{2,1,0:T(8,128)(2,1)}, f32[2,128]{1,0:T(2,128)S(1)}) custom-call(s32[1]{0:T(128)} %bitcast.at_ref.refs_0_, bf16[8,168,128]{2,1,0:T(8,128)(2,1)S(1)} %all_to_all.16.in_ref), custom_call_target="tpu_custom_call" | custom-call | tf_op jit(solution)/shard_map/pallas_call | solution.py:393
  69.4 4.0 %all-to-all-start.2 = ((bf16[8,160,128]{2,1,0:T(8,128)(2,1)}), bf16[8,160,128]{2,1,0:T(8,128)(2,1)S(1)}, u32[]{:S(2)}, u32[]{:S(2)}) async-start(bf16[8,160,128]{2,1,0:T(8,128)(2,1)} %get-tuple-element.48), calls=%async_computation.2 | async-start | bytes 655360 | tf_op jit(solution)/shard_map/all_to_all | solution.py:404
  73.5 1.2 %shard_map.68 = bf16[2048,256]{1,0:T(8,128)(2,1)} custom-call(f32[2,128]{1,0:T(2,128)S(1)} %get-tuple-element.49.shrink_ref, bf16[1024,256]{1,0:T(8,128)(2,1)S(1)} %get-tuple-element.50.refs_0_, bf16[512,256]{1,0:T(8,128)(2,1)S(1)} %get-tuple-element.51.refs_1_, bf16[512,256]{1,0:T(8,128)(2,1)S(1)} %get-tuple-element.52.refs_2_), custom_call_target="tpu_custom_call" | custom-call | tf_op jit(solution)/shard_map/pallas_call | solution.py:405
  74.7 6.7 %all-to-all-done.2.own_ref = bf16[8,160,128]{2,1,0:T(8,128)(2,1)S(1)} async-done(((bf16[8,160,128]{2,1,0:T(8,128)(2,1)}), bf16[8,160,128]{2,1,0:T(8,128)(2,1)S(1)}, u32[]{:S(2)}, u32[]{:S(2)}) %all-to-all-start.2) | async-done | bytes 327712 | tf_op jit(solution)/shard_map/all_to_all | solution.py:404
  81.4 4.2 %collective-permute-start.8 = (bf16[8,160,128]{2,1,0:T(8,128)(2,1)S(1)}, bf16[8,160,128]{2,1,0:T(8,128)(2,1)S(1)}, u32[]{:S(2)}, u32[]{:S(2)}) collective-permute-start(bf16[8,160,128]{2,1,0:T(8,128)(2,1)S(1)} %all-to-all-done.2.own_ref), channel_id=1, source_target_pairs={{0,8},{8,0},{1,9},{9,1},{2,10},{10,2},{3,11},{11,3},{4,12},{12,4},... | collective-permute-start | bytes 983048 | tf_op jit(solution)/shard_map/ppermute | solution.py:413
  85.6 1.3 %collective-permute-done.8.got_ref = bf16[8,160,128]{2,1,0:T(8,128)(2,1)S(1)} collective-permute-done((bf16[8,160,128]{2,1,0:T(8,128)(2,1)S(1)}, bf16[8,160,128]{2,1,0:T(8,128)(2,1)S(1)}, u32[]{:S(2)}, u32[]{:S(2)}) %collective-permute-start.8) | collective-permute-done | bytes 327712 | tf_op jit(solution)/shard_map/ppermute | solution.py:413
  86.8 1.2 %shard_map.69 = (f32[2,256,512]{2,1,0:T(8,128)}, f32[256,256]{1,0:T(8,128)}) custom-call(s32[1]{0:T(128)} %bitcast.at_ref.refs_0_, bf16[8,160,128]{2,1,0:T(8,128)(2,1)S(1)} %all-to-all-done.2.own_ref, bf16[8,160,128]{2,1,0:T(8,128)(2,1)S(1)} %collective-permute-done.8.got_ref), custom_call_target="tpu_custom_call" | custom-call | tf_op jit(solution)/shard_map/pallas_call | solution.py:414
Async XLA Ops:
  4.5 14.7 %collective-permute-start.6 = (bf16[1024,256]{1,0:T(8,128)(2,1)S(1)}, bf16[1024,256]{1,0:T(8,128)(2,1)S(1)}, u32[]{:S(2)}, u32[]{:S(2)}) collective-permute-start(bf16[1024,256]{1,0:T(8,128)(2,1)S(1)} %get-tuple-element.39.refs_2_), channel_id=1, source_target_pairs={{0,128},{128,0},{1,129},{129,1},{2,130},{130,2},{3,131},{131,3},{4... | collective-permute-start | bytes 1572872 | tf_op jit(solution)/shard_map/ppermute | solution.py:354
  6.6 7.2 %collective-permute-start = (bf16[4,64,256]{2,1,0:T(8,128)(2,1)S(1)}, bf16[4,64,256]{2,1,0:T(8,128)(2,1)S(1)}, u32[]{:S(2)}, u32[]{:S(2)}) collective-permute-start(bf16[4,64,256]{2,1,0:T(8,128)(2,1)S(1)} %get-tuple-element.31), channel_id=1, source_target_pairs={{0,8},{8,0},{1,9},{9,1},{2,10},{10,2},{3,11},{11,3},{4,12},{12,4},... | collective-permute-start | bytes 393224 | tf_op jit(solution)/shard_map/ppermute | solution.py:358
  7.9 6.6 %collective-permute-start.1 = (bf16[4,64,256]{2,1,0:T(8,128)(2,1)S(1)}, bf16[4,64,256]{2,1,0:T(8,128)(2,1)S(1)}, u32[]{:S(2)}, u32[]{:S(2)}) collective-permute-start(bf16[4,64,256]{2,1,0:T(8,128)(2,1)S(1)} %get-tuple-element.32), channel_id=1, source_target_pairs={{8,16},{16,8},{24,32},{32,24},{40,48},{48,40},{56,64},{64,56},{72,... | collective-permute-start | bytes 393224 | tf_op jit(solution)/shard_map/ppermute | solution.py:355
  10.6 3.2 %collective-permute-start.2 = (bf16[32,256]{1,0:T(8,128)(2,1)S(1)}, bf16[32,256]{1,0:T(8,128)(2,1)S(1)}, u32[]{:S(2)}, u32[]{:S(2)}) collective-permute-start(bf16[32,256]{1,0:T(8,128)(2,1)S(1)} %get-tuple-element.33), channel_id=1, source_target_pairs={{0,1},{1,0},{2,3},{3,2},{4,5},{5,4},{6,7},{7,6},{8,9},{9,8},{10,11... | collective-permute-start | bytes 49160 | tf_op jit(solution)/shard_map/ppermute | solution.py:356
  12.4 1.4 %collective-permute-start.3 = (bf16[32,256]{1,0:T(8,128)(2,1)S(1)}, bf16[32,256]{1,0:T(8,128)(2,1)S(1)}, u32[]{:S(2)}, u32[]{:S(2)}) collective-permute-start(bf16[32,256]{1,0:T(8,128)(2,1)S(1)} %get-tuple-element.34), channel_id=1, source_target_pairs={{1,2},{2,1},{3,4},{4,3},{5,6},{6,5},{9,10},{10,9},{11,12},{12,11},... | collective-permute-start | bytes 49160 | tf_op jit(solution)/shard_map/ppermute | solution.py:357
  15.4 8.7 %collective-permute-start.5 = (bf16[512,256]{1,0:T(8,128)(2,1)S(1)}, bf16[512,256]{1,0:T(8,128)(2,1)S(1)}, u32[]{:S(2)}, u32[]{:S(2)}) collective-permute-start(bf16[512,256]{1,0:T(8,128)(2,1)S(1)} %shard_map.60.refs_2_), channel_id=1, source_target_pairs={{0,128},{128,0},{1,129},{129,1},{2,130},{130,2},{3,131},{131,3},{4... | collective-permute-start | bytes 786440 | tf_op jit(solution)/shard_map/ppermute | solution.py:364
  19.1 10.6 %collective-permute-start.4 = (bf16[512,256]{1,0:T(8,128)(2,1)S(1)}, bf16[512,256]{1,0:T(8,128)(2,1)S(1)}, u32[]{:S(2)}, u32[]{:S(2)}) collective-permute-start(bf16[512,256]{1,0:T(8,128)(2,1)S(1)} %shard_map.61.refs_2_), channel_id=1, source_target_pairs={{0,128},{128,0},{1,129},{129,1},{2,130},{130,2},{3,131},{131,3},{4... | collective-permute-start | bytes 786440 | tf_op jit(solution)/shard_map/ppermute | solution.py:364
  30.6 2.4 %collective-permute-start.7 = (bf16[8,168,128]{2,1,0:T(8,128)(2,1)S(1)}, bf16[8,168,128]{2,1,0:T(8,128)(2,1)S(1)}, u32[]{:S(2)}, u32[]{:S(2)}) collective-permute-start(bf16[8,168,128]{2,1,0:T(8,128)(2,1)S(1)} %get-tuple-element.47), channel_id=1, source_target_pairs={{0,8},{8,0},{1,9},{9,1},{2,10},{10,2},{3,11},{11,3},{4,12},{12,4},... | collective-permute-start | bytes 1032200 | tf_op jit(solution)/shard_map/ppermute | solution.py:384
  69.4 11.9 %all-to-all-start.2 = ((bf16[8,160,128]{2,1,0:T(8,128)(2,1)}), bf16[8,160,128]{2,1,0:T(8,128)(2,1)S(1)}, u32[]{:S(2)}, u32[]{:S(2)}) async-start(bf16[8,160,128]{2,1,0:T(8,128)(2,1)} %get-tuple-element.48), calls=%async_computation.2 | async-start | bytes 655360 | tf_op jit(solution)/shard_map/all_to_all | solution.py:404
  81.4 5.4 %collective-permute-start.8 = (bf16[8,160,128]{2,1,0:T(8,128)(2,1)S(1)}, bf16[8,160,128]{2,1,0:T(8,128)(2,1)S(1)}, u32[]{:S(2)}, u32[]{:S(2)}) collective-permute-start(bf16[8,160,128]{2,1,0:T(8,128)(2,1)S(1)} %all-to-all-done.2.own_ref), channel_id=1, source_target_pairs={{0,8},{8,0},{1,9},{9,1},{2,10},{10,2},{3,11},{11,3},{4,12},{12,4},... | collective-permute-start | bytes 983048 | tf_op jit(solution)/shard_map/ppermute | solution.py:413

commit v5 on v4

--- a/solution.py
+++ b/solution.py
@@ -53,8 +53,15 @@
     return acc.astype(BF16)
 
 
+def edge_kernel(at_ref, m_hbm, out_ref, sem):
+    last = m_hbm.shape[1] - 1
+    copy = pltpu.make_async_copy(m_hbm.at[:, last * core_of(at_ref[0])], out_ref, sem)
+    copy.start()
+    copy.wait()
+
+
 def first_grad_kernel(count, at_ref, m_hbm, c_hbm, x_hbm, *refs):
-    g_ref, m_ref, c_ref, x_ref, xa_ref, xb_ref, za_ref, zb_ref, tmp_ref, sems = refs
+    g_ref, m_ref, c_ref, x_ref, xa_ref, za_ref, zb_ref, tmp_ref, sems = refs
     members, levels, cells, _ = x_hbm.shape
     _, rows_x, rows_y, width = m_ref.shape
     head, rest = pl.ds(0, count), pl.ds(count, levels - count)
@@ -83,7 +90,6 @@
     )
     core, even = core_of(at_ref[0]), parity_of(at_ref[0]) == 0
     xa_ref[...] = m_ref[:, (rows_x - 1) * (1 - core)]
-    xb_ref[...] = m_ref[:, (rows_x - 1) * core]
     tmp_ref[0] = m_ref[:, :, 0:8, :].reshape(levels * rows_x, 8, width).astype(F32)
     tmp_ref[1] = m_ref[:, :, rows_y - 8 : rows_y, :].reshape(levels * rows_x, 8, width).astype(F32)
     lo, hi = tmp_ref[0, :, 0, :], tmp_ref[1, :, 7, :]
@@ -120,7 +126,7 @@
     arrays = [modes, coefficients, series]
     outs = [jax.ShapeDtypeStruct((count * cells, width), BF16)]
     outs += [pltpu.VMEM(a.shape, a.dtype) for a in arrays]
-    outs += [jax.ShapeDtypeStruct((levels, rows_y, width), BF16)] * 2
+    outs += [jax.ShapeDtypeStruct((levels, rows_y, width), BF16)]
     outs += [jax.ShapeDtypeStruct((levels * rows_x, width), BF16)] * 2
     return pl.pallas_call(
         functools.partial(first_grad_kernel, count),
@@ -261,34 +267,37 @@
     return part[SUM_ROWS : SUM_ROWS + 2, :] + part[SUM_ROWS + 2 : SUM_ROWS + 4, :]
 
 
+def packed_squares(total):
+    return split_squares(whole_squares(total), 8).astype(BF16)
+
+
 def join_kernel(keep_ref, got_ref, out_ref):
     out_ref[:, 0:SUM_ROWS, :] = (
         keep_ref[:, 0:SUM_ROWS, :].astype(F32) + got_ref[:, 0:SUM_ROWS, :].astype(F32)
     ).astype(BF16)
-    tail = keep_ref[0, SUM_ROWS:PART_ROWS, :].astype(F32) + got_ref[0, SUM_ROWS:PART_ROWS, :].astype(F32)
-    packed = split_squares(tail[0:2, :] + tail[2:4, :], 8).astype(BF16)
+    tail = keep_ref[0].astype(F32) + got_ref[0].astype(F32)
+    packed = packed_squares(tail)
     for j in range(PARTS):
         out_ref[j, SUM_ROWS:PART_ROWS, :] = packed
 
 
-def gather_sum(in_ref):
+def plane_kernel(in_ref, out_ref):
     total = in_ref[0].astype(F32)
     for j in range(1, PARTS):
         total = total + in_ref[j].astype(F32)
-    return total
-
-
-def plane_kernel(in_ref, out_ref):
-    total = gather_sum(in_ref)
-    packed = split_squares(whole_squares(total), 8)
-    mine = jnp.concatenate([total[0:SUM_ROWS, :], packed], axis=0).astype(BF16)
-    for j in range(PARTS):
-        out_ref[j] = mine
-
-
-def reduce_kernel(total_cells, at_ref, in_ref, out_ref, shrink_ref, column_ref):
+    out_ref[0:SUM_ROWS, :] = total[0:SUM_ROWS, :].astype(BF16)
+    out_ref[SUM_ROWS:PART_ROWS, :] = packed_squares(total)
+
+
+def add_kernel(own_ref, got_ref, out_ref):
+    total = own_ref[...].astype(F32) + got_ref[...].astype(F32)
+    out_ref[0:SUM_ROWS, :] = total[0:SUM_ROWS, :].astype(BF16)
+    out_ref[SUM_ROWS:PART_ROWS, :] = packed_squares(total)
+
+
+def reduce_kernel(total_cells, at_ref, own_ref, got_ref, out_ref, shrink_ref, column_ref):
     core, part = core_of(at_ref[0]), part_of(at_ref[0])
-    total = gather_sum(in_ref)
+    total = own_ref[...].astype(F32) + got_ref[...].astype(F32)
     squares = whole_squares(total)
     shrink = jnp.maximum(0.0, 1.0 - TAU / jnp.sqrt(squares / total_cells + 1e-06))
     shrink_ref[...] = shrink
@@ -348,11 +357,21 @@
     swap = [(0, 1), (1, 0)]
 
     chunks = [(0, 2), (2, 1), (3, 1)]
-    g, modes, coefficients, series, edge_a, edge_b, row_a, row_b = first_grad(
+    edge_b = pl.pallas_call(
+        edge_kernel,
+        in_specs=[SM, HBM],
+        out_specs=VM,
+        out_shape=jax.ShapeDtypeStruct((levels, rows_y, width), BF16),
+        scratch_shapes=[pltpu.SemaphoreType.DMA],
+        compiler_params=PARAMS,
+    )(place, pltpu.with_memory_space_constraint(modes, pltpu.HBM))
+    xb = lax.ppermute(edge_b, SX, both_ways([(i, i + 1) for i in range(1, n_sx - 1, 2)]))
+    coefficients, _ = lax.optimization_barrier((coefficients, edge_b))
+    g, modes, coefficients, series, edge_a, row_a, row_b = first_grad(
         place, modes, coefficients, series, chunks[0][1]
     )
+    g, xb = lax.optimization_barrier((g, xb))
     own, got = [g], [lax.ppermute(g, "ens", swap)]
-    xb = lax.ppermute(edge_b, SX, both_ways([(i, i + 1) for i in range(1, n_sx - 1, 2)]))
     za = lax.ppermute(row_a, "z", both_ways([(i, i + 1) for i in range(0, n_z, 2)]))
     zb = lax.ppermute(row_b, "z", both_ways([(i, i + 1) for i in range(1, n_z - 1, 2)]))
     xa = lax.ppermute(edge_a, "c", swap)
@@ -363,7 +382,7 @@
         own.append(g)
         got.append(lax.ppermute(g, "ens", swap))
 
-    send_level(2, xa, xb, za, zb)
+    send_level(2, xa, za, zb)
     base = pl.pallas_call(
         base_kernel,
         in_specs=[SM] + [VM] * 5,
@@ -372,7 +391,7 @@
         compiler_params=PARAMS,
         cost_estimate=pl.CostEstimate(flops=12 * local_cells * width, bytes_accessed=6 * local_cells * width, transcendentals=0),
     )(place, modes, xa, xb, za, zb)
-    send_level(3, own[1], base)
+    send_level(3, own[1])
 
     moved, carry = [], None
     for i, (level, count) in enumerate(chunks):
@@ -386,13 +405,23 @@
         join_kernel, in_specs=[VM, VM], out_specs=VM, out_shape=part_shape, compiler_params=PARAMS
     )(keep, other)
     parts = lax.all_to_all(joined, PLANE, 0, 0)
-    planes = pl.pallas_call(
-        plane_kernel, in_specs=[VM], out_specs=VM, out_shape=part_shape, compiler_params=PARAMS
+    line_shape = jax.ShapeDtypeStruct((PART_ROWS, 128), BF16)
+    line = pl.pallas_call(
+        plane_kernel, in_specs=[VM], out_specs=VM, out_shape=line_shape, compiler_params=PARAMS
     )(parts)
-    planes = lax.all_to_all(planes, "z", 0, 0)
+    span = 2
+    while True:
+        pairs = [(i, i ^ (span - 1)) for i in range(n_z)]
+        near = lax.ppermute(line, "z", pairs)
+        if span == n_z:
+            break
+        line = pl.pallas_call(
+            add_kernel, in_specs=[VM, VM], out_specs=VM, out_shape=line_shape, compiler_params=PARAMS
+        )(line, near)
+        span *= 2
     spread, shrink = pl.pallas_call(
         functools.partial(reduce_kernel, total_cells),
-        in_specs=[SM, VM],
+        in_specs=[SM, VM, VM],
         out_specs=[VM, VM],
         out_shape=[
             jax.ShapeDtypeStruct((PARTS, SUM_ROWS, 128), BF16),
@@ -400,7 +429,7 @@
         ],
         scratch_shapes=[pltpu.VMEM((width, 128), F32)],
         compiler_params=PARAMS,
-    )(place, planes)
+    )(place, line, near)
     half = lax.all_to_all(spread, PLANE, 0, 0)
     new_modes = pl.pallas_call(
         scale_kernel,

time: 88.3 us -> 88.9 us (level)
  blocking collectives: 35.5 us -> 15.6 us
  starting transfers between devices: 19.7 us -> 30.4 us
  waiting for transfers between devices: 19.3 us -> 28.1 us
  Pallas kernels: 12.9 us -> 13.8 us
    all_to_all x1 -> x0, blocking collectives: 19.1 us -> none  [local(): planes = lax.all_to_all(planes, 'z', 0, 0)]
    ppermute x0 -> x3, starting transfers between devices: none -> 10.6 us  [local(): near = lax.ppermute(line, 'z', pairs)]
    ppermute x1, waiting for transfers between devices: 0.01 us -> 5.16 us  [local(): own, got = ([g], [lax.ppermute(g, 'ens', swap)])]
    ppermute x0 -> x3, waiting for transfers between devices: none -> 4.24 us  [local(): near = lax.ppermute(line, 'z', pairs)]
    ppermute x1, starting transfers between devices: 4.17 us -> 6.06 us  [local(): other_half = lax.ppermute(half, 'c', swap)]
    ppermute x1, starting transfers between devices: 2.74 us -> 4.59 us  [local(): lax.ppermute(edge_b, SX, both_ways([(i, i + 1) for i in range(1, n_sx - 1...]
    ppermute x1, starting transfers between devices: 1.29 us -> 0.01 us  [local(): xa = lax.ppermute(edge_a, 'c', swap)]
    pallas_call x1 -> x4, Pallas kernels: 0.06 us -> 1.01 us  [the longest x1 0.92 us: local(): pl.pallas_call(edge_kernel, in_specs=[SM, HBM], out_specs=VM, out_shape=j...]
  transfers between devices with their start and end apart: 10 -> 13, of which waited for: 7 -> 10; matrix products, arithmetic and copies ran while one was open for 0% -> 0% of each run, Pallas kernels for 7% -> 11%
where the time goes in v5:
time: 88.9 us; the launch traced here: 88.6 us
  starting transfers between devices  30.4 us (34%)
  waiting for transfers between devices  28.1 us (32%)
  blocking collectives  15.6 us (18%)
  Pallas kernels  13.8 us (16%)
    all_to_all x1, blocking collectives, local(): parts = lax.all_to_all(joined, PLANE, 0, 0)  15.6 us
    ppermute x3, starting transfers between devices, local(): near = lax.ppermute(line, 'z', pairs)  10.6 us
    ppermute x2, waiting for transfers between devices, send_level(): got.append(lax.ppermute(g, 'ens', swap))  8.84 us
    all_to_all x1, waiting for transfers between devices, local(): half = lax.all_to_all(spread, PLANE, 0, 0)  6.6 us
    ppermute x1, starting transfers between devices, local(): other_half = lax.ppermute(half, 'c', swap)  6.06 us
    ppermute x1, waiting for transfers between devices, local(): own, got = ([g], [lax.ppermute(g, 'ens', swap)])  5.16 us
    ppermute x1, starting transfers between devices, local(): lax.ppermute(edge_b, SX, both_ways([(i, i + 1) for i in range(1, n_sx - 1...  4.59 us
    ppermute x3, waiting for transfers between devices, local(): near = lax.ppermute(line, 'z', pairs)  4.24 us
  transfers between devices with their start and end apart: 13, of which 10 were waited for; matrix products, arithmetic and copies ran while one was open for 0% of the time, Pallas kernels for 11%

profile of v5, /device:TPU:1, one launch (start us, length us, event | category | flops | bytes accessed | tf_op | source)
XLA Modules:
  0.0 88.6 jit_solution(16775458474079839533)
XLA Ops:
  0.6 0.9 %shard_map.58 = bf16[4,64,256]{2,1,0:T(8,128)(2,1)S(1)} custom-call(s32[1]{0:T(128)} %bitcast.at_ref.refs_0_, bf16[4,8,64,256]{3,2,1,0:T(8,128)(2,1)} %m_hbm.3), custom_call_target="tpu_custom_call" | custom-call | tf_op jit(solution)/shard_map/pallas_call | solution.py:360
  1.6 4.6 %collective-permute-start.1 = (bf16[4,64,256]{2,1,0:T(8,128)(2,1)S(1)}, bf16[4,64,256]{2,1,0:T(8,128)(2,1)S(1)}, u32[]{:S(2)}, u32[]{:S(2)}) collective-permute-start(bf16[4,64,256]{2,1,0:T(8,128)(2,1)S(1)} %shard_map.58), channel_id=1, source_target_pairs={{8,16},{16,8},{24,32},{32,24},{40,48},{48,40},{56,64},{64,56},{72,... | collective-permute-start | bytes 393224 | tf_op jit(solution)/shard_map/ppermute | solution.py:368
  6.2 3.8 %shard_map.59 = (bf16[1024,256]{1,0:T(8,128)(2,1)S(1)}, bf16[4,8,64,256]{3,2,1,0:T(8,128)(2,1)S(1)}, bf16[2,256,512]{2,1,0:T(8,128)(2,1)S(1)}, bf16[2,4,512,512]...) custom-call(s32[1]{0:T(128)} %bitcast.at_ref.refs_0_, ...), custom_call_target="tpu_custom_call" | custom-call | flops 1073741824 | bytes 3670016 | tf_op jit(solution)/shard_map/pallas_call | solution.py:131
  10.0 0.0 collective-permute-done.1.xb_ref
  10.0 1.3 %collective-permute-start.6 = (bf16[1024,256]{1,0:T(8,128)(2,1)S(1)}, bf16[1024,256]{1,0:T(8,128)(2,1)S(1)}, u32[]{:S(2)}, u32[]{:S(2)}) collective-permute-start(bf16[1024,256]{1,0:T(8,128)(2,1)S(1)} %get-tuple-element.43.refs_2_), channel_id=1, source_target_pairs={{0,128},{128,0},{1,129},{129,1},{2,130},{130,2},{3,131},{131,3},{4... | collective-permute-start | bytes 1572872 | tf_op jit(solution)/shard_map/ppermute | solution.py:374
  11.3 0.0 collective-permute-start
  11.3 1.6 %collective-permute-start.2 = (bf16[32,256]{1,0:T(8,128)(2,1)S(1)}, bf16[32,256]{1,0:T(8,128)(2,1)S(1)}, u32[]{:S(2)}, u32[]{:S(2)}) collective-permute-start(bf16[32,256]{1,0:T(8,128)(2,1)S(1)} %get-tuple-element.37), channel_id=1, source_target_pairs={{0,1},{1,0},{2,3},{3,2},{4,5},{5,4},{6,7},{7,6},{8,9},{9,8},{10,11... | collective-permute-start | bytes 49160 | tf_op jit(solution)/shard_map/ppermute | solution.py:375
  12.9 0.7 collective-permute-start.3
  13.6 0.8 collective-permute-done.2.za_ref
  14.4 0.0 collective-permute-done.3.zb_ref
  14.4 0.0 collective-permute-done.xa_ref
  14.4 1.0 %shard_map.61.refs_2_ = bf16[512,256]{1,0:T(8,128)(2,1)S(1)} custom-call(bf16[4,8,64,256]{3,2,1,0:T(8,128)(2,1)S(1)} %get-tuple-element.33.m_ref, bf16[2,256,512]{2,1,0:T(8,128)(2,1)S(1)} %get-tuple-element.42.c_ref, bf16[2,4,512,512]{3,2,1,0:T(8,128)(2,1)S(1)} %get-tuple-element.41.x_ref.refs_4_), custom_call_target="tpu_custom_call" | custom-call | flops 536870912 | bytes 2097152 | tf_op jit(solution)/shard_map/pallas_call | solution.py:148
  15.3 0.3 collective-permute-start.5
  15.7 1.0 %shard_map.62.refs_2_ = bf16[512,256]{1,0:T(8,128)(2,1)S(1)} custom-call(bf16[4,8,64,256]{3,2,1,0:T(8,128)(2,1)S(1)} %get-tuple-element.33.m_ref, bf16[2,256,512]{2,1,0:T(8,128)(2,1)S(1)} %get-tuple-element.42.c_ref, bf16[2,4,512,512]{3,2,1,0:T(8,128)(2,1)S(1)} %get-tuple-element.41.x_ref.refs_4_), custom_call_target="tpu_custom_call" | custom-call | flops 536870912 | bytes 2097152 | tf_op jit(solution)/shard_map/pallas_call | solution.py:148
  16.6 1.3 %collective-permute-start.4 = (bf16[512,256]{1,0:T(8,128)(2,1)S(1)}, bf16[512,256]{1,0:T(8,128)(2,1)S(1)}, u32[]{:S(2)}, u32[]{:S(2)}) collective-permute-start(bf16[512,256]{1,0:T(8,128)(2,1)S(1)} %shard_map.62.refs_2_), channel_id=1, source_target_pairs={{0,128},{128,0},{1,129},{129,1},{2,130},{130,2},{3,131},{131,3},{4... | collective-permute-start | bytes 786440 | tf_op jit(solution)/shard_map/ppermute | solution.py:383
  17.9 0.9 %shard_map.60.refs_1_ = f32[4,512,256]{2,1,0:T(8,128)S(1)} custom-call(s32[1]{0:T(128)} %bitcast.at_ref.refs_0_, bf16[4,8,64,256]{3,2,1,0:T(8,128)(2,1)S(1)} %get-tuple-element.33.m_ref, bf16[4,64,256]{2,1,0:T(8,128)(2,1)S(1)} %collective-permute-done.xa_ref, bf16[4,64,256]{2,1,0:T(8,128)(2,1)S(1)} %collective-permute-done.1.xb_ref, ...), custom_call_target="tpu_custom_call" | custom-call | flops 6291456 | bytes 3145728 | tf_op jit(solution)/shard_map/pallas_call | solution.py:386
  18.9 5.2 %collective-permute-done.6.refs_3_ = bf16[1024,256]{1,0:T(8,128)(2,1)S(1)} collective-permute-done((bf16[1024,256]{1,0:T(8,128)(2,1)S(1)}, bf16[1024,256]{1,0:T(8,128)(2,1)S(1)}, u32[]{:S(2)}, u32[]{:S(2)}) %collective-permute-start.6) | collective-permute-done | bytes 524320 | tf_op jit(solution)/shard_map/ppermute | solution.py:374
  24.0 1.1 %shard_map.63 = (bf16[1024,256]{1,0:T(8,128)(2,1)S(1)}, f32[2,256,512]{2,1,0:T(8,128)S(1)}, f32[256,256]{1,0:T(8,128)S(1)}, f32[1,256]{1,0:T(1,128)S(1)}) custom-call(s32[1]{0:T(128)} %bitcast.at_ref.refs_0_, f32[4,512,256]{2,1,0:T(8,128)S(1)} %shard_map.60.refs_1_, bf16[1024,256]{1,0:T(8,128)(2,1)S(1)} %get-tuple-element.43.refs_2_, ...), custom_call_target="tpu_custom_call" | custom-call | flops 671088640 | bytes 4194304 | tf_op jit(solution)/shard_map/pallas_call | solution.py:250
  25.1 4.5 %collective-permute-done.5.refs_3_ = bf16[512,256]{1,0:T(8,128)(2,1)S(1)} collective-permute-done((bf16[512,256]{1,0:T(8,128)(2,1)S(1)}, bf16[512,256]{1,0:T(8,128)(2,1)S(1)}, u32[]{:S(2)}, u32[]{:S(2)}) %collective-permute-start.5) | collective-permute-done | bytes 262176 | tf_op jit(solution)/shard_map/ppermute | solution.py:383
  29.7 0.8 shard_map.64
  30.5 4.3 %collective-permute-done.4.refs_3_ = bf16[512,256]{1,0:T(8,128)(2,1)S(1)} collective-permute-done((bf16[512,256]{1,0:T(8,128)(2,1)S(1)}, bf16[512,256]{1,0:T(8,128)(2,1)S(1)}, u32[]{:S(2)}, u32[]{:S(2)}) %collective-permute-start.4) | collective-permute-done | bytes 262176 | tf_op jit(solution)/shard_map/ppermute | solution.py:383
  34.8 0.8 shard_map.65
  35.7 0.5 collective-permute-start.7
  36.1 1.3 %collective-permute-done.7.got_ref = bf16[8,168,128]{2,1,0:T(8,128)(2,1)S(1)} collective-permute-done((bf16[8,168,128]{2,1,0:T(8,128)(2,1)S(1)}, bf16[8,168,128]{2,1,0:T(8,128)(2,1)S(1)}, u32[]{:S(2)}, u32[]{:S(2)}) %collective-permute-start.7) | collective-permute-done | bytes 344096 | tf_op jit(solution)/shard_map/ppermute | solution.py:403
  37.4 0.1 shard_map.66
  37.5 15.6 %all_to_all.10.in_ref = bf16[8,168,128]{2,1,0:T(8,128)(2,1)S(1)} all-to-all(bf16[8,168,128]{2,1,0:T(8,128)(2,1)S(1)} %shard_map.66), channel_id=1, replica_groups=mesh['ens'=2,'xh'=2,'y'=4,'c'=2,'z'=8] {'xh','y'}, dimensions={0} | all-to-all | bytes 688128 | tf_op jit(solution)/shard_map/all_to_all | solution.py:407
  53.1 0.1 shard_map.67.own_ref
  53.1 1.7 %collective-permute-start.8 = (bf16[168,128]{1,0:T(8,128)(2,1)S(1)}, bf16[168,128]{1,0:T(8,128)(2,1)S(1)}, u32[]{:S(2)}, u32[]{:S(2)}) collective-permute-start(bf16[168,128]{1,0:T(8,128)(2,1)S(1)} %shard_map.67.own_ref), channel_id=1, source_target_pairs={{0,1},{1,0},{2,3},{3,2},{4,5},{5,4},{6,7},{7,6},{8,9},{9,8},{10,11... | collective-permute-start | bytes 129032 | tf_op jit(solution)/shard_map/ppermute | solution.py:415
  54.8 1.4 %collective-permute-done.8.got_ref = bf16[168,128]{1,0:T(8,128)(2,1)S(1)} collective-permute-done((bf16[168,128]{1,0:T(8,128)(2,1)S(1)}, bf16[168,128]{1,0:T(8,128)(2,1)S(1)}, u32[]{:S(2)}, u32[]{:S(2)}) %collective-permute-start.8) | collective-permute-done | bytes 43040 | tf_op jit(solution)/shard_map/ppermute | solution.py:415
  56.3 4.2 %collective-permute-start.9 = (bf16[168,128]{1,0:T(8,128)(2,1)S(1)}, bf16[168,128]{1,0:T(8,128)(2,1)S(1)}, u32[]{:S(2)}, u32[]{:S(2)}) collective-permute-start(bf16[168,128]{1,0:T(8,128)(2,1)S(1)} %shard_map.68.own_ref), channel_id=1, source_target_pairs={{0,3},{1,2},{2,1},{3,0},{4,7},{5,6},{6,5},{7,4},{8,11},{9,10},{10,... | collective-permute-start | bytes 129032 | tf_op jit(solution)/shard_map/ppermute | solution.py:415
  60.5 1.4 %collective-permute-done.9.got_ref = bf16[168,128]{1,0:T(8,128)(2,1)S(1)} collective-permute-done((bf16[168,128]{1,0:T(8,128)(2,1)S(1)}, bf16[168,128]{1,0:T(8,128)(2,1)S(1)}, u32[]{:S(2)}, u32[]{:S(2)}) %collective-permute-start.9) | collective-permute-done | bytes 43040 | tf_op jit(solution)/shard_map/ppermute | solution.py:415
  62.0 4.6 %collective-permute-start.10 = (bf16[168,128]{1,0:T(8,128)(2,1)S(1)}, bf16[168,128]{1,0:T(8,128)(2,1)S(1)}, u32[]{:S(2)}, u32[]{:S(2)}) collective-permute-start(bf16[168,128]{1,0:T(8,128)(2,1)S(1)} %shard_map.69.own_ref), channel_id=1, source_target_pairs={{0,7},{1,6},{2,5},{3,4},{4,3},{5,2},{6,1},{7,0},{8,15},{9,14},{10,... | collective-permute-start | bytes 129032 | tf_op jit(solution)/shard_map/ppermute | solution.py:415
  66.6 1.4 %collective-permute-done.10.got_ref = bf16[168,128]{1,0:T(8,128)(2,1)S(1)} collective-permute-done((bf16[168,128]{1,0:T(8,128)(2,1)S(1)}, bf16[168,128]{1,0:T(8,128)(2,1)S(1)}, u32[]{:S(2)}, u32[]{:S(2)}) %collective-permute-start.10) | collective-permute-done | bytes 43040 | tf_op jit(solution)/shard_map/ppermute | solution.py:415
  68.0 0.9 shard_map.70
  68.9 3.4 %all-to-all-start.1 = ((bf16[8,160,128]{2,1,0:T(8,128)(2,1)}), bf16[8,160,128]{2,1,0:T(8,128)(2,1)S(1)}, u32[]{:S(2)}, u32[]{:S(2)}) async-start(bf16[8,160,128]{2,1,0:T(8,128)(2,1)} %get-tuple-element.52), calls=%async_computation.1 | async-start | bytes 655360 | tf_op jit(solution)/shard_map/all_to_all | solution.py:433
  72.3 1.2 %shard_map.71 = bf16[2048,256]{1,0:T(8,128)(2,1)} custom-call(f32[2,128]{1,0:T(2,128)S(1)} %get-tuple-element.53.shrink_ref, bf16[1024,256]{1,0:T(8,128)(2,1)S(1)} %get-tuple-element.54.refs_0_, bf16[512,256]{1,0:T(8,128)(2,1)S(1)} %get-tuple-element.55.refs_1_, bf16[512,256]{1,0:T(8,128)(2,1)S(1)} %get-tuple-element.56.refs_2_), custom_call_target="tpu_custom_call" | custom-call | tf_op jit(solution)/shard_map/pallas_call | solution.py:434
  73.5 6.6 %all-to-all-done.1.own_ref = bf16[8,160,128]{2,1,0:T(8,128)(2,1)S(1)} async-done(((bf16[8,160,128]{2,1,0:T(8,128)(2,1)}), bf16[8,160,128]{2,1,0:T(8,128)(2,1)S(1)}, u32[]{:S(2)}, u32[]{:S(2)}) %all-to-all-start.1) | async-done | bytes 327712 | tf_op jit(solution)/shard_map/all_to_all | solution.py:433
  80.1 6.1 %collective-permute-start.11 = (bf16[8,160,128]{2,1,0:T(8,128)(2,1)S(1)}, bf16[8,160,128]{2,1,0:T(8,128)(2,1)S(1)}, u32[]{:S(2)}, u32[]{:S(2)}) collective-permute-start(bf16[8,160,128]{2,1,0:T(8,128)(2,1)S(1)} %all-to-all-done.1.own_ref), channel_id=1, source_target_pairs={{0,8},{8,0},{1,9},{9,1},{2,10},{10,2},{3,11},{11,3},{4,12},{12,4},... | collective-permute-start | bytes 983048 | tf_op jit(solution)/shard_map/ppermute | solution.py:442
  86.1 1.3 %collective-permute-done.11.got_ref = bf16[8,160,128]{2,1,0:T(8,128)(2,1)S(1)} collective-permute-done((bf16[8,160,128]{2,1,0:T(8,128)(2,1)S(1)}, bf16[8,160,128]{2,1,0:T(8,128)(2,1)S(1)}, u32[]{:S(2)}, u32[]{:S(2)}) %collective-permute-start.11) | collective-permute-done | bytes 327712 | tf_op jit(solution)/shard_map/ppermute | solution.py:442
  87.4 1.2 %shard_map.72 = (f32[2,256,512]{2,1,0:T(8,128)}, f32[256,256]{1,0:T(8,128)}) custom-call(s32[1]{0:T(128)} %bitcast.at_ref.refs_0_, bf16[8,160,128]{2,1,0:T(8,128)(2,1)S(1)} %all-to-all-done.1.own_ref, bf16[8,160,128]{2,1,0:T(8,128)(2,1)S(1)} %collective-permute-done.11.got_ref), custom_call_target="tpu_custom_call" | custom-call | tf_op jit(solution)/shard_map/pallas_call | solution.py:443
  (2 shorter events, 0.0 us)
Async XLA Ops:
  1.6 8.4 %collective-permute-start.1 = (bf16[4,64,256]{2,1,0:T(8,128)(2,1)S(1)}, bf16[4,64,256]{2,1,0:T(8,128)(2,1)S(1)}, u32[]{:S(2)}, u32[]{:S(2)}) collective-permute-start(bf16[4,64,256]{2,1,0:T(8,128)(2,1)S(1)} %shard_map.58), channel_id=1, source_target_pairs={{8,16},{16,8},{24,32},{32,24},{40,48},{48,40},{56,64},{64,56},{72,... | collective-permute-start | bytes 393224 | tf_op jit(solution)/shard_map/ppermute | solution.py:368
  10.0 14.0 %collective-permute-start.6 = (bf16[1024,256]{1,0:T(8,128)(2,1)S(1)}, bf16[1024,256]{1,0:T(8,128)(2,1)S(1)}, u32[]{:S(2)}, u32[]{:S(2)}) collective-permute-start(bf16[1024,256]{1,0:T(8,128)(2,1)S(1)} %get-tuple-element.43.refs_2_), channel_id=1, source_target_pairs={{0,128},{128,0},{1,129},{129,1},{2,130},{130,2},{3,131},{131,3},{4... | collective-permute-start | bytes 1572872 | tf_op jit(solution)/shard_map/ppermute | solution.py:374
  11.3 3.1 %collective-permute-start = (bf16[4,64,256]{2,1,0:T(8,128)(2,1)S(1)}, bf16[4,64,256]{2,1,0:T(8,128)(2,1)S(1)}, u32[]{:S(2)}, u32[]{:S(2)}) collective-permute-start(bf16[4,64,256]{2,1,0:T(8,128)(2,1)S(1)} %get-tuple-element.34), channel_id=1, source_target_pairs={{0,8},{8,0},{1,9},{9,1},{2,10},{10,2},{3,11},{11,3},{4,12},{12,4},... | collective-permute-start | bytes 393224 | tf_op jit(solution)/shard_map/ppermute | solution.py:377
  11.3 3.1 %collective-permute-start.2 = (bf16[32,256]{1,0:T(8,128)(2,1)S(1)}, bf16[32,256]{1,0:T(8,128)(2,1)S(1)}, u32[]{:S(2)}, u32[]{:S(2)}) collective-permute-start(bf16[32,256]{1,0:T(8,128)(2,1)S(1)} %get-tuple-element.37), channel_id=1, source_target_pairs={{0,1},{1,0},{2,3},{3,2},{4,5},{5,4},{6,7},{7,6},{8,9},{9,8},{10,11... | collective-permute-start | bytes 49160 | tf_op jit(solution)/shard_map/ppermute | solution.py:375
  12.9 1.4 %collective-permute-start.3 = (bf16[32,256]{1,0:T(8,128)(2,1)S(1)}, bf16[32,256]{1,0:T(8,128)(2,1)S(1)}, u32[]{:S(2)}, u32[]{:S(2)}) collective-permute-start(bf16[32,256]{1,0:T(8,128)(2,1)S(1)} %get-tuple-element.38), channel_id=1, source_target_pairs={{1,2},{2,1},{3,4},{4,3},{5,6},{6,5},{9,10},{10,9},{11,12},{12,11},... | collective-permute-start | bytes 49160 | tf_op jit(solution)/shard_map/ppermute | solution.py:376
  15.3 14.3 %collective-permute-start.5 = (bf16[512,256]{1,0:T(8,128)(2,1)S(1)}, bf16[512,256]{1,0:T(8,128)(2,1)S(1)}, u32[]{:S(2)}, u32[]{:S(2)}) collective-permute-start(bf16[512,256]{1,0:T(8,128)(2,1)S(1)} %shard_map.61.refs_2_), channel_id=1, source_target_pairs={{0,128},{128,0},{1,129},{129,1},{2,130},{130,2},{3,131},{131,3},{4... | collective-permute-start | bytes 786440 | tf_op jit(solution)/shard_map/ppermute | solution.py:383
  16.6 18.2 %collective-permute-start.4 = (bf16[512,256]{1,0:T(8,128)(2,1)S(1)}, bf16[512,256]{1,0:T(8,128)(2,1)S(1)}, u32[]{:S(2)}, u32[]{:S(2)}) collective-permute-start(bf16[512,256]{1,0:T(8,128)(2,1)S(1)} %shard_map.62.refs_2_), channel_id=1, source_target_pairs={{0,128},{128,0},{1,129},{129,1},{2,130},{130,2},{3,131},{131,3},{4... | collective-permute-start | bytes 786440 | tf_op jit(solution)/shard_map/ppermute | solution.py:383
  35.7 1.8 %collective-permute-start.7 = (bf16[8,168,128]{2,1,0:T(8,128)(2,1)S(1)}, bf16[8,168,128]{2,1,0:T(8,128)(2,1)S(1)}, u32[]{:S(2)}, u32[]{:S(2)}) collective-permute-start(bf16[8,168,128]{2,1,0:T(8,128)(2,1)S(1)} %get-tuple-element.51), channel_id=1, source_target_pairs={{0,8},{8,0},{1,9},{9,1},{2,10},{10,2},{3,11},{11,3},{4,12},{12,4},... | collective-permute-start | bytes 1032200 | tf_op jit(solution)/shard_map/ppermute | solution.py:403
  53.1 3.1 %collective-permute-start.8 = (bf16[168,128]{1,0:T(8,128)(2,1)S(1)}, bf16[168,128]{1,0:T(8,128)(2,1)S(1)}, u32[]{:S(2)}, u32[]{:S(2)}) collective-permute-start(bf16[168,128]{1,0:T(8,128)(2,1)S(1)} %shard_map.67.own_ref), channel_id=1, source_target_pairs={{0,1},{1,0},{2,3},{3,2},{4,5},{5,4},{6,7},{7,6},{8,9},{9,8},{10,11... | collective-permute-start | bytes 129032 | tf_op jit(solution)/shard_map/ppermute | solution.py:415
  56.3 5.7 %collective-permute-start.9 = (bf16[168,128]{1,0:T(8,128)(2,1)S(1)}, bf16[168,128]{1,0:T(8,128)(2,1)S(1)}, u32[]{:S(2)}, u32[]{:S(2)}) collective-permute-start(bf16[168,128]{1,0:T(8,128)(2,1)S(1)} %shard_map.68.own_ref), channel_id=1, source_target_pairs={{0,3},{1,2},{2,1},{3,0},{4,7},{5,6},{6,5},{7,4},{8,11},{9,10},{10,... | collective-permute-start | bytes 129032 | tf_op jit(solution)/shard_map/ppermute | solution.py:415
  62.0 6.0 %collective-permute-start.10 = (bf16[168,128]{1,0:T(8,128)(2,1)S(1)}, bf16[168,128]{1,0:T(8,128)(2,1)S(1)}, u32[]{:S(2)}, u32[]{:S(2)}) collective-permute-start(bf16[168,128]{1,0:T(8,128)(2,1)S(1)} %shard_map.69.own_ref), channel_id=1, source_target_pairs={{0,7},{1,6},{2,5},{3,4},{4,3},{5,2},{6,1},{7,0},{8,15},{9,14},{10,... | collective-permute-start | bytes 129032 | tf_op jit(solution)/shard_map/ppermute | solution.py:415
  68.9 11.2 %all-to-all-start.1 = ((bf16[8,160,128]{2,1,0:T(8,128)(2,1)}), bf16[8,160,128]{2,1,0:T(8,128)(2,1)S(1)}, u32[]{:S(2)}, u32[]{:S(2)}) async-start(bf16[8,160,128]{2,1,0:T(8,128)(2,1)} %get-tuple-element.52), calls=%async_computation.1 | async-start | bytes 655360 | tf_op jit(solution)/shard_map/all_to_all | solution.py:433
  80.1 7.3 %collective-permute-start.11 = (bf16[8,160,128]{2,1,0:T(8,128)(2,1)S(1)}, bf16[8,160,128]{2,1,0:T(8,128)(2,1)S(1)}, u32[]{:S(2)}, u32[]{:S(2)}) collective-permute-start(bf16[8,160,128]{2,1,0:T(8,128)(2,1)S(1)} %all-to-all-done.1.own_ref), channel_id=1, source_target_pairs={{0,8},{8,0},{1,9},{9,1},{2,10},{10,2},{3,11},{11,3},{4,12},{12,4},... | collective-permute-start | bytes 983048 | tf_op jit(solution)/shard_map/ppermute | solution.py:442

commit v6 on v5

--- a/solution.py
+++ b/solution.py
@@ -53,41 +53,49 @@
     return acc.astype(BF16)
 
 
-def edge_kernel(at_ref, m_hbm, out_ref, sem):
-    last = m_hbm.shape[1] - 1
-    copy = pltpu.make_async_copy(m_hbm.at[:, last * core_of(at_ref[0])], out_ref, sem)
-    copy.start()
-    copy.wait()
-
-
-def first_grad_kernel(count, at_ref, m_hbm, c_hbm, x_hbm, *refs):
-    g_ref, m_ref, c_ref, x_ref, xa_ref, za_ref, zb_ref, tmp_ref, sems = refs
-    members, levels, cells, _ = x_hbm.shape
-    _, rows_x, rows_y, width = m_ref.shape
-    head, rest = pl.ds(0, count), pl.ds(count, levels - count)
-    copies = [(m_hbm, m_ref)]
-    for e in range(members):
-        copies.append((c_hbm.at[e], c_ref.at[e]))
-        copies.append((x_hbm.at[e, head], x_ref.at[e, head]))
-    for e in range(members):
-        copies.append((x_hbm.at[e, rest], x_ref.at[e, rest]))
+def start_all(copies, sems):
     copies = [pltpu.make_async_copy(s, d, sems.at[i]) for i, (s, d) in enumerate(copies)]
     for copy in copies:
         copy.start()
+    return copies
+
+
+def after(copy, ref, *at):
+    def load():
+        copy.wait()
+        return ref[at].reshape(-1, ref.shape[-1])
+
+    return load
+
+
+def first_grad_kernel(at_ref, m_hbm, c_hbm, x_hbm, g_ref, c_ref, x_ref, xb_ref, m_ref, sems):
+    members = c_hbm.shape[0]
+    last = m_hbm.shape[1] - 1
+    copies = [(m_hbm.at[0], m_ref)]
+    for e in range(members):
+        copies.append((c_hbm.at[e], c_ref.at[e]))
+        copies.append((x_hbm.at[e, 0], x_ref.at[e]))
+    copies.append((m_hbm.at[:, last * core_of(at_ref[0])], xb_ref))
+    copies = start_all(copies, sems)
     copies[0].wait()
-
-    def part(copy, ref, *at):
-        def load():
-            copy.wait()
-            return ref[at].reshape(-1, ref.shape[-1])
-
-        return load
-
     g_ref[...] = gradient(
-        m_ref[0:count].reshape(count * cells, width),
-        [part(copies[1 + 2 * e], c_ref, e) for e in range(members)],
-        [part(copies[2 + 2 * e], x_ref, e, slice(0, count)) for e in range(members)],
+        m_ref[...].reshape(g_ref.shape),
+        [after(copies[1 + 2 * e], c_ref, e) for e in range(members)],
+        [after(copies[2 + 2 * e], x_ref, e) for e in range(members)],
     )
+    copies[-1].wait()
+
+
+def second_grad_kernel(count, at_ref, m_hbm, c_ref, x_hbm, *refs):
+    g_ref, m_ref, x_ref, xa_ref, za_ref, zb_ref, tmp_ref, sems = refs
+    members, levels, cells, _ = x_hbm.shape
+    _, rows_x, rows_y, width = m_ref.shape
+    copies = [(m_hbm, m_ref)]
+    for level in range(1, levels):
+        for e in range(members):
+            copies.append((x_hbm.at[e, level], x_ref.at[e, level - 1]))
+    copies = start_all(copies, sems)
+    copies[0].wait()
     core, even = core_of(at_ref[0]), parity_of(at_ref[0]) == 0
     xa_ref[...] = m_ref[:, (rows_x - 1) * (1 - core)]
     tmp_ref[0] = m_ref[:, :, 0:8, :].reshape(levels * rows_x, 8, width).astype(F32)
@@ -95,20 +103,22 @@
     lo, hi = tmp_ref[0, :, 0, :], tmp_ref[1, :, 7, :]
     za_ref[...] = jnp.where(even, hi, lo).astype(BF16)
     zb_ref[...] = jnp.where(even, lo, hi).astype(BF16)
-    for copy in copies[1 + 2 * members :]:
+    for i in range(count):
+        g_ref[i * cells : (i + 1) * cells, :] = gradient(
+            m_ref[1 + i].reshape(cells, width),
+            [functools.partial(c_ref.__getitem__, e) for e in range(members)],
+            [after(copies[1 + i * members + e], x_ref, e, i) for e in range(members)],
+        )
+    for copy in copies[1 + count * members :]:
         copy.wait()
 
 
 def grad_kernel(level, m_ref, c_ref, x_ref, g_ref):
     members = c_ref.shape[0]
-
-    def part(ref, *at):
-        return lambda: ref[at]
-
     g_ref[...] = gradient(
         m_ref[level].reshape(g_ref.shape),
-        [part(c_ref, e) for e in range(members)],
-        [part(x_ref, e, level) for e in range(members)],
+        [functools.partial(c_ref.__getitem__, e) for e in range(members)],
+        [functools.partial(x_ref.__getitem__, (e, level - 1)) for e in range(members)],
     )
 
 
@@ -120,26 +130,56 @@
     )
 
 
-def first_grad(place, modes, coefficients, series, count):
-    members, levels, cells, frames = series.shape
-    _, rows_x, rows_y, width = modes.shape
-    arrays = [modes, coefficients, series]
-    outs = [jax.ShapeDtypeStruct((count * cells, width), BF16)]
-    outs += [pltpu.VMEM(a.shape, a.dtype) for a in arrays]
-    outs += [jax.ShapeDtypeStruct((levels, rows_y, width), BF16)]
-    outs += [jax.ShapeDtypeStruct((levels * rows_x, width), BF16)] * 2
+def in_hbm(array):
+    return pltpu.with_memory_space_constraint(array, pltpu.HBM)
+
+
+def first_grad(place, modes, coefficients, series):
+    members, _, cells, frames = series.shape
+    levels, rows_x, rows_y, width = modes.shape
+    outs = [
+        jax.ShapeDtypeStruct((cells, width), BF16),
+        pltpu.VMEM(coefficients.shape, BF16),
+        pltpu.VMEM((members, cells, frames), BF16),
+        jax.ShapeDtypeStruct((levels, rows_y, width), BF16),
+    ]
     return pl.pallas_call(
-        functools.partial(first_grad_kernel, count),
+        first_grad_kernel,
         in_specs=[SM] + [HBM] * 3,
         out_specs=[VM] * len(outs),
         out_shape=outs,
         scratch_shapes=[
+            pltpu.VMEM((rows_x, rows_y, width), BF16),
+            pltpu.SemaphoreType.DMA((2 + 2 * members,)),
+        ],
+        compiler_params=PARAMS,
+        cost_estimate=grad_cost(members, cells, frames, width),
+    )(place, in_hbm(modes), in_hbm(coefficients), in_hbm(series))
+
+
+def second_grad(place, modes, coefficients, series, count):
+    members, levels, cells, frames = series.shape
+    _, rows_x, rows_y, width = modes.shape
+    outs = [
+        jax.ShapeDtypeStruct((count * cells, width), BF16),
+        pltpu.VMEM(modes.shape, BF16),
+        pltpu.VMEM((members, levels - 1, cells, frames), BF16),
+        jax.ShapeDtypeStruct((levels, rows_y, width), BF16),
+        jax.ShapeDtypeStruct((levels * rows_x, width), BF16),
+        jax.ShapeDtypeStruct((levels * rows_x, width), BF16),
+    ]
+    return pl.pallas_call(
+        functools.partial(second_grad_kernel, count),
+        in_specs=[SM, HBM, VM, HBM],
+        out_specs=[VM] * len(outs),
+        out_shape=outs,
+        scratch_shapes=[
             pltpu.VMEM((2, levels * rows_x, 8, width), F32),
-            pltpu.SemaphoreType.DMA((1 + 3 * members,)),
+            pltpu.SemaphoreType.DMA((1 + members * (levels - 1),)),
         ],
         compiler_params=PARAMS,
         cost_estimate=grad_cost(members, count * cells, frames, width),
-    )(place, *[pltpu.with_memory_space_constraint(a, pltpu.HBM) for a in arrays])
+    )(place, in_hbm(modes), coefficients, in_hbm(series))
 
 
 def grad_level(modes, coefficients, series, level):
@@ -213,7 +253,8 @@
     gram = jnp.dot(turned, moved, preferred_element_type=F32)
     gram_ref[...] = gram if first else gram_in[...] + gram
     for e in range(x_ref.shape[0]):
-        x = x_ref[e, levels].reshape(grad.shape[0], -1)
+        x = x_ref[e] if level == 0 else x_ref[e, level - 1 : level - 1 + count]
+        x = x.reshape(grad.shape[0], -1)
         proj = jnp.dot(turned, x, preferred_element_type=F32)
         proj_ref[e] = proj if first else proj_in[e] + proj
     if last:
@@ -227,9 +268,9 @@
 
 
 def step_levels(level, count, place, base, own, got, series, carry):
-    members, levels, cells, frames = series.shape
+    members, frames = series.shape[0], series.shape[-1]
     rows, width = own.shape
-    first, last = carry is None, level + count == levels
+    first, last = carry is None, level + count == base.shape[0]
     args = [place, base, own, got, series]
     if not first:
         args += list(carry)
@@ -295,9 +336,11 @@
     out_ref[SUM_ROWS:PART_ROWS, :] = packed_squares(total)
 
 
-def reduce_kernel(total_cells, at_ref, own_ref, got_ref, out_ref, shrink_ref, column_ref):
+def reduce_kernel(total_cells, at_ref, *refs):
+    *in_refs, out_ref, shrink_ref, column_ref = refs
     core, part = core_of(at_ref[0]), part_of(at_ref[0])
-    total = own_ref[...].astype(F32) + got_ref[...].astype(F32)
+    a, b, c, d = (ref[...].astype(F32) for ref in in_refs)
+    total = (a + b) + (c + d)
     squares = whole_squares(total)
     shrink = jnp.maximum(0.0, 1.0 - TAU / jnp.sqrt(squares / total_cells + 1e-06))
     shrink_ref[...] = shrink
@@ -356,33 +399,21 @@
     series = snapshots.reshape(members, levels, cells, frames)
     swap = [(0, 1), (1, 0)]
 
-    chunks = [(0, 2), (2, 1), (3, 1)]
-    edge_b = pl.pallas_call(
-        edge_kernel,
-        in_specs=[SM, HBM],
-        out_specs=VM,
-        out_shape=jax.ShapeDtypeStruct((levels, rows_y, width), BF16),
-        scratch_shapes=[pltpu.SemaphoreType.DMA],
-        compiler_params=PARAMS,
-    )(place, pltpu.with_memory_space_constraint(modes, pltpu.HBM))
+    chunks = [(0, 1), (1, 2), (3, 1)]
+    g, coefficients, head, edge_b = first_grad(place, modes, coefficients, series)
+    own, got = [g], [lax.ppermute(g, "ens", swap)]
     xb = lax.ppermute(edge_b, SX, both_ways([(i, i + 1) for i in range(1, n_sx - 1, 2)]))
-    coefficients, _ = lax.optimization_barrier((coefficients, edge_b))
-    g, modes, coefficients, series, edge_a, row_a, row_b = first_grad(
-        place, modes, coefficients, series, chunks[0][1]
-    )
+    g, modes, series, edge_a, row_a, row_b = second_grad(place, modes, coefficients, series, chunks[1][1])
     g, xb = lax.optimization_barrier((g, xb))
-    own, got = [g], [lax.ppermute(g, "ens", swap)]
+    own.append(g)
+    got.append(lax.ppermute(g, "ens", swap))
+    got[0], edge_a, row_a, row_b = lax.optimization_barrier((got[0], edge_a, row_a, row_b))
+    xa = lax.ppermute(edge_a, "c", swap)
     za = lax.ppermute(row_a, "z", both_ways([(i, i + 1) for i in range(0, n_z, 2)]))
     zb = lax.ppermute(row_b, "z", both_ways([(i, i + 1) for i in range(1, n_z - 1, 2)]))
-    xa = lax.ppermute(edge_a, "c", swap)
-
-    def send_level(level, *after):
-        c, *_ = lax.optimization_barrier((coefficients, *after))
-        g = grad_level(modes, c, series, level)
-        own.append(g)
-        got.append(lax.ppermute(g, "ens", swap))
-
-    send_level(2, xa, za, zb)
+    coefficients, *_ = lax.optimization_barrier((coefficients, xa, za, zb))
+    own.append(grad_level(modes, coefficients, series, chunks[2][0]))
+    got.append(lax.ppermute(own[2], "ens", swap))
     base = pl.pallas_call(
         base_kernel,
         in_specs=[SM] + [VM] * 5,
@@ -391,11 +422,11 @@
         compiler_params=PARAMS,
         cost_estimate=pl.CostEstimate(flops=12 * local_cells * width, bytes_accessed=6 * local_cells * width, transcendentals=0),
     )(place, modes, xa, xb, za, zb)
-    send_level(3, own[1])
 
     moved, carry = [], None
     for i, (level, count) in enumerate(chunks):
-        m, *carry = step_levels(level, count, place, base, own[i], got[i], series, carry)
+        x = head if level == 0 else series
+        m, *carry = step_levels(level, count, place, base, own[i], got[i], x, carry)
         moved.append(m)
     keep, send = carry
 
@@ -409,19 +440,14 @@
     line = pl.pallas_call(
         plane_kernel, in_specs=[VM], out_specs=VM, out_shape=line_shape, compiler_params=PARAMS
     )(parts)
-    span = 2
-    while True:
-        pairs = [(i, i ^ (span - 1)) for i in range(n_z)]
-        near = lax.ppermute(line, "z", pairs)
-        if span == n_z:
-            break
-        line = pl.pallas_call(
-            add_kernel, in_specs=[VM, VM], out_specs=VM, out_shape=line_shape, compiler_params=PARAMS
-        )(line, near)
-        span *= 2
+    near = lax.ppermute(line, "z", [(i, i ^ 1) for i in range(n_z)])
+    line = pl.pallas_call(
+        add_kernel, in_specs=[VM, VM], out_specs=VM, out_shape=line_shape, compiler_params=PARAMS
+    )(line, near)
+    others = [lax.ppermute(line, "z", [(i, i ^ k) for i in range(n_z)]) for k in (3, 5, 7)]
     spread, shrink = pl.pallas_call(
         functools.partial(reduce_kernel, total_cells),
-        in_specs=[SM, VM, VM],
+        in_specs=[SM] + [VM] * 4,
         out_specs=[VM, VM],
         out_shape=[
             jax.ShapeDtypeStruct((PARTS, SUM_ROWS, 128), BF16),
@@ -429,7 +455,7 @@
         ],
         scratch_shapes=[pltpu.VMEM((width, 128), F32)],
         compiler_params=PARAMS,
-    )(place, line, near)
+    )(place, line, *others)
     half = lax.all_to_all(spread, PLANE, 0, 0)
     new_modes = pl.pallas_call(
         scale_kernel,

time: 88.9 us -> 85.8 us (0.965)
  starting transfers between devices: 30.4 us -> 26.4 us
  Pallas kernels: 13.8 us -> 14.8 us
    ppermute x1, waiting for transfers between devices: 5.16 us -> 2.63 us  [local(): own, got = ([g], [lax.ppermute(g, 'ens', swap)])]
    pallas_call x2, Pallas kernels: 4.75 us -> 6.66 us  [the longest x1 4.13 us: second_grad(): pl.pallas_call(functools.partial(second_grad_kernel, count), in_specs=[SM...]
    ppermute x1, starting transfers between devices: 1.63 us -> 0.01 us  [local(): lax.ppermute(row_a, 'z', both_ways([(i, i + 1) for i in range(0, n_z, 2)]))]
    ppermute x5 -> x6, starting transfers between devices: 12.2 us -> 10.6 us  [the longest x3 7.31 us: local(): lax.ppermute(line, 'z', [(i, i ^ k) for i in range(n_z)])]
    ppermute x5 -> x6, waiting for transfers between devices: 13.1 us -> 14.6 us  [the longest x1 5.49 us: local(): got.append(lax.ppermute(g, 'ens', swap))]
    ppermute x1, waiting for transfers between devices: 0.76 us -> 2.22 us  [local(): lax.ppermute(row_a, 'z', both_ways([(i, i + 1) for i in range(0, n_z, 2)]))]
    ppermute x1, starting transfers between devices: 6.06 us -> 4.84 us  [local(): other_half = lax.ppermute(half, 'c', swap)]
    pallas_call x2 -> x1, Pallas kernels: 1.92 us -> 0.96 us  [grad_level(): pl.pallas_call(functools.partial(grad_kernel, level), in_specs=[VM] * 3,...]
  transfers between devices with their start and end apart: 13 -> 14, of which waited for: 10 -> 10; matrix products, arithmetic and copies ran while one was open for 0% -> 0% of each run, Pallas kernels for 11% -> 11%
where the time goes in v6:
time: 85.8 us; the launch traced here: 85.6 us
  waiting for transfers between devices  28.7 us (33%)
  starting transfers between devices  26.4 us (31%)
  blocking collectives  15 us (17%)
  Pallas kernels  14.8 us (17%)
    all_to_all x1, blocking collectives, local(): parts = lax.all_to_all(joined, PLANE, 0, 0)  15 us
    ppermute x3, starting transfers between devices, local(): lax.ppermute(line, 'z', [(i, i ^ k) for i in range(n_z)])  7.31 us
    all_to_all x1, waiting for transfers between devices, local(): half = lax.all_to_all(spread, PLANE, 0, 0)  6.67 us
    ppermute x1, waiting for transfers between devices, local(): got.append(lax.ppermute(g, 'ens', swap))  5.49 us
    ppermute x1, starting transfers between devices, local(): other_half = lax.ppermute(half, 'c', swap)  4.84 us
    ppermute x1, starting transfers between devices, local(): lax.ppermute(edge_b, SX, both_ways([(i, i + 1) for i in range(1, n_sx - 1...  4.58 us
    pallas_call x1, Pallas kernels, second_grad(): pl.pallas_call(functools.partial(second_grad_kernel, count), in_specs=[SM...  4.13 us
    all_to_all x1, starting transfers between devices, local(): half = lax.all_to_all(spread, PLANE, 0, 0)  3.96 us
  transfers between devices with their start and end apart: 14, of which 10 were waited for; matrix products, arithmetic and copies ran while one was open for 0% of the time, Pallas kernels for 11%

profile of v6, /device:TPU:1, one launch (start us, length us, event | category | flops | bytes accessed | tf_op | source)
XLA Modules:
  0.0 85.6 jit_solution(7328153358578525033)
XLA Ops:
  0.6 2.5 %shard_map.58 = (bf16[512,256]{1,0:T(8,128)(2,1)S(1)}, bf16[2,256,512]{2,1,0:T(8,128)(2,1)S(1)}, bf16[2,512,512]{2,1,0:T(8,128)(2,1)S(1)}, bf16[4,64,256]{2,1,0:T(8,128)(2,1)S(1)}) custom-call(s32[1]{0:T(128)} %bitcast.at_ref.refs_0_, bf16[4,8,64,256]{3,2,1,0:T(8,128)(2,1)} %m_hbm.3, bf16[2,256,512]{2,1,0:T(8,128)(2,1)} %c_hbm.1, ...), custom_call_target="tpu_custom_call" | custom-call | flops 536870912 | bytes 2097152 | tf_op jit(solution)/shard_map/pallas_call | solution.py:146
  3.2 4.6 %collective-permute-start.2 = (bf16[4,64,256]{2,1,0:T(8,128)(2,1)S(1)}, bf16[4,64,256]{2,1,0:T(8,128)(2,1)S(1)}, u32[]{:S(2)}, u32[]{:S(2)}) collective-permute-start(bf16[4,64,256]{2,1,0:T(8,128)(2,1)S(1)} %get-tuple-element.45), channel_id=1, source_target_pairs={{8,16},{16,8},{24,32},{32,24},{40,48},{48,40},{56,64},{64,56},{72,... | collective-permute-start | bytes 393224 | tf_op jit(solution)/shard_map/ppermute | solution.py:405
  7.8 1.3 %collective-permute-start = (bf16[512,256]{1,0:T(8,128)(2,1)S(1)}, bf16[512,256]{1,0:T(8,128)(2,1)S(1)}, u32[]{:S(2)}, u32[]{:S(2)}) collective-permute-start(bf16[512,256]{1,0:T(8,128)(2,1)S(1)} %get-tuple-element.39.refs_2_), channel_id=1, source_target_pairs={{0,128},{128,0},{1,129},{129,1},{2,130},{130,2},{3,131},{131,3},{4... | collective-permute-start | bytes 786440 | tf_op jit(solution)/shard_map/ppermute | solution.py:404
  9.1 4.1 %shard_map.59 = (bf16[1024,256]{1,0:T(8,128)(2,1)S(1)}, bf16[4,8,64,256]{3,2,1,0:T(8,128)(2,1)S(1)}, bf16[2,3,512,512]{3,2,1,0:T(8,128)(2,1)S(1)}, bf16[4,64,256...) custom-call(s32[1]{0:T(128)} %bitcast.at_ref.refs_0_, bf16[4,8,64,256]{3,2,1,0:T(8,128)(2,1)} %m_hbm.3, ...), custom_call_target="tpu_custom_call" | custom-call | flops 1073741824 | bytes 3670016 | tf_op jit(solution)/shard_map/pallas_call | solution.py:171
  13.2 0.0 collective-permute-done.2.xb_ref
  13.2 0.3 collective-permute-start.6
  13.6 2.6 %collective-permute-done.refs_3_ = bf16[512,256]{1,0:T(8,128)(2,1)S(1)} collective-permute-done((bf16[512,256]{1,0:T(8,128)(2,1)S(1)}, bf16[512,256]{1,0:T(8,128)(2,1)S(1)}, u32[]{:S(2)}, u32[]{:S(2)}) %collective-permute-start) | collective-permute-done | bytes 262176 | tf_op jit(solution)/shard_map/ppermute | solution.py:404
  16.2 0.0 collective-permute-start.1
  16.2 0.0 collective-permute-start.3
  16.2 0.7 collective-permute-start.4
  16.9 2.2 %collective-permute-done.3.za_ref = bf16[32,256]{1,0:T(8,128)(2,1)S(1)} collective-permute-done((bf16[32,256]{1,0:T(8,128)(2,1)S(1)}, bf16[32,256]{1,0:T(8,128)(2,1)S(1)}, u32[]{:S(2)}, u32[]{:S(2)}) %collective-permute-start.3) | collective-permute-done | bytes 16416 | tf_op jit(solution)/shard_map/ppermute | solution.py:412
  19.1 0.0 collective-permute-done.4.zb_ref
  19.1 0.0 collective-permute-done.1.xa_ref
  19.1 1.0 %shard_map.61.refs_2_ = bf16[512,256]{1,0:T(8,128)(2,1)S(1)} custom-call(bf16[4,8,64,256]{3,2,1,0:T(8,128)(2,1)S(1)} %get-tuple-element.38.m_ref, bf16[2,256,512]{2,1,0:T(8,128)(2,1)S(1)} %get-tuple-element.49.c_ref, bf16[2,3,512,512]{3,2,1,0:T(8,128)(2,1)S(1)} %get-tuple-element.50.x_ref.refs_4_), custom_call_target="tpu_custom_call" | custom-call | flops 536870912 | bytes 2097152 | tf_op jit(solution)/shard_map/pallas_call | solution.py:188
  20.0 0.3 collective-permute-start.5
  20.3 0.9 %shard_map.60.refs_1_ = f32[4,512,256]{2,1,0:T(8,128)S(1)} custom-call(s32[1]{0:T(128)} %bitcast.at_ref.refs_0_, bf16[4,8,64,256]{3,2,1,0:T(8,128)(2,1)S(1)} %get-tuple-element.38.m_ref, bf16[4,64,256]{2,1,0:T(8,128)(2,1)S(1)} %collective-permute-done.1.xa_ref, bf16[4,64,256]{2,1,0:T(8,128)(2,1)S(1)} %collective-permute-done.2.xb_ref, ...), custom_call_target="tpu_custom_call" | custom-call | flops 6291456 | bytes 3145728 | tf_op jit(solution)/shard_map/pallas_call | solution.py:417
  21.3 0.6 shard_map.62
  21.9 5.5 %collective-permute-done.6.refs_3_ = bf16[1024,256]{1,0:T(8,128)(2,1)S(1)} collective-permute-done((bf16[1024,256]{1,0:T(8,128)(2,1)S(1)}, bf16[1024,256]{1,0:T(8,128)(2,1)S(1)}, u32[]{:S(2)}, u32[]{:S(2)}) %collective-permute-start.6) | collective-permute-done | bytes 524320 | tf_op jit(solution)/shard_map/ppermute | solution.py:409
  27.4 1.3 %shard_map.63 = (bf16[1024,256]{1,0:T(8,128)(2,1)S(1)}, f32[2,256,512]{2,1,0:T(8,128)S(1)}, f32[256,256]{1,0:T(8,128)S(1)}, f32[1,256]{1,0:T(1,128)S(1)}) custom-call(s32[1]{0:T(128)} %bitcast.at_ref.refs_0_, f32[4,512,256]{2,1,0:T(8,128)S(1)} %shard_map.60.refs_1_, ...), custom_call_target="tpu_custom_call", output_to_operand_aliasing={{1}: (5, {}), {2}: (6, {}), {3}: (7, {})} | custom-call | flops 671088640 | bytes 4194304 | tf_op jit(solution)/shard_map/pallas_call | solution.py:291
  28.7 3.9 %collective-permute-done.5.refs_3_ = bf16[512,256]{1,0:T(8,128)(2,1)S(1)} collective-permute-done((bf16[512,256]{1,0:T(8,128)(2,1)S(1)}, bf16[512,256]{1,0:T(8,128)(2,1)S(1)}, u32[]{:S(2)}, u32[]{:S(2)}) %collective-permute-start.5) | collective-permute-done | bytes 262176 | tf_op jit(solution)/shard_map/ppermute | solution.py:416
  32.6 0.9 shard_map.64
  33.5 0.5 collective-permute-start.7
  33.9 1.3 %collective-permute-done.7.got_ref = bf16[8,168,128]{2,1,0:T(8,128)(2,1)S(1)} collective-permute-done((bf16[8,168,128]{2,1,0:T(8,128)(2,1)S(1)}, bf16[8,168,128]{2,1,0:T(8,128)(2,1)S(1)}, u32[]{:S(2)}, u32[]{:S(2)}) %collective-permute-start.7) | collective-permute-done | bytes 344096 | tf_op jit(solution)/shard_map/ppermute | solution.py:434
  35.2 0.1 shard_map.65
  35.3 15.0 %all_to_all.10.in_ref = bf16[8,168,128]{2,1,0:T(8,128)(2,1)S(1)} all-to-all(bf16[8,168,128]{2,1,0:T(8,128)(2,1)S(1)} %shard_map.65), channel_id=1, replica_groups=mesh['ens'=2,'xh'=2,'y'=4,'c'=2,'z'=8] {'xh','y'}, dimensions={0} | all-to-all | bytes 688128 | tf_op jit(solution)/shard_map/all_to_all | solution.py:438
  50.3 0.1 shard_map.66.own_ref
  50.4 2.6 %collective-permute-start.8 = (bf16[168,128]{1,0:T(8,128)(2,1)S(1)}, bf16[168,128]{1,0:T(8,128)(2,1)S(1)}, u32[]{:S(2)}, u32[]{:S(2)}) collective-permute-start(bf16[168,128]{1,0:T(8,128)(2,1)S(1)} %shard_map.66.own_ref), channel_id=1, source_target_pairs={{0,1},{1,0},{2,3},{3,2},{4,5},{5,4},{6,7},{7,6},{8,9},{9,8},{10,11... | collective-permute-start | bytes 129032 | tf_op jit(solution)/shard_map/ppermute | solution.py:443
  53.0 1.4 %collective-permute-done.8.got_ref = bf16[168,128]{1,0:T(8,128)(2,1)S(1)} collective-permute-done((bf16[168,128]{1,0:T(8,128)(2,1)S(1)}, bf16[168,128]{1,0:T(8,128)(2,1)S(1)}, u32[]{:S(2)}, u32[]{:S(2)}) %collective-permute-start.8) | collective-permute-done | bytes 43040 | tf_op jit(solution)/shard_map/ppermute | solution.py:443
  54.4 4.6 %collective-permute-start.11 = (bf16[168,128]{1,0:T(8,128)(2,1)S(1)}, bf16[168,128]{1,0:T(8,128)(2,1)S(1)}, u32[]{:S(2)}, u32[]{:S(2)}) collective-permute-start(bf16[168,128]{1,0:T(8,128)(2,1)S(1)} %shard_map.67.refs_0_), channel_id=1, source_target_pairs={{0,7},{1,6},{2,5},{3,4},{4,3},{5,2},{6,1},{7,0},{8,15},{9,14},{10,... | collective-permute-start | bytes 129032 | tf_op jit(solution)/shard_map/ppermute | solution.py:447
  59.0 1.8 %collective-permute-start.10 = (bf16[168,128]{1,0:T(8,128)(2,1)S(1)}, bf16[168,128]{1,0:T(8,128)(2,1)S(1)}, u32[]{:S(2)}, u32[]{:S(2)}) collective-permute-start(bf16[168,128]{1,0:T(8,128)(2,1)S(1)} %shard_map.67.refs_0_), channel_id=1, source_target_pairs={{0,5},{1,4},{2,7},{3,6},{4,1},{5,0},{6,3},{7,2},{8,13},{9,12},{10,... | collective-permute-start | bytes 129032 | tf_op jit(solution)/shard_map/ppermute | solution.py:447
  60.8 0.9 %collective-permute-start.9 = (bf16[168,128]{1,0:T(8,128)(2,1)S(1)}, bf16[168,128]{1,0:T(8,128)(2,1)S(1)}, u32[]{:S(2)}, u32[]{:S(2)}) collective-permute-start(bf16[168,128]{1,0:T(8,128)(2,1)S(1)} %shard_map.67.refs_0_), channel_id=1, source_target_pairs={{0,3},{1,2},{2,1},{3,0},{4,7},{5,6},{6,5},{7,4},{8,11},{9,10},{10,... | collective-permute-start | bytes 129032 | tf_op jit(solution)/shard_map/ppermute | solution.py:447
  61.8 0.0 collective-permute-done.11.refs_3_
  61.8 3.1 %collective-permute-done.10.refs_2_ = bf16[168,128]{1,0:T(8,128)(2,1)S(1)} collective-permute-done((bf16[168,128]{1,0:T(8,128)(2,1)S(1)}, bf16[168,128]{1,0:T(8,128)(2,1)S(1)}, u32[]{:S(2)}, u32[]{:S(2)}) %collective-permute-start.10) | collective-permute-done | bytes 43040 | tf_op jit(solution)/shard_map/ppermute | solution.py:447
  64.9 0.7 collective-permute-done.9.refs_1_
  65.6 0.9 %shard_map.68 = (bf16[8,160,128]{2,1,0:T(8,128)(2,1)}, f32[2,128]{1,0:T(2,128)S(1)}) custom-call(s32[1]{0:T(128)} %bitcast.at_ref.refs_0_, bf16[168,128]{1,0:T(8,128)(2,1)S(1)} %shard_map.67.refs_0_, bf16[168,128]{1,0:T(8,128)(2,1)S(1)} %collective-permute-done.9.refs_1_, bf16[168,128]{1,0:T(8,128)(2,1)S(1)} %collective-permute-done.10.refs_2_, ...), custom_call_target="tpu_custom_call" | custom-call | tf_op jit(solution)/shard_map/pallas_call | solution.py:448
  66.5 4.0 %all-to-all-start.1 = ((bf16[8,160,128]{2,1,0:T(8,128)(2,1)}), bf16[8,160,128]{2,1,0:T(8,128)(2,1)S(1)}, u32[]{:S(2)}, u32[]{:S(2)}) async-start(bf16[8,160,128]{2,1,0:T(8,128)(2,1)} %get-tuple-element.62), calls=%async_computation.1 | async-start | bytes 655360 | tf_op jit(solution)/shard_map/all_to_all | solution.py:459
  70.4 1.2 %shard_map.69 = bf16[2048,256]{1,0:T(8,128)(2,1)} custom-call(f32[2,128]{1,0:T(2,128)S(1)} %get-tuple-element.63.shrink_ref, bf16[512,256]{1,0:T(8,128)(2,1)S(1)} %get-tuple-element.64.refs_0_, bf16[1024,256]{1,0:T(8,128)(2,1)S(1)} %get-tuple-element.65.refs_1_, bf16[512,256]{1,0:T(8,128)(2,1)S(1)} %get-tuple-element.66.refs_2_), custom_call_target="tpu_custom_call" | custom-call | tf_op jit(solution)/shard_map/pallas_call | solution.py:460
  71.6 6.7 %all-to-all-done.1.own_ref = bf16[8,160,128]{2,1,0:T(8,128)(2,1)S(1)} async-done(((bf16[8,160,128]{2,1,0:T(8,128)(2,1)}), bf16[8,160,128]{2,1,0:T(8,128)(2,1)S(1)}, u32[]{:S(2)}, u32[]{:S(2)}) %all-to-all-start.1) | async-done | bytes 327712 | tf_op jit(solution)/shard_map/all_to_all | solution.py:459
  78.3 4.8 %collective-permute-start.12 = (bf16[8,160,128]{2,1,0:T(8,128)(2,1)S(1)}, bf16[8,160,128]{2,1,0:T(8,128)(2,1)S(1)}, u32[]{:S(2)}, u32[]{:S(2)}) collective-permute-start(bf16[8,160,128]{2,1,0:T(8,128)(2,1)S(1)} %all-to-all-done.1.own_ref), channel_id=1, source_target_pairs={{0,8},{8,0},{1,9},{9,1},{2,10},{10,2},{3,11},{11,3},{4,12},{12,4},... | collective-permute-start | bytes 983048 | tf_op jit(solution)/shard_map/ppermute | solution.py:468
  83.1 1.3 %collective-permute-done.12.got_ref = bf16[8,160,128]{2,1,0:T(8,128)(2,1)S(1)} collective-permute-done((bf16[8,160,128]{2,1,0:T(8,128)(2,1)S(1)}, bf16[8,160,128]{2,1,0:T(8,128)(2,1)S(1)}, u32[]{:S(2)}, u32[]{:S(2)}) %collective-permute-start.12) | collective-permute-done | bytes 327712 | tf_op jit(solution)/shard_map/ppermute | solution.py:468
  84.4 1.2 %shard_map.70 = (f32[2,256,512]{2,1,0:T(8,128)}, f32[256,256]{1,0:T(8,128)}) custom-call(s32[1]{0:T(128)} %bitcast.at_ref.refs_0_, bf16[8,160,128]{2,1,0:T(8,128)(2,1)S(1)} %all-to-all-done.1.own_ref, bf16[8,160,128]{2,1,0:T(8,128)(2,1)S(1)} %collective-permute-done.12.got_ref), custom_call_target="tpu_custom_call" | custom-call | tf_op jit(solution)/shard_map/pallas_call | solution.py:469
  (1 shorter events, 0.0 us)
Async XLA Ops:
  3.2 10.0 %collective-permute-start.2 = (bf16[4,64,256]{2,1,0:T(8,128)(2,1)S(1)}, bf16[4,64,256]{2,1,0:T(8,128)(2,1)S(1)}, u32[]{:S(2)}, u32[]{:S(2)}) collective-permute-start(bf16[4,64,256]{2,1,0:T(8,128)(2,1)S(1)} %get-tuple-element.45), channel_id=1, source_target_pairs={{8,16},{16,8},{24,32},{32,24},{40,48},{48,40},{56,64},{64,56},{72,... | collective-permute-start | bytes 393224 | tf_op jit(solution)/shard_map/ppermute | solution.py:405
  7.8 8.4 %collective-permute-start = (bf16[512,256]{1,0:T(8,128)(2,1)S(1)}, bf16[512,256]{1,0:T(8,128)(2,1)S(1)}, u32[]{:S(2)}, u32[]{:S(2)}) collective-permute-start(bf16[512,256]{1,0:T(8,128)(2,1)S(1)} %get-tuple-element.39.refs_2_), channel_id=1, source_target_pairs={{0,128},{128,0},{1,129},{129,1},{2,130},{130,2},{3,131},{131,3},{4... | collective-permute-start | bytes 786440 | tf_op jit(solution)/shard_map/ppermute | solution.py:404
  13.2 14.2 %collective-permute-start.6 = (bf16[1024,256]{1,0:T(8,128)(2,1)S(1)}, bf16[1024,256]{1,0:T(8,128)(2,1)S(1)}, u32[]{:S(2)}, u32[]{:S(2)}) collective-permute-start(bf16[1024,256]{1,0:T(8,128)(2,1)S(1)} %get-tuple-element.51.refs_2_), channel_id=1, source_target_pairs={{0,128},{128,0},{1,129},{129,1},{2,130},{130,2},{3,131},{131,3},{4... | collective-permute-start | bytes 1572872 | tf_op jit(solution)/shard_map/ppermute | solution.py:409
  16.2 2.9 %collective-permute-start.1 = (bf16[4,64,256]{2,1,0:T(8,128)(2,1)S(1)}, bf16[4,64,256]{2,1,0:T(8,128)(2,1)S(1)}, u32[]{:S(2)}, u32[]{:S(2)}) collective-permute-start(bf16[4,64,256]{2,1,0:T(8,128)(2,1)S(1)} %get-tuple-element.43), channel_id=1, source_target_pairs={{0,8},{8,0},{1,9},{9,1},{2,10},{10,2},{3,11},{11,3},{4,12},{12,4},... | collective-permute-start | bytes 393224 | tf_op jit(solution)/shard_map/ppermute | solution.py:411
  16.2 2.9 %collective-permute-start.3 = (bf16[32,256]{1,0:T(8,128)(2,1)S(1)}, bf16[32,256]{1,0:T(8,128)(2,1)S(1)}, u32[]{:S(2)}, u32[]{:S(2)}) collective-permute-start(bf16[32,256]{1,0:T(8,128)(2,1)S(1)} %get-tuple-element.47), channel_id=1, source_target_pairs={{0,1},{1,0},{2,3},{3,2},{4,5},{5,4},{6,7},{7,6},{8,9},{9,8},{10,11... | collective-permute-start | bytes 49160 | tf_op jit(solution)/shard_map/ppermute | solution.py:412
  16.2 2.9 %collective-permute-start.4 = (bf16[32,256]{1,0:T(8,128)(2,1)S(1)}, bf16[32,256]{1,0:T(8,128)(2,1)S(1)}, u32[]{:S(2)}, u32[]{:S(2)}) collective-permute-start(bf16[32,256]{1,0:T(8,128)(2,1)S(1)} %get-tuple-element.48), channel_id=1, source_target_pairs={{1,2},{2,1},{3,4},{4,3},{5,6},{6,5},{9,10},{10,9},{11,12},{12,11},... | collective-permute-start | bytes 49160 | tf_op jit(solution)/shard_map/ppermute | solution.py:413
  20.0 12.5 %collective-permute-start.5 = (bf16[512,256]{1,0:T(8,128)(2,1)S(1)}, bf16[512,256]{1,0:T(8,128)(2,1)S(1)}, u32[]{:S(2)}, u32[]{:S(2)}) collective-permute-start(bf16[512,256]{1,0:T(8,128)(2,1)S(1)} %shard_map.61.refs_2_), channel_id=1, source_target_pairs={{0,128},{128,0},{1,129},{129,1},{2,130},{130,2},{3,131},{131,3},{4... | collective-permute-start | bytes 786440 | tf_op jit(solution)/shard_map/ppermute | solution.py:416
  33.5 1.8 %collective-permute-start.7 = (bf16[8,168,128]{2,1,0:T(8,128)(2,1)S(1)}, bf16[8,168,128]{2,1,0:T(8,128)(2,1)S(1)}, u32[]{:S(2)}, u32[]{:S(2)}) collective-permute-start(bf16[8,168,128]{2,1,0:T(8,128)(2,1)S(1)} %get-tuple-element.61), channel_id=1, source_target_pairs={{0,8},{8,0},{1,9},{9,1},{2,10},{10,2},{3,11},{11,3},{4,12},{12,4},... | collective-permute-start | bytes 1032200 | tf_op jit(solution)/shard_map/ppermute | solution.py:434
  50.4 4.1 %collective-permute-start.8 = (bf16[168,128]{1,0:T(8,128)(2,1)S(1)}, bf16[168,128]{1,0:T(8,128)(2,1)S(1)}, u32[]{:S(2)}, u32[]{:S(2)}) collective-permute-start(bf16[168,128]{1,0:T(8,128)(2,1)S(1)} %shard_map.66.own_ref), channel_id=1, source_target_pairs={{0,1},{1,0},{2,3},{3,2},{4,5},{5,4},{6,7},{7,6},{8,9},{9,8},{10,11... | collective-permute-start | bytes 129032 | tf_op jit(solution)/shard_map/ppermute | solution.py:443
  54.4 7.3 %collective-permute-start.11 = (bf16[168,128]{1,0:T(8,128)(2,1)S(1)}, bf16[168,128]{1,0:T(8,128)(2,1)S(1)}, u32[]{:S(2)}, u32[]{:S(2)}) collective-permute-start(bf16[168,128]{1,0:T(8,128)(2,1)S(1)} %shard_map.67.refs_0_), channel_id=1, source_target_pairs={{0,7},{1,6},{2,5},{3,4},{4,3},{5,2},{6,1},{7,0},{8,15},{9,14},{10,... | collective-permute-start | bytes 129032 | tf_op jit(solution)/shard_map/ppermute | solution.py:447
  59.0 5.9 %collective-permute-start.10 = (bf16[168,128]{1,0:T(8,128)(2,1)S(1)}, bf16[168,128]{1,0:T(8,128)(2,1)S(1)}, u32[]{:S(2)}, u32[]{:S(2)}) collective-permute-start(bf16[168,128]{1,0:T(8,128)(2,1)S(1)} %shard_map.67.refs_0_), channel_id=1, source_target_pairs={{0,5},{1,4},{2,7},{3,6},{4,1},{5,0},{6,3},{7,2},{8,13},{9,12},{10,... | collective-permute-start | bytes 129032 | tf_op jit(solution)/shard_map/ppermute | solution.py:447
  60.8 4.7 %collective-permute-start.9 = (bf16[168,128]{1,0:T(8,128)(2,1)S(1)}, bf16[168,128]{1,0:T(8,128)(2,1)S(1)}, u32[]{:S(2)}, u32[]{:S(2)}) collective-permute-start(bf16[168,128]{1,0:T(8,128)(2,1)S(1)} %shard_map.67.refs_0_), channel_id=1, source_target_pairs={{0,3},{1,2},{2,1},{3,0},{4,7},{5,6},{6,5},{7,4},{8,11},{9,10},{10,... | collective-permute-start | bytes 129032 | tf_op jit(solution)/shard_map/ppermute | solution.py:447
  66.5 11.8 %all-to-all-start.1 = ((bf16[8,160,128]{2,1,0:T(8,128)(2,1)}), bf16[8,160,128]{2,1,0:T(8,128)(2,1)S(1)}, u32[]{:S(2)}, u32[]{:S(2)}) async-start(bf16[8,160,128]{2,1,0:T(8,128)(2,1)} %get-tuple-element.62), calls=%async_computation.1 | async-start | bytes 655360 | tf_op jit(solution)/shard_map/all_to_all | solution.py:459
  78.3 6.1 %collective-permute-start.12 = (bf16[8,160,128]{2,1,0:T(8,128)(2,1)S(1)}, bf16[8,160,128]{2,1,0:T(8,128)(2,1)S(1)}, u32[]{:S(2)}, u32[]{:S(2)}) collective-permute-start(bf16[8,160,128]{2,1,0:T(8,128)(2,1)S(1)} %all-to-all-done.1.own_ref), channel_id=1, source_target_pairs={{0,8},{8,0},{1,9},{9,1},{2,10},{10,2},{3,11},{11,3},{4,12},{12,4},... | collective-permute-start | bytes 983048 | tf_op jit(solution)/shard_map/ppermute | solution.py:468

commit v7 on v6

--- a/solution.py
+++ b/solution.py
@@ -18,10 +18,11 @@
 PARAMS = pltpu.CompilerParams(vmem_limit_bytes=VMEM_LIMIT)
 
 SX = ("xh", "y", "c")
-PLANE = ("xh", "y")
-PARTS = 8
-PROJ_ROWS = 128
-GRAM_ROWS = 32
+SY = ("zh", "zl")
+GROUP = ("xh", "y", "zl")
+PARTS = 16
+PROJ_ROWS = 64
+GRAM_ROWS = 16
 SUM_ROWS = PROJ_ROWS + GRAM_ROWS
 PART_ROWS = SUM_ROWS + 8
 
@@ -86,8 +87,8 @@
     copies[-1].wait()
 
 
-def second_grad_kernel(count, at_ref, m_hbm, c_ref, x_hbm, *refs):
-    g_ref, m_ref, x_ref, xa_ref, za_ref, zb_ref, tmp_ref, sems = refs
+def second_grad_kernel(at_ref, m_hbm, c_ref, x_hbm, *refs):
+    *g_refs, m_ref, x_ref, xa_ref, za_ref, zb_ref, tmp_ref, sems = refs
     members, levels, cells, _ = x_hbm.shape
     _, rows_x, rows_y, width = m_ref.shape
     copies = [(m_hbm, m_ref)]
@@ -103,23 +104,15 @@
     lo, hi = tmp_ref[0, :, 0, :], tmp_ref[1, :, 7, :]
     za_ref[...] = jnp.where(even, hi, lo).astype(BF16)
     zb_ref[...] = jnp.where(even, lo, hi).astype(BF16)
-    for i in range(count):
-        g_ref[i * cells : (i + 1) * cells, :] = gradient(
-            m_ref[1 + i].reshape(cells, width),
-            [functools.partial(c_ref.__getitem__, e) for e in range(members)],
-            [after(copies[1 + i * members + e], x_ref, e, i) for e in range(members)],
-        )
-    for copy in copies[1 + count * members :]:
-        copy.wait()
-
-
-def grad_kernel(level, m_ref, c_ref, x_ref, g_ref):
-    members = c_ref.shape[0]
-    g_ref[...] = gradient(
-        m_ref[level].reshape(g_ref.shape),
-        [functools.partial(c_ref.__getitem__, e) for e in range(members)],
-        [functools.partial(x_ref.__getitem__, (e, level - 1)) for e in range(members)],
-    )
+    at = 0
+    for g_ref in g_refs:
+        for first in range(0, g_ref.shape[0], cells):
+            g_ref[first : first + cells, :] = gradient(
+                m_ref[1 + at].reshape(cells, width),
+                [functools.partial(c_ref.__getitem__, e) for e in range(members)],
+                [after(copies[1 + at * members + e], x_ref, e, at) for e in range(members)],
+            )
+            at += 1
 
 
 def grad_cost(members, cells, frames, width):
@@ -157,11 +150,11 @@
     )(place, in_hbm(modes), in_hbm(coefficients), in_hbm(series))
 
 
-def second_grad(place, modes, coefficients, series, count):
+def second_grad(place, modes, coefficients, series, counts):
     members, levels, cells, frames = series.shape
     _, rows_x, rows_y, width = modes.shape
-    outs = [
-        jax.ShapeDtypeStruct((count * cells, width), BF16),
+    outs = [jax.ShapeDtypeStruct((count * cells, width), BF16) for count in counts]
+    outs += [
         pltpu.VMEM(modes.shape, BF16),
         pltpu.VMEM((members, levels - 1, cells, frames), BF16),
         jax.ShapeDtypeStruct((levels, rows_y, width), BF16),
@@ -169,7 +162,7 @@
         jax.ShapeDtypeStruct((levels * rows_x, width), BF16),
     ]
     return pl.pallas_call(
-        functools.partial(second_grad_kernel, count),
+        second_grad_kernel,
         in_specs=[SM, HBM, VM, HBM],
         out_specs=[VM] * len(outs),
         out_shape=outs,
@@ -178,21 +171,8 @@
             pltpu.SemaphoreType.DMA((1 + members * (levels - 1),)),
         ],
         compiler_params=PARAMS,
-        cost_estimate=grad_cost(members, count * cells, frames, width),
+        cost_estimate=grad_cost(members, sum(counts) * cells, frames, width),
     )(place, in_hbm(modes), coefficients, in_hbm(series))
-
-
-def grad_level(modes, coefficients, series, level):
-    members, _, cells, frames = series.shape
-    width = modes.shape[3]
-    return pl.pallas_call(
-        functools.partial(grad_kernel, level),
-        in_specs=[VM] * 3,
-        out_specs=VM,
-        out_shape=jax.ShapeDtypeStruct((cells, width), BF16),
-        compiler_params=PARAMS,
-        cost_estimate=grad_cost(members, cells, frames, width),
-    )(modes, coefficients, series)
 
 
 def base_kernel(at_ref, m_ref, xa_ref, xb_ref, za_ref, zb_ref, base_ref):
@@ -223,9 +203,9 @@
 def emit(out_ref, half, proj_ref, gram_ref, squares):
     members = proj_ref.shape[0]
     for j in range(PARTS):
-        tb, m, r = j // 4, (j // 2) % members, j % 2
+        tb, m, r = j // 8, (j // 4) % members, j % 4
         at = pl.multiple_of((half * 2 + tb) * 128, 128)
-        block = proj_ref[m, r * 128 : (r + 1) * 128, pl.ds(at, 128)]
+        block = proj_ref[m, r * PROJ_ROWS : (r + 1) * PROJ_ROWS, pl.ds(at, 128)]
         out_ref[j, 0:PROJ_ROWS, :] = block.astype(BF16)
         at = pl.multiple_of(half * 128, 128)
         block = gram_ref[j * GRAM_ROWS : (j + 1) * GRAM_ROWS, pl.ds(at, 128)]
@@ -322,16 +302,10 @@
         out_ref[j, SUM_ROWS:PART_ROWS, :] = packed
 
 
-def plane_kernel(in_ref, out_ref):
+def group_kernel(in_ref, out_ref):
     total = in_ref[0].astype(F32)
     for j in range(1, PARTS):
         total = total + in_ref[j].astype(F32)
-    out_ref[0:SUM_ROWS, :] = total[0:SUM_ROWS, :].astype(BF16)
-    out_ref[SUM_ROWS:PART_ROWS, :] = packed_squares(total)
-
-
-def add_kernel(own_ref, got_ref, out_ref):
-    total = own_ref[...].astype(F32) + got_ref[...].astype(F32)
     out_ref[0:SUM_ROWS, :] = total[0:SUM_ROWS, :].astype(BF16)
     out_ref[SUM_ROWS:PART_ROWS, :] = packed_squares(total)
 
@@ -346,8 +320,8 @@
     shrink_ref[...] = shrink
     for k in range(2):
         column_ref[k * 128 : (k + 1) * 128, :] = jnp.broadcast_to(shrink[k : k + 1, :], (128, 128)).T
-    at = pl.multiple_of(lax.rem(part, 2) * 128, 128)
-    proj = column_ref[pl.ds(at, 128), :] * total[0:PROJ_ROWS, :] * (1.0 / math.sqrt(total_cells))
+    at = pl.multiple_of((part & 3) * PROJ_ROWS, PROJ_ROWS)
+    proj = column_ref[pl.ds(at, PROJ_ROWS), :] * total[0:PROJ_ROWS, :] * (1.0 / math.sqrt(total_cells))
     at = pl.multiple_of(part * GRAM_ROWS, GRAM_ROWS)
     lanes = jnp.where(core == 0, shrink[0:1, :], shrink[1:2, :])
     gram = column_ref[pl.ds(at, GRAM_ROWS), :] * total[PROJ_ROWS:SUM_ROWS, :] * lanes * (1.0 / total_cells)
@@ -372,9 +346,10 @@
     members = proj_ref.shape[0]
     for ref, half in ((own_ref, core), (got_ref, 1 - core)):
         for j in range(PARTS):
-            tb, m, r = j // 4, (j // 2) % members, j % 2
+            tb, m, r = j // 8, (j // 4) % members, j % 4
             at = pl.multiple_of((half * 2 + tb) * 128, 128)
-            proj_ref[m, r * 128 : (r + 1) * 128, pl.ds(at, 128)] = ref[j, 0:PROJ_ROWS, :].astype(F32)
+            rows = slice(r * PROJ_ROWS, (r + 1) * PROJ_ROWS)
+            proj_ref[m, rows, pl.ds(at, 128)] = ref[j, 0:PROJ_ROWS, :].astype(F32)
             at = pl.multiple_of(half * 128, 128)
             gram_ref[j * GRAM_ROWS : (j + 1) * GRAM_ROWS, pl.ds(at, 128)] = (
                 ref[j, PROJ_ROWS:SUM_ROWS, :].astype(F32)
@@ -390,11 +365,11 @@
     width = modes.shape[3]
     cells = rows_x * rows_y
     local_cells = levels * cells
-    n_sx, n_z = lax.axis_size(SX), lax.axis_size("z")
+    n_sx, n_z = lax.axis_size(SX), lax.axis_size(SY)
     total_cells = local_cells * n_sx * n_z
     core = lax.axis_index("c").astype(jnp.int32)
-    parity = lax.axis_index("z").astype(jnp.int32) & 1
-    part = lax.axis_index(PLANE).astype(jnp.int32)
+    parity = lax.axis_index("zl").astype(jnp.int32)
+    part = lax.axis_index(GROUP).astype(jnp.int32)
     place = (core + 2 * parity + 4 * part).reshape(1)
     series = snapshots.reshape(members, levels, cells, frames)
     swap = [(0, 1), (1, 0)]
@@ -403,17 +378,19 @@
     g, coefficients, head, edge_b = first_grad(place, modes, coefficients, series)
     own, got = [g], [lax.ppermute(g, "ens", swap)]
     xb = lax.ppermute(edge_b, SX, both_ways([(i, i + 1) for i in range(1, n_sx - 1, 2)]))
-    g, modes, series, edge_a, row_a, row_b = second_grad(place, modes, coefficients, series, chunks[1][1])
-    g, xb = lax.optimization_barrier((g, xb))
-    own.append(g)
-    got.append(lax.ppermute(g, "ens", swap))
+    counts = [count for _, count in chunks[1:]]
+    mid, tail, modes, series, edge_a, row_a, row_b = second_grad(
+        place, modes, coefficients, series, counts
+    )
+    mid, xb = lax.optimization_barrier((mid, xb))
+    got.append(lax.ppermute(mid, "ens", swap))
     got[0], edge_a, row_a, row_b = lax.optimization_barrier((got[0], edge_a, row_a, row_b))
+    own += [mid, tail]
     xa = lax.ppermute(edge_a, "c", swap)
-    za = lax.ppermute(row_a, "z", both_ways([(i, i + 1) for i in range(0, n_z, 2)]))
-    zb = lax.ppermute(row_b, "z", both_ways([(i, i + 1) for i in range(1, n_z - 1, 2)]))
-    coefficients, *_ = lax.optimization_barrier((coefficients, xa, za, zb))
-    own.append(grad_level(modes, coefficients, series, chunks[2][0]))
-    got.append(lax.ppermute(own[2], "ens", swap))
+    za = lax.ppermute(row_a, SY, both_ways([(i, i + 1) for i in range(0, n_z, 2)]))
+    zb = lax.ppermute(row_b, SY, both_ways([(i, i + 1) for i in range(1, n_z - 1, 2)]))
+    tail, xa, za, zb = lax.optimization_barrier((tail, xa, za, zb))
+    got.append(lax.ppermute(tail, "ens", swap))
     base = pl.pallas_call(
         base_kernel,
         in_specs=[SM] + [VM] * 5,
@@ -435,16 +412,13 @@
     joined = pl.pallas_call(
         join_kernel, in_specs=[VM, VM], out_specs=VM, out_shape=part_shape, compiler_params=PARAMS
     )(keep, other)
-    parts = lax.all_to_all(joined, PLANE, 0, 0)
+    parts = lax.all_to_all(joined, GROUP, 0, 0)
     line_shape = jax.ShapeDtypeStruct((PART_ROWS, 128), BF16)
     line = pl.pallas_call(
-        plane_kernel, in_specs=[VM], out_specs=VM, out_shape=line_shape, compiler_params=PARAMS
+        group_kernel, in_specs=[VM], out_specs=VM, out_shape=line_shape, compiler_params=PARAMS
     )(parts)
-    near = lax.ppermute(line, "z", [(i, i ^ 1) for i in range(n_z)])
-    line = pl.pallas_call(
-        add_kernel, in_specs=[VM, VM], out_specs=VM, out_shape=line_shape, compiler_params=PARAMS
-    )(line, near)
-    others = [lax.ppermute(line, "z", [(i, i ^ k) for i in range(n_z)]) for k in (3, 5, 7)]
+    pairs = lax.axis_size("zh")
+    others = [lax.ppermute(line, "zh", [(i, i ^ k) for i in range(pairs)]) for k in (1, 2, 3)]
     spread, shrink = pl.pallas_call(
         functools.partial(reduce_kernel, total_cells),
         in_specs=[SM] + [VM] * 4,
@@ -456,7 +430,7 @@
         scratch_shapes=[pltpu.VMEM((width, 128), F32)],
         compiler_params=PARAMS,
     )(place, line, *others)
-    half = lax.all_to_all(spread, PLANE, 0, 0)
+    half = lax.all_to_all(spread, GROUP, 0, 0)
     new_modes = pl.pallas_call(
         scale_kernel,
         in_specs=[VM] * (1 + len(moved)),
@@ -481,7 +455,7 @@
 
 def solution(mesh):
     ens, n_sx, n_sy = (mesh.shape[a] for a in ("ens", "sx", "sy"))
-    fine = Mesh(mesh.devices.reshape(ens, 2, n_sx // 4, 2, n_sy), ("ens", "xh", "y", "c", "z"))
-    in_specs = (P("ens", None, SX, "z", None), P("ens", None, None), P(None, SX, "z", None))
-    out_specs = (P(None, SX, "z", None), P(), P("ens", None, None))
+    fine = Mesh(mesh.devices.reshape(ens, 2, n_sx // 4, 2, n_sy // 2, 2), ("ens", *SX, *SY))
+    in_specs = (P("ens", None, SX, SY, None), P("ens", None, None), P(None, SX, SY, None))
+    out_specs = (P(None, SX, SY, None), P(), P("ens", None, None))
     return jax.shard_map(local, mesh=fine, in_specs=in_specs, out_specs=out_specs, check_vma=False)

time: 85.8 us -> 85.7 us (level)
  waiting for transfers between devices: 28.7 us -> 26.2 us
  blocking collectives: 15 us -> 16.8 us
    ppermute x1, waiting for transfers between devices: 2.63 us -> 0.01 us  [local(): own, got = ([g], [lax.ppermute(g, 'ens', swap)])]
    all_to_all x1, blocking collectives: 15 us -> 16.8 us  [local(): parts = lax.all_to_all(joined, GROUP, 0, 0)]
    pallas_call x4 -> x2, Pallas kernels: 5.16 us -> 5.45 us  [the longest x1 5.4 us: second_grad(): pl.pallas_call(second_grad_kernel, in_specs=[SM, HBM, VM, HBM], out_specs...]
    ppermute x8 -> x7, waiting for transfers between devices: 16.8 us -> 16.7 us  [the longest x1 7.88 us: local(): got.append(lax.ppermute(mid, 'ens', swap))]
    ppermute x8 -> x7, starting transfers between devices: 11.2 us -> 11.2 us  [the longest x3 7.38 us: local(): lax.ppermute(line, 'zh', [(i, i ^ k) for i in range(pairs)])]
  transfers between devices with their start and end apart: 14 -> 13, of which waited for: 10 -> 8; matrix products, arithmetic and copies ran while one was open for 0% -> 0% of each run, Pallas kernels for 11% -> 11%
where the time goes in v7:
time: 85.7 us; the launch traced here: 85.4 us
  starting transfers between devices  26.6 us (31%)
  waiting for transfers between devices  26.2 us (31%)
  blocking collectives  16.8 us (20%)
  Pallas kernels  15.1 us (18%)
    all_to_all x1, blocking collectives, local(): parts = lax.all_to_all(joined, GROUP, 0, 0)  16.8 us
    ppermute x1, waiting for transfers between devices, local(): got.append(lax.ppermute(mid, 'ens', swap))  7.88 us
    ppermute x3, starting transfers between devices, local(): lax.ppermute(line, 'zh', [(i, i ^ k) for i in range(pairs)])  7.38 us
    all_to_all x1, waiting for transfers between devices, local(): half = lax.all_to_all(spread, GROUP, 0, 0)  6.59 us
    ppermute x3, waiting for transfers between devices, local(): lax.ppermute(line, 'zh', [(i, i ^ k) for i in range(pairs)])  5.78 us
    pallas_call x1, Pallas kernels, second_grad(): pl.pallas_call(second_grad_kernel, in_specs=[SM, HBM, VM, HBM], out_specs...  5.4 us
    ppermute x1, starting transfers between devices, local(): other_half = lax.ppermute(half, 'c', swap)  4.86 us
    all_to_all x1, starting transfers between devices, local(): half = lax.all_to_all(spread, GROUP, 0, 0)  4.28 us
  transfers between devices with their start and end apart: 13, of which 8 were waited for; matrix products, arithmetic and copies ran while one was open for 0% of the time, Pallas kernels for 11%

profile of v7, /device:TPU:1, one launch (start us, length us, event | category | flops | bytes accessed | tf_op | source)
XLA Modules:
  0.0 85.4 jit_solution(16675856180876017273)
XLA Ops:
  0.6 2.5 %shard_map.58 = (bf16[512,256]{1,0:T(8,128)(2,1)S(1)}, bf16[2,256,512]{2,1,0:T(8,128)(2,1)S(1)}, bf16[2,512,512]{2,1,0:T(8,128)(2,1)S(1)}, bf16[4,64,256]{2,1,0:T(8,128)(2,1)S(1)}) custom-call(s32[1]{0:T(128)} %bitcast.at_ref.refs_0_, bf16[4,8,64,256]{3,2,1,0:T(8,128)(2,1)} %m_hbm.3, bf16[2,256,512]{2,1,0:T(8,128)(2,1)} %c_hbm.1, ...), custom_call_target="tpu_custom_call" | custom-call | flops 536870912 | bytes 2097152 | tf_op jit(solution)/shard_map/pallas_call | solution.py:139
  3.2 2.1 %collective-permute-start = (bf16[512,256]{1,0:T(8,128)(2,1)S(1)}, bf16[512,256]{1,0:T(8,128)(2,1)S(1)}, u32[]{:S(2)}, u32[]{:S(2)}) collective-permute-start(bf16[512,256]{1,0:T(8,128)(2,1)S(1)} %get-tuple-element.44.refs_2_), channel_id=1, source_target_pairs={{0,128},{128,0},{1,129},{129,1},{2,130},{130,2},{3,131},{131,3},{4... | collective-permute-start | bytes 786440 | tf_op jit(solution)/shard_map/ppermute | solution.py:379
  5.3 4.0 %collective-permute-start.4 = (bf16[4,64,256]{2,1,0:T(8,128)(2,1)S(1)}, bf16[4,64,256]{2,1,0:T(8,128)(2,1)S(1)}, u32[]{:S(2)}, u32[]{:S(2)}) collective-permute-start(bf16[4,64,256]{2,1,0:T(8,128)(2,1)S(1)} %get-tuple-element.53), channel_id=1, source_target_pairs={{8,16},{16,8},{24,32},{32,24},{40,48},{48,40},{56,64},{64,56},{72,... | collective-permute-start | bytes 393224 | tf_op jit(solution)/shard_map/ppermute | solution.py:380
  9.3 5.4 %shard_map.59 = (bf16[1024,256]{1,0:T(8,128)(2,1)S(1)}, bf16[512,256]{1,0:T(8,128)(2,1)S(1)}, bf16[4,8,64,256]{3,2,1,0:T(8,128)(2,1)S(1)}, bf16[2,3,512,512]{3,2...) custom-call(s32[1]{0:T(128)} %bitcast.at_ref.refs_0_, ...), custom_call_target="tpu_custom_call" | custom-call | flops 1610612736 | bytes 5242880 | tf_op jit(solution)/shard_map/pallas_call | solution.py:164
  14.8 0.0 collective-permute-done.4.xb_ref
  14.8 0.3 collective-permute-start.6
  15.1 0.0 collective-permute-done.refs_3_
  15.1 0.0 collective-permute-start.1
  15.1 1.6 %collective-permute-start.2 = (bf16[32,256]{1,0:T(8,128)(2,1)S(1)}, bf16[32,256]{1,0:T(8,128)(2,1)S(1)}, u32[]{:S(2)}, u32[]{:S(2)}) collective-permute-start(bf16[32,256]{1,0:T(8,128)(2,1)S(1)} %get-tuple-element.49), channel_id=1, source_target_pairs={{0,1},{1,0},{2,3},{3,2},{4,5},{5,4},{6,7},{7,6},{8,9},{9,8},{10,11... | collective-permute-start | bytes 49160 | tf_op jit(solution)/shard_map/ppermute | solution.py:390
  16.8 0.7 collective-permute-start.3
  17.4 0.8 collective-permute-done.2.za_ref
  18.2 0.0 collective-permute-done.3.zb_ref
  18.2 0.0 collective-permute-done.1.xa_ref
  18.2 1.2 %collective-permute-start.5 = (bf16[512,256]{1,0:T(8,128)(2,1)S(1)}, bf16[512,256]{1,0:T(8,128)(2,1)S(1)}, u32[]{:S(2)}, u32[]{:S(2)}) collective-permute-start(bf16[512,256]{1,0:T(8,128)(2,1)S(1)} %get-tuple-element.57.refs_2_), channel_id=1, source_target_pairs={{0,128},{128,0},{1,129},{129,1},{2,130},{130,2},{3,131},{131,3},{4... | collective-permute-start | bytes 786440 | tf_op jit(solution)/shard_map/ppermute | solution.py:393
  19.4 0.9 %shard_map.60.refs_1_ = f32[4,512,256]{2,1,0:T(8,128)S(1)} custom-call(s32[1]{0:T(128)} %bitcast.at_ref.refs_0_, bf16[4,8,64,256]{3,2,1,0:T(8,128)(2,1)S(1)} %get-tuple-element.42.m_ref, bf16[4,64,256]{2,1,0:T(8,128)(2,1)S(1)} %collective-permute-done.1.xa_ref, bf16[4,64,256]{2,1,0:T(8,128)(2,1)S(1)} %collective-permute-done.4.xb_ref, ...), custom_call_target="tpu_custom_call" | custom-call | flops 6291456 | bytes 3145728 | tf_op jit(solution)/shard_map/pallas_call | solution.py:394
  20.3 0.6 shard_map.61
  21.0 7.9 %collective-permute-done.6.refs_3_ = bf16[1024,256]{1,0:T(8,128)(2,1)S(1)} collective-permute-done((bf16[1024,256]{1,0:T(8,128)(2,1)S(1)}, bf16[1024,256]{1,0:T(8,128)(2,1)S(1)}, u32[]{:S(2)}, u32[]{:S(2)}) %collective-permute-start.6) | collective-permute-done | bytes 524320 | tf_op jit(solution)/shard_map/ppermute | solution.py:386
  28.9 1.3 %shard_map.62 = (bf16[1024,256]{1,0:T(8,128)(2,1)S(1)}, f32[2,256,512]{2,1,0:T(8,128)S(1)}, f32[256,256]{1,0:T(8,128)S(1)}, f32[1,256]{1,0:T(1,128)S(1)}) custom-call(s32[1]{0:T(128)} %bitcast.at_ref.refs_0_, f32[4,512,256]{2,1,0:T(8,128)S(1)} %shard_map.60.refs_1_, ...), custom_call_target="tpu_custom_call", output_to_operand_aliasing={{1}: (5, {}), {2}: (6, {}), {3}: (7, {})} | custom-call | flops 671088640 | bytes 4194304 | tf_op jit(solution)/shard_map/pallas_call | solution.py:271
  30.2 2.3 %collective-permute-done.5.refs_3_ = bf16[512,256]{1,0:T(8,128)(2,1)S(1)} collective-permute-done((bf16[512,256]{1,0:T(8,128)(2,1)S(1)}, bf16[512,256]{1,0:T(8,128)(2,1)S(1)}, u32[]{:S(2)}, u32[]{:S(2)}) %collective-permute-start.5) | collective-permute-done | bytes 262176 | tf_op jit(solution)/shard_map/ppermute | solution.py:393
  32.4 0.9 %shard_map.63 = (bf16[512,256]{1,0:T(8,128)(2,1)S(1)}, bf16[16,88,128]{2,1,0:T(8,128)(2,1)S(1)}, bf16[16,88,128]{2,1,0:T(8,128)(2,1)S(1)}) custom-call(s32[1]{0:T(128)} %bitcast.at_ref.refs_0_, f32[4,512,256]{2,1,0:T(8,128)S(1)} %shard_map.60.refs_1_, bf16[512,256]{1,0:T(8,128)(2,1)S(1)} %get-tuple-element.57.refs_2_, ...), custom_call_target="tpu_custom_call" | custom-call | flops 335544320 | bytes 2097152 | tf_op jit(solution)/shard_map/pallas_call | solution.py:271
  33.3 0.1 collective-permute-start.7
  33.4 1.7 %collective-permute-done.7.got_ref = bf16[16,88,128]{2,1,0:T(8,128)(2,1)S(1)} collective-permute-done((bf16[16,88,128]{2,1,0:T(8,128)(2,1)S(1)}, bf16[16,88,128]{2,1,0:T(8,128)(2,1)S(1)}, u32[]{:S(2)}, u32[]{:S(2)}) %collective-permute-start.7) | collective-permute-done | bytes 360480 | tf_op jit(solution)/shard_map/ppermute | solution.py:411
  35.1 0.1 shard_map.64
  35.2 16.8 %all_to_all.10.in_ref = bf16[16,88,128]{2,1,0:T(8,128)(2,1)S(1)} all-to-all(bf16[16,88,128]{2,1,0:T(8,128)(2,1)S(1)} %shard_map.64), channel_id=1, replica_groups=mesh['ens'=2,'xh'=2,'y'=4,'c'=2,'zh'=4,'zl'=2] {'xh','y','zl'}, dimensions={0} | all-to-all | bytes 720896 | tf_op jit(solution)/shard_map/all_to_all | solution.py:415
  51.9 0.1 shard_map.65.refs_0_
  52.0 5.2 %collective-permute-start.10 = (bf16[88,128]{1,0:T(8,128)(2,1)S(1)}, bf16[88,128]{1,0:T(8,128)(2,1)S(1)}, u32[]{:S(2)}, u32[]{:S(2)}) collective-permute-start(bf16[88,128]{1,0:T(8,128)(2,1)S(1)} %shard_map.65.refs_0_), channel_id=1, source_target_pairs={{0,6},{2,4},{4,2},{6,0},{1,7},{3,5},{5,3},{7,1},{8,14},{10,12},{12... | collective-permute-start | bytes 67592 | tf_op jit(solution)/shard_map/ppermute | solution.py:421
  57.2 1.2 %collective-permute-start.8 = (bf16[88,128]{1,0:T(8,128)(2,1)S(1)}, bf16[88,128]{1,0:T(8,128)(2,1)S(1)}, u32[]{:S(2)}, u32[]{:S(2)}) collective-permute-start(bf16[88,128]{1,0:T(8,128)(2,1)S(1)} %shard_map.65.refs_0_), channel_id=1, source_target_pairs={{0,2},{2,0},{4,6},{6,4},{1,3},{3,1},{5,7},{7,5},{8,10},{10,8},{12,... | collective-permute-start | bytes 67592 | tf_op jit(solution)/shard_map/ppermute | solution.py:421
  58.3 1.0 %collective-permute-start.9 = (bf16[88,128]{1,0:T(8,128)(2,1)S(1)}, bf16[88,128]{1,0:T(8,128)(2,1)S(1)}, u32[]{:S(2)}, u32[]{:S(2)}) collective-permute-start(bf16[88,128]{1,0:T(8,128)(2,1)S(1)} %shard_map.65.refs_0_), channel_id=1, source_target_pairs={{0,4},{2,6},{4,0},{6,2},{1,5},{3,7},{5,1},{7,3},{8,12},{10,14},{12... | collective-permute-start | bytes 67592 | tf_op jit(solution)/shard_map/ppermute | solution.py:421
  59.3 0.0 collective-permute-done.10.refs_3_
  59.4 1.7 %collective-permute-done.8.refs_1_ = bf16[88,128]{1,0:T(8,128)(2,1)S(1)} collective-permute-done((bf16[88,128]{1,0:T(8,128)(2,1)S(1)}, bf16[88,128]{1,0:T(8,128)(2,1)S(1)}, u32[]{:S(2)}, u32[]{:S(2)}) %collective-permute-start.8) | collective-permute-done | bytes 22560 | tf_op jit(solution)/shard_map/ppermute | solution.py:421
  61.0 4.1 %collective-permute-done.9.refs_2_ = bf16[88,128]{1,0:T(8,128)(2,1)S(1)} collective-permute-done((bf16[88,128]{1,0:T(8,128)(2,1)S(1)}, bf16[88,128]{1,0:T(8,128)(2,1)S(1)}, u32[]{:S(2)}, u32[]{:S(2)}) %collective-permute-start.9) | collective-permute-done | bytes 22560 | tf_op jit(solution)/shard_map/ppermute | solution.py:421
  65.1 0.9 %shard_map.66 = (bf16[16,80,128]{2,1,0:T(8,128)(2,1)}, f32[2,128]{1,0:T(2,128)S(1)}) custom-call(s32[1]{0:T(128)} %bitcast.at_ref.refs_0_, bf16[88,128]{1,0:T(8,128)(2,1)S(1)} %shard_map.65.refs_0_, bf16[88,128]{1,0:T(8,128)(2,1)S(1)} %collective-permute-done.8.refs_1_, bf16[88,128]{1,0:T(8,128)(2,1)S(1)} %collective-permute-done.9.refs_2_, ...), custom_call_target="tpu_custom_call" | custom-call | tf_op jit(solution)/shard_map/pallas_call | solution.py:422
  66.0 4.3 %all-to-all-start.1 = ((bf16[16,80,128]{2,1,0:T(8,128)(2,1)}), bf16[16,80,128]{2,1,0:T(8,128)(2,1)S(1)}, u32[]{:S(2)}, u32[]{:S(2)}) async-start(bf16[16,80,128]{2,1,0:T(8,128)(2,1)} %get-tuple-element.70), calls=%async_computation.1 | async-start | bytes 655360 | tf_op jit(solution)/shard_map/all_to_all | solution.py:433
  70.3 1.2 %shard_map.67 = bf16[2048,256]{1,0:T(8,128)(2,1)} custom-call(f32[2,128]{1,0:T(2,128)S(1)} %get-tuple-element.71.shrink_ref, bf16[512,256]{1,0:T(8,128)(2,1)S(1)} %get-tuple-element.72.refs_0_, bf16[1024,256]{1,0:T(8,128)(2,1)S(1)} %get-tuple-element.73.refs_1_, bf16[512,256]{1,0:T(8,128)(2,1)S(1)} %get-tuple-element.74.refs_2_), custom_call_target="tpu_custom_call" | custom-call | tf_op jit(solution)/shard_map/pallas_call | solution.py:434
  71.5 6.6 %all-to-all-done.1.own_ref = bf16[16,80,128]{2,1,0:T(8,128)(2,1)S(1)} async-done(((bf16[16,80,128]{2,1,0:T(8,128)(2,1)}), bf16[16,80,128]{2,1,0:T(8,128)(2,1)S(1)}, u32[]{:S(2)}, u32[]{:S(2)}) %all-to-all-start.1) | async-done | bytes 327712 | tf_op jit(solution)/shard_map/all_to_all | solution.py:433
  78.1 4.9 %collective-permute-start.11 = (bf16[16,80,128]{2,1,0:T(8,128)(2,1)S(1)}, bf16[16,80,128]{2,1,0:T(8,128)(2,1)S(1)}, u32[]{:S(2)}, u32[]{:S(2)}) collective-permute-start(bf16[16,80,128]{2,1,0:T(8,128)(2,1)S(1)} %all-to-all-done.1.own_ref), channel_id=1, source_target_pairs={{0,8},{8,0},{1,9},{9,1},{2,10},{10,2},{3,11},{11,3},{4,12},{12,4},... | collective-permute-start | bytes 983048 | tf_op jit(solution)/shard_map/ppermute | solution.py:442
  82.9 1.3 %collective-permute-done.11.got_ref = bf16[16,80,128]{2,1,0:T(8,128)(2,1)S(1)} collective-permute-done((bf16[16,80,128]{2,1,0:T(8,128)(2,1)S(1)}, bf16[16,80,128]{2,1,0:T(8,128)(2,1)S(1)}, u32[]{:S(2)}, u32[]{:S(2)}) %collective-permute-start.11) | collective-permute-done | bytes 327712 | tf_op jit(solution)/shard_map/ppermute | solution.py:442
  84.2 1.2 %shard_map.68 = (f32[2,256,512]{2,1,0:T(8,128)}, f32[256,256]{1,0:T(8,128)}) custom-call(s32[1]{0:T(128)} %bitcast.at_ref.refs_0_, bf16[16,80,128]{2,1,0:T(8,128)(2,1)S(1)} %all-to-all-done.1.own_ref, bf16[16,80,128]{2,1,0:T(8,128)(2,1)S(1)} %collective-permute-done.11.got_ref), custom_call_target="tpu_custom_call" | custom-call | tf_op jit(solution)/shard_map/pallas_call | solution.py:443
Async XLA Ops:
  3.2 11.9 %collective-permute-start = (bf16[512,256]{1,0:T(8,128)(2,1)S(1)}, bf16[512,256]{1,0:T(8,128)(2,1)S(1)}, u32[]{:S(2)}, u32[]{:S(2)}) collective-permute-start(bf16[512,256]{1,0:T(8,128)(2,1)S(1)} %get-tuple-element.44.refs_2_), channel_id=1, source_target_pairs={{0,128},{128,0},{1,129},{129,1},{2,130},{130,2},{3,131},{131,3},{4... | collective-permute-start | bytes 786440 | tf_op jit(solution)/shard_map/ppermute | solution.py:379
  5.3 9.5 %collective-permute-start.4 = (bf16[4,64,256]{2,1,0:T(8,128)(2,1)S(1)}, bf16[4,64,256]{2,1,0:T(8,128)(2,1)S(1)}, u32[]{:S(2)}, u32[]{:S(2)}) collective-permute-start(bf16[4,64,256]{2,1,0:T(8,128)(2,1)S(1)} %get-tuple-element.53), channel_id=1, source_target_pairs={{8,16},{16,8},{24,32},{32,24},{40,48},{48,40},{56,64},{64,56},{72,... | collective-permute-start | bytes 393224 | tf_op jit(solution)/shard_map/ppermute | solution.py:380
  14.8 14.1 %collective-permute-start.6 = (bf16[1024,256]{1,0:T(8,128)(2,1)S(1)}, bf16[1024,256]{1,0:T(8,128)(2,1)S(1)}, u32[]{:S(2)}, u32[]{:S(2)}) collective-permute-start(bf16[1024,256]{1,0:T(8,128)(2,1)S(1)} %get-tuple-element.59.refs_2_), channel_id=1, source_target_pairs={{0,128},{128,0},{1,129},{129,1},{2,130},{130,2},{3,131},{131,3},{4... | collective-permute-start | bytes 1572872 | tf_op jit(solution)/shard_map/ppermute | solution.py:386
  15.1 3.1 %collective-permute-start.1 = (bf16[4,64,256]{2,1,0:T(8,128)(2,1)S(1)}, bf16[4,64,256]{2,1,0:T(8,128)(2,1)S(1)}, u32[]{:S(2)}, u32[]{:S(2)}) collective-permute-start(bf16[4,64,256]{2,1,0:T(8,128)(2,1)S(1)} %get-tuple-element.48), channel_id=1, source_target_pairs={{0,8},{8,0},{1,9},{9,1},{2,10},{10,2},{3,11},{11,3},{4,12},{12,4},... | collective-permute-start | bytes 393224 | tf_op jit(solution)/shard_map/ppermute | solution.py:389
  15.1 3.1 %collective-permute-start.2 = (bf16[32,256]{1,0:T(8,128)(2,1)S(1)}, bf16[32,256]{1,0:T(8,128)(2,1)S(1)}, u32[]{:S(2)}, u32[]{:S(2)}) collective-permute-start(bf16[32,256]{1,0:T(8,128)(2,1)S(1)} %get-tuple-element.49), channel_id=1, source_target_pairs={{0,1},{1,0},{2,3},{3,2},{4,5},{5,4},{6,7},{7,6},{8,9},{9,8},{10,11... | collective-permute-start | bytes 49160 | tf_op jit(solution)/shard_map/ppermute | solution.py:390
  16.8 1.4 %collective-permute-start.3 = (bf16[32,256]{1,0:T(8,128)(2,1)S(1)}, bf16[32,256]{1,0:T(8,128)(2,1)S(1)}, u32[]{:S(2)}, u32[]{:S(2)}) collective-permute-start(bf16[32,256]{1,0:T(8,128)(2,1)S(1)} %get-tuple-element.50), channel_id=1, source_target_pairs={{1,2},{2,1},{3,4},{4,3},{5,6},{6,5},{9,10},{10,9},{11,12},{12,11},... | collective-permute-start | bytes 49160 | tf_op jit(solution)/shard_map/ppermute | solution.py:391
  18.2 14.2 %collective-permute-start.5 = (bf16[512,256]{1,0:T(8,128)(2,1)S(1)}, bf16[512,256]{1,0:T(8,128)(2,1)S(1)}, u32[]{:S(2)}, u32[]{:S(2)}) collective-permute-start(bf16[512,256]{1,0:T(8,128)(2,1)S(1)} %get-tuple-element.57.refs_2_), channel_id=1, source_target_pairs={{0,128},{128,0},{1,129},{129,1},{2,130},{130,2},{3,131},{131,3},{4... | collective-permute-start | bytes 786440 | tf_op jit(solution)/shard_map/ppermute | solution.py:393
  33.3 1.8 %collective-permute-start.7 = (bf16[16,88,128]{2,1,0:T(8,128)(2,1)S(1)}, bf16[16,88,128]{2,1,0:T(8,128)(2,1)S(1)}, u32[]{:S(2)}, u32[]{:S(2)}) collective-permute-start(bf16[16,88,128]{2,1,0:T(8,128)(2,1)S(1)} %get-tuple-element.69), channel_id=1, source_target_pairs={{0,8},{8,0},{1,9},{9,1},{2,10},{10,2},{3,11},{11,3},{4,12},{12,4},... | collective-permute-start | bytes 1081352 | tf_op jit(solution)/shard_map/ppermute | solution.py:411
  52.0 7.4 %collective-permute-start.10 = (bf16[88,128]{1,0:T(8,128)(2,1)S(1)}, bf16[88,128]{1,0:T(8,128)(2,1)S(1)}, u32[]{:S(2)}, u32[]{:S(2)}) collective-permute-start(bf16[88,128]{1,0:T(8,128)(2,1)S(1)} %shard_map.65.refs_0_), channel_id=1, source_target_pairs={{0,6},{2,4},{4,2},{6,0},{1,7},{3,5},{5,3},{7,1},{8,14},{10,12},{12... | collective-permute-start | bytes 67592 | tf_op jit(solution)/shard_map/ppermute | solution.py:421
  57.2 3.8 %collective-permute-start.8 = (bf16[88,128]{1,0:T(8,128)(2,1)S(1)}, bf16[88,128]{1,0:T(8,128)(2,1)S(1)}, u32[]{:S(2)}, u32[]{:S(2)}) collective-permute-start(bf16[88,128]{1,0:T(8,128)(2,1)S(1)} %shard_map.65.refs_0_), channel_id=1, source_target_pairs={{0,2},{2,0},{4,6},{6,4},{1,3},{3,1},{5,7},{7,5},{8,10},{10,8},{12,... | collective-permute-start | bytes 67592 | tf_op jit(solution)/shard_map/ppermute | solution.py:421
  58.3 6.8 %collective-permute-start.9 = (bf16[88,128]{1,0:T(8,128)(2,1)S(1)}, bf16[88,128]{1,0:T(8,128)(2,1)S(1)}, u32[]{:S(2)}, u32[]{:S(2)}) collective-permute-start(bf16[88,128]{1,0:T(8,128)(2,1)S(1)} %shard_map.65.refs_0_), channel_id=1, source_target_pairs={{0,4},{2,6},{4,0},{6,2},{1,5},{3,7},{5,1},{7,3},{8,12},{10,14},{12... | collective-permute-start | bytes 67592 | tf_op jit(solution)/shard_map/ppermute | solution.py:421
  66.0 12.1 %all-to-all-start.1 = ((bf16[16,80,128]{2,1,0:T(8,128)(2,1)}), bf16[16,80,128]{2,1,0:T(8,128)(2,1)S(1)}, u32[]{:S(2)}, u32[]{:S(2)}) async-start(bf16[16,80,128]{2,1,0:T(8,128)(2,1)} %get-tuple-element.70), calls=%async_computation.1 | async-start | bytes 655360 | tf_op jit(solution)/shard_map/all_to_all | solution.py:433
  78.1 6.1 %collective-permute-start.11 = (bf16[16,80,128]{2,1,0:T(8,128)(2,1)S(1)}, bf16[16,80,128]{2,1,0:T(8,128)(2,1)S(1)}, u32[]{:S(2)}, u32[]{:S(2)}) collective-permute-start(bf16[16,80,128]{2,1,0:T(8,128)(2,1)S(1)} %all-to-all-done.1.own_ref), channel_id=1, source_target_pairs={{0,8},{8,0},{1,9},{9,1},{2,10},{10,2},{3,11},{11,3},{4,12},{12,4},... | collective-permute-start | bytes 983048 | tf_op jit(solution)/shard_map/ppermute | solution.py:442

commit v8 on v7

--- a/solution.py
+++ b/solution.py
@@ -87,14 +87,28 @@
     copies[-1].wait()
 
 
-def second_grad_kernel(at_ref, m_hbm, c_ref, x_hbm, *refs):
+def second_grad_kernel(level, m_hbm, c_ref, x_hbm, g_ref, x_ref, m_ref, sems):
+    members = c_ref.shape[0]
+    copies = [(m_hbm.at[level], m_ref)]
+    for e in range(members):
+        copies.append((x_hbm.at[e, level], x_ref.at[e]))
+    copies = start_all(copies, sems)
+    copies[0].wait()
+    g_ref[...] = gradient(
+        m_ref[...].reshape(g_ref.shape),
+        [functools.partial(c_ref.__getitem__, e) for e in range(members)],
+        [after(copies[1 + e], x_ref, e) for e in range(members)],
+    )
+
+
+def rest_grad_kernel(begin, at_ref, m_hbm, c_ref, x_hbm, *refs):
     *g_refs, m_ref, x_ref, xa_ref, za_ref, zb_ref, tmp_ref, sems = refs
     members, levels, cells, _ = x_hbm.shape
     _, rows_x, rows_y, width = m_ref.shape
     copies = [(m_hbm, m_ref)]
-    for level in range(1, levels):
+    for level in range(begin, levels):
         for e in range(members):
-            copies.append((x_hbm.at[e, level], x_ref.at[e, level - 1]))
+            copies.append((x_hbm.at[e, level], x_ref.at[e, level - begin]))
     copies = start_all(copies, sems)
     copies[0].wait()
     core, even = core_of(at_ref[0]), parity_of(at_ref[0]) == 0
@@ -104,15 +118,12 @@
     lo, hi = tmp_ref[0, :, 0, :], tmp_ref[1, :, 7, :]
     za_ref[...] = jnp.where(even, hi, lo).astype(BF16)
     zb_ref[...] = jnp.where(even, lo, hi).astype(BF16)
-    at = 0
-    for g_ref in g_refs:
-        for first in range(0, g_ref.shape[0], cells):
-            g_ref[first : first + cells, :] = gradient(
-                m_ref[1 + at].reshape(cells, width),
-                [functools.partial(c_ref.__getitem__, e) for e in range(members)],
-                [after(copies[1 + at * members + e], x_ref, e, at) for e in range(members)],
-            )
-            at += 1
+    for i, g_ref in enumerate(g_refs):
+        g_ref[...] = gradient(
+            m_ref[begin + i].reshape(g_ref.shape),
+            [functools.partial(c_ref.__getitem__, e) for e in range(members)],
+            [after(copies[1 + i * members + e], x_ref, e, i) for e in range(members)],
+        )
 
 
 def grad_cost(members, cells, frames, width):
@@ -150,28 +161,47 @@
     )(place, in_hbm(modes), in_hbm(coefficients), in_hbm(series))
 
 
-def second_grad(place, modes, coefficients, series, counts):
+def second_grad(modes, coefficients, series, level):
+    members, _, cells, frames = series.shape
+    _, rows_x, rows_y, width = modes.shape
+    outs = [jax.ShapeDtypeStruct((cells, width), BF16), pltpu.VMEM((members, cells, frames), BF16)]
+    return pl.pallas_call(
+        functools.partial(second_grad_kernel, level),
+        in_specs=[HBM, VM, HBM],
+        out_specs=[VM] * len(outs),
+        out_shape=outs,
+        scratch_shapes=[
+            pltpu.VMEM((rows_x, rows_y, width), BF16),
+            pltpu.SemaphoreType.DMA((1 + members,)),
+        ],
+        compiler_params=PARAMS,
+        cost_estimate=grad_cost(members, cells, frames, width),
+    )(in_hbm(modes), coefficients, in_hbm(series))
+
+
+def rest_grad(place, modes, coefficients, series, begin):
     members, levels, cells, frames = series.shape
     _, rows_x, rows_y, width = modes.shape
-    outs = [jax.ShapeDtypeStruct((count * cells, width), BF16) for count in counts]
+    count = levels - begin
+    outs = [jax.ShapeDtypeStruct((cells, width), BF16)] * count
     outs += [
         pltpu.VMEM(modes.shape, BF16),
-        pltpu.VMEM((members, levels - 1, cells, frames), BF16),
+        pltpu.VMEM((members, count, cells, frames), BF16),
         jax.ShapeDtypeStruct((levels, rows_y, width), BF16),
         jax.ShapeDtypeStruct((levels * rows_x, width), BF16),
         jax.ShapeDtypeStruct((levels * rows_x, width), BF16),
     ]
     return pl.pallas_call(
-        second_grad_kernel,
+        functools.partial(rest_grad_kernel, begin),
         in_specs=[SM, HBM, VM, HBM],
         out_specs=[VM] * len(outs),
         out_shape=outs,
         scratch_shapes=[
             pltpu.VMEM((2, levels * rows_x, 8, width), F32),
-            pltpu.SemaphoreType.DMA((1 + members * (levels - 1),)),
+            pltpu.SemaphoreType.DMA((1 + members * count,)),
         ],
         compiler_params=PARAMS,
-        cost_estimate=grad_cost(members, sum(counts) * cells, frames, width),
+        cost_estimate=grad_cost(members, count * cells, frames, width),
     )(place, in_hbm(modes), coefficients, in_hbm(series))
 
 
@@ -213,7 +243,7 @@
         out_ref[j, SUM_ROWS:PART_ROWS, :] = squares
 
 
-def step_kernel(level, count, first, last, *refs):
+def step_kernel(level, x_at, first, last, *refs):
     (at_ref, base_ref, own_ref, got_ref, x_ref), refs = refs[:5], refs[5:]
     if not first:
         (proj_in, gram_in, squares_in), refs = refs[:3], refs[3:]
@@ -222,8 +252,7 @@
     else:
         moved_ref, proj_ref, gram_ref, squares_ref = refs
     grad = own_ref[...].astype(F32) + got_ref[...].astype(F32)
-    levels = slice(level, level + count)
-    moved = (base_ref[levels].reshape(grad.shape) - ETA * grad).astype(BF16)
+    moved = (base_ref[level] - ETA * grad).astype(BF16)
     moved_ref[...] = moved
     wide = moved.astype(F32)
     squares = jnp.sum(wide * wide, axis=0, keepdims=True)
@@ -233,8 +262,7 @@
     gram = jnp.dot(turned, moved, preferred_element_type=F32)
     gram_ref[...] = gram if first else gram_in[...] + gram
     for e in range(x_ref.shape[0]):
-        x = x_ref[e] if level == 0 else x_ref[e, level - 1 : level - 1 + count]
-        x = x.reshape(grad.shape[0], -1)
+        x = x_ref[e] if x_at is None else x_ref[e, x_at]
         proj = jnp.dot(turned, x, preferred_element_type=F32)
         proj_ref[e] = proj if first else proj_in[e] + proj
     if last:
@@ -247,10 +275,10 @@
         squares_ref[...] = squares
 
 
-def step_levels(level, count, place, base, own, got, series, carry):
+def step_level(level, x_at, place, base, own, got, series, carry):
     members, frames = series.shape[0], series.shape[-1]
     rows, width = own.shape
-    first, last = carry is None, level + count == base.shape[0]
+    first, last = carry is None, level == base.shape[0] - 1
     args = [place, base, own, got, series]
     if not first:
         args += list(carry)
@@ -269,7 +297,7 @@
         if not first:
             aliases = {5 + i: 1 + i for i in range(3)}
     return pl.pallas_call(
-        functools.partial(step_kernel, level, count, first, last),
+        functools.partial(step_kernel, level, x_at, first, last),
         in_specs=[SM] + [VM] * (len(args) - 1),
         out_specs=[VM] * len(outs),
         out_shape=outs,
@@ -310,11 +338,15 @@
     out_ref[SUM_ROWS:PART_ROWS, :] = packed_squares(total)
 
 
-def reduce_kernel(total_cells, at_ref, *refs):
-    *in_refs, out_ref, shrink_ref, column_ref = refs
+def add_kernel(own_ref, got_ref, out_ref):
+    total = own_ref[...].astype(F32) + got_ref[...].astype(F32)
+    out_ref[0:SUM_ROWS, :] = total[0:SUM_ROWS, :].astype(BF16)
+    out_ref[SUM_ROWS:PART_ROWS, :] = packed_squares(total)
+
+
+def reduce_kernel(total_cells, at_ref, own_ref, got_ref, out_ref, shrink_ref, column_ref):
     core, part = core_of(at_ref[0]), part_of(at_ref[0])
-    a, b, c, d = (ref[...].astype(F32) for ref in in_refs)
-    total = (a + b) + (c + d)
+    total = own_ref[...].astype(F32) + got_ref[...].astype(F32)
     squares = whole_squares(total)
     shrink = jnp.maximum(0.0, 1.0 - TAU / jnp.sqrt(squares / total_cells + 1e-06))
     shrink_ref[...] = shrink
@@ -374,23 +406,21 @@
     series = snapshots.reshape(members, levels, cells, frames)
     swap = [(0, 1), (1, 0)]
 
-    chunks = [(0, 1), (1, 2), (3, 1)]
-    g, coefficients, head, edge_b = first_grad(place, modes, coefficients, series)
-    own, got = [g], [lax.ppermute(g, "ens", swap)]
+    g0, coefficients, x0, edge_b = first_grad(place, modes, coefficients, series)
+    got0 = lax.ppermute(g0, "ens", swap)
     xb = lax.ppermute(edge_b, SX, both_ways([(i, i + 1) for i in range(1, n_sx - 1, 2)]))
-    counts = [count for _, count in chunks[1:]]
-    mid, tail, modes, series, edge_a, row_a, row_b = second_grad(
-        place, modes, coefficients, series, counts
-    )
-    mid, xb = lax.optimization_barrier((mid, xb))
-    got.append(lax.ppermute(mid, "ens", swap))
-    got[0], edge_a, row_a, row_b = lax.optimization_barrier((got[0], edge_a, row_a, row_b))
-    own += [mid, tail]
+    g1, x1 = second_grad(modes, coefficients, series, 1)
+    g1, xb = lax.optimization_barrier((g1, xb))
+    got1 = lax.ppermute(g1, "ens", swap)
+    coefficients, _ = lax.optimization_barrier((coefficients, g1))
+    g2, g3, modes, series, edge_a, row_a, row_b = rest_grad(place, modes, coefficients, series, 2)
+    got2 = lax.ppermute(g2, "ens", swap)
+    got0, g3 = lax.optimization_barrier((got0, g3))
+    got3 = lax.ppermute(g3, "ens", swap)
+    got1, edge_a, row_a, row_b = lax.optimization_barrier((got1, edge_a, row_a, row_b))
     xa = lax.ppermute(edge_a, "c", swap)
     za = lax.ppermute(row_a, SY, both_ways([(i, i + 1) for i in range(0, n_z, 2)]))
     zb = lax.ppermute(row_b, SY, both_ways([(i, i + 1) for i in range(1, n_z - 1, 2)]))
-    tail, xa, za, zb = lax.optimization_barrier((tail, xa, za, zb))
-    got.append(lax.ppermute(tail, "ens", swap))
     base = pl.pallas_call(
         base_kernel,
         in_specs=[SM] + [VM] * 5,
@@ -401,9 +431,9 @@
     )(place, modes, xa, xb, za, zb)
 
     moved, carry = [], None
-    for i, (level, count) in enumerate(chunks):
-        x = head if level == 0 else series
-        m, *carry = step_levels(level, count, place, base, own[i], got[i], x, carry)
+    work = [(None, g0, got0, x0), (None, g1, got1, x1), (0, g2, got2, series), (1, g3, got3, series)]
+    for level, (x_at, own, got, x) in enumerate(work):
+        m, *carry = step_level(level, x_at, place, base, own, got, x, carry)
         moved.append(m)
     keep, send = carry
 
@@ -418,10 +448,14 @@
         group_kernel, in_specs=[VM], out_specs=VM, out_shape=line_shape, compiler_params=PARAMS
     )(parts)
     pairs = lax.axis_size("zh")
-    others = [lax.ppermute(line, "zh", [(i, i ^ k) for i in range(pairs)]) for k in (1, 2, 3)]
+    near = lax.ppermute(line, "zh", [(i, i ^ 1) for i in range(pairs)])
+    line = pl.pallas_call(
+        add_kernel, in_specs=[VM, VM], out_specs=VM, out_shape=line_shape, compiler_params=PARAMS
+    )(line, near)
+    near = lax.ppermute(line, "zh", [(i, i ^ 3) for i in range(pairs)])
     spread, shrink = pl.pallas_call(
         functools.partial(reduce_kernel, total_cells),
-        in_specs=[SM] + [VM] * 4,
+        in_specs=[SM, VM, VM],
         out_specs=[VM, VM],
         out_shape=[
             jax.ShapeDtypeStruct((PARTS, SUM_ROWS, 128), BF16),
@@ -429,7 +463,7 @@
         ],
         scratch_shapes=[pltpu.VMEM((width, 128), F32)],
         compiler_params=PARAMS,
-    )(place, line, *others)
+    )(place, line, near)
     half = lax.all_to_all(spread, GROUP, 0, 0)
     new_modes = pl.pallas_call(
         scale_kernel,

time: 85.7 us -> 84 us (0.980)
  waiting for transfers between devices: 26.2 us -> 22 us
  Pallas kernels: 15.1 us -> 16.5 us
  blocking collectives: 16.8 us -> 18.1 us
    ppermute x6, waiting for transfers between devices: 15.9 us -> 11.9 us  [the longest x1 4.33 us: local(): got3 = lax.ppermute(g3, 'ens', swap)]
    pallas_call x4 -> x7, Pallas kernels: 8.21 us -> 9.66 us  [the longest x1 4.11 us: rest_grad(): pl.pallas_call(functools.partial(rest_grad_kernel, begin), in_specs=[SM,...]
    ppermute x6, starting transfers between devices: 11 us -> 9.69 us  [the longest x1 3.39 us: local(): near = lax.ppermute(line, 'zh', [(i, i ^ 1) for i in range(pairs)])]
    all_to_all x1, blocking collectives: 16.8 us -> 18.1 us  [local(): parts = lax.all_to_all(joined, GROUP, 0, 0)]
  transfers between devices with their start and end apart: 13 -> 13, of which waited for: 8 -> 9; matrix products, arithmetic and copies ran while one was open for 0% -> 0% of each run, Pallas kernels for 11% -> 13%
where the time goes in v8:
time: 84 us; the launch traced here: 83.7 us
  starting transfers between devices  26.3 us (31%)
  waiting for transfers between devices  22 us (26%)
  blocking collectives  18.1 us (22%)
  Pallas kernels  16.5 us (20%)
    all_to_all x1, blocking collectives, local(): parts = lax.all_to_all(joined, GROUP, 0, 0)  18.1 us
    all_to_all x1, waiting for transfers between devices, local(): half = lax.all_to_all(spread, GROUP, 0, 0)  6.59 us
    ppermute x1, starting transfers between devices, local(): other_half = lax.ppermute(half, 'c', swap)  5.21 us
    ppermute x1, starting transfers between devices, local(): lax.ppermute(edge_b, SX, both_ways([(i, i + 1) for i in range(1, n_sx - 1...  4.61 us
    all_to_all x1, starting transfers between devices, local(): half = lax.all_to_all(spread, GROUP, 0, 0)  4.49 us
    ppermute x1, waiting for transfers between devices, local(): got3 = lax.ppermute(g3, 'ens', swap)  4.33 us
    ppermute x1, waiting for transfers between devices, local(): got1 = lax.ppermute(g1, 'ens', swap)  4.2 us
    pallas_call x1, Pallas kernels, rest_grad(): pl.pallas_call(functools.partial(rest_grad_kernel, begin), in_specs=[SM,...  4.11 us
  transfers between devices with their start and end apart: 13, of which 9 were waited for; matrix products, arithmetic and copies ran while one was open for 0% of the time, Pallas kernels for 13%

profile of v8, /device:TPU:1, one launch (start us, length us, event | category | flops | bytes accessed | tf_op | source)
XLA Modules:
  0.0 83.7 jit_solution(4698279294265525507)
XLA Ops:
  0.6 2.5 %shard_map.58 = (bf16[512,256]{1,0:T(8,128)(2,1)S(1)}, bf16[2,256,512]{2,1,0:T(8,128)(2,1)S(1)}, bf16[2,512,512]{2,1,0:T(8,128)(2,1)S(1)}, bf16[4,64,256]{2,1,0:T(8,128)(2,1)S(1)}) custom-call(s32[1]{0:T(128)} %bitcast.at_ref.refs_0_, bf16[4,8,64,256]{3,2,1,0:T(8,128)(2,1)} %m_hbm.5, bf16[2,256,512]{2,1,0:T(8,128)(2,1)} %c_hbm.1, ...), custom_call_target="tpu_custom_call" | custom-call | flops 536870912 | bytes 2097152 | tf_op jit(solution)/shard_map/pallas_call | solution.py:150
  3.2 4.6 %collective-permute-start = (bf16[4,64,256]{2,1,0:T(8,128)(2,1)S(1)}, bf16[4,64,256]{2,1,0:T(8,128)(2,1)S(1)}, u32[]{:S(2)}, u32[]{:S(2)}) collective-permute-start(bf16[4,64,256]{2,1,0:T(8,128)(2,1)S(1)} %get-tuple-element.48), channel_id=1, source_target_pairs={{8,16},{16,8},{24,32},{32,24},{40,48},{48,40},{56,64},{64,56},{72,... | collective-permute-start | bytes 393224 | tf_op jit(solution)/shard_map/ppermute | solution.py:411
  7.8 1.3 %collective-permute-start.5 = (bf16[512,256]{1,0:T(8,128)(2,1)S(1)}, bf16[512,256]{1,0:T(8,128)(2,1)S(1)}, u32[]{:S(2)}, u32[]{:S(2)}) collective-permute-start(bf16[512,256]{1,0:T(8,128)(2,1)S(1)} %get-tuple-element.59.refs_2_), channel_id=1, source_target_pairs={{0,128},{128,0},{1,129},{129,1},{2,130},{130,2},{3,131},{131,3},{4... | collective-permute-start | bytes 786440 | tf_op jit(solution)/shard_map/ppermute | solution.py:410
  9.1 2.4 %shard_map.59 = (bf16[512,256]{1,0:T(8,128)(2,1)S(1)}, bf16[2,512,512]{2,1,0:T(8,128)(2,1)S(1)}) custom-call(bf16[4,8,64,256]{3,2,1,0:T(8,128)(2,1)} %m_hbm.5, bf16[2,256,512]{2,1,0:T(8,128)(2,1)S(1)} %get-tuple-element.50.c_ref, bf16[2,4,512,512]{3,2,1,0:T(8,128)(2,1)} %bitcast.4), custom_call_target="tpu_custom_call" | custom-call | flops 536870912 | bytes 2097152 | tf_op jit(solution)/shard_map/pallas_call | solution.py:168
  11.5 0.0 collective-permute-done.xb_ref
  11.5 0.4 collective-permute-start.1
  11.9 4.1 %shard_map.60 = (bf16[512,256]{1,0:T(8,128)(2,1)S(1)}, bf16[512,256]{1,0:T(8,128)(2,1)S(1)}, bf16[4,8,64,256]{3,2,1,0:T(8,128)(2,1)S(1)}, bf16[2,2,512,512]{3,2,...) custom-call(s32[1]{0:T(128)} %bitcast.at_ref.refs_0_, ...), custom_call_target="tpu_custom_call" | custom-call | flops 1073741824 | bytes 3670016 | tf_op jit(solution)/shard_map/pallas_call | solution.py:194
  16.0 1.2 %collective-permute-start.7 = (bf16[512,256]{1,0:T(8,128)(2,1)S(1)}, bf16[512,256]{1,0:T(8,128)(2,1)S(1)}, u32[]{:S(2)}, u32[]{:S(2)}) collective-permute-start(bf16[512,256]{1,0:T(8,128)(2,1)S(1)} %get-tuple-element.63.refs_2_), channel_id=1, source_target_pairs={{0,128},{128,0},{1,129},{129,1},{2,130},{130,2},{3,131},{131,3},{4... | collective-permute-start | bytes 786440 | tf_op jit(solution)/shard_map/ppermute | solution.py:417
  17.2 0.0 collective-permute-done.5.refs_3_
  17.3 0.3 collective-permute-start.6
  17.6 4.2 %collective-permute-done.1.refs_3_ = bf16[512,256]{1,0:T(8,128)(2,1)S(1)} collective-permute-done((bf16[512,256]{1,0:T(8,128)(2,1)S(1)}, bf16[512,256]{1,0:T(8,128)(2,1)S(1)}, u32[]{:S(2)}, u32[]{:S(2)}) %collective-permute-start.1) | collective-permute-done | bytes 262176 | tf_op jit(solution)/shard_map/ppermute | solution.py:414
  21.8 0.0 collective-permute-start.2
  21.8 1.2 %collective-permute-start.3 = (bf16[32,256]{1,0:T(8,128)(2,1)S(1)}, bf16[32,256]{1,0:T(8,128)(2,1)S(1)}, u32[]{:S(2)}, u32[]{:S(2)}) collective-permute-start(bf16[32,256]{1,0:T(8,128)(2,1)S(1)} %get-tuple-element.57), channel_id=1, source_target_pairs={{0,1},{1,0},{2,3},{3,2},{4,5},{5,4},{6,7},{7,6},{8,9},{9,8},{10,11... | collective-permute-start | bytes 49160 | tf_op jit(solution)/shard_map/ppermute | solution.py:422
  23.0 0.7 collective-permute-start.4
  23.7 1.0 %collective-permute-done.3.za_ref = bf16[32,256]{1,0:T(8,128)(2,1)S(1)} collective-permute-done((bf16[32,256]{1,0:T(8,128)(2,1)S(1)}, bf16[32,256]{1,0:T(8,128)(2,1)S(1)}, u32[]{:S(2)}, u32[]{:S(2)}) %collective-permute-start.3) | collective-permute-done | bytes 16416 | tf_op jit(solution)/shard_map/ppermute | solution.py:422
  24.7 0.0 collective-permute-done.4.zb_ref
  24.7 0.0 collective-permute-done.2.xa_ref
  24.7 0.9 %shard_map.61.refs_1_ = f32[4,512,256]{2,1,0:T(8,128)S(1)} custom-call(s32[1]{0:T(128)} %bitcast.at_ref.refs_0_, bf16[4,8,64,256]{3,2,1,0:T(8,128)(2,1)S(1)} %get-tuple-element.51.m_ref, bf16[4,64,256]{2,1,0:T(8,128)(2,1)S(1)} %collective-permute-done.2.xa_ref, bf16[4,64,256]{2,1,0:T(8,128)(2,1)S(1)} %collective-permute-done.xb_ref, ...), custom_call_target="tpu_custom_call" | custom-call | flops 6291456 | bytes 3145728 | tf_op jit(solution)/shard_map/pallas_call | solution.py:424
  25.6 0.6 shard_map.62
  26.3 0.8 shard_map.63
  27.1 0.3 collective-permute-done.7.refs_3_
  27.4 0.8 shard_map.64
  28.2 4.3 %collective-permute-done.6.refs_3_ = bf16[512,256]{1,0:T(8,128)(2,1)S(1)} collective-permute-done((bf16[512,256]{1,0:T(8,128)(2,1)S(1)}, bf16[512,256]{1,0:T(8,128)(2,1)S(1)}, u32[]{:S(2)}, u32[]{:S(2)}) %collective-permute-start.6) | collective-permute-done | bytes 262176 | tf_op jit(solution)/shard_map/ppermute | solution.py:419
  32.6 0.9 %shard_map.65 = (bf16[512,256]{1,0:T(8,128)(2,1)S(1)}, bf16[16,88,128]{2,1,0:T(8,128)(2,1)S(1)}, bf16[16,88,128]{2,1,0:T(8,128)(2,1)S(1)}) custom-call(s32[1]{0:T(128)} %bitcast.at_ref.refs_0_, f32[4,512,256]{2,1,0:T(8,128)S(1)} %shard_map.61.refs_1_, bf16[512,256]{1,0:T(8,128)(2,1)S(1)} %get-tuple-element.61.refs_2_, ...), custom_call_target="tpu_custom_call" | custom-call | flops 335544320 | bytes 2097152 | tf_op jit(solution)/shard_map/pallas_call | solution.py:299
  33.4 0.5 collective-permute-start.8
  33.9 1.3 %collective-permute-done.8.got_ref = bf16[16,88,128]{2,1,0:T(8,128)(2,1)S(1)} collective-permute-done((bf16[16,88,128]{2,1,0:T(8,128)(2,1)S(1)}, bf16[16,88,128]{2,1,0:T(8,128)(2,1)S(1)}, u32[]{:S(2)}, u32[]{:S(2)}) %collective-permute-start.8) | collective-permute-done | bytes 360480 | tf_op jit(solution)/shard_map/ppermute | solution.py:441
  35.2 0.1 shard_map.66
  35.3 18.1 %all_to_all.10.in_ref = bf16[16,88,128]{2,1,0:T(8,128)(2,1)S(1)} all-to-all(bf16[16,88,128]{2,1,0:T(8,128)(2,1)S(1)} %shard_map.66), channel_id=1, replica_groups=mesh['ens'=2,'xh'=2,'y'=4,'c'=2,'zh'=4,'zl'=2] {'xh','y','zl'}, dimensions={0} | all-to-all | bytes 720896 | tf_op jit(solution)/shard_map/all_to_all | solution.py:445
  53.4 0.1 shard_map.67.own_ref
  53.4 3.4 %collective-permute-start.9 = (bf16[88,128]{1,0:T(8,128)(2,1)S(1)}, bf16[88,128]{1,0:T(8,128)(2,1)S(1)}, u32[]{:S(2)}, u32[]{:S(2)}) collective-permute-start(bf16[88,128]{1,0:T(8,128)(2,1)S(1)} %shard_map.67.own_ref), channel_id=1, source_target_pairs={{0,2},{2,0},{4,6},{6,4},{1,3},{3,1},{5,7},{7,5},{8,10},{10,8},{12,... | collective-permute-start | bytes 67592 | tf_op jit(solution)/shard_map/ppermute | solution.py:451
  56.8 1.2 %collective-permute-done.9.got_ref = bf16[88,128]{1,0:T(8,128)(2,1)S(1)} collective-permute-done((bf16[88,128]{1,0:T(8,128)(2,1)S(1)}, bf16[88,128]{1,0:T(8,128)(2,1)S(1)}, u32[]{:S(2)}, u32[]{:S(2)}) %collective-permute-start.9) | collective-permute-done | bytes 22560 | tf_op jit(solution)/shard_map/ppermute | solution.py:451
  58.0 3.0 %collective-permute-start.10 = (bf16[88,128]{1,0:T(8,128)(2,1)S(1)}, bf16[88,128]{1,0:T(8,128)(2,1)S(1)}, u32[]{:S(2)}, u32[]{:S(2)}) collective-permute-start(bf16[88,128]{1,0:T(8,128)(2,1)S(1)} %shard_map.68.own_ref), channel_id=1, source_target_pairs={{0,6},{2,4},{4,2},{6,0},{1,7},{3,5},{5,3},{7,1},{8,14},{10,12},{12... | collective-permute-start | bytes 67592 | tf_op jit(solution)/shard_map/ppermute | solution.py:455
  61.1 1.8 %collective-permute-done.10.got_ref = bf16[88,128]{1,0:T(8,128)(2,1)S(1)} collective-permute-done((bf16[88,128]{1,0:T(8,128)(2,1)S(1)}, bf16[88,128]{1,0:T(8,128)(2,1)S(1)}, u32[]{:S(2)}, u32[]{:S(2)}) %collective-permute-start.10) | collective-permute-done | bytes 22560 | tf_op jit(solution)/shard_map/ppermute | solution.py:455
  62.9 0.9 %shard_map.69 = (bf16[16,80,128]{2,1,0:T(8,128)(2,1)}, f32[2,128]{1,0:T(2,128)S(1)}) custom-call(s32[1]{0:T(128)} %bitcast.at_ref.refs_0_, bf16[88,128]{1,0:T(8,128)(2,1)S(1)} %shard_map.68.own_ref, bf16[88,128]{1,0:T(8,128)(2,1)S(1)} %collective-permute-done.10.got_ref), custom_call_target="tpu_custom_call" | custom-call | tf_op jit(solution)/shard_map/pallas_call | solution.py:456
  63.8 4.5 %all-to-all-start.1 = ((bf16[16,80,128]{2,1,0:T(8,128)(2,1)}), bf16[16,80,128]{2,1,0:T(8,128)(2,1)S(1)}, u32[]{:S(2)}, u32[]{:S(2)}) async-start(bf16[16,80,128]{2,1,0:T(8,128)(2,1)} %get-tuple-element.79), calls=%async_computation.1 | async-start | bytes 655360 | tf_op jit(solution)/shard_map/all_to_all | solution.py:467
  68.3 1.2 %shard_map.70 = bf16[2048,256]{1,0:T(8,128)(2,1)} custom-call(f32[2,128]{1,0:T(2,128)S(1)} %get-tuple-element.80.shrink_ref, bf16[512,256]{1,0:T(8,128)(2,1)S(1)} %get-tuple-element.81.refs_0_, bf16[512,256]{1,0:T(8,128)(2,1)S(1)} %get-tuple-element.82.refs_1_, bf16[512,256]{1,0:T(8,128)(2,1)S(1)} %get-tuple-element.83.refs_2_, ...), custom_call_target="tpu_custom_call" | custom-call | tf_op jit(solution)/shard_map/pallas_call | solution.py:468
  69.4 6.6 %all-to-all-done.1.own_ref = bf16[16,80,128]{2,1,0:T(8,128)(2,1)S(1)} async-done(((bf16[16,80,128]{2,1,0:T(8,128)(2,1)}), bf16[16,80,128]{2,1,0:T(8,128)(2,1)S(1)}, u32[]{:S(2)}, u32[]{:S(2)}) %all-to-all-start.1) | async-done | bytes 327712 | tf_op jit(solution)/shard_map/all_to_all | solution.py:467
  76.0 5.2 %collective-permute-start.11 = (bf16[16,80,128]{2,1,0:T(8,128)(2,1)S(1)}, bf16[16,80,128]{2,1,0:T(8,128)(2,1)S(1)}, u32[]{:S(2)}, u32[]{:S(2)}) collective-permute-start(bf16[16,80,128]{2,1,0:T(8,128)(2,1)S(1)} %all-to-all-done.1.own_ref), channel_id=1, source_target_pairs={{0,8},{8,0},{1,9},{9,1},{2,10},{10,2},{3,11},{11,3},{4,12},{12,4},... | collective-permute-start | bytes 983048 | tf_op jit(solution)/shard_map/ppermute | solution.py:476
  81.2 1.3 %collective-permute-done.11.got_ref = bf16[16,80,128]{2,1,0:T(8,128)(2,1)S(1)} collective-permute-done((bf16[16,80,128]{2,1,0:T(8,128)(2,1)S(1)}, bf16[16,80,128]{2,1,0:T(8,128)(2,1)S(1)}, u32[]{:S(2)}, u32[]{:S(2)}) %collective-permute-start.11) | collective-permute-done | bytes 327712 | tf_op jit(solution)/shard_map/ppermute | solution.py:476
  82.5 1.2 %shard_map.71 = (f32[2,256,512]{2,1,0:T(8,128)}, f32[256,256]{1,0:T(8,128)}) custom-call(s32[1]{0:T(128)} %bitcast.at_ref.refs_0_, bf16[16,80,128]{2,1,0:T(8,128)(2,1)S(1)} %all-to-all-done.1.own_ref, bf16[16,80,128]{2,1,0:T(8,128)(2,1)S(1)} %collective-permute-done.11.got_ref), custom_call_target="tpu_custom_call" | custom-call | tf_op jit(solution)/shard_map/pallas_call | solution.py:477
  (1 shorter events, 0.0 us)
Async XLA Ops:
  3.2 8.3 %collective-permute-start = (bf16[4,64,256]{2,1,0:T(8,128)(2,1)S(1)}, bf16[4,64,256]{2,1,0:T(8,128)(2,1)S(1)}, u32[]{:S(2)}, u32[]{:S(2)}) collective-permute-start(bf16[4,64,256]{2,1,0:T(8,128)(2,1)S(1)} %get-tuple-element.48), channel_id=1, source_target_pairs={{8,16},{16,8},{24,32},{32,24},{40,48},{48,40},{56,64},{64,56},{72,... | collective-permute-start | bytes 393224 | tf_op jit(solution)/shard_map/ppermute | solution.py:411
  7.8 9.5 %collective-permute-start.5 = (bf16[512,256]{1,0:T(8,128)(2,1)S(1)}, bf16[512,256]{1,0:T(8,128)(2,1)S(1)}, u32[]{:S(2)}, u32[]{:S(2)}) collective-permute-start(bf16[512,256]{1,0:T(8,128)(2,1)S(1)} %get-tuple-element.59.refs_2_), channel_id=1, source_target_pairs={{0,128},{128,0},{1,129},{129,1},{2,130},{130,2},{3,131},{131,3},{4... | collective-permute-start | bytes 786440 | tf_op jit(solution)/shard_map/ppermute | solution.py:410
  11.5 10.3 %collective-permute-start.1 = (bf16[512,256]{1,0:T(8,128)(2,1)S(1)}, bf16[512,256]{1,0:T(8,128)(2,1)S(1)}, u32[]{:S(2)}, u32[]{:S(2)}) collective-permute-start(bf16[512,256]{1,0:T(8,128)(2,1)S(1)} %get-tuple-element.49.refs_2_), channel_id=1, source_target_pairs={{0,128},{128,0},{1,129},{129,1},{2,130},{130,2},{3,131},{131,3},{4... | collective-permute-start | bytes 786440 | tf_op jit(solution)/shard_map/ppermute | solution.py:414
  16.0 11.4 %collective-permute-start.7 = (bf16[512,256]{1,0:T(8,128)(2,1)S(1)}, bf16[512,256]{1,0:T(8,128)(2,1)S(1)}, u32[]{:S(2)}, u32[]{:S(2)}) collective-permute-start(bf16[512,256]{1,0:T(8,128)(2,1)S(1)} %get-tuple-element.63.refs_2_), channel_id=1, source_target_pairs={{0,128},{128,0},{1,129},{129,1},{2,130},{130,2},{3,131},{131,3},{4... | collective-permute-start | bytes 786440 | tf_op jit(solution)/shard_map/ppermute | solution.py:417
  17.3 15.3 %collective-permute-start.6 = (bf16[512,256]{1,0:T(8,128)(2,1)S(1)}, bf16[512,256]{1,0:T(8,128)(2,1)S(1)}, u32[]{:S(2)}, u32[]{:S(2)}) collective-permute-start(bf16[512,256]{1,0:T(8,128)(2,1)S(1)} %get-tuple-element.61.refs_2_), channel_id=1, source_target_pairs={{0,128},{128,0},{1,129},{129,1},{2,130},{130,2},{3,131},{131,3},{4... | collective-permute-start | bytes 786440 | tf_op jit(solution)/shard_map/ppermute | solution.py:419
  21.8 2.9 %collective-permute-start.2 = (bf16[4,64,256]{2,1,0:T(8,128)(2,1)S(1)}, bf16[4,64,256]{2,1,0:T(8,128)(2,1)S(1)}, u32[]{:S(2)}, u32[]{:S(2)}) collective-permute-start(bf16[4,64,256]{2,1,0:T(8,128)(2,1)S(1)} %get-tuple-element.55), channel_id=1, source_target_pairs={{0,8},{8,0},{1,9},{9,1},{2,10},{10,2},{3,11},{11,3},{4,12},{12,4},... | collective-permute-start | bytes 393224 | tf_op jit(solution)/shard_map/ppermute | solution.py:421
  21.8 2.9 %collective-permute-start.3 = (bf16[32,256]{1,0:T(8,128)(2,1)S(1)}, bf16[32,256]{1,0:T(8,128)(2,1)S(1)}, u32[]{:S(2)}, u32[]{:S(2)}) collective-permute-start(bf16[32,256]{1,0:T(8,128)(2,1)S(1)} %get-tuple-element.57), channel_id=1, source_target_pairs={{0,1},{1,0},{2,3},{3,2},{4,5},{5,4},{6,7},{7,6},{8,9},{9,8},{10,11... | collective-permute-start | bytes 49160 | tf_op jit(solution)/shard_map/ppermute | solution.py:422
  23.0 1.7 %collective-permute-start.4 = (bf16[32,256]{1,0:T(8,128)(2,1)S(1)}, bf16[32,256]{1,0:T(8,128)(2,1)S(1)}, u32[]{:S(2)}, u32[]{:S(2)}) collective-permute-start(bf16[32,256]{1,0:T(8,128)(2,1)S(1)} %get-tuple-element.58), channel_id=1, source_target_pairs={{1,2},{2,1},{3,4},{4,3},{5,6},{6,5},{9,10},{10,9},{11,12},{12,11},... | collective-permute-start | bytes 49160 | tf_op jit(solution)/shard_map/ppermute | solution.py:423
  33.4 1.8 %collective-permute-start.8 = (bf16[16,88,128]{2,1,0:T(8,128)(2,1)S(1)}, bf16[16,88,128]{2,1,0:T(8,128)(2,1)S(1)}, u32[]{:S(2)}, u32[]{:S(2)}) collective-permute-start(bf16[16,88,128]{2,1,0:T(8,128)(2,1)S(1)} %get-tuple-element.78), channel_id=1, source_target_pairs={{0,8},{8,0},{1,9},{9,1},{2,10},{10,2},{3,11},{11,3},{4,12},{12,4},... | collective-permute-start | bytes 1081352 | tf_op jit(solution)/shard_map/ppermute | solution.py:441
  53.4 4.6 %collective-permute-start.9 = (bf16[88,128]{1,0:T(8,128)(2,1)S(1)}, bf16[88,128]{1,0:T(8,128)(2,1)S(1)}, u32[]{:S(2)}, u32[]{:S(2)}) collective-permute-start(bf16[88,128]{1,0:T(8,128)(2,1)S(1)} %shard_map.67.own_ref), channel_id=1, source_target_pairs={{0,2},{2,0},{4,6},{6,4},{1,3},{3,1},{5,7},{7,5},{8,10},{10,8},{12,... | collective-permute-start | bytes 67592 | tf_op jit(solution)/shard_map/ppermute | solution.py:451
  58.0 4.9 %collective-permute-start.10 = (bf16[88,128]{1,0:T(8,128)(2,1)S(1)}, bf16[88,128]{1,0:T(8,128)(2,1)S(1)}, u32[]{:S(2)}, u32[]{:S(2)}) collective-permute-start(bf16[88,128]{1,0:T(8,128)(2,1)S(1)} %shard_map.68.own_ref), channel_id=1, source_target_pairs={{0,6},{2,4},{4,2},{6,0},{1,7},{3,5},{5,3},{7,1},{8,14},{10,12},{12... | collective-permute-start | bytes 67592 | tf_op jit(solution)/shard_map/ppermute | solution.py:455
  63.8 12.3 %all-to-all-start.1 = ((bf16[16,80,128]{2,1,0:T(8,128)(2,1)}), bf16[16,80,128]{2,1,0:T(8,128)(2,1)S(1)}, u32[]{:S(2)}, u32[]{:S(2)}) async-start(bf16[16,80,128]{2,1,0:T(8,128)(2,1)} %get-tuple-element.79), calls=%async_computation.1 | async-start | bytes 655360 | tf_op jit(solution)/shard_map/all_to_all | solution.py:467
  76.0 6.5 %collective-permute-start.11 = (bf16[16,80,128]{2,1,0:T(8,128)(2,1)S(1)}, bf16[16,80,128]{2,1,0:T(8,128)(2,1)S(1)}, u32[]{:S(2)}, u32[]{:S(2)}) collective-permute-start(bf16[16,80,128]{2,1,0:T(8,128)(2,1)S(1)} %all-to-all-done.1.own_ref), channel_id=1, source_target_pairs={{0,8},{8,0},{1,9},{9,1},{2,10},{10,2},{3,11},{11,3},{4,12},{12,4},... | collective-permute-start | bytes 983048 | tf_op jit(solution)/shard_map/ppermute | solution.py:476

commit v9 on v8

--- a/solution.py
+++ b/solution.py
@@ -412,15 +412,15 @@
     g1, x1 = second_grad(modes, coefficients, series, 1)
     g1, xb = lax.optimization_barrier((g1, xb))
     got1 = lax.ppermute(g1, "ens", swap)
-    coefficients, _ = lax.optimization_barrier((coefficients, g1))
+    coefficients, got0, _ = lax.optimization_barrier((coefficients, got0, g1))
     g2, g3, modes, series, edge_a, row_a, row_b = rest_grad(place, modes, coefficients, series, 2)
     got2 = lax.ppermute(g2, "ens", swap)
-    got0, g3 = lax.optimization_barrier((got0, g3))
     got3 = lax.ppermute(g3, "ens", swap)
-    got1, edge_a, row_a, row_b = lax.optimization_barrier((got1, edge_a, row_a, row_b))
-    xa = lax.ppermute(edge_a, "c", swap)
+    got0, row_a, row_b = lax.optimization_barrier((got0, row_a, row_b))
     za = lax.ppermute(row_a, SY, both_ways([(i, i + 1) for i in range(0, n_z, 2)]))
     zb = lax.ppermute(row_b, SY, both_ways([(i, i + 1) for i in range(1, n_z - 1, 2)]))
+    got1, edge_a, za, zb = lax.optimization_barrier((got1, edge_a, za, zb))
+    xa = lax.ppermute(edge_a, "c", swap)
     base = pl.pallas_call(
         base_kernel,
         in_specs=[SM] + [VM] * 5,

time: 84 us -> 82.6 us (0.983)
  waiting for transfers between devices: 22 us -> 17.3 us
  starting transfers between devices: 26.3 us -> 29.2 us
    ppermute x1, waiting for transfers between devices: 4.2 us -> 0.01 us  [local(): got1 = lax.ppermute(g1, 'ens', swap)]
    ppermute x1, starting transfers between devices: 0.01 us -> 1.58 us  [local(): xa = lax.ppermute(edge_a, 'c', swap)]
    ppermute x1, waiting for transfers between devices: 4.33 us -> 2.84 us  [local(): got3 = lax.ppermute(g3, 'ens', swap)]
    ppermute x1, waiting for transfers between devices: 0.01 us -> 0.99 us  [local(): xa = lax.ppermute(edge_a, 'c', swap)]
    ppermute x1, starting transfers between devices: 1.29 us -> 2.13 us  [local(): got0 = lax.ppermute(g0, 'ens', swap)]
where the time goes in v9:
time: 82.6 us; the launch traced here: 82.3 us
  starting transfers between devices  29.2 us (35%)
  blocking collectives  18.6 us (23%)
  waiting for transfers between devices  17.3 us (21%)
  Pallas kernels  16.5 us (20%)
    all_to_all x1, blocking collectives, local(): parts = lax.all_to_all(joined, GROUP, 0, 0)  18.6 us
    all_to_all x1, waiting for transfers between devices, local(): half = lax.all_to_all(spread, GROUP, 0, 0)  6.59 us
    ppermute x1, starting transfers between devices, local(): other_half = lax.ppermute(half, 'c', swap)  5.2 us
    all_to_all x1, starting transfers between devices, local(): half = lax.all_to_all(spread, GROUP, 0, 0)  4.49 us
    pallas_call x1, Pallas kernels, rest_grad(): pl.pallas_call(functools.partial(rest_grad_kernel, begin), in_specs=[SM,...  4.11 us
    ppermute x1, starting transfers between devices, local(): lax.ppermute(edge_b, SX, both_ways([(i, i + 1) for i in range(1, n_sx - 1...  4.03 us
    ppermute x1, starting transfers between devices, local(): near = lax.ppermute(line, 'zh', [(i, i ^ 1) for i in range(pairs)])  3.38 us
    pallas_call x4, Pallas kernels, step_level(): pl.pallas_call(functools.partial(step_kernel, level, x_at, first, last),...  3.13 us
  transfers between devices with their start and end apart: 13, of which 9 were waited for; matrix products, arithmetic and copies ran while one was open for 0% of the time, Pallas kernels for 13%

profile of v9, /device:TPU:1, one launch (start us, length us, event | category | flops | bytes accessed | tf_op | source)
XLA Modules:
  0.0 82.3 jit_solution(4978614103175502230)
XLA Ops:
  0.6 2.5 %shard_map.58 = (bf16[512,256]{1,0:T(8,128)(2,1)S(1)}, bf16[2,256,512]{2,1,0:T(8,128)(2,1)S(1)}, bf16[2,512,512]{2,1,0:T(8,128)(2,1)S(1)}, bf16[4,64,256]{2,1,0:T(8,128)(2,1)S(1)}) custom-call(s32[1]{0:T(128)} %bitcast.at_ref.refs_0_, bf16[4,8,64,256]{3,2,1,0:T(8,128)(2,1)} %m_hbm.5, bf16[2,256,512]{2,1,0:T(8,128)(2,1)} %c_hbm.1, ...), custom_call_target="tpu_custom_call" | custom-call | flops 536870912 | bytes 2097152 | tf_op jit(solution)/shard_map/pallas_call | solution.py:150
  3.2 2.1 %collective-permute-start = (bf16[512,256]{1,0:T(8,128)(2,1)S(1)}, bf16[512,256]{1,0:T(8,128)(2,1)S(1)}, u32[]{:S(2)}, u32[]{:S(2)}) collective-permute-start(bf16[512,256]{1,0:T(8,128)(2,1)S(1)} %get-tuple-element.49.refs_2_), channel_id=1, source_target_pairs={{0,128},{128,0},{1,129},{129,1},{2,130},{130,2},{3,131},{131,3},{4... | collective-permute-start | bytes 786440 | tf_op jit(solution)/shard_map/ppermute | solution.py:410
  5.3 4.0 %collective-permute-start.1 = (bf16[4,64,256]{2,1,0:T(8,128)(2,1)S(1)}, bf16[4,64,256]{2,1,0:T(8,128)(2,1)S(1)}, u32[]{:S(2)}, u32[]{:S(2)}) collective-permute-start(bf16[4,64,256]{2,1,0:T(8,128)(2,1)S(1)} %get-tuple-element.51), channel_id=1, source_target_pairs={{8,16},{16,8},{24,32},{32,24},{40,48},{48,40},{56,64},{64,56},{72,... | collective-permute-start | bytes 393224 | tf_op jit(solution)/shard_map/ppermute | solution.py:411
  9.3 2.4 %shard_map.59 = (bf16[512,256]{1,0:T(8,128)(2,1)S(1)}, bf16[2,512,512]{2,1,0:T(8,128)(2,1)S(1)}) custom-call(bf16[4,8,64,256]{3,2,1,0:T(8,128)(2,1)} %m_hbm.5, bf16[2,256,512]{2,1,0:T(8,128)(2,1)S(1)} %get-tuple-element.53.c_ref, bf16[2,4,512,512]{3,2,1,0:T(8,128)(2,1)} %bitcast.4), custom_call_target="tpu_custom_call" | custom-call | flops 536870912 | bytes 2097152 | tf_op jit(solution)/shard_map/pallas_call | solution.py:168
  11.8 0.5 collective-permute-done.1.xb_ref
  12.3 0.3 collective-permute-start.2
  12.5 0.0 collective-permute-done.refs_3_
  12.5 4.1 %shard_map.60 = (bf16[512,256]{1,0:T(8,128)(2,1)S(1)}, bf16[512,256]{1,0:T(8,128)(2,1)S(1)}, bf16[4,8,64,256]{3,2,1,0:T(8,128)(2,1)S(1)}, bf16[2,2,512,512]{3,2,...) custom-call(s32[1]{0:T(128)} %bitcast.at_ref.refs_0_, ...), custom_call_target="tpu_custom_call" | custom-call | flops 1073741824 | bytes 3670016 | tf_op jit(solution)/shard_map/pallas_call | solution.py:194
  16.7 1.3 %collective-permute-start.7 = (bf16[512,256]{1,0:T(8,128)(2,1)S(1)}, bf16[512,256]{1,0:T(8,128)(2,1)S(1)}, u32[]{:S(2)}, u32[]{:S(2)}) collective-permute-start(bf16[512,256]{1,0:T(8,128)(2,1)S(1)} %get-tuple-element.67.refs_2_), channel_id=1, source_target_pairs={{0,128},{128,0},{1,129},{129,1},{2,130},{130,2},{3,131},{131,3},{4... | collective-permute-start | bytes 786440 | tf_op jit(solution)/shard_map/ppermute | solution.py:417
  17.9 0.3 collective-permute-start.6
  18.2 1.6 %collective-permute-start.3 = (bf16[32,256]{1,0:T(8,128)(2,1)S(1)}, bf16[32,256]{1,0:T(8,128)(2,1)S(1)}, u32[]{:S(2)}, u32[]{:S(2)}) collective-permute-start(bf16[32,256]{1,0:T(8,128)(2,1)S(1)} %get-tuple-element.59), channel_id=1, source_target_pairs={{0,1},{1,0},{2,3},{3,2},{4,5},{5,4},{6,7},{7,6},{8,9},{9,8},{10,11... | collective-permute-start | bytes 49160 | tf_op jit(solution)/shard_map/ppermute | solution.py:420
  19.8 0.7 collective-permute-start.4
  20.5 0.8 collective-permute-done.3.za_ref
  21.3 0.0 collective-permute-done.4.zb_ref
  21.3 0.0 collective-permute-done.2.refs_3_
  21.3 1.6 %collective-permute-start.5 = (bf16[4,64,256]{2,1,0:T(8,128)(2,1)S(1)}, bf16[4,64,256]{2,1,0:T(8,128)(2,1)S(1)}, u32[]{:S(2)}, u32[]{:S(2)}) collective-permute-start(bf16[4,64,256]{2,1,0:T(8,128)(2,1)S(1)} %get-tuple-element.61), channel_id=1, source_target_pairs={{0,8},{8,0},{1,9},{9,1},{2,10},{10,2},{3,11},{11,3},{4,12},{12,4},... | collective-permute-start | bytes 393224 | tf_op jit(solution)/shard_map/ppermute | solution.py:423
  22.8 1.0 %collective-permute-done.5.xa_ref = bf16[4,64,256]{2,1,0:T(8,128)(2,1)S(1)} collective-permute-done((bf16[4,64,256]{2,1,0:T(8,128)(2,1)S(1)}, bf16[4,64,256]{2,1,0:T(8,128)(2,1)S(1)}, u32[]{:S(2)}, u32[]{:S(2)}) %collective-permute-start.5) | collective-permute-done | bytes 131104 | tf_op jit(solution)/shard_map/ppermute | solution.py:423
  23.8 0.9 %shard_map.61.refs_1_ = f32[4,512,256]{2,1,0:T(8,128)S(1)} custom-call(s32[1]{0:T(128)} %bitcast.at_ref.refs_0_, bf16[4,8,64,256]{3,2,1,0:T(8,128)(2,1)S(1)} %get-tuple-element.54.m_ref, bf16[4,64,256]{2,1,0:T(8,128)(2,1)S(1)} %collective-permute-done.5.xa_ref, bf16[4,64,256]{2,1,0:T(8,128)(2,1)S(1)} %collective-permute-done.1.xb_ref, ...), custom_call_target="tpu_custom_call" | custom-call | flops 6291456 | bytes 3145728 | tf_op jit(solution)/shard_map/pallas_call | solution.py:424
  24.8 0.6 shard_map.62
  25.4 0.8 shard_map.63
  26.2 0.0 collective-permute-done.7.refs_3_
  26.3 0.8 shard_map.64
  27.1 2.8 %collective-permute-done.6.refs_3_ = bf16[512,256]{1,0:T(8,128)(2,1)S(1)} collective-permute-done((bf16[512,256]{1,0:T(8,128)(2,1)S(1)}, bf16[512,256]{1,0:T(8,128)(2,1)S(1)}, u32[]{:S(2)}, u32[]{:S(2)}) %collective-permute-start.6) | collective-permute-done | bytes 262176 | tf_op jit(solution)/shard_map/ppermute | solution.py:418
  29.9 0.9 %shard_map.65 = (bf16[512,256]{1,0:T(8,128)(2,1)S(1)}, bf16[16,88,128]{2,1,0:T(8,128)(2,1)S(1)}, bf16[16,88,128]{2,1,0:T(8,128)(2,1)S(1)}) custom-call(s32[1]{0:T(128)} %bitcast.at_ref.refs_0_, f32[4,512,256]{2,1,0:T(8,128)S(1)} %shard_map.61.refs_1_, bf16[512,256]{1,0:T(8,128)(2,1)S(1)} %get-tuple-element.65.refs_2_, ...), custom_call_target="tpu_custom_call" | custom-call | flops 335544320 | bytes 2097152 | tf_op jit(solution)/shard_map/pallas_call | solution.py:299
  30.8 1.2 %collective-permute-start.8 = (bf16[16,88,128]{2,1,0:T(8,128)(2,1)S(1)}, bf16[16,88,128]{2,1,0:T(8,128)(2,1)S(1)}, u32[]{:S(2)}, u32[]{:S(2)}) collective-permute-start(bf16[16,88,128]{2,1,0:T(8,128)(2,1)S(1)} %get-tuple-element.82), channel_id=1, source_target_pairs={{0,8},{8,0},{1,9},{9,1},{2,10},{10,2},{3,11},{11,3},{4,12},{12,4},... | collective-permute-start | bytes 1081352 | tf_op jit(solution)/shard_map/ppermute | solution.py:441
  32.0 1.3 %collective-permute-done.8.got_ref = bf16[16,88,128]{2,1,0:T(8,128)(2,1)S(1)} collective-permute-done((bf16[16,88,128]{2,1,0:T(8,128)(2,1)S(1)}, bf16[16,88,128]{2,1,0:T(8,128)(2,1)S(1)}, u32[]{:S(2)}, u32[]{:S(2)}) %collective-permute-start.8) | collective-permute-done | bytes 360480 | tf_op jit(solution)/shard_map/ppermute | solution.py:441
  33.3 0.1 shard_map.66
  33.4 18.6 %all_to_all.10.in_ref = bf16[16,88,128]{2,1,0:T(8,128)(2,1)S(1)} all-to-all(bf16[16,88,128]{2,1,0:T(8,128)(2,1)S(1)} %shard_map.66), channel_id=1, replica_groups=mesh['ens'=2,'xh'=2,'y'=4,'c'=2,'zh'=4,'zl'=2] {'xh','y','zl'}, dimensions={0} | all-to-all | bytes 720896 | tf_op jit(solution)/shard_map/all_to_all | solution.py:445
  52.0 0.1 shard_map.67.own_ref
  52.1 3.4 %collective-permute-start.9 = (bf16[88,128]{1,0:T(8,128)(2,1)S(1)}, bf16[88,128]{1,0:T(8,128)(2,1)S(1)}, u32[]{:S(2)}, u32[]{:S(2)}) collective-permute-start(bf16[88,128]{1,0:T(8,128)(2,1)S(1)} %shard_map.67.own_ref), channel_id=1, source_target_pairs={{0,2},{2,0},{4,6},{6,4},{1,3},{3,1},{5,7},{7,5},{8,10},{10,8},{12,... | collective-permute-start | bytes 67592 | tf_op jit(solution)/shard_map/ppermute | solution.py:451
  55.5 1.2 %collective-permute-done.9.got_ref = bf16[88,128]{1,0:T(8,128)(2,1)S(1)} collective-permute-done((bf16[88,128]{1,0:T(8,128)(2,1)S(1)}, bf16[88,128]{1,0:T(8,128)(2,1)S(1)}, u32[]{:S(2)}, u32[]{:S(2)}) %collective-permute-start.9) | collective-permute-done | bytes 22560 | tf_op jit(solution)/shard_map/ppermute | solution.py:451
  56.7 3.0 %collective-permute-start.10 = (bf16[88,128]{1,0:T(8,128)(2,1)S(1)}, bf16[88,128]{1,0:T(8,128)(2,1)S(1)}, u32[]{:S(2)}, u32[]{:S(2)}) collective-permute-start(bf16[88,128]{1,0:T(8,128)(2,1)S(1)} %shard_map.68.own_ref), channel_id=1, source_target_pairs={{0,6},{2,4},{4,2},{6,0},{1,7},{3,5},{5,3},{7,1},{8,14},{10,12},{12... | collective-permute-start | bytes 67592 | tf_op jit(solution)/shard_map/ppermute | solution.py:455
  59.7 1.8 %collective-permute-done.10.got_ref = bf16[88,128]{1,0:T(8,128)(2,1)S(1)} collective-permute-done((bf16[88,128]{1,0:T(8,128)(2,1)S(1)}, bf16[88,128]{1,0:T(8,128)(2,1)S(1)}, u32[]{:S(2)}, u32[]{:S(2)}) %collective-permute-start.10) | collective-permute-done | bytes 22560 | tf_op jit(solution)/shard_map/ppermute | solution.py:455
  61.5 0.9 %shard_map.69 = (bf16[16,80,128]{2,1,0:T(8,128)(2,1)}, f32[2,128]{1,0:T(2,128)S(1)}) custom-call(s32[1]{0:T(128)} %bitcast.at_ref.refs_0_, bf16[88,128]{1,0:T(8,128)(2,1)S(1)} %shard_map.68.own_ref, bf16[88,128]{1,0:T(8,128)(2,1)S(1)} %collective-permute-done.10.got_ref), custom_call_target="tpu_custom_call" | custom-call | tf_op jit(solution)/shard_map/pallas_call | solution.py:456
  62.4 4.5 %all-to-all-start.1 = ((bf16[16,80,128]{2,1,0:T(8,128)(2,1)}), bf16[16,80,128]{2,1,0:T(8,128)(2,1)S(1)}, u32[]{:S(2)}, u32[]{:S(2)}) async-start(bf16[16,80,128]{2,1,0:T(8,128)(2,1)} %get-tuple-element.83), calls=%async_computation.1 | async-start | bytes 655360 | tf_op jit(solution)/shard_map/all_to_all | solution.py:467
  66.9 1.2 %shard_map.70 = bf16[2048,256]{1,0:T(8,128)(2,1)} custom-call(f32[2,128]{1,0:T(2,128)S(1)} %get-tuple-element.84.shrink_ref, bf16[512,256]{1,0:T(8,128)(2,1)S(1)} %get-tuple-element.85.refs_0_, bf16[512,256]{1,0:T(8,128)(2,1)S(1)} %get-tuple-element.86.refs_1_, bf16[512,256]{1,0:T(8,128)(2,1)S(1)} %get-tuple-element.87.refs_2_, ...), custom_call_target="tpu_custom_call" | custom-call | tf_op jit(solution)/shard_map/pallas_call | solution.py:468
  68.1 6.6 %all-to-all-done.1.own_ref = bf16[16,80,128]{2,1,0:T(8,128)(2,1)S(1)} async-done(((bf16[16,80,128]{2,1,0:T(8,128)(2,1)}), bf16[16,80,128]{2,1,0:T(8,128)(2,1)S(1)}, u32[]{:S(2)}, u32[]{:S(2)}) %all-to-all-start.1) | async-done | bytes 327712 | tf_op jit(solution)/shard_map/all_to_all | solution.py:467
  74.7 5.2 %collective-permute-start.11 = (bf16[16,80,128]{2,1,0:T(8,128)(2,1)S(1)}, bf16[16,80,128]{2,1,0:T(8,128)(2,1)S(1)}, u32[]{:S(2)}, u32[]{:S(2)}) collective-permute-start(bf16[16,80,128]{2,1,0:T(8,128)(2,1)S(1)} %all-to-all-done.1.own_ref), channel_id=1, source_target_pairs={{0,8},{8,0},{1,9},{9,1},{2,10},{10,2},{3,11},{11,3},{4,12},{12,4},... | collective-permute-start | bytes 983048 | tf_op jit(solution)/shard_map/ppermute | solution.py:476
  79.9 1.3 %collective-permute-done.11.got_ref = bf16[16,80,128]{2,1,0:T(8,128)(2,1)S(1)} collective-permute-done((bf16[16,80,128]{2,1,0:T(8,128)(2,1)S(1)}, bf16[16,80,128]{2,1,0:T(8,128)(2,1)S(1)}, u32[]{:S(2)}, u32[]{:S(2)}) %collective-permute-start.11) | collective-permute-done | bytes 327712 | tf_op jit(solution)/shard_map/ppermute | solution.py:476
  81.1 1.2 %shard_map.71 = (f32[2,256,512]{2,1,0:T(8,128)}, f32[256,256]{1,0:T(8,128)}) custom-call(s32[1]{0:T(128)} %bitcast.at_ref.refs_0_, bf16[16,80,128]{2,1,0:T(8,128)(2,1)S(1)} %all-to-all-done.1.own_ref, bf16[16,80,128]{2,1,0:T(8,128)(2,1)S(1)} %collective-permute-done.11.got_ref), custom_call_target="tpu_custom_call" | custom-call | tf_op jit(solution)/shard_map/pallas_call | solution.py:477
  (1 shorter events, 0.0 us)
Async XLA Ops:
  3.2 9.4 %collective-permute-start = (bf16[512,256]{1,0:T(8,128)(2,1)S(1)}, bf16[512,256]{1,0:T(8,128)(2,1)S(1)}, u32[]{:S(2)}, u32[]{:S(2)}) collective-permute-start(bf16[512,256]{1,0:T(8,128)(2,1)S(1)} %get-tuple-element.49.refs_2_), channel_id=1, source_target_pairs={{0,128},{128,0},{1,129},{129,1},{2,130},{130,2},{3,131},{131,3},{4... | collective-permute-start | bytes 786440 | tf_op jit(solution)/shard_map/ppermute | solution.py:410
  5.3 7.0 %collective-permute-start.1 = (bf16[4,64,256]{2,1,0:T(8,128)(2,1)S(1)}, bf16[4,64,256]{2,1,0:T(8,128)(2,1)S(1)}, u32[]{:S(2)}, u32[]{:S(2)}) collective-permute-start(bf16[4,64,256]{2,1,0:T(8,128)(2,1)S(1)} %get-tuple-element.51), channel_id=1, source_target_pairs={{8,16},{16,8},{24,32},{32,24},{40,48},{48,40},{56,64},{64,56},{72,... | collective-permute-start | bytes 393224 | tf_op jit(solution)/shard_map/ppermute | solution.py:411
  12.3 9.0 %collective-permute-start.2 = (bf16[512,256]{1,0:T(8,128)(2,1)S(1)}, bf16[512,256]{1,0:T(8,128)(2,1)S(1)}, u32[]{:S(2)}, u32[]{:S(2)}) collective-permute-start(bf16[512,256]{1,0:T(8,128)(2,1)S(1)} %get-tuple-element.52.refs_2_), channel_id=1, source_target_pairs={{0,128},{128,0},{1,129},{129,1},{2,130},{130,2},{3,131},{131,3},{4... | collective-permute-start | bytes 786440 | tf_op jit(solution)/shard_map/ppermute | solution.py:414
  16.7 9.6 %collective-permute-start.7 = (bf16[512,256]{1,0:T(8,128)(2,1)S(1)}, bf16[512,256]{1,0:T(8,128)(2,1)S(1)}, u32[]{:S(2)}, u32[]{:S(2)}) collective-permute-start(bf16[512,256]{1,0:T(8,128)(2,1)S(1)} %get-tuple-element.67.refs_2_), channel_id=1, source_target_pairs={{0,128},{128,0},{1,129},{129,1},{2,130},{130,2},{3,131},{131,3},{4... | collective-permute-start | bytes 786440 | tf_op jit(solution)/shard_map/ppermute | solution.py:417
  17.9 12.0 %collective-permute-start.6 = (bf16[512,256]{1,0:T(8,128)(2,1)S(1)}, bf16[512,256]{1,0:T(8,128)(2,1)S(1)}, u32[]{:S(2)}, u32[]{:S(2)}) collective-permute-start(bf16[512,256]{1,0:T(8,128)(2,1)S(1)} %get-tuple-element.65.refs_2_), channel_id=1, source_target_pairs={{0,128},{128,0},{1,129},{129,1},{2,130},{130,2},{3,131},{131,3},{4... | collective-permute-start | bytes 786440 | tf_op jit(solution)/shard_map/ppermute | solution.py:418
  18.2 3.0 %collective-permute-start.3 = (bf16[32,256]{1,0:T(8,128)(2,1)S(1)}, bf16[32,256]{1,0:T(8,128)(2,1)S(1)}, u32[]{:S(2)}, u32[]{:S(2)}) collective-permute-start(bf16[32,256]{1,0:T(8,128)(2,1)S(1)} %get-tuple-element.59), channel_id=1, source_target_pairs={{0,1},{1,0},{2,3},{3,2},{4,5},{5,4},{6,7},{7,6},{8,9},{9,8},{10,11... | collective-permute-start | bytes 49160 | tf_op jit(solution)/shard_map/ppermute | solution.py:420
  19.8 1.4 %collective-permute-start.4 = (bf16[32,256]{1,0:T(8,128)(2,1)S(1)}, bf16[32,256]{1,0:T(8,128)(2,1)S(1)}, u32[]{:S(2)}, u32[]{:S(2)}) collective-permute-start(bf16[32,256]{1,0:T(8,128)(2,1)S(1)} %get-tuple-element.60), channel_id=1, source_target_pairs={{1,2},{2,1},{3,4},{4,3},{5,6},{6,5},{9,10},{10,9},{11,12},{12,11},... | collective-permute-start | bytes 49160 | tf_op jit(solution)/shard_map/ppermute | solution.py:421
  21.3 2.6 %collective-permute-start.5 = (bf16[4,64,256]{2,1,0:T(8,128)(2,1)S(1)}, bf16[4,64,256]{2,1,0:T(8,128)(2,1)S(1)}, u32[]{:S(2)}, u32[]{:S(2)}) collective-permute-start(bf16[4,64,256]{2,1,0:T(8,128)(2,1)S(1)} %get-tuple-element.61), channel_id=1, source_target_pairs={{0,8},{8,0},{1,9},{9,1},{2,10},{10,2},{3,11},{11,3},{4,12},{12,4},... | collective-permute-start | bytes 393224 | tf_op jit(solution)/shard_map/ppermute | solution.py:423
  30.8 2.5 %collective-permute-start.8 = (bf16[16,88,128]{2,1,0:T(8,128)(2,1)S(1)}, bf16[16,88,128]{2,1,0:T(8,128)(2,1)S(1)}, u32[]{:S(2)}, u32[]{:S(2)}) collective-permute-start(bf16[16,88,128]{2,1,0:T(8,128)(2,1)S(1)} %get-tuple-element.82), channel_id=1, source_target_pairs={{0,8},{8,0},{1,9},{9,1},{2,10},{10,2},{3,11},{11,3},{4,12},{12,4},... | collective-permute-start | bytes 1081352 | tf_op jit(solution)/shard_map/ppermute | solution.py:441
  52.1 4.6 %collective-permute-start.9 = (bf16[88,128]{1,0:T(8,128)(2,1)S(1)}, bf16[88,128]{1,0:T(8,128)(2,1)S(1)}, u32[]{:S(2)}, u32[]{:S(2)}) collective-permute-start(bf16[88,128]{1,0:T(8,128)(2,1)S(1)} %shard_map.67.own_ref), channel_id=1, source_target_pairs={{0,2},{2,0},{4,6},{6,4},{1,3},{3,1},{5,7},{7,5},{8,10},{10,8},{12,... | collective-permute-start | bytes 67592 | tf_op jit(solution)/shard_map/ppermute | solution.py:451
  56.7 4.9 %collective-permute-start.10 = (bf16[88,128]{1,0:T(8,128)(2,1)S(1)}, bf16[88,128]{1,0:T(8,128)(2,1)S(1)}, u32[]{:S(2)}, u32[]{:S(2)}) collective-permute-start(bf16[88,128]{1,0:T(8,128)(2,1)S(1)} %shard_map.68.own_ref), channel_id=1, source_target_pairs={{0,6},{2,4},{4,2},{6,0},{1,7},{3,5},{5,3},{7,1},{8,14},{10,12},{12... | collective-permute-start | bytes 67592 | tf_op jit(solution)/shard_map/ppermute | solution.py:455
  62.4 12.3 %all-to-all-start.1 = ((bf16[16,80,128]{2,1,0:T(8,128)(2,1)}), bf16[16,80,128]{2,1,0:T(8,128)(2,1)S(1)}, u32[]{:S(2)}, u32[]{:S(2)}) async-start(bf16[16,80,128]{2,1,0:T(8,128)(2,1)} %get-tuple-element.83), calls=%async_computation.1 | async-start | bytes 655360 | tf_op jit(solution)/shard_map/all_to_all | solution.py:467
  74.7 6.5 %collective-permute-start.11 = (bf16[16,80,128]{2,1,0:T(8,128)(2,1)S(1)}, bf16[16,80,128]{2,1,0:T(8,128)(2,1)S(1)}, u32[]{:S(2)}, u32[]{:S(2)}) collective-permute-start(bf16[16,80,128]{2,1,0:T(8,128)(2,1)S(1)} %all-to-all-done.1.own_ref), channel_id=1, source_target_pairs={{0,8},{8,0},{1,9},{9,1},{2,10},{10,2},{3,11},{11,3},{4,12},{12,4},... | collective-permute-start | bytes 983048 | tf_op jit(solution)/shard_map/ppermute | solution.py:476

commit v10 on v9

--- a/solution.py
+++ b/solution.py
@@ -40,7 +40,11 @@
 
 
 def part_of(place):
-    return place >> 2
+    return (place >> 2) & 15
+
+
+def at_end(place, which):
+    return ((place >> (6 + which)) & 1) == 1
 
 
 def gradient(m, coefficients, series):
@@ -205,24 +209,27 @@
     )(place, in_hbm(modes), coefficients, in_hbm(series))
 
 
-def base_kernel(at_ref, m_ref, xa_ref, xb_ref, za_ref, zb_ref, base_ref):
-    levels, rows_x, rows_y, width = m_ref.shape
-    lower, even = core_of(at_ref[0]) == 0, parity_of(at_ref[0]) == 0
+def base_of(level, place, m_ref, xa_ref, xb_ref, za_ref, zb_ref):
+    _, rows_x, rows_y, width = m_ref.shape
+    lower, even = core_of(place) == 0, parity_of(place) == 0
     shape = (rows_x, rows_y, width)
+    f = m_ref[level].astype(F32)
+    xa, xb = xa_ref[level : level + 1].astype(F32), xb_ref[level : level + 1].astype(F32)
+    rows = slice(level * rows_x, (level + 1) * rows_x)
+    za, zb = za_ref[rows, :].astype(F32), zb_ref[rows, :].astype(F32)
+    xlo = jnp.where(at_end(place, 0), 0.0, jnp.where(lower, xb, xa))
+    xhi = jnp.where(at_end(place, 1), 0.0, jnp.where(lower, xa, xb))
+    zlo = jnp.where(at_end(place, 2), 0.0, jnp.where(even, zb, za))
+    zhi = jnp.where(at_end(place, 3), 0.0, jnp.where(even, za, zb))
+    up = jnp.concatenate([xlo, f[:-1]], axis=0)
+    down = jnp.concatenate([f[1:], xhi], axis=0)
     at = lax.broadcasted_iota(jnp.int32, shape, 1)
-    for level in range(levels):
-        f = m_ref[level].astype(F32)
-        xa, xb = xa_ref[level : level + 1].astype(F32), xb_ref[level : level + 1].astype(F32)
-        rows = slice(level * rows_x, (level + 1) * rows_x)
-        za, zb = za_ref[rows, :].astype(F32), zb_ref[rows, :].astype(F32)
-        up = jnp.concatenate([jnp.where(lower, xb, xa), f[:-1]], axis=0)
-        down = jnp.concatenate([f[1:], jnp.where(lower, xa, xb)], axis=0)
-        zlo = jnp.broadcast_to(jnp.where(even, zb, za)[:, None, :], shape)
-        zhi = jnp.broadcast_to(jnp.where(even, za, zb)[:, None, :], shape)
-        left = jnp.where(at == 0, zlo, pltpu.roll(f, 1, 1))
-        right = jnp.where(at == rows_y - 1, zhi, pltpu.roll(f, rows_y - 1, 1))
-        bent = 4.0 * f - (down + up + right + left)
-        base_ref[level] = (f - (ETA * LAM) * bent).reshape(rows_x * rows_y, width)
+    left = jnp.where(at == 0, jnp.broadcast_to(zlo[:, None, :], shape), pltpu.roll(f, 1, 1))
+    right = jnp.where(
+        at == rows_y - 1, jnp.broadcast_to(zhi[:, None, :], shape), pltpu.roll(f, rows_y - 1, 1)
+    )
+    bent = 4.0 * f - (down + up + right + left)
+    return (f - (ETA * LAM) * bent).reshape(rows_x * rows_y, width)
 
 
 def split_squares(squares, rows):
@@ -243,73 +250,93 @@
         out_ref[j, SUM_ROWS:PART_ROWS, :] = squares
 
 
-def step_kernel(level, x_at, first, last, *refs):
-    (at_ref, base_ref, own_ref, got_ref, x_ref), refs = refs[:5], refs[5:]
-    if not first:
-        (proj_in, gram_in, squares_in), refs = refs[:3], refs[3:]
-    if last:
-        moved_ref, keep_ref, send_ref, proj_ref, gram_ref = refs
-    else:
-        moved_ref, proj_ref, gram_ref, squares_ref = refs
+def move(base, own_ref, got_ref):
     grad = own_ref[...].astype(F32) + got_ref[...].astype(F32)
-    moved = (base_ref[level] - ETA * grad).astype(BF16)
+    moved = (base - ETA * grad).astype(BF16)
+    wide = moved.astype(F32)
+    return moved, jnp.sum(wide * wide, axis=0, keepdims=True)
+
+
+def most_kernel(at_ref, m_ref, xa_ref, xb_ref, za_ref, zb_ref, *refs):
+    *refs, base_ref, moved_ref, proj_ref, gram_ref, squares_ref = refs
+    halos = (xa_ref, xb_ref, za_ref, zb_ref)
+    count = len(refs) // 3
+    owns, gots, xs = refs[:count], refs[count : 2 * count], refs[2 * count :]
+    squares = None
+    for level in range(count):
+        moved, part = move(base_of(level, at_ref[0], m_ref, *halos), owns[level], gots[level])
+        squares = part if level == 0 else squares + part
+        moved_ref[level * moved.shape[0] : (level + 1) * moved.shape[0], :] = moved
+        turned = moved.T
+        gram = jnp.dot(turned, moved, preferred_element_type=F32)
+        gram_ref[...] = gram if level == 0 else gram_ref[...] + gram
+        for e in range(proj_ref.shape[0]):
+            x = xs[level][e] if len(xs[level].shape) == 3 else xs[level][e, 0]
+            proj = jnp.dot(turned, x, preferred_element_type=F32)
+            proj_ref[e] = proj if level == 0 else proj_ref[e] + proj
+    squares_ref[...] = squares
+    base_ref[...] = base_of(count, at_ref[0], m_ref, *halos)
+
+
+def last_kernel(at_ref, base_ref, own_ref, got_ref, x_ref, proj_in, gram_in, squares_in, *refs):
+    moved_ref, keep_ref, send_ref, proj_ref, gram_ref = refs
+    moved, squares = move(base_ref[...], own_ref, got_ref)
     moved_ref[...] = moved
-    wide = moved.astype(F32)
-    squares = jnp.sum(wide * wide, axis=0, keepdims=True)
-    if not first:
-        squares = squares + squares_in[...]
+    squares = squares + squares_in[...]
     turned = moved.T
-    gram = jnp.dot(turned, moved, preferred_element_type=F32)
-    gram_ref[...] = gram if first else gram_in[...] + gram
-    for e in range(x_ref.shape[0]):
-        x = x_ref[e] if x_at is None else x_ref[e, x_at]
-        proj = jnp.dot(turned, x, preferred_element_type=F32)
-        proj_ref[e] = proj if first else proj_in[e] + proj
-    if last:
-        core = core_of(at_ref[0])
-        pair = jnp.concatenate([squares[:, 0:128], squares[:, 128:256]], axis=0)
-        packed = split_squares(pair, 8).astype(BF16)
-        emit(send_ref, 1 - core, proj_ref, gram_ref, packed)
-        emit(keep_ref, core, proj_ref, gram_ref, packed)
-    else:
-        squares_ref[...] = squares
-
-
-def step_level(level, x_at, place, base, own, got, series, carry):
-    members, frames = series.shape[0], series.shape[-1]
-    rows, width = own.shape
-    first, last = carry is None, level == base.shape[0] - 1
-    args = [place, base, own, got, series]
-    if not first:
-        args += list(carry)
+    gram_ref[...] = gram_in[...] + jnp.dot(turned, moved, preferred_element_type=F32)
+    for e in range(proj_ref.shape[0]):
+        proj = jnp.dot(turned, x_ref[e, x_ref.shape[1] - 1], preferred_element_type=F32)
+        proj_ref[e] = proj_in[e] + proj
+    core = core_of(at_ref[0])
+    pair = jnp.concatenate([squares[:, 0:128], squares[:, 128:256]], axis=0)
+    packed = split_squares(pair, 8).astype(BF16)
+    emit(send_ref, 1 - core, proj_ref, gram_ref, packed)
+    emit(keep_ref, core, proj_ref, gram_ref, packed)
+
+
+def step_cost(members, cells, frames, width):
+    return pl.CostEstimate(
+        flops=2 * cells * width * (width + members * frames),
+        bytes_accessed=2 * cells * (4 * width + members * frames),
+        transcendentals=0,
+    )
+
+
+def steps(place, modes, halos, owns, gots, series):
+    members, frames = series[0].shape[0], series[0].shape[-1]
+    cells, width = owns[0].shape
+    most = len(owns) - 1
     sums = [
         jax.ShapeDtypeStruct((members, width, frames), F32),
         jax.ShapeDtypeStruct((width, width), F32),
         jax.ShapeDtypeStruct((1, width), F32),
     ]
-    outs = [jax.ShapeDtypeStruct((rows, width), BF16)]
-    scratch, aliases = [], {}
-    if last:
-        outs += [jax.ShapeDtypeStruct((PARTS, PART_ROWS, 128), BF16)] * 2
-        scratch = [pltpu.VMEM(s.shape, F32) for s in sums[:2]]
-    else:
-        outs += sums
-        if not first:
-            aliases = {5 + i: 1 + i for i in range(3)}
-    return pl.pallas_call(
-        functools.partial(step_kernel, level, x_at, first, last),
-        in_specs=[SM] + [VM] * (len(args) - 1),
-        out_specs=[VM] * len(outs),
-        out_shape=outs,
-        scratch_shapes=scratch,
-        input_output_aliases=aliases,
-        compiler_params=PARAMS,
-        cost_estimate=pl.CostEstimate(
-            flops=2 * rows * width * (width + members * frames),
-            bytes_accessed=2 * rows * (4 * width + members * frames),
-            transcendentals=0,
-        ),
-    )(*args)
+    args = [modes, *halos, *owns[:most], *gots[:most], *series[:most]]
+    base, moved, *carry = pl.pallas_call(
+        most_kernel,
+        in_specs=[SM] + [VM] * len(args),
+        out_specs=[VM] * 5,
+        out_shape=[
+            jax.ShapeDtypeStruct((cells, width), F32),
+            jax.ShapeDtypeStruct((most * cells, width), BF16),
+            *sums,
+        ],
+        compiler_params=PARAMS,
+        cost_estimate=step_cost(members, most * cells, frames, width),
+    )(place, *args)
+    args = [base, owns[most], gots[most], series[most], *carry]
+    tail, keep, send = pl.pallas_call(
+        last_kernel,
+        in_specs=[SM] + [VM] * len(args),
+        out_specs=[VM] * 3,
+        out_shape=[jax.ShapeDtypeStruct((cells, width), BF16)]
+        + [jax.ShapeDtypeStruct((PARTS, PART_ROWS, 128), BF16)] * 2,
+        scratch_shapes=[pltpu.VMEM(s.shape, F32) for s in sums[:2]],
+        compiler_params=PARAMS,
+        cost_estimate=step_cost(members, cells, frames, width),
+    )(place, *args)
+    return [moved, tail], keep, send
 
 
 def whole_squares(part):
@@ -402,13 +429,17 @@
     core = lax.axis_index("c").astype(jnp.int32)
     parity = lax.axis_index("zl").astype(jnp.int32)
     part = lax.axis_index(GROUP).astype(jnp.int32)
-    place = (core + 2 * parity + 4 * part).reshape(1)
+    x_at, z_at = lax.axis_index(SX), lax.axis_index(SY)
+    place = core + 2 * parity + 4 * part
+    for i, end in enumerate((x_at == 0, x_at == n_sx - 1, z_at == 0, z_at == n_z - 1)):
+        place = place + end.astype(jnp.int32) * (64 << i)
+    place = place.reshape(1)
     series = snapshots.reshape(members, levels, cells, frames)
     swap = [(0, 1), (1, 0)]
 
     g0, coefficients, x0, edge_b = first_grad(place, modes, coefficients, series)
     got0 = lax.ppermute(g0, "ens", swap)
-    xb = lax.ppermute(edge_b, SX, both_ways([(i, i + 1) for i in range(1, n_sx - 1, 2)]))
+    xb = lax.ppermute(edge_b, SX, both_ways([(i, (i + 1) % n_sx) for i in range(1, n_sx, 2)]))
     g1, x1 = second_grad(modes, coefficients, series, 1)
     g1, xb = lax.optimization_barrier((g1, xb))
     got1 = lax.ppermute(g1, "ens", swap)
@@ -418,24 +449,17 @@
     got3 = lax.ppermute(g3, "ens", swap)
     got0, row_a, row_b = lax.optimization_barrier((got0, row_a, row_b))
     za = lax.ppermute(row_a, SY, both_ways([(i, i + 1) for i in range(0, n_z, 2)]))
-    zb = lax.ppermute(row_b, SY, both_ways([(i, i + 1) for i in range(1, n_z - 1, 2)]))
+    zb = lax.ppermute(row_b, SY, both_ways([(i, (i + 1) % n_z) for i in range(1, n_z, 2)]))
     got1, edge_a, za, zb = lax.optimization_barrier((got1, edge_a, za, zb))
     xa = lax.ppermute(edge_a, "c", swap)
-    base = pl.pallas_call(
-        base_kernel,
-        in_specs=[SM] + [VM] * 5,
-        out_specs=VM,
-        out_shape=jax.ShapeDtypeStruct((levels, cells, width), F32),
-        compiler_params=PARAMS,
-        cost_estimate=pl.CostEstimate(flops=12 * local_cells * width, bytes_accessed=6 * local_cells * width, transcendentals=0),
-    )(place, modes, xa, xb, za, zb)
-
-    moved, carry = [], None
-    work = [(None, g0, got0, x0), (None, g1, got1, x1), (0, g2, got2, series), (1, g3, got3, series)]
-    for level, (x_at, own, got, x) in enumerate(work):
-        m, *carry = step_level(level, x_at, place, base, own, got, x, carry)
-        moved.append(m)
-    keep, send = carry
+    moved, keep, send = steps(
+        place,
+        modes,
+        (xa, xb, za, zb),
+        (g0, g1, g2, g3),
+        (got0, got1, got2, got3),
+        (x0, x1, series, series),
+    )
 
     part_shape = jax.ShapeDtypeStruct((PARTS, PART_ROWS, 128), BF16)
     other = lax.ppermute(send, "c", swap)

time: 82.6 us -> 82.4 us (level)
  starting transfers between devices: 29.2 us -> 40.5 us
  blocking collectives: 18.6 us -> 10.7 us
  waiting for transfers between devices: 17.3 us -> 14.4 us
    ppermute x1, starting transfers between devices: 1.58 us -> 9.78 us  [local(): xa = lax.ppermute(edge_a, 'c', swap)]
    all_to_all x1, blocking collectives: 18.6 us -> 10.7 us  [local(): parts = lax.all_to_all(joined, GROUP, 0, 0)]
    ppermute x1, waiting for transfers between devices: 2.84 us -> 0.01 us  [local(): got3 = lax.ppermute(g3, 'ens', swap)]
    ppermute x2, starting transfers between devices: 4.68 us -> 6.82 us  [the longest x1 4.69 us: local(): lax.ppermute(row_b, SY, both_ways([(i, (i + 1) % n_z) for i in range(1, n...]
    ppermute x1, starting transfers between devices: 3.03 us -> 4.58 us  [local(): near = lax.ppermute(line, 'zh', [(i, i ^ 3) for i in range(pairs)])]
    ppermute x2, waiting for transfers between devices: 0.51 us -> 1.66 us  [the longest x1 1.12 us: local(): lax.ppermute(row_b, SY, both_ways([(i, (i + 1) % n_z) for i in range(1, n...]
    pallas_call x5 -> x2, Pallas kernels: 4.07 us -> 3.32 us  [the longest x1 2.42 us: steps(): pl.pallas_call(most_kernel, in_specs=[SM] + [VM] * len(args), out_specs=[...]
  transfers between devices with their start and end apart: 13 -> 13, of which waited for: 9 -> 8; matrix products, arithmetic and copies ran while one was open for 0% -> 0% of each run, Pallas kernels for 13% -> 12%
where the time goes in v10:
time: 82.4 us; the launch traced here: 82.1 us
  starting transfers between devices  40.5 us (49%)
  Pallas kernels  15.8 us (19%)
  waiting for transfers between devices  14.4 us (17%)
  blocking collectives  10.7 us (13%)
    all_to_all x1, blocking collectives, local(): parts = lax.all_to_all(joined, GROUP, 0, 0)  10.7 us
    ppermute x1, starting transfers between devices, local(): xa = lax.ppermute(edge_a, 'c', swap)  9.78 us
    all_to_all x1, waiting for transfers between devices, local(): half = lax.all_to_all(spread, GROUP, 0, 0)  6.59 us
    ppermute x1, starting transfers between devices, local(): other_half = lax.ppermute(half, 'c', swap)  5.22 us
    ppermute x1, starting transfers between devices, local(): lax.ppermute(row_b, SY, both_ways([(i, (i + 1) % n_z) for i in range(1, n...  4.69 us
    ppermute x1, starting transfers between devices, local(): near = lax.ppermute(line, 'zh', [(i, i ^ 3) for i in range(pairs)])  4.58 us
    all_to_all x1, starting transfers between devices, local(): half = lax.all_to_all(spread, GROUP, 0, 0)  4.32 us
    pallas_call x1, Pallas kernels, rest_grad(): pl.pallas_call(functools.partial(rest_grad_kernel, begin), in_specs=[SM,...  4.11 us
  transfers between devices with their start and end apart: 13, of which 8 were waited for; matrix products, arithmetic and copies ran while one was open for 0% of the time, Pallas kernels for 12%

profile of v10, /device:TPU:1, one launch (start us, length us, event | category | flops | bytes accessed | tf_op | source)
XLA Modules:
  0.0 82.1 jit_solution(3291713793367458449)
XLA Ops:
  0.7 2.5 %shard_map.58 = (bf16[512,256]{1,0:T(8,128)(2,1)S(1)}, bf16[2,256,512]{2,1,0:T(8,128)(2,1)S(1)}, bf16[2,512,512]{2,1,0:T(8,128)(2,1)S(1)}, bf16[4,64,256]{2,1,0:T(8,128)(2,1)S(1)}) custom-call(s32[1]{0:T(128)} %bitcast.at_ref, bf16[4,8,64,256]{3,2,1,0:T(8,128)(2,1)} %m_hbm.5, bf16[2,256,512]{2,1,0:T(8,128)(2,1)} %c_hbm.1, bf16[2,4,512,512]{3,2,1,0:T(8,128)(2,1)} %bitcast.3), custom_call_target="tpu_custom_call" | custom-call | flops 536870912 | bytes 2097152 | tf_op jit(solution)/shard_map/pallas_call | solution.py:154
  3.2 2.1 %collective-permute-start = (bf16[512,256]{1,0:T(8,128)(2,1)S(1)}, bf16[512,256]{1,0:T(8,128)(2,1)S(1)}, u32[]{:S(2)}, u32[]{:S(2)}) collective-permute-start(bf16[512,256]{1,0:T(8,128)(2,1)S(1)} %get-tuple-element.42.refs_0_), channel_id=1, source_target_pairs={{0,128},{128,0},{1,129},{129,1},{2,130},{130,2},{3,131},{131,3},{4... | collective-permute-start | bytes 786440 | tf_op jit(solution)/shard_map/ppermute | solution.py:441
  5.3 2.1 %collective-permute-start.1 = (bf16[4,64,256]{2,1,0:T(8,128)(2,1)S(1)}, bf16[4,64,256]{2,1,0:T(8,128)(2,1)S(1)}, u32[]{:S(2)}, u32[]{:S(2)}) collective-permute-start(bf16[4,64,256]{2,1,0:T(8,128)(2,1)S(1)} %get-tuple-element.44), channel_id=1, source_target_pairs={{8,16},{16,8},{24,32},{32,24},{40,48},{48,40},{56,64},{64,56},{72,... | collective-permute-start | bytes 393224 | tf_op jit(solution)/shard_map/ppermute | solution.py:442
  7.5 2.4 %shard_map.59 = (bf16[512,256]{1,0:T(8,128)(2,1)S(1)}, bf16[2,512,512]{2,1,0:T(8,128)(2,1)S(1)}) custom-call(bf16[4,8,64,256]{3,2,1,0:T(8,128)(2,1)} %m_hbm.5, bf16[2,256,512]{2,1,0:T(8,128)(2,1)S(1)} %get-tuple-element.46.c_ref, bf16[2,4,512,512]{3,2,1,0:T(8,128)(2,1)} %bitcast.4), custom_call_target="tpu_custom_call" | custom-call | flops 536870912 | bytes 2097152 | tf_op jit(solution)/shard_map/pallas_call | solution.py:172
  9.9 0.5 collective-permute-done.1.xb_ref
  10.4 0.3 collective-permute-start.2
  10.7 0.0 collective-permute-done.refs_3_
  10.7 4.1 %shard_map.60 = (bf16[512,256]{1,0:T(8,128)(2,1)S(1)}, bf16[512,256]{1,0:T(8,128)(2,1)S(1)}, bf16[4,8,64,256]{3,2,1,0:T(8,128)(2,1)S(1)}, bf16[2,2,512,512]{3,2,...) custom-call(s32[1]{0:T(128)} %bitcast.at_ref, ...), custom_call_target="tpu_custom_call" | custom-call | flops 1073741824 | bytes 3670016 | tf_op jit(solution)/shard_map/pallas_call | solution.py:198
  14.8 1.7 %collective-permute-start.6 = (bf16[512,256]{1,0:T(8,128)(2,1)S(1)}, bf16[512,256]{1,0:T(8,128)(2,1)S(1)}, u32[]{:S(2)}, u32[]{:S(2)}) collective-permute-start(bf16[512,256]{1,0:T(8,128)(2,1)S(1)} %get-tuple-element.58.refs_2_), channel_id=1, source_target_pairs={{0,128},{128,0},{1,129},{129,1},{2,130},{130,2},{3,131},{131,3},{4... | collective-permute-start | bytes 786440 | tf_op jit(solution)/shard_map/ppermute | solution.py:448
  16.4 0.1 collective-permute-start.7
  16.5 2.1 %collective-permute-start.3 = (bf16[32,256]{1,0:T(8,128)(2,1)S(1)}, bf16[32,256]{1,0:T(8,128)(2,1)S(1)}, u32[]{:S(2)}, u32[]{:S(2)}) collective-permute-start(bf16[32,256]{1,0:T(8,128)(2,1)S(1)} %get-tuple-element.52), channel_id=1, source_target_pairs={{0,1},{1,0},{2,3},{3,2},{4,5},{5,4},{6,7},{7,6},{8,9},{9,8},{10,11... | collective-permute-start | bytes 49160 | tf_op jit(solution)/shard_map/ppermute | solution.py:451
  18.6 4.7 %collective-permute-start.4 = (bf16[32,256]{1,0:T(8,128)(2,1)S(1)}, bf16[32,256]{1,0:T(8,128)(2,1)S(1)}, u32[]{:S(2)}, u32[]{:S(2)}) collective-permute-start(bf16[32,256]{1,0:T(8,128)(2,1)S(1)} %get-tuple-element.53), channel_id=1, source_target_pairs={{1,2},{2,1},{3,4},{4,3},{5,6},{6,5},{7,0},{0,7},{9,10},{10,9},{11,... | collective-permute-start | bytes 49160 | tf_op jit(solution)/shard_map/ppermute | solution.py:452
  23.3 0.0 collective-permute-done.3.za_ref
  23.3 1.1 %collective-permute-done.4.zb_ref = bf16[32,256]{1,0:T(8,128)(2,1)S(1)} collective-permute-done((bf16[32,256]{1,0:T(8,128)(2,1)S(1)}, bf16[32,256]{1,0:T(8,128)(2,1)S(1)}, u32[]{:S(2)}, u32[]{:S(2)}) %collective-permute-start.4) | collective-permute-done | bytes 16416 | tf_op jit(solution)/shard_map/ppermute | solution.py:452
  24.4 0.0 collective-permute-done.2.refs_4_
  24.4 9.8 %collective-permute-start.5 = (bf16[4,64,256]{2,1,0:T(8,128)(2,1)S(1)}, bf16[4,64,256]{2,1,0:T(8,128)(2,1)S(1)}, u32[]{:S(2)}, u32[]{:S(2)}) collective-permute-start(bf16[4,64,256]{2,1,0:T(8,128)(2,1)S(1)} %get-tuple-element.54), channel_id=1, source_target_pairs={{0,8},{8,0},{1,9},{9,1},{2,10},{10,2},{3,11},{11,3},{4,12},{12,4},... | collective-permute-start | bytes 393224 | tf_op jit(solution)/shard_map/ppermute | solution.py:454
  34.2 1.0 %collective-permute-done.5.xa_ref = bf16[4,64,256]{2,1,0:T(8,128)(2,1)S(1)} collective-permute-done((bf16[4,64,256]{2,1,0:T(8,128)(2,1)S(1)}, bf16[4,64,256]{2,1,0:T(8,128)(2,1)S(1)}, u32[]{:S(2)}, u32[]{:S(2)}) %collective-permute-start.5) | collective-permute-done | bytes 131104 | tf_op jit(solution)/shard_map/ppermute | solution.py:454
  35.2 0.0 collective-permute-done.6.refs_5_
  35.2 2.4 %shard_map.61 = (f32[512,256]{1,0:T(8,128)S(1)}, bf16[1536,256]{1,0:T(8,128)(2,1)S(1)}, f32[2,256,512]{2,1,0:T(8,128)S(1)}, f32[256,256]{1,0:T(8,128)S(1)}, f32[1,256]{1,0:T(1,128)S(1)}) custom-call(s32[1]{0:T(128)} %bitcast.at_ref, bf16[4,8,64,256]{3,2,1,0:T(8,128)(2,1)S(1)} %get-tuple-element.47.m_ref, ...), custom_call_target="tpu_custom_call" | custom-call | flops 1006632960 | bytes 6291456 | tf_op jit(solution)/shard_map/pallas_call | solution.py:316
  37.6 0.0 collective-permute-done.7.got_ref
  37.6 0.9 %shard_map.62 = (bf16[512,256]{1,0:T(8,128)(2,1)S(1)}, bf16[16,88,128]{2,1,0:T(8,128)(2,1)S(1)}, bf16[16,88,128]{2,1,0:T(8,128)(2,1)S(1)}) custom-call(s32[1]{0:T(128)} %bitcast.at_ref, f32[512,256]{1,0:T(8,128)S(1)} %get-tuple-element.64.base_ref, bf16[512,256]{1,0:T(8,128)(2,1)S(1)} %get-tuple-element.65.own_ref, ...), custom_call_target="tpu_custom_call" | custom-call | flops 335544320 | bytes 2097152 | tf_op jit(solution)/shard_map/pallas_call | solution.py:329
  38.5 0.6 collective-permute-start.8
  39.2 1.3 %collective-permute-done.8.got_ref = bf16[16,88,128]{2,1,0:T(8,128)(2,1)S(1)} collective-permute-done((bf16[16,88,128]{2,1,0:T(8,128)(2,1)S(1)}, bf16[16,88,128]{2,1,0:T(8,128)(2,1)S(1)}, u32[]{:S(2)}, u32[]{:S(2)}) %collective-permute-start.8) | collective-permute-done | bytes 360480 | tf_op jit(solution)/shard_map/ppermute | solution.py:465
  40.5 0.1 shard_map.63
  40.6 10.7 %all_to_all.10.in_ref = bf16[16,88,128]{2,1,0:T(8,128)(2,1)S(1)} all-to-all(bf16[16,88,128]{2,1,0:T(8,128)(2,1)S(1)} %shard_map.63), channel_id=1, replica_groups=mesh['ens'=2,'xh'=2,'y'=4,'c'=2,'zh'=4,'zl'=2] {'xh','y','zl'}, dimensions={0} | all-to-all | bytes 720896 | tf_op jit(solution)/shard_map/all_to_all | solution.py:469
  51.3 0.1 shard_map.64.own_ref
  51.3 3.0 %collective-permute-start.9 = (bf16[88,128]{1,0:T(8,128)(2,1)S(1)}, bf16[88,128]{1,0:T(8,128)(2,1)S(1)}, u32[]{:S(2)}, u32[]{:S(2)}) collective-permute-start(bf16[88,128]{1,0:T(8,128)(2,1)S(1)} %shard_map.64.own_ref), channel_id=1, source_target_pairs={{0,2},{2,0},{4,6},{6,4},{1,3},{3,1},{5,7},{7,5},{8,10},{10,8},{12,... | collective-permute-start | bytes 67592 | tf_op jit(solution)/shard_map/ppermute | solution.py:475
  54.3 1.2 %collective-permute-done.9.got_ref = bf16[88,128]{1,0:T(8,128)(2,1)S(1)} collective-permute-done((bf16[88,128]{1,0:T(8,128)(2,1)S(1)}, bf16[88,128]{1,0:T(8,128)(2,1)S(1)}, u32[]{:S(2)}, u32[]{:S(2)}) %collective-permute-start.9) | collective-permute-done | bytes 22560 | tf_op jit(solution)/shard_map/ppermute | solution.py:475
  55.5 4.6 %collective-permute-start.10 = (bf16[88,128]{1,0:T(8,128)(2,1)S(1)}, bf16[88,128]{1,0:T(8,128)(2,1)S(1)}, u32[]{:S(2)}, u32[]{:S(2)}) collective-permute-start(bf16[88,128]{1,0:T(8,128)(2,1)S(1)} %shard_map.65.own_ref), channel_id=1, source_target_pairs={{0,6},{2,4},{4,2},{6,0},{1,7},{3,5},{5,3},{7,1},{8,14},{10,12},{12... | collective-permute-start | bytes 67592 | tf_op jit(solution)/shard_map/ppermute | solution.py:479
  60.1 1.4 %collective-permute-done.10.got_ref = bf16[88,128]{1,0:T(8,128)(2,1)S(1)} collective-permute-done((bf16[88,128]{1,0:T(8,128)(2,1)S(1)}, bf16[88,128]{1,0:T(8,128)(2,1)S(1)}, u32[]{:S(2)}, u32[]{:S(2)}) %collective-permute-start.10) | collective-permute-done | bytes 22560 | tf_op jit(solution)/shard_map/ppermute | solution.py:479
  61.5 0.9 %shard_map.66 = (bf16[16,80,128]{2,1,0:T(8,128)(2,1)}, f32[2,128]{1,0:T(2,128)S(1)}) custom-call(s32[1]{0:T(128)} %bitcast.at_ref, bf16[88,128]{1,0:T(8,128)(2,1)S(1)} %shard_map.65.own_ref, bf16[88,128]{1,0:T(8,128)(2,1)S(1)} %collective-permute-done.10.got_ref), custom_call_target="tpu_custom_call" | custom-call | tf_op jit(solution)/shard_map/pallas_call | solution.py:480
  62.3 4.3 %all-to-all-start.1 = ((bf16[16,80,128]{2,1,0:T(8,128)(2,1)}), bf16[16,80,128]{2,1,0:T(8,128)(2,1)S(1)}, u32[]{:S(2)}, u32[]{:S(2)}) async-start(bf16[16,80,128]{2,1,0:T(8,128)(2,1)} %get-tuple-element.71), calls=%async_computation.1 | async-start | bytes 655360 | tf_op jit(solution)/shard_map/all_to_all | solution.py:491
  66.7 1.2 %shard_map.67 = bf16[2048,256]{1,0:T(8,128)(2,1)} custom-call(f32[2,128]{1,0:T(2,128)S(1)} %get-tuple-element.72.shrink_ref, bf16[1536,256]{1,0:T(8,128)(2,1)S(1)} %get-tuple-element.73.refs_0_, bf16[512,256]{1,0:T(8,128)(2,1)S(1)} %get-tuple-element.74.refs_1_), custom_call_target="tpu_custom_call" | custom-call | tf_op jit(solution)/shard_map/pallas_call | solution.py:492
  67.8 6.6 %all-to-all-done.1.own_ref = bf16[16,80,128]{2,1,0:T(8,128)(2,1)S(1)} async-done(((bf16[16,80,128]{2,1,0:T(8,128)(2,1)}), bf16[16,80,128]{2,1,0:T(8,128)(2,1)S(1)}, u32[]{:S(2)}, u32[]{:S(2)}) %all-to-all-start.1) | async-done | bytes 327712 | tf_op jit(solution)/shard_map/all_to_all | solution.py:491
  74.4 5.2 %collective-permute-start.11 = (bf16[16,80,128]{2,1,0:T(8,128)(2,1)S(1)}, bf16[16,80,128]{2,1,0:T(8,128)(2,1)S(1)}, u32[]{:S(2)}, u32[]{:S(2)}) collective-permute-start(bf16[16,80,128]{2,1,0:T(8,128)(2,1)S(1)} %all-to-all-done.1.own_ref), channel_id=1, source_target_pairs={{0,8},{8,0},{1,9},{9,1},{2,10},{10,2},{3,11},{11,3},{4,12},{12,4},... | collective-permute-start | bytes 983048 | tf_op jit(solution)/shard_map/ppermute | solution.py:500
  79.7 1.3 %collective-permute-done.11.got_ref = bf16[16,80,128]{2,1,0:T(8,128)(2,1)S(1)} collective-permute-done((bf16[16,80,128]{2,1,0:T(8,128)(2,1)S(1)}, bf16[16,80,128]{2,1,0:T(8,128)(2,1)S(1)}, u32[]{:S(2)}, u32[]{:S(2)}) %collective-permute-start.11) | collective-permute-done | bytes 327712 | tf_op jit(solution)/shard_map/ppermute | solution.py:500
  80.9 1.2 %shard_map.68 = (f32[2,256,512]{2,1,0:T(8,128)}, f32[256,256]{1,0:T(8,128)}) custom-call(s32[1]{0:T(128)} %bitcast.at_ref, bf16[16,80,128]{2,1,0:T(8,128)(2,1)S(1)} %all-to-all-done.1.own_ref, bf16[16,80,128]{2,1,0:T(8,128)(2,1)S(1)} %collective-permute-done.11.got_ref), custom_call_target="tpu_custom_call" | custom-call | tf_op jit(solution)/shard_map/pallas_call | solution.py:501
  (1 shorter events, 0.0 us)
Async XLA Ops:
  3.2 7.5 %collective-permute-start = (bf16[512,256]{1,0:T(8,128)(2,1)S(1)}, bf16[512,256]{1,0:T(8,128)(2,1)S(1)}, u32[]{:S(2)}, u32[]{:S(2)}) collective-permute-start(bf16[512,256]{1,0:T(8,128)(2,1)S(1)} %get-tuple-element.42.refs_0_), channel_id=1, source_target_pairs={{0,128},{128,0},{1,129},{129,1},{2,130},{130,2},{3,131},{131,3},{4... | collective-permute-start | bytes 786440 | tf_op jit(solution)/shard_map/ppermute | solution.py:441
  5.3 5.1 %collective-permute-start.1 = (bf16[4,64,256]{2,1,0:T(8,128)(2,1)S(1)}, bf16[4,64,256]{2,1,0:T(8,128)(2,1)S(1)}, u32[]{:S(2)}, u32[]{:S(2)}) collective-permute-start(bf16[4,64,256]{2,1,0:T(8,128)(2,1)S(1)} %get-tuple-element.44), channel_id=1, source_target_pairs={{8,16},{16,8},{24,32},{32,24},{40,48},{48,40},{56,64},{64,56},{72,... | collective-permute-start | bytes 393224 | tf_op jit(solution)/shard_map/ppermute | solution.py:442
  10.4 14.0 %collective-permute-start.2 = (bf16[512,256]{1,0:T(8,128)(2,1)S(1)}, bf16[512,256]{1,0:T(8,128)(2,1)S(1)}, u32[]{:S(2)}, u32[]{:S(2)}) collective-permute-start(bf16[512,256]{1,0:T(8,128)(2,1)S(1)} %get-tuple-element.45.refs_1_), channel_id=1, source_target_pairs={{0,128},{128,0},{1,129},{129,1},{2,130},{130,2},{3,131},{131,3},{4... | collective-permute-start | bytes 786440 | tf_op jit(solution)/shard_map/ppermute | solution.py:445
  14.8 20.4 %collective-permute-start.6 = (bf16[512,256]{1,0:T(8,128)(2,1)S(1)}, bf16[512,256]{1,0:T(8,128)(2,1)S(1)}, u32[]{:S(2)}, u32[]{:S(2)}) collective-permute-start(bf16[512,256]{1,0:T(8,128)(2,1)S(1)} %get-tuple-element.58.refs_2_), channel_id=1, source_target_pairs={{0,128},{128,0},{1,129},{129,1},{2,130},{130,2},{3,131},{131,3},{4... | collective-permute-start | bytes 786440 | tf_op jit(solution)/shard_map/ppermute | solution.py:448
  16.4 21.2 %collective-permute-start.7 = (bf16[512,256]{1,0:T(8,128)(2,1)S(1)}, bf16[512,256]{1,0:T(8,128)(2,1)S(1)}, u32[]{:S(2)}, u32[]{:S(2)}) collective-permute-start(bf16[512,256]{1,0:T(8,128)(2,1)S(1)} %get-tuple-element.65.own_ref), channel_id=1, source_target_pairs={{0,128},{128,0},{1,129},{129,1},{2,130},{130,2},{3,131},{131,3},{4... | collective-permute-start | bytes 786440 | tf_op jit(solution)/shard_map/ppermute | solution.py:449
  16.5 6.7 %collective-permute-start.3 = (bf16[32,256]{1,0:T(8,128)(2,1)S(1)}, bf16[32,256]{1,0:T(8,128)(2,1)S(1)}, u32[]{:S(2)}, u32[]{:S(2)}) collective-permute-start(bf16[32,256]{1,0:T(8,128)(2,1)S(1)} %get-tuple-element.52), channel_id=1, source_target_pairs={{0,1},{1,0},{2,3},{3,2},{4,5},{5,4},{6,7},{7,6},{8,9},{9,8},{10,11... | collective-permute-start | bytes 49160 | tf_op jit(solution)/shard_map/ppermute | solution.py:451
  18.6 5.8 %collective-permute-start.4 = (bf16[32,256]{1,0:T(8,128)(2,1)S(1)}, bf16[32,256]{1,0:T(8,128)(2,1)S(1)}, u32[]{:S(2)}, u32[]{:S(2)}) collective-permute-start(bf16[32,256]{1,0:T(8,128)(2,1)S(1)} %get-tuple-element.53), channel_id=1, source_target_pairs={{1,2},{2,1},{3,4},{4,3},{5,6},{6,5},{7,0},{0,7},{9,10},{10,9},{11,... | collective-permute-start | bytes 49160 | tf_op jit(solution)/shard_map/ppermute | solution.py:452
  24.4 10.8 %collective-permute-start.5 = (bf16[4,64,256]{2,1,0:T(8,128)(2,1)S(1)}, bf16[4,64,256]{2,1,0:T(8,128)(2,1)S(1)}, u32[]{:S(2)}, u32[]{:S(2)}) collective-permute-start(bf16[4,64,256]{2,1,0:T(8,128)(2,1)S(1)} %get-tuple-element.54), channel_id=1, source_target_pairs={{0,8},{8,0},{1,9},{9,1},{2,10},{10,2},{3,11},{11,3},{4,12},{12,4},... | collective-permute-start | bytes 393224 | tf_op jit(solution)/shard_map/ppermute | solution.py:454
  38.5 1.9 %collective-permute-start.8 = (bf16[16,88,128]{2,1,0:T(8,128)(2,1)S(1)}, bf16[16,88,128]{2,1,0:T(8,128)(2,1)S(1)}, u32[]{:S(2)}, u32[]{:S(2)}) collective-permute-start(bf16[16,88,128]{2,1,0:T(8,128)(2,1)S(1)} %get-tuple-element.70), channel_id=1, source_target_pairs={{0,8},{8,0},{1,9},{9,1},{2,10},{10,2},{3,11},{11,3},{4,12},{12,4},... | collective-permute-start | bytes 1081352 | tf_op jit(solution)/shard_map/ppermute | solution.py:465
  51.3 4.2 %collective-permute-start.9 = (bf16[88,128]{1,0:T(8,128)(2,1)S(1)}, bf16[88,128]{1,0:T(8,128)(2,1)S(1)}, u32[]{:S(2)}, u32[]{:S(2)}) collective-permute-start(bf16[88,128]{1,0:T(8,128)(2,1)S(1)} %shard_map.64.own_ref), channel_id=1, source_target_pairs={{0,2},{2,0},{4,6},{6,4},{1,3},{3,1},{5,7},{7,5},{8,10},{10,8},{12,... | collective-permute-start | bytes 67592 | tf_op jit(solution)/shard_map/ppermute | solution.py:475
  55.5 5.9 %collective-permute-start.10 = (bf16[88,128]{1,0:T(8,128)(2,1)S(1)}, bf16[88,128]{1,0:T(8,128)(2,1)S(1)}, u32[]{:S(2)}, u32[]{:S(2)}) collective-permute-start(bf16[88,128]{1,0:T(8,128)(2,1)S(1)} %shard_map.65.own_ref), channel_id=1, source_target_pairs={{0,6},{2,4},{4,2},{6,0},{1,7},{3,5},{5,3},{7,1},{8,14},{10,12},{12... | collective-permute-start | bytes 67592 | tf_op jit(solution)/shard_map/ppermute | solution.py:479
  62.3 12.1 %all-to-all-start.1 = ((bf16[16,80,128]{2,1,0:T(8,128)(2,1)}), bf16[16,80,128]{2,1,0:T(8,128)(2,1)S(1)}, u32[]{:S(2)}, u32[]{:S(2)}) async-start(bf16[16,80,128]{2,1,0:T(8,128)(2,1)} %get-tuple-element.71), calls=%async_computation.1 | async-start | bytes 655360 | tf_op jit(solution)/shard_map/all_to_all | solution.py:491
  74.4 6.5 %collective-permute-start.11 = (bf16[16,80,128]{2,1,0:T(8,128)(2,1)S(1)}, bf16[16,80,128]{2,1,0:T(8,128)(2,1)S(1)}, u32[]{:S(2)}, u32[]{:S(2)}) collective-permute-start(bf16[16,80,128]{2,1,0:T(8,128)(2,1)S(1)} %all-to-all-done.1.own_ref), channel_id=1, source_target_pairs={{0,8},{8,0},{1,9},{9,1},{2,10},{10,2},{3,11},{11,3},{4,12},{12,4},... | collective-permute-start | bytes 983048 | tf_op jit(solution)/shard_map/ppermute | solution.py:500

commit v11 on v10

--- a/solution.py
+++ b/solution.py
@@ -441,13 +441,12 @@
     got0 = lax.ppermute(g0, "ens", swap)
     xb = lax.ppermute(edge_b, SX, both_ways([(i, (i + 1) % n_sx) for i in range(1, n_sx, 2)]))
     g1, x1 = second_grad(modes, coefficients, series, 1)
-    g1, xb = lax.optimization_barrier((g1, xb))
     got1 = lax.ppermute(g1, "ens", swap)
-    coefficients, got0, _ = lax.optimization_barrier((coefficients, got0, g1))
+    coefficients, _ = lax.optimization_barrier((coefficients, g1))
     g2, g3, modes, series, edge_a, row_a, row_b = rest_grad(place, modes, coefficients, series, 2)
     got2 = lax.ppermute(g2, "ens", swap)
     got3 = lax.ppermute(g3, "ens", swap)
-    got0, row_a, row_b = lax.optimization_barrier((got0, row_a, row_b))
+    got0, xb, row_a, row_b = lax.optimization_barrier((got0, xb, row_a, row_b))
     za = lax.ppermute(row_a, SY, both_ways([(i, i + 1) for i in range(0, n_z, 2)]))
     zb = lax.ppermute(row_b, SY, both_ways([(i, (i + 1) % n_z) for i in range(1, n_z, 2)]))
     got1, edge_a, za, zb = lax.optimization_barrier((got1, edge_a, za, zb))

time: 82.4 us -> 80.5 us (0.977)
  starting transfers between devices: 40.5 us -> 36.7 us
  waiting for transfers between devices: 14.4 us -> 15.5 us
    ppermute x1, starting transfers between devices: 2.97 us -> 1.19 us  [local(): near = lax.ppermute(line, 'zh', [(i, i ^ 1) for i in range(pairs)])]
    ppermute x1, waiting for transfers between devices: 1.19 us -> 2.45 us  [local(): near = lax.ppermute(line, 'zh', [(i, i ^ 1) for i in range(pairs)])]
    ppermute x1, starting transfers between devices: 4.58 us -> 3.33 us  [local(): near = lax.ppermute(line, 'zh', [(i, i ^ 3) for i in range(pairs)])]
  transfers between devices with their start and end apart: 13 -> 13, of which waited for: 8 -> 7; matrix products, arithmetic and copies ran while one was open for 0% -> 0% of each run, Pallas kernels for 12% -> 13%
where the time goes in v11:
time: 80.5 us; the launch traced here: 80.2 us
  starting transfers between devices  36.7 us (46%)
  Pallas kernels  15.8 us (20%)
  waiting for transfers between devices  15.5 us (19%)
  blocking collectives  11.5 us (14%)
    all_to_all x1, blocking collectives, local(): parts = lax.all_to_all(joined, GROUP, 0, 0)  11.5 us
    ppermute x1, starting transfers between devices, local(): xa = lax.ppermute(edge_a, 'c', swap)  9.43 us
    all_to_all x1, waiting for transfers between devices, local(): half = lax.all_to_all(spread, GROUP, 0, 0)  6.59 us
    ppermute x1, starting transfers between devices, local(): other_half = lax.ppermute(half, 'c', swap)  5.21 us
    ppermute x1, starting transfers between devices, local(): lax.ppermute(row_b, SY, both_ways([(i, (i + 1) % n_z) for i in range(1, n...  4.67 us
    all_to_all x1, starting transfers between devices, local(): half = lax.all_to_all(spread, GROUP, 0, 0)  4.17 us
    pallas_call x1, Pallas kernels, rest_grad(): pl.pallas_call(functools.partial(rest_grad_kernel, begin), in_specs=[SM,...  4.1 us
    ppermute x1, starting transfers between devices, local(): near = lax.ppermute(line, 'zh', [(i, i ^ 3) for i in range(pairs)])  3.33 us
  transfers between devices with their start and end apart: 13, of which 7 were waited for; matrix products, arithmetic and copies ran while one was open for 0% of the time, Pallas kernels for 13%

profile of v11, /device:TPU:1, one launch (start us, length us, event | category | flops | bytes accessed | tf_op | source)
XLA Modules:
  0.0 80.2 jit_solution(8385654361248623000)
XLA Ops:
  0.7 2.5 %shard_map.58 = (bf16[512,256]{1,0:T(8,128)(2,1)S(1)}, bf16[2,256,512]{2,1,0:T(8,128)(2,1)S(1)}, bf16[2,512,512]{2,1,0:T(8,128)(2,1)S(1)}, bf16[4,64,256]{2,1,0:T(8,128)(2,1)S(1)}) custom-call(s32[1]{0:T(128)} %bitcast.at_ref, bf16[4,8,64,256]{3,2,1,0:T(8,128)(2,1)} %m_hbm.5, bf16[2,256,512]{2,1,0:T(8,128)(2,1)} %c_hbm.1, bf16[2,4,512,512]{3,2,1,0:T(8,128)(2,1)} %bitcast.3), custom_call_target="tpu_custom_call" | custom-call | flops 536870912 | bytes 2097152 | tf_op jit(solution)/shard_map/pallas_call | solution.py:154
  3.2 2.1 %collective-permute-start.1 = (bf16[512,256]{1,0:T(8,128)(2,1)S(1)}, bf16[512,256]{1,0:T(8,128)(2,1)S(1)}, u32[]{:S(2)}, u32[]{:S(2)}) collective-permute-start(bf16[512,256]{1,0:T(8,128)(2,1)S(1)} %get-tuple-element.44.refs_0_), channel_id=1, source_target_pairs={{0,128},{128,0},{1,129},{129,1},{2,130},{130,2},{3,131},{131,3},{4... | collective-permute-start | bytes 786440 | tf_op jit(solution)/shard_map/ppermute | solution.py:441
  5.3 2.4 %shard_map.59 = (bf16[512,256]{1,0:T(8,128)(2,1)S(1)}, bf16[2,512,512]{2,1,0:T(8,128)(2,1)S(1)}) custom-call(bf16[4,8,64,256]{3,2,1,0:T(8,128)(2,1)} %m_hbm.5, bf16[2,256,512]{2,1,0:T(8,128)(2,1)S(1)} %get-tuple-element.41.c_ref, bf16[2,4,512,512]{3,2,1,0:T(8,128)(2,1)} %bitcast.4), custom_call_target="tpu_custom_call" | custom-call | flops 536870912 | bytes 2097152 | tf_op jit(solution)/shard_map/pallas_call | solution.py:172
  7.7 0.1 collective-permute-start
  7.8 2.7 %collective-permute-start.2 = (bf16[4,64,256]{2,1,0:T(8,128)(2,1)S(1)}, bf16[4,64,256]{2,1,0:T(8,128)(2,1)S(1)}, u32[]{:S(2)}, u32[]{:S(2)}) collective-permute-start(bf16[4,64,256]{2,1,0:T(8,128)(2,1)S(1)} %get-tuple-element.45), channel_id=1, source_target_pairs={{8,16},{16,8},{24,32},{32,24},{40,48},{48,40},{56,64},{64,56},{72,... | collective-permute-start | bytes 393224 | tf_op jit(solution)/shard_map/ppermute | solution.py:442
  10.5 4.1 %shard_map.60 = (bf16[512,256]{1,0:T(8,128)(2,1)S(1)}, bf16[512,256]{1,0:T(8,128)(2,1)S(1)}, bf16[4,8,64,256]{3,2,1,0:T(8,128)(2,1)S(1)}, bf16[2,2,512,512]{3,2,...) custom-call(s32[1]{0:T(128)} %bitcast.at_ref, ...), custom_call_target="tpu_custom_call" | custom-call | flops 1073741824 | bytes 3670016 | tf_op jit(solution)/shard_map/pallas_call | solution.py:198
  14.6 1.3 %collective-permute-start.6 = (bf16[512,256]{1,0:T(8,128)(2,1)S(1)}, bf16[512,256]{1,0:T(8,128)(2,1)S(1)}, u32[]{:S(2)}, u32[]{:S(2)}) collective-permute-start(bf16[512,256]{1,0:T(8,128)(2,1)S(1)} %get-tuple-element.54.refs_2_), channel_id=1, source_target_pairs={{0,128},{128,0},{1,129},{129,1},{2,130},{130,2},{3,131},{131,3},{4... | collective-permute-start | bytes 786440 | tf_op jit(solution)/shard_map/ppermute | solution.py:447
  15.9 0.2 collective-permute-start.7
  16.1 0.0 collective-permute-done.2.xb_ref
  16.2 0.0 collective-permute-done.1.refs_3_
  16.2 1.6 %collective-permute-start.3 = (bf16[32,256]{1,0:T(8,128)(2,1)S(1)}, bf16[32,256]{1,0:T(8,128)(2,1)S(1)}, u32[]{:S(2)}, u32[]{:S(2)}) collective-permute-start(bf16[32,256]{1,0:T(8,128)(2,1)S(1)} %get-tuple-element.48), channel_id=1, source_target_pairs={{0,1},{1,0},{2,3},{3,2},{4,5},{5,4},{6,7},{7,6},{8,9},{9,8},{10,11... | collective-permute-start | bytes 49160 | tf_op jit(solution)/shard_map/ppermute | solution.py:450
  17.8 4.7 %collective-permute-start.4 = (bf16[32,256]{1,0:T(8,128)(2,1)S(1)}, bf16[32,256]{1,0:T(8,128)(2,1)S(1)}, u32[]{:S(2)}, u32[]{:S(2)}) collective-permute-start(bf16[32,256]{1,0:T(8,128)(2,1)S(1)} %get-tuple-element.49), channel_id=1, source_target_pairs={{1,2},{2,1},{3,4},{4,3},{5,6},{6,5},{7,0},{0,7},{9,10},{10,9},{11,... | collective-permute-start | bytes 49160 | tf_op jit(solution)/shard_map/ppermute | solution.py:451
  22.5 0.0 collective-permute-done.refs_4_
  22.5 0.0 collective-permute-done.3.za_ref
  22.5 1.4 %collective-permute-done.4.zb_ref = bf16[32,256]{1,0:T(8,128)(2,1)S(1)} collective-permute-done((bf16[32,256]{1,0:T(8,128)(2,1)S(1)}, bf16[32,256]{1,0:T(8,128)(2,1)S(1)}, u32[]{:S(2)}, u32[]{:S(2)}) %collective-permute-start.4) | collective-permute-done | bytes 16416 | tf_op jit(solution)/shard_map/ppermute | solution.py:451
  23.9 9.4 %collective-permute-start.5 = (bf16[4,64,256]{2,1,0:T(8,128)(2,1)S(1)}, bf16[4,64,256]{2,1,0:T(8,128)(2,1)S(1)}, u32[]{:S(2)}, u32[]{:S(2)}) collective-permute-start(bf16[4,64,256]{2,1,0:T(8,128)(2,1)S(1)} %get-tuple-element.50), channel_id=1, source_target_pairs={{0,8},{8,0},{1,9},{9,1},{2,10},{10,2},{3,11},{11,3},{4,12},{12,4},... | collective-permute-start | bytes 393224 | tf_op jit(solution)/shard_map/ppermute | solution.py:453
  33.3 0.0 collective-permute-done.6.refs_5_
  33.3 1.0 %collective-permute-done.5.xa_ref = bf16[4,64,256]{2,1,0:T(8,128)(2,1)S(1)} collective-permute-done((bf16[4,64,256]{2,1,0:T(8,128)(2,1)S(1)}, bf16[4,64,256]{2,1,0:T(8,128)(2,1)S(1)}, u32[]{:S(2)}, u32[]{:S(2)}) %collective-permute-start.5) | collective-permute-done | bytes 131104 | tf_op jit(solution)/shard_map/ppermute | solution.py:453
  34.3 2.4 %shard_map.61 = (f32[512,256]{1,0:T(8,128)S(1)}, bf16[1536,256]{1,0:T(8,128)(2,1)S(1)}, f32[2,256,512]{2,1,0:T(8,128)S(1)}, f32[256,256]{1,0:T(8,128)S(1)}, f32[1,256]{1,0:T(1,128)S(1)}) custom-call(s32[1]{0:T(128)} %bitcast.at_ref, bf16[4,8,64,256]{3,2,1,0:T(8,128)(2,1)S(1)} %get-tuple-element.42.m_ref, ...), custom_call_target="tpu_custom_call" | custom-call | flops 1006632960 | bytes 6291456 | tf_op jit(solution)/shard_map/pallas_call | solution.py:316
  36.7 0.0 collective-permute-done.7.got_ref
  36.7 0.9 %shard_map.62 = (bf16[512,256]{1,0:T(8,128)(2,1)S(1)}, bf16[16,88,128]{2,1,0:T(8,128)(2,1)S(1)}, bf16[16,88,128]{2,1,0:T(8,128)(2,1)S(1)}) custom-call(s32[1]{0:T(128)} %bitcast.at_ref, f32[512,256]{1,0:T(8,128)S(1)} %get-tuple-element.60.base_ref, bf16[512,256]{1,0:T(8,128)(2,1)S(1)} %get-tuple-element.61.own_ref, ...), custom_call_target="tpu_custom_call" | custom-call | flops 335544320 | bytes 2097152 | tf_op jit(solution)/shard_map/pallas_call | solution.py:329
  37.7 0.6 collective-permute-start.8
  38.3 1.3 %collective-permute-done.8.got_ref = bf16[16,88,128]{2,1,0:T(8,128)(2,1)S(1)} collective-permute-done((bf16[16,88,128]{2,1,0:T(8,128)(2,1)S(1)}, bf16[16,88,128]{2,1,0:T(8,128)(2,1)S(1)}, u32[]{:S(2)}, u32[]{:S(2)}) %collective-permute-start.8) | collective-permute-done | bytes 360480 | tf_op jit(solution)/shard_map/ppermute | solution.py:464
  39.6 0.1 shard_map.63
  39.7 11.5 %all_to_all.10.in_ref = bf16[16,88,128]{2,1,0:T(8,128)(2,1)S(1)} all-to-all(bf16[16,88,128]{2,1,0:T(8,128)(2,1)S(1)} %shard_map.63), channel_id=1, replica_groups=mesh['ens'=2,'xh'=2,'y'=4,'c'=2,'zh'=4,'zl'=2] {'xh','y','zl'}, dimensions={0} | all-to-all | bytes 720896 | tf_op jit(solution)/shard_map/all_to_all | solution.py:468
  51.2 0.1 shard_map.64.own_ref
  51.2 1.2 %collective-permute-start.9 = (bf16[88,128]{1,0:T(8,128)(2,1)S(1)}, bf16[88,128]{1,0:T(8,128)(2,1)S(1)}, u32[]{:S(2)}, u32[]{:S(2)}) collective-permute-start(bf16[88,128]{1,0:T(8,128)(2,1)S(1)} %shard_map.64.own_ref), channel_id=1, source_target_pairs={{0,2},{2,0},{4,6},{6,4},{1,3},{3,1},{5,7},{7,5},{8,10},{10,8},{12,... | collective-permute-start | bytes 67592 | tf_op jit(solution)/shard_map/ppermute | solution.py:474
  52.4 2.4 %collective-permute-done.9.got_ref = bf16[88,128]{1,0:T(8,128)(2,1)S(1)} collective-permute-done((bf16[88,128]{1,0:T(8,128)(2,1)S(1)}, bf16[88,128]{1,0:T(8,128)(2,1)S(1)}, u32[]{:S(2)}, u32[]{:S(2)}) %collective-permute-start.9) | collective-permute-done | bytes 22560 | tf_op jit(solution)/shard_map/ppermute | solution.py:474
  54.9 3.3 %collective-permute-start.10 = (bf16[88,128]{1,0:T(8,128)(2,1)S(1)}, bf16[88,128]{1,0:T(8,128)(2,1)S(1)}, u32[]{:S(2)}, u32[]{:S(2)}) collective-permute-start(bf16[88,128]{1,0:T(8,128)(2,1)S(1)} %shard_map.65.own_ref), channel_id=1, source_target_pairs={{0,6},{2,4},{4,2},{6,0},{1,7},{3,5},{5,3},{7,1},{8,14},{10,12},{12... | collective-permute-start | bytes 67592 | tf_op jit(solution)/shard_map/ppermute | solution.py:478
  58.2 1.5 %collective-permute-done.10.got_ref = bf16[88,128]{1,0:T(8,128)(2,1)S(1)} collective-permute-done((bf16[88,128]{1,0:T(8,128)(2,1)S(1)}, bf16[88,128]{1,0:T(8,128)(2,1)S(1)}, u32[]{:S(2)}, u32[]{:S(2)}) %collective-permute-start.10) | collective-permute-done | bytes 22560 | tf_op jit(solution)/shard_map/ppermute | solution.py:478
  59.7 0.9 %shard_map.66 = (bf16[16,80,128]{2,1,0:T(8,128)(2,1)}, f32[2,128]{1,0:T(2,128)S(1)}) custom-call(s32[1]{0:T(128)} %bitcast.at_ref, bf16[88,128]{1,0:T(8,128)(2,1)S(1)} %shard_map.65.own_ref, bf16[88,128]{1,0:T(8,128)(2,1)S(1)} %collective-permute-done.10.got_ref), custom_call_target="tpu_custom_call" | custom-call | tf_op jit(solution)/shard_map/pallas_call | solution.py:479
  60.6 4.2 %all-to-all-start.1 = ((bf16[16,80,128]{2,1,0:T(8,128)(2,1)}), bf16[16,80,128]{2,1,0:T(8,128)(2,1)S(1)}, u32[]{:S(2)}, u32[]{:S(2)}) async-start(bf16[16,80,128]{2,1,0:T(8,128)(2,1)} %get-tuple-element.67), calls=%async_computation.1 | async-start | bytes 655360 | tf_op jit(solution)/shard_map/all_to_all | solution.py:490
  64.8 1.2 %shard_map.67 = bf16[2048,256]{1,0:T(8,128)(2,1)} custom-call(f32[2,128]{1,0:T(2,128)S(1)} %get-tuple-element.68.shrink_ref, bf16[1536,256]{1,0:T(8,128)(2,1)S(1)} %get-tuple-element.69.refs_0_, bf16[512,256]{1,0:T(8,128)(2,1)S(1)} %get-tuple-element.70.refs_1_), custom_call_target="tpu_custom_call" | custom-call | tf_op jit(solution)/shard_map/pallas_call | solution.py:491
  66.0 6.6 %all-to-all-done.1.own_ref = bf16[16,80,128]{2,1,0:T(8,128)(2,1)S(1)} async-done(((bf16[16,80,128]{2,1,0:T(8,128)(2,1)}), bf16[16,80,128]{2,1,0:T(8,128)(2,1)S(1)}, u32[]{:S(2)}, u32[]{:S(2)}) %all-to-all-start.1) | async-done | bytes 327712 | tf_op jit(solution)/shard_map/all_to_all | solution.py:490
  72.6 5.2 %collective-permute-start.11 = (bf16[16,80,128]{2,1,0:T(8,128)(2,1)S(1)}, bf16[16,80,128]{2,1,0:T(8,128)(2,1)S(1)}, u32[]{:S(2)}, u32[]{:S(2)}) collective-permute-start(bf16[16,80,128]{2,1,0:T(8,128)(2,1)S(1)} %all-to-all-done.1.own_ref), channel_id=1, source_target_pairs={{0,8},{8,0},{1,9},{9,1},{2,10},{10,2},{3,11},{11,3},{4,12},{12,4},... | collective-permute-start | bytes 983048 | tf_op jit(solution)/shard_map/ppermute | solution.py:499
  77.8 1.3 %collective-permute-done.11.got_ref = bf16[16,80,128]{2,1,0:T(8,128)(2,1)S(1)} collective-permute-done((bf16[16,80,128]{2,1,0:T(8,128)(2,1)S(1)}, bf16[16,80,128]{2,1,0:T(8,128)(2,1)S(1)}, u32[]{:S(2)}, u32[]{:S(2)}) %collective-permute-start.11) | collective-permute-done | bytes 327712 | tf_op jit(solution)/shard_map/ppermute | solution.py:499
  79.0 1.2 %shard_map.68 = (f32[2,256,512]{2,1,0:T(8,128)}, f32[256,256]{1,0:T(8,128)}) custom-call(s32[1]{0:T(128)} %bitcast.at_ref, bf16[16,80,128]{2,1,0:T(8,128)(2,1)S(1)} %all-to-all-done.1.own_ref, bf16[16,80,128]{2,1,0:T(8,128)(2,1)S(1)} %collective-permute-done.11.got_ref), custom_call_target="tpu_custom_call" | custom-call | tf_op jit(solution)/shard_map/pallas_call | solution.py:500
  (1 shorter events, 0.0 us)
Async XLA Ops:
  3.2 13.0 %collective-permute-start.1 = (bf16[512,256]{1,0:T(8,128)(2,1)S(1)}, bf16[512,256]{1,0:T(8,128)(2,1)S(1)}, u32[]{:S(2)}, u32[]{:S(2)}) collective-permute-start(bf16[512,256]{1,0:T(8,128)(2,1)S(1)} %get-tuple-element.44.refs_0_), channel_id=1, source_target_pairs={{0,128},{128,0},{1,129},{129,1},{2,130},{130,2},{3,131},{131,3},{4... | collective-permute-start | bytes 786440 | tf_op jit(solution)/shard_map/ppermute | solution.py:441
  7.7 14.8 %collective-permute-start = (bf16[512,256]{1,0:T(8,128)(2,1)S(1)}, bf16[512,256]{1,0:T(8,128)(2,1)S(1)}, u32[]{:S(2)}, u32[]{:S(2)}) collective-permute-start(bf16[512,256]{1,0:T(8,128)(2,1)S(1)} %get-tuple-element.40.refs_1_), channel_id=1, source_target_pairs={{0,128},{128,0},{1,129},{129,1},{2,130},{130,2},{3,131},{131,3},{4... | collective-permute-start | bytes 786440 | tf_op jit(solution)/shard_map/ppermute | solution.py:444
  7.8 8.3 %collective-permute-start.2 = (bf16[4,64,256]{2,1,0:T(8,128)(2,1)S(1)}, bf16[4,64,256]{2,1,0:T(8,128)(2,1)S(1)}, u32[]{:S(2)}, u32[]{:S(2)}) collective-permute-start(bf16[4,64,256]{2,1,0:T(8,128)(2,1)S(1)} %get-tuple-element.45), channel_id=1, source_target_pairs={{8,16},{16,8},{24,32},{32,24},{40,48},{48,40},{56,64},{64,56},{72,... | collective-permute-start | bytes 393224 | tf_op jit(solution)/shard_map/ppermute | solution.py:442
  14.6 18.7 %collective-permute-start.6 = (bf16[512,256]{1,0:T(8,128)(2,1)S(1)}, bf16[512,256]{1,0:T(8,128)(2,1)S(1)}, u32[]{:S(2)}, u32[]{:S(2)}) collective-permute-start(bf16[512,256]{1,0:T(8,128)(2,1)S(1)} %get-tuple-element.54.refs_2_), channel_id=1, source_target_pairs={{0,128},{128,0},{1,129},{129,1},{2,130},{130,2},{3,131},{131,3},{4... | collective-permute-start | bytes 786440 | tf_op jit(solution)/shard_map/ppermute | solution.py:447
  15.9 20.8 %collective-permute-start.7 = (bf16[512,256]{1,0:T(8,128)(2,1)S(1)}, bf16[512,256]{1,0:T(8,128)(2,1)S(1)}, u32[]{:S(2)}, u32[]{:S(2)}) collective-permute-start(bf16[512,256]{1,0:T(8,128)(2,1)S(1)} %get-tuple-element.61.own_ref), channel_id=1, source_target_pairs={{0,128},{128,0},{1,129},{129,1},{2,130},{130,2},{3,131},{131,3},{4... | collective-permute-start | bytes 786440 | tf_op jit(solution)/shard_map/ppermute | solution.py:448
  16.2 6.3 %collective-permute-start.3 = (bf16[32,256]{1,0:T(8,128)(2,1)S(1)}, bf16[32,256]{1,0:T(8,128)(2,1)S(1)}, u32[]{:S(2)}, u32[]{:S(2)}) collective-permute-start(bf16[32,256]{1,0:T(8,128)(2,1)S(1)} %get-tuple-element.48), channel_id=1, source_target_pairs={{0,1},{1,0},{2,3},{3,2},{4,5},{5,4},{6,7},{7,6},{8,9},{9,8},{10,11... | collective-permute-start | bytes 49160 | tf_op jit(solution)/shard_map/ppermute | solution.py:450
  17.8 6.1 %collective-permute-start.4 = (bf16[32,256]{1,0:T(8,128)(2,1)S(1)}, bf16[32,256]{1,0:T(8,128)(2,1)S(1)}, u32[]{:S(2)}, u32[]{:S(2)}) collective-permute-start(bf16[32,256]{1,0:T(8,128)(2,1)S(1)} %get-tuple-element.49), channel_id=1, source_target_pairs={{1,2},{2,1},{3,4},{4,3},{5,6},{6,5},{7,0},{0,7},{9,10},{10,9},{11,... | collective-permute-start | bytes 49160 | tf_op jit(solution)/shard_map/ppermute | solution.py:451
  23.9 10.4 %collective-permute-start.5 = (bf16[4,64,256]{2,1,0:T(8,128)(2,1)S(1)}, bf16[4,64,256]{2,1,0:T(8,128)(2,1)S(1)}, u32[]{:S(2)}, u32[]{:S(2)}) collective-permute-start(bf16[4,64,256]{2,1,0:T(8,128)(2,1)S(1)} %get-tuple-element.50), channel_id=1, source_target_pairs={{0,8},{8,0},{1,9},{9,1},{2,10},{10,2},{3,11},{11,3},{4,12},{12,4},... | collective-permute-start | bytes 393224 | tf_op jit(solution)/shard_map/ppermute | solution.py:453
  37.7 1.9 %collective-permute-start.8 = (bf16[16,88,128]{2,1,0:T(8,128)(2,1)S(1)}, bf16[16,88,128]{2,1,0:T(8,128)(2,1)S(1)}, u32[]{:S(2)}, u32[]{:S(2)}) collective-permute-start(bf16[16,88,128]{2,1,0:T(8,128)(2,1)S(1)} %get-tuple-element.66), channel_id=1, source_target_pairs={{0,8},{8,0},{1,9},{9,1},{2,10},{10,2},{3,11},{11,3},{4,12},{12,4},... | collective-permute-start | bytes 1081352 | tf_op jit(solution)/shard_map/ppermute | solution.py:464
  51.2 3.6 %collective-permute-start.9 = (bf16[88,128]{1,0:T(8,128)(2,1)S(1)}, bf16[88,128]{1,0:T(8,128)(2,1)S(1)}, u32[]{:S(2)}, u32[]{:S(2)}) collective-permute-start(bf16[88,128]{1,0:T(8,128)(2,1)S(1)} %shard_map.64.own_ref), channel_id=1, source_target_pairs={{0,2},{2,0},{4,6},{6,4},{1,3},{3,1},{5,7},{7,5},{8,10},{10,8},{12,... | collective-permute-start | bytes 67592 | tf_op jit(solution)/shard_map/ppermute | solution.py:474
  54.9 4.9 %collective-permute-start.10 = (bf16[88,128]{1,0:T(8,128)(2,1)S(1)}, bf16[88,128]{1,0:T(8,128)(2,1)S(1)}, u32[]{:S(2)}, u32[]{:S(2)}) collective-permute-start(bf16[88,128]{1,0:T(8,128)(2,1)S(1)} %shard_map.65.own_ref), channel_id=1, source_target_pairs={{0,6},{2,4},{4,2},{6,0},{1,7},{3,5},{5,3},{7,1},{8,14},{10,12},{12... | collective-permute-start | bytes 67592 | tf_op jit(solution)/shard_map/ppermute | solution.py:478
  60.6 11.9 %all-to-all-start.1 = ((bf16[16,80,128]{2,1,0:T(8,128)(2,1)}), bf16[16,80,128]{2,1,0:T(8,128)(2,1)S(1)}, u32[]{:S(2)}, u32[]{:S(2)}) async-start(bf16[16,80,128]{2,1,0:T(8,128)(2,1)} %get-tuple-element.67), calls=%async_computation.1 | async-start | bytes 655360 | tf_op jit(solution)/shard_map/all_to_all | solution.py:490
  72.6 6.5 %collective-permute-start.11 = (bf16[16,80,128]{2,1,0:T(8,128)(2,1)S(1)}, bf16[16,80,128]{2,1,0:T(8,128)(2,1)S(1)}, u32[]{:S(2)}, u32[]{:S(2)}) collective-permute-start(bf16[16,80,128]{2,1,0:T(8,128)(2,1)S(1)} %all-to-all-done.1.own_ref), channel_id=1, source_target_pairs={{0,8},{8,0},{1,9},{9,1},{2,10},{10,2},{3,11},{11,3},{4,12},{12,4},... | collective-permute-start | bytes 983048 | tf_op jit(solution)/shard_map/ppermute | solution.py:499

commit v12 on v11

--- a/solution.py
+++ b/solution.py
@@ -446,10 +446,10 @@
     g2, g3, modes, series, edge_a, row_a, row_b = rest_grad(place, modes, coefficients, series, 2)
     got2 = lax.ppermute(g2, "ens", swap)
     got3 = lax.ppermute(g3, "ens", swap)
-    got0, xb, row_a, row_b = lax.optimization_barrier((got0, xb, row_a, row_b))
+    got0, got1, row_a, row_b = lax.optimization_barrier((got0, got1, row_a, row_b))
     za = lax.ppermute(row_a, SY, both_ways([(i, i + 1) for i in range(0, n_z, 2)]))
     zb = lax.ppermute(row_b, SY, both_ways([(i, (i + 1) % n_z) for i in range(1, n_z, 2)]))
-    got1, edge_a, za, zb = lax.optimization_barrier((got1, edge_a, za, zb))
+    xb, edge_a, za, zb = lax.optimization_barrier((xb, edge_a, za, zb))
     xa = lax.ppermute(edge_a, "c", swap)
     moved, keep, send = steps(
         place,

time: 80.5 us -> 80.5 us (level)
  blocking collectives: 11.5 us -> 14.4 us
  waiting for transfers between devices: 15.5 us -> 13.9 us
  starting transfers between devices: 36.7 us -> 35.4 us
    ppermute x1, starting transfers between devices: 9.43 us -> 4.13 us  [local(): xa = lax.ppermute(edge_a, 'c', swap)]
    all_to_all x1, blocking collectives: 11.5 us -> 14.4 us  [local(): parts = lax.all_to_all(joined, GROUP, 0, 0)]
    ppermute x1, starting transfers between devices: 1.19 us -> 3.07 us  [local(): near = lax.ppermute(line, 'zh', [(i, i ^ 1) for i in range(pairs)])]
    ppermute x1, waiting for transfers between devices: 2.45 us -> 1.19 us  [local(): near = lax.ppermute(line, 'zh', [(i, i ^ 1) for i in range(pairs)])]
    ppermute x1, starting transfers between devices: 3.33 us -> 4.58 us  [local(): near = lax.ppermute(line, 'zh', [(i, i ^ 3) for i in range(pairs)])]
where the time goes in v12:
time: 80.5 us; the launch traced here: 80.2 us
  starting transfers between devices  35.4 us (44%)
  Pallas kernels  15.8 us (20%)
  blocking collectives  14.4 us (18%)
  waiting for transfers between devices  13.9 us (17%)
    all_to_all x1, blocking collectives, local(): parts = lax.all_to_all(joined, GROUP, 0, 0)  14.4 us
    all_to_all x1, waiting for transfers between devices, local(): half = lax.all_to_all(spread, GROUP, 0, 0)  6.59 us
    ppermute x1, starting transfers between devices, local(): other_half = lax.ppermute(half, 'c', swap)  5.22 us
    ppermute x1, starting transfers between devices, local(): lax.ppermute(row_b, SY, both_ways([(i, (i + 1) % n_z) for i in range(1, n...  4.68 us
    ppermute x1, starting transfers between devices, local(): near = lax.ppermute(line, 'zh', [(i, i ^ 3) for i in range(pairs)])  4.58 us
    all_to_all x1, starting transfers between devices, local(): half = lax.all_to_all(spread, GROUP, 0, 0)  4.32 us
    ppermute x1, starting transfers between devices, local(): xa = lax.ppermute(edge_a, 'c', swap)  4.13 us
    pallas_call x1, Pallas kernels, rest_grad(): pl.pallas_call(functools.partial(rest_grad_kernel, begin), in_specs=[SM,...  4.1 us
  transfers between devices with their start and end apart: 13, of which 7 were waited for; matrix products, arithmetic and copies ran while one was open for 0% of the time, Pallas kernels for 13%

profile of v12, /device:TPU:1, one launch (start us, length us, event | category | flops | bytes accessed | tf_op | source)
XLA Modules:
  0.0 80.2 jit_solution(1635853929096107553)
XLA Ops:
  0.7 2.5 %shard_map.58 = (bf16[512,256]{1,0:T(8,128)(2,1)S(1)}, bf16[2,256,512]{2,1,0:T(8,128)(2,1)S(1)}, bf16[2,512,512]{2,1,0:T(8,128)(2,1)S(1)}, bf16[4,64,256]{2,1,0:T(8,128)(2,1)S(1)}) custom-call(s32[1]{0:T(128)} %bitcast.at_ref, bf16[4,8,64,256]{3,2,1,0:T(8,128)(2,1)} %m_hbm.5, bf16[2,256,512]{2,1,0:T(8,128)(2,1)} %c_hbm.1, bf16[2,4,512,512]{3,2,1,0:T(8,128)(2,1)} %bitcast.3), custom_call_target="tpu_custom_call" | custom-call | flops 536870912 | bytes 2097152 | tf_op jit(solution)/shard_map/pallas_call | solution.py:154
  3.2 2.1 %collective-permute-start.1 = (bf16[512,256]{1,0:T(8,128)(2,1)S(1)}, bf16[512,256]{1,0:T(8,128)(2,1)S(1)}, u32[]{:S(2)}, u32[]{:S(2)}) collective-permute-start(bf16[512,256]{1,0:T(8,128)(2,1)S(1)} %get-tuple-element.45.refs_0_), channel_id=1, source_target_pairs={{0,128},{128,0},{1,129},{129,1},{2,130},{130,2},{3,131},{131,3},{4... | collective-permute-start | bytes 786440 | tf_op jit(solution)/shard_map/ppermute | solution.py:441
  5.3 2.4 %shard_map.59 = (bf16[512,256]{1,0:T(8,128)(2,1)S(1)}, bf16[2,512,512]{2,1,0:T(8,128)(2,1)S(1)}) custom-call(bf16[4,8,64,256]{3,2,1,0:T(8,128)(2,1)} %m_hbm.5, bf16[2,256,512]{2,1,0:T(8,128)(2,1)S(1)} %get-tuple-element.41.c_ref, bf16[2,4,512,512]{3,2,1,0:T(8,128)(2,1)} %bitcast.4), custom_call_target="tpu_custom_call" | custom-call | flops 536870912 | bytes 2097152 | tf_op jit(solution)/shard_map/pallas_call | solution.py:172
  7.7 0.1 collective-permute-start.2
  7.8 2.7 %collective-permute-start = (bf16[4,64,256]{2,1,0:T(8,128)(2,1)S(1)}, bf16[4,64,256]{2,1,0:T(8,128)(2,1)S(1)}, u32[]{:S(2)}, u32[]{:S(2)}) collective-permute-start(bf16[4,64,256]{2,1,0:T(8,128)(2,1)S(1)} %get-tuple-element.43), channel_id=1, source_target_pairs={{8,16},{16,8},{24,32},{32,24},{40,48},{48,40},{56,64},{64,56},{72,... | collective-permute-start | bytes 393224 | tf_op jit(solution)/shard_map/ppermute | solution.py:442
  10.5 4.1 %shard_map.60 = (bf16[512,256]{1,0:T(8,128)(2,1)S(1)}, bf16[512,256]{1,0:T(8,128)(2,1)S(1)}, bf16[4,8,64,256]{3,2,1,0:T(8,128)(2,1)S(1)}, bf16[2,2,512,512]{3,2,...) custom-call(s32[1]{0:T(128)} %bitcast.at_ref, ...), custom_call_target="tpu_custom_call" | custom-call | flops 1073741824 | bytes 3670016 | tf_op jit(solution)/shard_map/pallas_call | solution.py:198
  14.6 1.3 %collective-permute-start.6 = (bf16[512,256]{1,0:T(8,128)(2,1)S(1)}, bf16[512,256]{1,0:T(8,128)(2,1)S(1)}, u32[]{:S(2)}, u32[]{:S(2)}) collective-permute-start(bf16[512,256]{1,0:T(8,128)(2,1)S(1)} %get-tuple-element.54.refs_2_), channel_id=1, source_target_pairs={{0,128},{128,0},{1,129},{129,1},{2,130},{130,2},{3,131},{131,3},{4... | collective-permute-start | bytes 786440 | tf_op jit(solution)/shard_map/ppermute | solution.py:447
  15.9 0.2 collective-permute-start.7
  16.1 0.0 collective-permute-done.1.refs_3_
  16.2 0.0 collective-permute-done.2.refs_4_
  16.2 2.4 %collective-permute-start.3 = (bf16[32,256]{1,0:T(8,128)(2,1)S(1)}, bf16[32,256]{1,0:T(8,128)(2,1)S(1)}, u32[]{:S(2)}, u32[]{:S(2)}) collective-permute-start(bf16[32,256]{1,0:T(8,128)(2,1)S(1)} %get-tuple-element.48), channel_id=1, source_target_pairs={{0,1},{1,0},{2,3},{3,2},{4,5},{5,4},{6,7},{7,6},{8,9},{9,8},{10,11... | collective-permute-start | bytes 49160 | tf_op jit(solution)/shard_map/ppermute | solution.py:450
  18.5 4.7 %collective-permute-start.4 = (bf16[32,256]{1,0:T(8,128)(2,1)S(1)}, bf16[32,256]{1,0:T(8,128)(2,1)S(1)}, u32[]{:S(2)}, u32[]{:S(2)}) collective-permute-start(bf16[32,256]{1,0:T(8,128)(2,1)S(1)} %get-tuple-element.49), channel_id=1, source_target_pairs={{1,2},{2,1},{3,4},{4,3},{5,6},{6,5},{7,0},{0,7},{9,10},{10,9},{11,... | collective-permute-start | bytes 49160 | tf_op jit(solution)/shard_map/ppermute | solution.py:451
  23.2 0.0 collective-permute-done.xb_ref
  23.2 0.0 collective-permute-done.3.za_ref
  23.2 1.1 %collective-permute-done.4.zb_ref = bf16[32,256]{1,0:T(8,128)(2,1)S(1)} collective-permute-done((bf16[32,256]{1,0:T(8,128)(2,1)S(1)}, bf16[32,256]{1,0:T(8,128)(2,1)S(1)}, u32[]{:S(2)}, u32[]{:S(2)}) %collective-permute-start.4) | collective-permute-done | bytes 16416 | tf_op jit(solution)/shard_map/ppermute | solution.py:451
  24.4 4.1 %collective-permute-start.5 = (bf16[4,64,256]{2,1,0:T(8,128)(2,1)S(1)}, bf16[4,64,256]{2,1,0:T(8,128)(2,1)S(1)}, u32[]{:S(2)}, u32[]{:S(2)}) collective-permute-start(bf16[4,64,256]{2,1,0:T(8,128)(2,1)S(1)} %get-tuple-element.50), channel_id=1, source_target_pairs={{0,8},{8,0},{1,9},{9,1},{2,10},{10,2},{3,11},{11,3},{4,12},{12,4},... | collective-permute-start | bytes 393224 | tf_op jit(solution)/shard_map/ppermute | solution.py:453
  28.5 0.0 collective-permute-done.6.refs_5_
  28.5 1.0 %collective-permute-done.5.xa_ref = bf16[4,64,256]{2,1,0:T(8,128)(2,1)S(1)} collective-permute-done((bf16[4,64,256]{2,1,0:T(8,128)(2,1)S(1)}, bf16[4,64,256]{2,1,0:T(8,128)(2,1)S(1)}, u32[]{:S(2)}, u32[]{:S(2)}) %collective-permute-start.5) | collective-permute-done | bytes 131104 | tf_op jit(solution)/shard_map/ppermute | solution.py:453
  29.5 2.4 %shard_map.61 = (f32[512,256]{1,0:T(8,128)S(1)}, bf16[1536,256]{1,0:T(8,128)(2,1)S(1)}, f32[2,256,512]{2,1,0:T(8,128)S(1)}, f32[256,256]{1,0:T(8,128)S(1)}, f32[1,256]{1,0:T(1,128)S(1)}) custom-call(s32[1]{0:T(128)} %bitcast.at_ref, bf16[4,8,64,256]{3,2,1,0:T(8,128)(2,1)S(1)} %get-tuple-element.42.m_ref, ...), custom_call_target="tpu_custom_call" | custom-call | flops 1006632960 | bytes 6291456 | tf_op jit(solution)/shard_map/pallas_call | solution.py:316
  31.9 0.0 collective-permute-done.7.got_ref
  31.9 0.9 %shard_map.62 = (bf16[512,256]{1,0:T(8,128)(2,1)S(1)}, bf16[16,88,128]{2,1,0:T(8,128)(2,1)S(1)}, bf16[16,88,128]{2,1,0:T(8,128)(2,1)S(1)}) custom-call(s32[1]{0:T(128)} %bitcast.at_ref, f32[512,256]{1,0:T(8,128)S(1)} %get-tuple-element.60.base_ref, bf16[512,256]{1,0:T(8,128)(2,1)S(1)} %get-tuple-element.61.own_ref, ...), custom_call_target="tpu_custom_call" | custom-call | flops 335544320 | bytes 2097152 | tf_op jit(solution)/shard_map/pallas_call | solution.py:329
  32.8 0.6 collective-permute-start.8
  33.5 1.3 %collective-permute-done.8.got_ref = bf16[16,88,128]{2,1,0:T(8,128)(2,1)S(1)} collective-permute-done((bf16[16,88,128]{2,1,0:T(8,128)(2,1)S(1)}, bf16[16,88,128]{2,1,0:T(8,128)(2,1)S(1)}, u32[]{:S(2)}, u32[]{:S(2)}) %collective-permute-start.8) | collective-permute-done | bytes 360480 | tf_op jit(solution)/shard_map/ppermute | solution.py:464
  34.8 0.1 shard_map.63
  34.9 14.4 %all_to_all.10.in_ref = bf16[16,88,128]{2,1,0:T(8,128)(2,1)S(1)} all-to-all(bf16[16,88,128]{2,1,0:T(8,128)(2,1)S(1)} %shard_map.63), channel_id=1, replica_groups=mesh['ens'=2,'xh'=2,'y'=4,'c'=2,'zh'=4,'zl'=2] {'xh','y','zl'}, dimensions={0} | all-to-all | bytes 720896 | tf_op jit(solution)/shard_map/all_to_all | solution.py:468
  49.3 0.1 shard_map.64.own_ref
  49.4 3.1 %collective-permute-start.9 = (bf16[88,128]{1,0:T(8,128)(2,1)S(1)}, bf16[88,128]{1,0:T(8,128)(2,1)S(1)}, u32[]{:S(2)}, u32[]{:S(2)}) collective-permute-start(bf16[88,128]{1,0:T(8,128)(2,1)S(1)} %shard_map.64.own_ref), channel_id=1, source_target_pairs={{0,2},{2,0},{4,6},{6,4},{1,3},{3,1},{5,7},{7,5},{8,10},{10,8},{12,... | collective-permute-start | bytes 67592 | tf_op jit(solution)/shard_map/ppermute | solution.py:474
  52.4 1.2 %collective-permute-done.9.got_ref = bf16[88,128]{1,0:T(8,128)(2,1)S(1)} collective-permute-done((bf16[88,128]{1,0:T(8,128)(2,1)S(1)}, bf16[88,128]{1,0:T(8,128)(2,1)S(1)}, u32[]{:S(2)}, u32[]{:S(2)}) %collective-permute-start.9) | collective-permute-done | bytes 22560 | tf_op jit(solution)/shard_map/ppermute | solution.py:474
  53.6 4.6 %collective-permute-start.10 = (bf16[88,128]{1,0:T(8,128)(2,1)S(1)}, bf16[88,128]{1,0:T(8,128)(2,1)S(1)}, u32[]{:S(2)}, u32[]{:S(2)}) collective-permute-start(bf16[88,128]{1,0:T(8,128)(2,1)S(1)} %shard_map.65.own_ref), channel_id=1, source_target_pairs={{0,6},{2,4},{4,2},{6,0},{1,7},{3,5},{5,3},{7,1},{8,14},{10,12},{12... | collective-permute-start | bytes 67592 | tf_op jit(solution)/shard_map/ppermute | solution.py:478
  58.2 1.4 %collective-permute-done.10.got_ref = bf16[88,128]{1,0:T(8,128)(2,1)S(1)} collective-permute-done((bf16[88,128]{1,0:T(8,128)(2,1)S(1)}, bf16[88,128]{1,0:T(8,128)(2,1)S(1)}, u32[]{:S(2)}, u32[]{:S(2)}) %collective-permute-start.10) | collective-permute-done | bytes 22560 | tf_op jit(solution)/shard_map/ppermute | solution.py:478
  59.6 0.9 %shard_map.66 = (bf16[16,80,128]{2,1,0:T(8,128)(2,1)}, f32[2,128]{1,0:T(2,128)S(1)}) custom-call(s32[1]{0:T(128)} %bitcast.at_ref, bf16[88,128]{1,0:T(8,128)(2,1)S(1)} %shard_map.65.own_ref, bf16[88,128]{1,0:T(8,128)(2,1)S(1)} %collective-permute-done.10.got_ref), custom_call_target="tpu_custom_call" | custom-call | tf_op jit(solution)/shard_map/pallas_call | solution.py:479
  60.5 4.3 %all-to-all-start.1 = ((bf16[16,80,128]{2,1,0:T(8,128)(2,1)}), bf16[16,80,128]{2,1,0:T(8,128)(2,1)S(1)}, u32[]{:S(2)}, u32[]{:S(2)}) async-start(bf16[16,80,128]{2,1,0:T(8,128)(2,1)} %get-tuple-element.67), calls=%async_computation.1 | async-start | bytes 655360 | tf_op jit(solution)/shard_map/all_to_all | solution.py:490
  64.8 1.2 %shard_map.67 = bf16[2048,256]{1,0:T(8,128)(2,1)} custom-call(f32[2,128]{1,0:T(2,128)S(1)} %get-tuple-element.68.shrink_ref, bf16[1536,256]{1,0:T(8,128)(2,1)S(1)} %get-tuple-element.69.refs_0_, bf16[512,256]{1,0:T(8,128)(2,1)S(1)} %get-tuple-element.70.refs_1_), custom_call_target="tpu_custom_call" | custom-call | tf_op jit(solution)/shard_map/pallas_call | solution.py:491
  66.0 6.6 %all-to-all-done.1.own_ref = bf16[16,80,128]{2,1,0:T(8,128)(2,1)S(1)} async-done(((bf16[16,80,128]{2,1,0:T(8,128)(2,1)}), bf16[16,80,128]{2,1,0:T(8,128)(2,1)S(1)}, u32[]{:S(2)}, u32[]{:S(2)}) %all-to-all-start.1) | async-done | bytes 327712 | tf_op jit(solution)/shard_map/all_to_all | solution.py:490
  72.6 5.2 %collective-permute-start.11 = (bf16[16,80,128]{2,1,0:T(8,128)(2,1)S(1)}, bf16[16,80,128]{2,1,0:T(8,128)(2,1)S(1)}, u32[]{:S(2)}, u32[]{:S(2)}) collective-permute-start(bf16[16,80,128]{2,1,0:T(8,128)(2,1)S(1)} %all-to-all-done.1.own_ref), channel_id=1, source_target_pairs={{0,8},{8,0},{1,9},{9,1},{2,10},{10,2},{3,11},{11,3},{4,12},{12,4},... | collective-permute-start | bytes 983048 | tf_op jit(solution)/shard_map/ppermute | solution.py:499
  77.8 1.3 %collective-permute-done.11.got_ref = bf16[16,80,128]{2,1,0:T(8,128)(2,1)S(1)} collective-permute-done((bf16[16,80,128]{2,1,0:T(8,128)(2,1)S(1)}, bf16[16,80,128]{2,1,0:T(8,128)(2,1)S(1)}, u32[]{:S(2)}, u32[]{:S(2)}) %collective-permute-start.11) | collective-permute-done | bytes 327712 | tf_op jit(solution)/shard_map/ppermute | solution.py:499
  79.0 1.2 %shard_map.68 = (f32[2,256,512]{2,1,0:T(8,128)}, f32[256,256]{1,0:T(8,128)}) custom-call(s32[1]{0:T(128)} %bitcast.at_ref, bf16[16,80,128]{2,1,0:T(8,128)(2,1)S(1)} %all-to-all-done.1.own_ref, bf16[16,80,128]{2,1,0:T(8,128)(2,1)S(1)} %collective-permute-done.11.got_ref), custom_call_target="tpu_custom_call" | custom-call | tf_op jit(solution)/shard_map/pallas_call | solution.py:500
  (1 shorter events, 0.0 us)
Async XLA Ops:
  3.2 13.0 %collective-permute-start.1 = (bf16[512,256]{1,0:T(8,128)(2,1)S(1)}, bf16[512,256]{1,0:T(8,128)(2,1)S(1)}, u32[]{:S(2)}, u32[]{:S(2)}) collective-permute-start(bf16[512,256]{1,0:T(8,128)(2,1)S(1)} %get-tuple-element.45.refs_0_), channel_id=1, source_target_pairs={{0,128},{128,0},{1,129},{129,1},{2,130},{130,2},{3,131},{131,3},{4... | collective-permute-start | bytes 786440 | tf_op jit(solution)/shard_map/ppermute | solution.py:441
  7.7 8.4 %collective-permute-start.2 = (bf16[512,256]{1,0:T(8,128)(2,1)S(1)}, bf16[512,256]{1,0:T(8,128)(2,1)S(1)}, u32[]{:S(2)}, u32[]{:S(2)}) collective-permute-start(bf16[512,256]{1,0:T(8,128)(2,1)S(1)} %get-tuple-element.40.refs_1_), channel_id=1, source_target_pairs={{0,128},{128,0},{1,129},{129,1},{2,130},{130,2},{3,131},{131,3},{4... | collective-permute-start | bytes 786440 | tf_op jit(solution)/shard_map/ppermute | solution.py:444
  7.8 15.4 %collective-permute-start = (bf16[4,64,256]{2,1,0:T(8,128)(2,1)S(1)}, bf16[4,64,256]{2,1,0:T(8,128)(2,1)S(1)}, u32[]{:S(2)}, u32[]{:S(2)}) collective-permute-start(bf16[4,64,256]{2,1,0:T(8,128)(2,1)S(1)} %get-tuple-element.43), channel_id=1, source_target_pairs={{8,16},{16,8},{24,32},{32,24},{40,48},{48,40},{56,64},{64,56},{72,... | collective-permute-start | bytes 393224 | tf_op jit(solution)/shard_map/ppermute | solution.py:442
  14.6 13.9 %collective-permute-start.6 = (bf16[512,256]{1,0:T(8,128)(2,1)S(1)}, bf16[512,256]{1,0:T(8,128)(2,1)S(1)}, u32[]{:S(2)}, u32[]{:S(2)}) collective-permute-start(bf16[512,256]{1,0:T(8,128)(2,1)S(1)} %get-tuple-element.54.refs_2_), channel_id=1, source_target_pairs={{0,128},{128,0},{1,129},{129,1},{2,130},{130,2},{3,131},{131,3},{4... | collective-permute-start | bytes 786440 | tf_op jit(solution)/shard_map/ppermute | solution.py:447
  15.9 16.0 %collective-permute-start.7 = (bf16[512,256]{1,0:T(8,128)(2,1)S(1)}, bf16[512,256]{1,0:T(8,128)(2,1)S(1)}, u32[]{:S(2)}, u32[]{:S(2)}) collective-permute-start(bf16[512,256]{1,0:T(8,128)(2,1)S(1)} %get-tuple-element.61.own_ref), channel_id=1, source_target_pairs={{0,128},{128,0},{1,129},{129,1},{2,130},{130,2},{3,131},{131,3},{4... | collective-permute-start | bytes 786440 | tf_op jit(solution)/shard_map/ppermute | solution.py:448
  16.2 7.1 %collective-permute-start.3 = (bf16[32,256]{1,0:T(8,128)(2,1)S(1)}, bf16[32,256]{1,0:T(8,128)(2,1)S(1)}, u32[]{:S(2)}, u32[]{:S(2)}) collective-permute-start(bf16[32,256]{1,0:T(8,128)(2,1)S(1)} %get-tuple-element.48), channel_id=1, source_target_pairs={{0,1},{1,0},{2,3},{3,2},{4,5},{5,4},{6,7},{7,6},{8,9},{9,8},{10,11... | collective-permute-start | bytes 49160 | tf_op jit(solution)/shard_map/ppermute | solution.py:450
  18.5 5.8 %collective-permute-start.4 = (bf16[32,256]{1,0:T(8,128)(2,1)S(1)}, bf16[32,256]{1,0:T(8,128)(2,1)S(1)}, u32[]{:S(2)}, u32[]{:S(2)}) collective-permute-start(bf16[32,256]{1,0:T(8,128)(2,1)S(1)} %get-tuple-element.49), channel_id=1, source_target_pairs={{1,2},{2,1},{3,4},{4,3},{5,6},{6,5},{7,0},{0,7},{9,10},{10,9},{11,... | collective-permute-start | bytes 49160 | tf_op jit(solution)/shard_map/ppermute | solution.py:451
  24.4 5.1 %collective-permute-start.5 = (bf16[4,64,256]{2,1,0:T(8,128)(2,1)S(1)}, bf16[4,64,256]{2,1,0:T(8,128)(2,1)S(1)}, u32[]{:S(2)}, u32[]{:S(2)}) collective-permute-start(bf16[4,64,256]{2,1,0:T(8,128)(2,1)S(1)} %get-tuple-element.50), channel_id=1, source_target_pairs={{0,8},{8,0},{1,9},{9,1},{2,10},{10,2},{3,11},{11,3},{4,12},{12,4},... | collective-permute-start | bytes 393224 | tf_op jit(solution)/shard_map/ppermute | solution.py:453
  32.8 1.9 %collective-permute-start.8 = (bf16[16,88,128]{2,1,0:T(8,128)(2,1)S(1)}, bf16[16,88,128]{2,1,0:T(8,128)(2,1)S(1)}, u32[]{:S(2)}, u32[]{:S(2)}) collective-permute-start(bf16[16,88,128]{2,1,0:T(8,128)(2,1)S(1)} %get-tuple-element.66), channel_id=1, source_target_pairs={{0,8},{8,0},{1,9},{9,1},{2,10},{10,2},{3,11},{11,3},{4,12},{12,4},... | collective-permute-start | bytes 1081352 | tf_op jit(solution)/shard_map/ppermute | solution.py:464
  49.4 4.3 %collective-permute-start.9 = (bf16[88,128]{1,0:T(8,128)(2,1)S(1)}, bf16[88,128]{1,0:T(8,128)(2,1)S(1)}, u32[]{:S(2)}, u32[]{:S(2)}) collective-permute-start(bf16[88,128]{1,0:T(8,128)(2,1)S(1)} %shard_map.64.own_ref), channel_id=1, source_target_pairs={{0,2},{2,0},{4,6},{6,4},{1,3},{3,1},{5,7},{7,5},{8,10},{10,8},{12,... | collective-permute-start | bytes 67592 | tf_op jit(solution)/shard_map/ppermute | solution.py:474
  53.6 5.9 %collective-permute-start.10 = (bf16[88,128]{1,0:T(8,128)(2,1)S(1)}, bf16[88,128]{1,0:T(8,128)(2,1)S(1)}, u32[]{:S(2)}, u32[]{:S(2)}) collective-permute-start(bf16[88,128]{1,0:T(8,128)(2,1)S(1)} %shard_map.65.own_ref), channel_id=1, source_target_pairs={{0,6},{2,4},{4,2},{6,0},{1,7},{3,5},{5,3},{7,1},{8,14},{10,12},{12... | collective-permute-start | bytes 67592 | tf_op jit(solution)/shard_map/ppermute | solution.py:478
  60.5 12.1 %all-to-all-start.1 = ((bf16[16,80,128]{2,1,0:T(8,128)(2,1)}), bf16[16,80,128]{2,1,0:T(8,128)(2,1)S(1)}, u32[]{:S(2)}, u32[]{:S(2)}) async-start(bf16[16,80,128]{2,1,0:T(8,128)(2,1)} %get-tuple-element.67), calls=%async_computation.1 | async-start | bytes 655360 | tf_op jit(solution)/shard_map/all_to_all | solution.py:490
  72.6 6.5 %collective-permute-start.11 = (bf16[16,80,128]{2,1,0:T(8,128)(2,1)S(1)}, bf16[16,80,128]{2,1,0:T(8,128)(2,1)S(1)}, u32[]{:S(2)}, u32[]{:S(2)}) collective-permute-start(bf16[16,80,128]{2,1,0:T(8,128)(2,1)S(1)} %all-to-all-done.1.own_ref), channel_id=1, source_target_pairs={{0,8},{8,0},{1,9},{9,1},{2,10},{10,2},{3,11},{11,3},{4,12},{12,4},... | collective-permute-start | bytes 983048 | tf_op jit(solution)/shard_map/ppermute | solution.py:499

commit v13 on v12

--- a/solution.py
+++ b/solution.py
@@ -19,7 +19,7 @@
 
 SX = ("xh", "y", "c")
 SY = ("zh", "zl")
-GROUP = ("xh", "y", "zl")
+GROUP = ("y", "xh", "zl")
 PARTS = 16
 PROJ_ROWS = 64
 GRAM_ROWS = 16

time: 80.5 us -> 80.8 us (level)
  no operation moved by 1% of the time
where the time goes in v13:
time: 80.8 us; the launch traced here: 80.5 us
  starting transfers between devices  35.5 us (44%)
  Pallas kernels  15.8 us (20%)
  blocking collectives  14.6 us (18%)
  waiting for transfers between devices  13.9 us (17%)
    all_to_all x1, blocking collectives, local(): parts = lax.all_to_all(joined, GROUP, 0, 0)  14.6 us
    all_to_all x1, waiting for transfers between devices, local(): half = lax.all_to_all(spread, GROUP, 0, 0)  6.81 us
    ppermute x1, starting transfers between devices, local(): other_half = lax.ppermute(half, 'c', swap)  4.94 us
    all_to_all x1, starting transfers between devices, local(): half = lax.all_to_all(spread, GROUP, 0, 0)  4.69 us
    ppermute x1, starting transfers between devices, local(): lax.ppermute(row_b, SY, both_ways([(i, (i + 1) % n_z) for i in range(1, n...  4.69 us
    ppermute x1, starting transfers between devices, local(): near = lax.ppermute(line, 'zh', [(i, i ^ 3) for i in range(pairs)])  4.57 us
    pallas_call x1, Pallas kernels, rest_grad(): pl.pallas_call(functools.partial(rest_grad_kernel, begin), in_specs=[SM,...  4.12 us
    ppermute x1, starting transfers between devices, local(): xa = lax.ppermute(edge_a, 'c', swap)  4.1 us
  transfers between devices with their start and end apart: 13, of which 7 were waited for; matrix products, arithmetic and copies ran while one was open for 0% of the time, Pallas kernels for 13%

profile of v13, /device:TPU:1, one launch (start us, length us, event | category | flops | bytes accessed | tf_op | source)
XLA Modules:
  0.0 80.5 jit_solution(13757223504993666059)
XLA Ops:
  0.7 2.5 %shard_map.58 = (bf16[512,256]{1,0:T(8,128)(2,1)S(1)}, bf16[2,256,512]{2,1,0:T(8,128)(2,1)S(1)}, bf16[2,512,512]{2,1,0:T(8,128)(2,1)S(1)}, bf16[4,64,256]{2,1,0:T(8,128)(2,1)S(1)}) custom-call(s32[1]{0:T(128)} %bitcast.at_ref, bf16[4,8,64,256]{3,2,1,0:T(8,128)(2,1)} %m_hbm.5, bf16[2,256,512]{2,1,0:T(8,128)(2,1)} %c_hbm.1, bf16[2,4,512,512]{3,2,1,0:T(8,128)(2,1)} %bitcast.3), custom_call_target="tpu_custom_call" | custom-call | flops 536870912 | bytes 2097152 | tf_op jit(solution)/shard_map/pallas_call | solution.py:154
  3.2 2.1 %collective-permute-start.1 = (bf16[512,256]{1,0:T(8,128)(2,1)S(1)}, bf16[512,256]{1,0:T(8,128)(2,1)S(1)}, u32[]{:S(2)}, u32[]{:S(2)}) collective-permute-start(bf16[512,256]{1,0:T(8,128)(2,1)S(1)} %get-tuple-element.45.refs_0_), channel_id=1, source_target_pairs={{0,128},{128,0},{1,129},{129,1},{2,130},{130,2},{3,131},{131,3},{4... | collective-permute-start | bytes 786440 | tf_op jit(solution)/shard_map/ppermute | solution.py:441
  5.3 2.4 %shard_map.59 = (bf16[512,256]{1,0:T(8,128)(2,1)S(1)}, bf16[2,512,512]{2,1,0:T(8,128)(2,1)S(1)}) custom-call(bf16[4,8,64,256]{3,2,1,0:T(8,128)(2,1)} %m_hbm.5, bf16[2,256,512]{2,1,0:T(8,128)(2,1)S(1)} %get-tuple-element.41.c_ref, bf16[2,4,512,512]{3,2,1,0:T(8,128)(2,1)} %bitcast.4), custom_call_target="tpu_custom_call" | custom-call | flops 536870912 | bytes 2097152 | tf_op jit(solution)/shard_map/pallas_call | solution.py:172
  7.7 0.1 collective-permute-start.2
  7.8 2.6 %collective-permute-start = (bf16[4,64,256]{2,1,0:T(8,128)(2,1)S(1)}, bf16[4,64,256]{2,1,0:T(8,128)(2,1)S(1)}, u32[]{:S(2)}, u32[]{:S(2)}) collective-permute-start(bf16[4,64,256]{2,1,0:T(8,128)(2,1)S(1)} %get-tuple-element.43), channel_id=1, source_target_pairs={{8,16},{16,8},{24,32},{32,24},{40,48},{48,40},{56,64},{64,56},{72,... | collective-permute-start | bytes 393224 | tf_op jit(solution)/shard_map/ppermute | solution.py:442
  10.5 4.1 %shard_map.60 = (bf16[512,256]{1,0:T(8,128)(2,1)S(1)}, bf16[512,256]{1,0:T(8,128)(2,1)S(1)}, bf16[4,8,64,256]{3,2,1,0:T(8,128)(2,1)S(1)}, bf16[2,2,512,512]{3,2,...) custom-call(s32[1]{0:T(128)} %bitcast.at_ref, ...), custom_call_target="tpu_custom_call" | custom-call | flops 1073741824 | bytes 3670016 | tf_op jit(solution)/shard_map/pallas_call | solution.py:198
  14.6 1.3 %collective-permute-start.6 = (bf16[512,256]{1,0:T(8,128)(2,1)S(1)}, bf16[512,256]{1,0:T(8,128)(2,1)S(1)}, u32[]{:S(2)}, u32[]{:S(2)}) collective-permute-start(bf16[512,256]{1,0:T(8,128)(2,1)S(1)} %get-tuple-element.54.refs_2_), channel_id=1, source_target_pairs={{0,128},{128,0},{1,129},{129,1},{2,130},{130,2},{3,131},{131,3},{4... | collective-permute-start | bytes 786440 | tf_op jit(solution)/shard_map/ppermute | solution.py:447
  15.9 0.3 collective-permute-start.7
  16.2 0.0 collective-permute-done.1.refs_3_
  16.2 0.0 collective-permute-done.2.refs_4_
  16.2 2.4 %collective-permute-start.3 = (bf16[32,256]{1,0:T(8,128)(2,1)S(1)}, bf16[32,256]{1,0:T(8,128)(2,1)S(1)}, u32[]{:S(2)}, u32[]{:S(2)}) collective-permute-start(bf16[32,256]{1,0:T(8,128)(2,1)S(1)} %get-tuple-element.48), channel_id=1, source_target_pairs={{0,1},{1,0},{2,3},{3,2},{4,5},{5,4},{6,7},{7,6},{8,9},{9,8},{10,11... | collective-permute-start | bytes 49160 | tf_op jit(solution)/shard_map/ppermute | solution.py:450
  18.5 4.7 %collective-permute-start.4 = (bf16[32,256]{1,0:T(8,128)(2,1)S(1)}, bf16[32,256]{1,0:T(8,128)(2,1)S(1)}, u32[]{:S(2)}, u32[]{:S(2)}) collective-permute-start(bf16[32,256]{1,0:T(8,128)(2,1)S(1)} %get-tuple-element.49), channel_id=1, source_target_pairs={{1,2},{2,1},{3,4},{4,3},{5,6},{6,5},{7,0},{0,7},{9,10},{10,9},{11,... | collective-permute-start | bytes 49160 | tf_op jit(solution)/shard_map/ppermute | solution.py:451
  23.2 0.0 collective-permute-done.xb_ref
  23.2 0.0 collective-permute-done.3.za_ref
  23.2 1.1 %collective-permute-done.4.zb_ref = bf16[32,256]{1,0:T(8,128)(2,1)S(1)} collective-permute-done((bf16[32,256]{1,0:T(8,128)(2,1)S(1)}, bf16[32,256]{1,0:T(8,128)(2,1)S(1)}, u32[]{:S(2)}, u32[]{:S(2)}) %collective-permute-start.4) | collective-permute-done | bytes 16416 | tf_op jit(solution)/shard_map/ppermute | solution.py:451
  24.4 4.1 %collective-permute-start.5 = (bf16[4,64,256]{2,1,0:T(8,128)(2,1)S(1)}, bf16[4,64,256]{2,1,0:T(8,128)(2,1)S(1)}, u32[]{:S(2)}, u32[]{:S(2)}) collective-permute-start(bf16[4,64,256]{2,1,0:T(8,128)(2,1)S(1)} %get-tuple-element.50), channel_id=1, source_target_pairs={{0,8},{8,0},{1,9},{9,1},{2,10},{10,2},{3,11},{11,3},{4,12},{12,4},... | collective-permute-start | bytes 393224 | tf_op jit(solution)/shard_map/ppermute | solution.py:453
  28.5 0.0 collective-permute-done.6.refs_5_
  28.5 1.0 %collective-permute-done.5.xa_ref = bf16[4,64,256]{2,1,0:T(8,128)(2,1)S(1)} collective-permute-done((bf16[4,64,256]{2,1,0:T(8,128)(2,1)S(1)}, bf16[4,64,256]{2,1,0:T(8,128)(2,1)S(1)}, u32[]{:S(2)}, u32[]{:S(2)}) %collective-permute-start.5) | collective-permute-done | bytes 131104 | tf_op jit(solution)/shard_map/ppermute | solution.py:453
  29.5 2.4 %shard_map.61 = (f32[512,256]{1,0:T(8,128)S(1)}, bf16[1536,256]{1,0:T(8,128)(2,1)S(1)}, f32[2,256,512]{2,1,0:T(8,128)S(1)}, f32[256,256]{1,0:T(8,128)S(1)}, f32[1,256]{1,0:T(1,128)S(1)}) custom-call(s32[1]{0:T(128)} %bitcast.at_ref, bf16[4,8,64,256]{3,2,1,0:T(8,128)(2,1)S(1)} %get-tuple-element.42.m_ref, ...), custom_call_target="tpu_custom_call" | custom-call | flops 1006632960 | bytes 6291456 | tf_op jit(solution)/shard_map/pallas_call | solution.py:316
  31.9 0.0 collective-permute-done.7.got_ref
  31.9 0.9 %shard_map.62 = (bf16[512,256]{1,0:T(8,128)(2,1)S(1)}, bf16[16,88,128]{2,1,0:T(8,128)(2,1)S(1)}, bf16[16,88,128]{2,1,0:T(8,128)(2,1)S(1)}) custom-call(s32[1]{0:T(128)} %bitcast.at_ref, f32[512,256]{1,0:T(8,128)S(1)} %get-tuple-element.60.base_ref, bf16[512,256]{1,0:T(8,128)(2,1)S(1)} %get-tuple-element.61.own_ref, ...), custom_call_target="tpu_custom_call" | custom-call | flops 335544320 | bytes 2097152 | tf_op jit(solution)/shard_map/pallas_call | solution.py:329
  32.8 0.6 collective-permute-start.8
  33.4 1.3 %collective-permute-done.8.got_ref = bf16[16,88,128]{2,1,0:T(8,128)(2,1)S(1)} collective-permute-done((bf16[16,88,128]{2,1,0:T(8,128)(2,1)S(1)}, bf16[16,88,128]{2,1,0:T(8,128)(2,1)S(1)}, u32[]{:S(2)}, u32[]{:S(2)}) %collective-permute-start.8) | collective-permute-done | bytes 360480 | tf_op jit(solution)/shard_map/ppermute | solution.py:464
  34.8 0.1 shard_map.63
  34.8 14.6 %all_to_all.10.in_ref = bf16[16,88,128]{2,1,0:T(8,128)(2,1)S(1)} all-to-all(bf16[16,88,128]{2,1,0:T(8,128)(2,1)S(1)} %shard_map.63), channel_id=1, replica_groups=mesh['ens'=2,'xh'=2,'y'=4,'c'=2,'zh'=4,'zl'=2] {'y','xh','zl'}, dimensions={0} | all-to-all | bytes 720896 | tf_op jit(solution)/shard_map/all_to_all | solution.py:468
  49.4 0.1 shard_map.64.own_ref
  49.5 3.1 %collective-permute-start.9 = (bf16[88,128]{1,0:T(8,128)(2,1)S(1)}, bf16[88,128]{1,0:T(8,128)(2,1)S(1)}, u32[]{:S(2)}, u32[]{:S(2)}) collective-permute-start(bf16[88,128]{1,0:T(8,128)(2,1)S(1)} %shard_map.64.own_ref), channel_id=1, source_target_pairs={{0,2},{2,0},{4,6},{6,4},{1,3},{3,1},{5,7},{7,5},{8,10},{10,8},{12,... | collective-permute-start | bytes 67592 | tf_op jit(solution)/shard_map/ppermute | solution.py:474
  52.6 1.2 %collective-permute-done.9.got_ref = bf16[88,128]{1,0:T(8,128)(2,1)S(1)} collective-permute-done((bf16[88,128]{1,0:T(8,128)(2,1)S(1)}, bf16[88,128]{1,0:T(8,128)(2,1)S(1)}, u32[]{:S(2)}, u32[]{:S(2)}) %collective-permute-start.9) | collective-permute-done | bytes 22560 | tf_op jit(solution)/shard_map/ppermute | solution.py:474
  53.8 4.6 %collective-permute-start.10 = (bf16[88,128]{1,0:T(8,128)(2,1)S(1)}, bf16[88,128]{1,0:T(8,128)(2,1)S(1)}, u32[]{:S(2)}, u32[]{:S(2)}) collective-permute-start(bf16[88,128]{1,0:T(8,128)(2,1)S(1)} %shard_map.65.own_ref), channel_id=1, source_target_pairs={{0,6},{2,4},{4,2},{6,0},{1,7},{3,5},{5,3},{7,1},{8,14},{10,12},{12... | collective-permute-start | bytes 67592 | tf_op jit(solution)/shard_map/ppermute | solution.py:478
  58.4 1.2 %collective-permute-done.10.got_ref = bf16[88,128]{1,0:T(8,128)(2,1)S(1)} collective-permute-done((bf16[88,128]{1,0:T(8,128)(2,1)S(1)}, bf16[88,128]{1,0:T(8,128)(2,1)S(1)}, u32[]{:S(2)}, u32[]{:S(2)}) %collective-permute-start.10) | collective-permute-done | bytes 22560 | tf_op jit(solution)/shard_map/ppermute | solution.py:478
  59.6 0.9 %shard_map.66 = (bf16[16,80,128]{2,1,0:T(8,128)(2,1)}, f32[2,128]{1,0:T(2,128)S(1)}) custom-call(s32[1]{0:T(128)} %bitcast.at_ref, bf16[88,128]{1,0:T(8,128)(2,1)S(1)} %shard_map.65.own_ref, bf16[88,128]{1,0:T(8,128)(2,1)S(1)} %collective-permute-done.10.got_ref), custom_call_target="tpu_custom_call" | custom-call | tf_op jit(solution)/shard_map/pallas_call | solution.py:479
  60.5 4.7 %all-to-all-start.1 = ((bf16[16,80,128]{2,1,0:T(8,128)(2,1)}), bf16[16,80,128]{2,1,0:T(8,128)(2,1)S(1)}, u32[]{:S(2)}, u32[]{:S(2)}) async-start(bf16[16,80,128]{2,1,0:T(8,128)(2,1)} %get-tuple-element.67), calls=%async_computation.1 | async-start | bytes 655360 | tf_op jit(solution)/shard_map/all_to_all | solution.py:490
  65.2 1.2 %shard_map.67 = bf16[2048,256]{1,0:T(8,128)(2,1)} custom-call(f32[2,128]{1,0:T(2,128)S(1)} %get-tuple-element.68.shrink_ref, bf16[1536,256]{1,0:T(8,128)(2,1)S(1)} %get-tuple-element.69.refs_0_, bf16[512,256]{1,0:T(8,128)(2,1)S(1)} %get-tuple-element.70.refs_1_), custom_call_target="tpu_custom_call" | custom-call | tf_op jit(solution)/shard_map/pallas_call | solution.py:491
  66.3 6.8 %all-to-all-done.1.own_ref = bf16[16,80,128]{2,1,0:T(8,128)(2,1)S(1)} async-done(((bf16[16,80,128]{2,1,0:T(8,128)(2,1)}), bf16[16,80,128]{2,1,0:T(8,128)(2,1)S(1)}, u32[]{:S(2)}, u32[]{:S(2)}) %all-to-all-start.1) | async-done | bytes 327712 | tf_op jit(solution)/shard_map/all_to_all | solution.py:490
  73.1 4.9 %collective-permute-start.11 = (bf16[16,80,128]{2,1,0:T(8,128)(2,1)S(1)}, bf16[16,80,128]{2,1,0:T(8,128)(2,1)S(1)}, u32[]{:S(2)}, u32[]{:S(2)}) collective-permute-start(bf16[16,80,128]{2,1,0:T(8,128)(2,1)S(1)} %all-to-all-done.1.own_ref), channel_id=1, source_target_pairs={{0,8},{8,0},{1,9},{9,1},{2,10},{10,2},{3,11},{11,3},{4,12},{12,4},... | collective-permute-start | bytes 983048 | tf_op jit(solution)/shard_map/ppermute | solution.py:499
  78.1 1.3 %collective-permute-done.11.got_ref = bf16[16,80,128]{2,1,0:T(8,128)(2,1)S(1)} collective-permute-done((bf16[16,80,128]{2,1,0:T(8,128)(2,1)S(1)}, bf16[16,80,128]{2,1,0:T(8,128)(2,1)S(1)}, u32[]{:S(2)}, u32[]{:S(2)}) %collective-permute-start.11) | collective-permute-done | bytes 327712 | tf_op jit(solution)/shard_map/ppermute | solution.py:499
  79.3 1.2 %shard_map.68 = (f32[2,256,512]{2,1,0:T(8,128)}, f32[256,256]{1,0:T(8,128)}) custom-call(s32[1]{0:T(128)} %bitcast.at_ref, bf16[16,80,128]{2,1,0:T(8,128)(2,1)S(1)} %all-to-all-done.1.own_ref, bf16[16,80,128]{2,1,0:T(8,128)(2,1)S(1)} %collective-permute-done.11.got_ref), custom_call_target="tpu_custom_call" | custom-call | tf_op jit(solution)/shard_map/pallas_call | solution.py:500
  (1 shorter events, 0.0 us)
Async XLA Ops:
  3.2 13.0 %collective-permute-start.1 = (bf16[512,256]{1,0:T(8,128)(2,1)S(1)}, bf16[512,256]{1,0:T(8,128)(2,1)S(1)}, u32[]{:S(2)}, u32[]{:S(2)}) collective-permute-start(bf16[512,256]{1,0:T(8,128)(2,1)S(1)} %get-tuple-element.45.refs_0_), channel_id=1, source_target_pairs={{0,128},{128,0},{1,129},{129,1},{2,130},{130,2},{3,131},{131,3},{4... | collective-permute-start | bytes 786440 | tf_op jit(solution)/shard_map/ppermute | solution.py:441
  7.7 8.4 %collective-permute-start.2 = (bf16[512,256]{1,0:T(8,128)(2,1)S(1)}, bf16[512,256]{1,0:T(8,128)(2,1)S(1)}, u32[]{:S(2)}, u32[]{:S(2)}) collective-permute-start(bf16[512,256]{1,0:T(8,128)(2,1)S(1)} %get-tuple-element.40.refs_1_), channel_id=1, source_target_pairs={{0,128},{128,0},{1,129},{129,1},{2,130},{130,2},{3,131},{131,3},{4... | collective-permute-start | bytes 786440 | tf_op jit(solution)/shard_map/ppermute | solution.py:444
  7.8 15.4 %collective-permute-start = (bf16[4,64,256]{2,1,0:T(8,128)(2,1)S(1)}, bf16[4,64,256]{2,1,0:T(8,128)(2,1)S(1)}, u32[]{:S(2)}, u32[]{:S(2)}) collective-permute-start(bf16[4,64,256]{2,1,0:T(8,128)(2,1)S(1)} %get-tuple-element.43), channel_id=1, source_target_pairs={{8,16},{16,8},{24,32},{32,24},{40,48},{48,40},{56,64},{64,56},{72,... | collective-permute-start | bytes 393224 | tf_op jit(solution)/shard_map/ppermute | solution.py:442
  14.6 13.9 %collective-permute-start.6 = (bf16[512,256]{1,0:T(8,128)(2,1)S(1)}, bf16[512,256]{1,0:T(8,128)(2,1)S(1)}, u32[]{:S(2)}, u32[]{:S(2)}) collective-permute-start(bf16[512,256]{1,0:T(8,128)(2,1)S(1)} %get-tuple-element.54.refs_2_), channel_id=1, source_target_pairs={{0,128},{128,0},{1,129},{129,1},{2,130},{130,2},{3,131},{131,3},{4... | collective-permute-start | bytes 786440 | tf_op jit(solution)/shard_map/ppermute | solution.py:447
  15.9 16.0 %collective-permute-start.7 = (bf16[512,256]{1,0:T(8,128)(2,1)S(1)}, bf16[512,256]{1,0:T(8,128)(2,1)S(1)}, u32[]{:S(2)}, u32[]{:S(2)}) collective-permute-start(bf16[512,256]{1,0:T(8,128)(2,1)S(1)} %get-tuple-element.61.own_ref), channel_id=1, source_target_pairs={{0,128},{128,0},{1,129},{129,1},{2,130},{130,2},{3,131},{131,3},{4... | collective-permute-start | bytes 786440 | tf_op jit(solution)/shard_map/ppermute | solution.py:448
  16.2 7.1 %collective-permute-start.3 = (bf16[32,256]{1,0:T(8,128)(2,1)S(1)}, bf16[32,256]{1,0:T(8,128)(2,1)S(1)}, u32[]{:S(2)}, u32[]{:S(2)}) collective-permute-start(bf16[32,256]{1,0:T(8,128)(2,1)S(1)} %get-tuple-element.48), channel_id=1, source_target_pairs={{0,1},{1,0},{2,3},{3,2},{4,5},{5,4},{6,7},{7,6},{8,9},{9,8},{10,11... | collective-permute-start | bytes 49160 | tf_op jit(solution)/shard_map/ppermute | solution.py:450
  18.5 5.8 %collective-permute-start.4 = (bf16[32,256]{1,0:T(8,128)(2,1)S(1)}, bf16[32,256]{1,0:T(8,128)(2,1)S(1)}, u32[]{:S(2)}, u32[]{:S(2)}) collective-permute-start(bf16[32,256]{1,0:T(8,128)(2,1)S(1)} %get-tuple-element.49), channel_id=1, source_target_pairs={{1,2},{2,1},{3,4},{4,3},{5,6},{6,5},{7,0},{0,7},{9,10},{10,9},{11,... | collective-permute-start | bytes 49160 | tf_op jit(solution)/shard_map/ppermute | solution.py:451
  24.4 5.1 %collective-permute-start.5 = (bf16[4,64,256]{2,1,0:T(8,128)(2,1)S(1)}, bf16[4,64,256]{2,1,0:T(8,128)(2,1)S(1)}, u32[]{:S(2)}, u32[]{:S(2)}) collective-permute-start(bf16[4,64,256]{2,1,0:T(8,128)(2,1)S(1)} %get-tuple-element.50), channel_id=1, source_target_pairs={{0,8},{8,0},{1,9},{9,1},{2,10},{10,2},{3,11},{11,3},{4,12},{12,4},... | collective-permute-start | bytes 393224 | tf_op jit(solution)/shard_map/ppermute | solution.py:453
  32.8 1.9 %collective-permute-start.8 = (bf16[16,88,128]{2,1,0:T(8,128)(2,1)S(1)}, bf16[16,88,128]{2,1,0:T(8,128)(2,1)S(1)}, u32[]{:S(2)}, u32[]{:S(2)}) collective-permute-start(bf16[16,88,128]{2,1,0:T(8,128)(2,1)S(1)} %get-tuple-element.66), channel_id=1, source_target_pairs={{0,8},{8,0},{1,9},{9,1},{2,10},{10,2},{3,11},{11,3},{4,12},{12,4},... | collective-permute-start | bytes 1081352 | tf_op jit(solution)/shard_map/ppermute | solution.py:464
  49.5 4.3 %collective-permute-start.9 = (bf16[88,128]{1,0:T(8,128)(2,1)S(1)}, bf16[88,128]{1,0:T(8,128)(2,1)S(1)}, u32[]{:S(2)}, u32[]{:S(2)}) collective-permute-start(bf16[88,128]{1,0:T(8,128)(2,1)S(1)} %shard_map.64.own_ref), channel_id=1, source_target_pairs={{0,2},{2,0},{4,6},{6,4},{1,3},{3,1},{5,7},{7,5},{8,10},{10,8},{12,... | collective-permute-start | bytes 67592 | tf_op jit(solution)/shard_map/ppermute | solution.py:474
  53.8 5.8 %collective-permute-start.10 = (bf16[88,128]{1,0:T(8,128)(2,1)S(1)}, bf16[88,128]{1,0:T(8,128)(2,1)S(1)}, u32[]{:S(2)}, u32[]{:S(2)}) collective-permute-start(bf16[88,128]{1,0:T(8,128)(2,1)S(1)} %shard_map.65.own_ref), channel_id=1, source_target_pairs={{0,6},{2,4},{4,2},{6,0},{1,7},{3,5},{5,3},{7,1},{8,14},{10,12},{12... | collective-permute-start | bytes 67592 | tf_op jit(solution)/shard_map/ppermute | solution.py:478
  60.5 12.7 %all-to-all-start.1 = ((bf16[16,80,128]{2,1,0:T(8,128)(2,1)}), bf16[16,80,128]{2,1,0:T(8,128)(2,1)S(1)}, u32[]{:S(2)}, u32[]{:S(2)}) async-start(bf16[16,80,128]{2,1,0:T(8,128)(2,1)} %get-tuple-element.67), calls=%async_computation.1 | async-start | bytes 655360 | tf_op jit(solution)/shard_map/all_to_all | solution.py:490
  73.1 6.2 %collective-permute-start.11 = (bf16[16,80,128]{2,1,0:T(8,128)(2,1)S(1)}, bf16[16,80,128]{2,1,0:T(8,128)(2,1)S(1)}, u32[]{:S(2)}, u32[]{:S(2)}) collective-permute-start(bf16[16,80,128]{2,1,0:T(8,128)(2,1)S(1)} %all-to-all-done.1.own_ref), channel_id=1, source_target_pairs={{0,8},{8,0},{1,9},{9,1},{2,10},{10,2},{3,11},{11,3},{4,12},{12,4},... | collective-permute-start | bytes 983048 | tf_op jit(solution)/shard_map/ppermute | solution.py:499

commit v14 on v12

--- a/solution.py
+++ b/solution.py
@@ -495,7 +495,6 @@
         out_shape=jax.ShapeDtypeStruct((local_cells, width), BF16),
         compiler_params=PARAMS,
     )(shrink, *moved)
-    half, new_modes = lax.optimization_barrier((half, new_modes))
     other_half = lax.ppermute(half, "c", swap)
     projected, gram = pl.pallas_call(
         final_kernel,

time: 80.5 us -> 79.5 us (0.988)
  blocking collectives: 14.4 us -> 26.3 us
  waiting for transfers between devices: 13.9 us -> 6.09 us
  starting transfers between devices: 35.4 us -> 31.1 us
    all_to_all x0 -> x1, blocking collectives: none -> 11.9 us  [local(): half = lax.all_to_all(spread, GROUP, 0, 0)]
    all_to_all x1 -> x0, waiting for transfers between devices: 6.59 us -> none  [local(): half = lax.all_to_all(spread, GROUP, 0, 0)]
    all_to_all x1 -> x0, starting transfers between devices: 4.32 us -> none  [local(): half = lax.all_to_all(spread, GROUP, 0, 0)]
    ppermute x1, waiting for transfers between devices: 1.26 us -> 0.08 us  [local(): other_half = lax.ppermute(half, 'c', swap)]
  transfers between devices with their start and end apart: 13 -> 12, of which waited for: 7 -> 6; matrix products, arithmetic and copies ran while one was open for 0% -> 0% of each run, Pallas kernels for 13% -> 13%
where the time goes in v14:
time: 79.5 us; the launch traced here: 79.3 us
  starting transfers between devices  31.1 us (39%)
  blocking collectives  26.3 us (33%)
  Pallas kernels  15 us (19%)
  waiting for transfers between devices  6.09 us (8%)
    all_to_all x1, blocking collectives, local(): parts = lax.all_to_all(joined, GROUP, 0, 0)  14.4 us
    all_to_all x1, blocking collectives, local(): half = lax.all_to_all(spread, GROUP, 0, 0)  11.9 us
    ppermute x1, starting transfers between devices, local(): other_half = lax.ppermute(half, 'c', swap)  5.22 us
    ppermute x1, starting transfers between devices, local(): lax.ppermute(row_b, SY, both_ways([(i, (i + 1) % n_z) for i in range(1, n...  4.68 us
    ppermute x1, starting transfers between devices, local(): near = lax.ppermute(line, 'zh', [(i, i ^ 3) for i in range(pairs)])  4.58 us
    ppermute x1, starting transfers between devices, local(): xa = lax.ppermute(edge_a, 'c', swap)  4.13 us
    pallas_call x1, Pallas kernels, rest_grad(): pl.pallas_call(functools.partial(rest_grad_kernel, begin), in_specs=[SM,...  4.1 us
    ppermute x1, starting transfers between devices, local(): near = lax.ppermute(line, 'zh', [(i, i ^ 1) for i in range(pairs)])  3.07 us
  transfers between devices with their start and end apart: 12, of which 6 were waited for; matrix products, arithmetic and copies ran while one was open for 0% of the time, Pallas kernels for 13%

profile of v14, /device:TPU:1, one launch (start us, length us, event | category | flops | bytes accessed | tf_op | source)
XLA Modules:
  0.0 79.3 jit_solution(17987191613467815750)
XLA Ops:
  0.7 2.5 %shard_map.58 = (bf16[512,256]{1,0:T(8,128)(2,1)S(1)}, bf16[2,256,512]{2,1,0:T(8,128)(2,1)S(1)}, bf16[2,512,512]{2,1,0:T(8,128)(2,1)S(1)}, bf16[4,64,256]{2,1,0:T(8,128)(2,1)S(1)}) custom-call(s32[1]{0:T(128)} %bitcast.at_ref, bf16[4,8,64,256]{3,2,1,0:T(8,128)(2,1)} %m_hbm.5, bf16[2,256,512]{2,1,0:T(8,128)(2,1)} %c_hbm.1, bf16[2,4,512,512]{3,2,1,0:T(8,128)(2,1)} %bitcast.3), custom_call_target="tpu_custom_call" | custom-call | flops 536870912 | bytes 2097152 | tf_op jit(solution)/shard_map/pallas_call | solution.py:154
  3.2 2.1 %collective-permute-start.1 = (bf16[512,256]{1,0:T(8,128)(2,1)S(1)}, bf16[512,256]{1,0:T(8,128)(2,1)S(1)}, u32[]{:S(2)}, u32[]{:S(2)}) collective-permute-start(bf16[512,256]{1,0:T(8,128)(2,1)S(1)} %get-tuple-element.43.refs_0_), channel_id=1, source_target_pairs={{0,128},{128,0},{1,129},{129,1},{2,130},{130,2},{3,131},{131,3},{4... | collective-permute-start | bytes 786440 | tf_op jit(solution)/shard_map/ppermute | solution.py:441
  5.3 2.4 %shard_map.59 = (bf16[512,256]{1,0:T(8,128)(2,1)S(1)}, bf16[2,512,512]{2,1,0:T(8,128)(2,1)S(1)}) custom-call(bf16[4,8,64,256]{3,2,1,0:T(8,128)(2,1)} %m_hbm.5, bf16[2,256,512]{2,1,0:T(8,128)(2,1)S(1)} %get-tuple-element.39.c_ref, bf16[2,4,512,512]{3,2,1,0:T(8,128)(2,1)} %bitcast.4), custom_call_target="tpu_custom_call" | custom-call | flops 536870912 | bytes 2097152 | tf_op jit(solution)/shard_map/pallas_call | solution.py:172
  7.7 0.1 collective-permute-start.2
  7.8 2.7 %collective-permute-start = (bf16[4,64,256]{2,1,0:T(8,128)(2,1)S(1)}, bf16[4,64,256]{2,1,0:T(8,128)(2,1)S(1)}, u32[]{:S(2)}, u32[]{:S(2)}) collective-permute-start(bf16[4,64,256]{2,1,0:T(8,128)(2,1)S(1)} %get-tuple-element.41), channel_id=1, source_target_pairs={{8,16},{16,8},{24,32},{32,24},{40,48},{48,40},{56,64},{64,56},{72,... | collective-permute-start | bytes 393224 | tf_op jit(solution)/shard_map/ppermute | solution.py:442
  10.5 4.1 %shard_map.60 = (bf16[512,256]{1,0:T(8,128)(2,1)S(1)}, bf16[512,256]{1,0:T(8,128)(2,1)S(1)}, bf16[4,8,64,256]{3,2,1,0:T(8,128)(2,1)S(1)}, bf16[2,2,512,512]{3,2,...) custom-call(s32[1]{0:T(128)} %bitcast.at_ref, ...), custom_call_target="tpu_custom_call" | custom-call | flops 1073741824 | bytes 3670016 | tf_op jit(solution)/shard_map/pallas_call | solution.py:198
  14.6 1.3 %collective-permute-start.6 = (bf16[512,256]{1,0:T(8,128)(2,1)S(1)}, bf16[512,256]{1,0:T(8,128)(2,1)S(1)}, u32[]{:S(2)}, u32[]{:S(2)}) collective-permute-start(bf16[512,256]{1,0:T(8,128)(2,1)S(1)} %get-tuple-element.52.refs_2_), channel_id=1, source_target_pairs={{0,128},{128,0},{1,129},{129,1},{2,130},{130,2},{3,131},{131,3},{4... | collective-permute-start | bytes 786440 | tf_op jit(solution)/shard_map/ppermute | solution.py:447
  15.9 0.2 collective-permute-start.7
  16.1 0.0 collective-permute-done.1.refs_3_
  16.2 0.0 collective-permute-done.2.refs_4_
  16.2 2.4 %collective-permute-start.3 = (bf16[32,256]{1,0:T(8,128)(2,1)S(1)}, bf16[32,256]{1,0:T(8,128)(2,1)S(1)}, u32[]{:S(2)}, u32[]{:S(2)}) collective-permute-start(bf16[32,256]{1,0:T(8,128)(2,1)S(1)} %get-tuple-element.46), channel_id=1, source_target_pairs={{0,1},{1,0},{2,3},{3,2},{4,5},{5,4},{6,7},{7,6},{8,9},{9,8},{10,11... | collective-permute-start | bytes 49160 | tf_op jit(solution)/shard_map/ppermute | solution.py:450
  18.5 4.7 %collective-permute-start.4 = (bf16[32,256]{1,0:T(8,128)(2,1)S(1)}, bf16[32,256]{1,0:T(8,128)(2,1)S(1)}, u32[]{:S(2)}, u32[]{:S(2)}) collective-permute-start(bf16[32,256]{1,0:T(8,128)(2,1)S(1)} %get-tuple-element.47), channel_id=1, source_target_pairs={{1,2},{2,1},{3,4},{4,3},{5,6},{6,5},{7,0},{0,7},{9,10},{10,9},{11,... | collective-permute-start | bytes 49160 | tf_op jit(solution)/shard_map/ppermute | solution.py:451
  23.2 0.0 collective-permute-done.xb_ref
  23.2 0.0 collective-permute-done.3.za_ref
  23.2 1.1 %collective-permute-done.4.zb_ref = bf16[32,256]{1,0:T(8,128)(2,1)S(1)} collective-permute-done((bf16[32,256]{1,0:T(8,128)(2,1)S(1)}, bf16[32,256]{1,0:T(8,128)(2,1)S(1)}, u32[]{:S(2)}, u32[]{:S(2)}) %collective-permute-start.4) | collective-permute-done | bytes 16416 | tf_op jit(solution)/shard_map/ppermute | solution.py:451
  24.4 4.1 %collective-permute-start.5 = (bf16[4,64,256]{2,1,0:T(8,128)(2,1)S(1)}, bf16[4,64,256]{2,1,0:T(8,128)(2,1)S(1)}, u32[]{:S(2)}, u32[]{:S(2)}) collective-permute-start(bf16[4,64,256]{2,1,0:T(8,128)(2,1)S(1)} %get-tuple-element.48), channel_id=1, source_target_pairs={{0,8},{8,0},{1,9},{9,1},{2,10},{10,2},{3,11},{11,3},{4,12},{12,4},... | collective-permute-start | bytes 393224 | tf_op jit(solution)/shard_map/ppermute | solution.py:453
  28.5 0.0 collective-permute-done.6.refs_5_
  28.5 1.0 %collective-permute-done.5.xa_ref = bf16[4,64,256]{2,1,0:T(8,128)(2,1)S(1)} collective-permute-done((bf16[4,64,256]{2,1,0:T(8,128)(2,1)S(1)}, bf16[4,64,256]{2,1,0:T(8,128)(2,1)S(1)}, u32[]{:S(2)}, u32[]{:S(2)}) %collective-permute-start.5) | collective-permute-done | bytes 131104 | tf_op jit(solution)/shard_map/ppermute | solution.py:453
  29.5 2.4 %shard_map.61 = (f32[512,256]{1,0:T(8,128)S(1)}, bf16[1536,256]{1,0:T(8,128)(2,1)S(1)}, f32[2,256,512]{2,1,0:T(8,128)S(1)}, f32[256,256]{1,0:T(8,128)S(1)}, f32[1,256]{1,0:T(1,128)S(1)}) custom-call(s32[1]{0:T(128)} %bitcast.at_ref, bf16[4,8,64,256]{3,2,1,0:T(8,128)(2,1)S(1)} %get-tuple-element.40.m_ref, ...), custom_call_target="tpu_custom_call" | custom-call | flops 1006632960 | bytes 6291456 | tf_op jit(solution)/shard_map/pallas_call | solution.py:316
  31.9 0.0 collective-permute-done.7.got_ref
  31.9 0.9 %shard_map.62 = (bf16[512,256]{1,0:T(8,128)(2,1)S(1)}, bf16[16,88,128]{2,1,0:T(8,128)(2,1)S(1)}, bf16[16,88,128]{2,1,0:T(8,128)(2,1)S(1)}) custom-call(s32[1]{0:T(128)} %bitcast.at_ref, f32[512,256]{1,0:T(8,128)S(1)} %get-tuple-element.58.base_ref, bf16[512,256]{1,0:T(8,128)(2,1)S(1)} %get-tuple-element.59.own_ref, ...), custom_call_target="tpu_custom_call" | custom-call | flops 335544320 | bytes 2097152 | tf_op jit(solution)/shard_map/pallas_call | solution.py:329
  32.8 0.6 collective-permute-start.8
  33.5 1.3 %collective-permute-done.8.got_ref = bf16[16,88,128]{2,1,0:T(8,128)(2,1)S(1)} collective-permute-done((bf16[16,88,128]{2,1,0:T(8,128)(2,1)S(1)}, bf16[16,88,128]{2,1,0:T(8,128)(2,1)S(1)}, u32[]{:S(2)}, u32[]{:S(2)}) %collective-permute-start.8) | collective-permute-done | bytes 360480 | tf_op jit(solution)/shard_map/ppermute | solution.py:464
  34.8 0.1 shard_map.63
  34.9 14.4 %all_to_all.10.in_ref = bf16[16,88,128]{2,1,0:T(8,128)(2,1)S(1)} all-to-all(bf16[16,88,128]{2,1,0:T(8,128)(2,1)S(1)} %shard_map.63), channel_id=1, replica_groups=mesh['ens'=2,'xh'=2,'y'=4,'c'=2,'zh'=4,'zl'=2] {'xh','y','zl'}, dimensions={0} | all-to-all | bytes 720896 | tf_op jit(solution)/shard_map/all_to_all | solution.py:468
  49.3 0.1 shard_map.64.own_ref
  49.4 3.1 %collective-permute-start.9 = (bf16[88,128]{1,0:T(8,128)(2,1)S(1)}, bf16[88,128]{1,0:T(8,128)(2,1)S(1)}, u32[]{:S(2)}, u32[]{:S(2)}) collective-permute-start(bf16[88,128]{1,0:T(8,128)(2,1)S(1)} %shard_map.64.own_ref), channel_id=1, source_target_pairs={{0,2},{2,0},{4,6},{6,4},{1,3},{3,1},{5,7},{7,5},{8,10},{10,8},{12,... | collective-permute-start | bytes 67592 | tf_op jit(solution)/shard_map/ppermute | solution.py:474
  52.4 1.2 %collective-permute-done.9.got_ref = bf16[88,128]{1,0:T(8,128)(2,1)S(1)} collective-permute-done((bf16[88,128]{1,0:T(8,128)(2,1)S(1)}, bf16[88,128]{1,0:T(8,128)(2,1)S(1)}, u32[]{:S(2)}, u32[]{:S(2)}) %collective-permute-start.9) | collective-permute-done | bytes 22560 | tf_op jit(solution)/shard_map/ppermute | solution.py:474
  53.6 4.6 %collective-permute-start.10 = (bf16[88,128]{1,0:T(8,128)(2,1)S(1)}, bf16[88,128]{1,0:T(8,128)(2,1)S(1)}, u32[]{:S(2)}, u32[]{:S(2)}) collective-permute-start(bf16[88,128]{1,0:T(8,128)(2,1)S(1)} %shard_map.65.own_ref), channel_id=1, source_target_pairs={{0,6},{2,4},{4,2},{6,0},{1,7},{3,5},{5,3},{7,1},{8,14},{10,12},{12... | collective-permute-start | bytes 67592 | tf_op jit(solution)/shard_map/ppermute | solution.py:478
  58.2 1.4 %collective-permute-done.10.got_ref = bf16[88,128]{1,0:T(8,128)(2,1)S(1)} collective-permute-done((bf16[88,128]{1,0:T(8,128)(2,1)S(1)}, bf16[88,128]{1,0:T(8,128)(2,1)S(1)}, u32[]{:S(2)}, u32[]{:S(2)}) %collective-permute-start.10) | collective-permute-done | bytes 22560 | tf_op jit(solution)/shard_map/ppermute | solution.py:478
  59.6 0.1 shard_map.66
  59.7 11.9 %all_to_all.11.own_ref = bf16[16,80,128]{2,1,0:T(8,128)(2,1)S(1)} all-to-all(bf16[16,80,128]{2,1,0:T(8,128)(2,1)S(1)} %get-tuple-element.68), channel_id=1, replica_groups=mesh['ens'=2,'xh'=2,'y'=4,'c'=2,'zh'=4,'zl'=2] {'xh','y','zl'}, dimensions={0} | all-to-all | bytes 655360 | tf_op jit(solution)/shard_map/all_to_all | solution.py:490
  71.6 5.2 %collective-permute-start.11 = (bf16[16,80,128]{2,1,0:T(8,128)(2,1)S(1)}, bf16[16,80,128]{2,1,0:T(8,128)(2,1)S(1)}, u32[]{:S(2)}, u32[]{:S(2)}) collective-permute-start(bf16[16,80,128]{2,1,0:T(8,128)(2,1)S(1)} %all_to_all.11.own_ref), channel_id=1, source_target_pairs={{0,8},{8,0},{1,9},{9,1},{2,10},{10,2},{3,11},{11,3},{4,12},{12,4},... | collective-permute-start | bytes 983048 | tf_op jit(solution)/shard_map/ppermute | solution.py:498
  76.9 1.2 %shard_map.67 = bf16[2048,256]{1,0:T(8,128)(2,1)} custom-call(f32[2,128]{1,0:T(2,128)S(1)} %get-tuple-element.65.shrink_ref, bf16[1536,256]{1,0:T(8,128)(2,1)S(1)} %get-tuple-element.66.refs_0_, bf16[512,256]{1,0:T(8,128)(2,1)S(1)} %get-tuple-element.67.refs_1_), custom_call_target="tpu_custom_call" | custom-call | tf_op jit(solution)/shard_map/pallas_call | solution.py:491
  78.0 0.1 collective-permute-done.11.got_ref
  78.1 1.2 %shard_map.68 = (f32[2,256,512]{2,1,0:T(8,128)}, f32[256,256]{1,0:T(8,128)}) custom-call(s32[1]{0:T(128)} %bitcast.at_ref, bf16[16,80,128]{2,1,0:T(8,128)(2,1)S(1)} %all_to_all.11.own_ref, bf16[16,80,128]{2,1,0:T(8,128)(2,1)S(1)} %collective-permute-done.11.got_ref), custom_call_target="tpu_custom_call" | custom-call | tf_op jit(solution)/shard_map/pallas_call | solution.py:499
  (1 shorter events, 0.0 us)
Async XLA Ops:
  3.2 13.0 %collective-permute-start.1 = (bf16[512,256]{1,0:T(8,128)(2,1)S(1)}, bf16[512,256]{1,0:T(8,128)(2,1)S(1)}, u32[]{:S(2)}, u32[]{:S(2)}) collective-permute-start(bf16[512,256]{1,0:T(8,128)(2,1)S(1)} %get-tuple-element.43.refs_0_), channel_id=1, source_target_pairs={{0,128},{128,0},{1,129},{129,1},{2,130},{130,2},{3,131},{131,3},{4... | collective-permute-start | bytes 786440 | tf_op jit(solution)/shard_map/ppermute | solution.py:441
  7.7 8.4 %collective-permute-start.2 = (bf16[512,256]{1,0:T(8,128)(2,1)S(1)}, bf16[512,256]{1,0:T(8,128)(2,1)S(1)}, u32[]{:S(2)}, u32[]{:S(2)}) collective-permute-start(bf16[512,256]{1,0:T(8,128)(2,1)S(1)} %get-tuple-element.38.refs_1_), channel_id=1, source_target_pairs={{0,128},{128,0},{1,129},{129,1},{2,130},{130,2},{3,131},{131,3},{4... | collective-permute-start | bytes 786440 | tf_op jit(solution)/shard_map/ppermute | solution.py:444
  7.8 15.4 %collective-permute-start = (bf16[4,64,256]{2,1,0:T(8,128)(2,1)S(1)}, bf16[4,64,256]{2,1,0:T(8,128)(2,1)S(1)}, u32[]{:S(2)}, u32[]{:S(2)}) collective-permute-start(bf16[4,64,256]{2,1,0:T(8,128)(2,1)S(1)} %get-tuple-element.41), channel_id=1, source_target_pairs={{8,16},{16,8},{24,32},{32,24},{40,48},{48,40},{56,64},{64,56},{72,... | collective-permute-start | bytes 393224 | tf_op jit(solution)/shard_map/ppermute | solution.py:442
  14.6 13.9 %collective-permute-start.6 = (bf16[512,256]{1,0:T(8,128)(2,1)S(1)}, bf16[512,256]{1,0:T(8,128)(2,1)S(1)}, u32[]{:S(2)}, u32[]{:S(2)}) collective-permute-start(bf16[512,256]{1,0:T(8,128)(2,1)S(1)} %get-tuple-element.52.refs_2_), channel_id=1, source_target_pairs={{0,128},{128,0},{1,129},{129,1},{2,130},{130,2},{3,131},{131,3},{4... | collective-permute-start | bytes 786440 | tf_op jit(solution)/shard_map/ppermute | solution.py:447
  15.9 16.0 %collective-permute-start.7 = (bf16[512,256]{1,0:T(8,128)(2,1)S(1)}, bf16[512,256]{1,0:T(8,128)(2,1)S(1)}, u32[]{:S(2)}, u32[]{:S(2)}) collective-permute-start(bf16[512,256]{1,0:T(8,128)(2,1)S(1)} %get-tuple-element.59.own_ref), channel_id=1, source_target_pairs={{0,128},{128,0},{1,129},{129,1},{2,130},{130,2},{3,131},{131,3},{4... | collective-permute-start | bytes 786440 | tf_op jit(solution)/shard_map/ppermute | solution.py:448
  16.2 7.1 %collective-permute-start.3 = (bf16[32,256]{1,0:T(8,128)(2,1)S(1)}, bf16[32,256]{1,0:T(8,128)(2,1)S(1)}, u32[]{:S(2)}, u32[]{:S(2)}) collective-permute-start(bf16[32,256]{1,0:T(8,128)(2,1)S(1)} %get-tuple-element.46), channel_id=1, source_target_pairs={{0,1},{1,0},{2,3},{3,2},{4,5},{5,4},{6,7},{7,6},{8,9},{9,8},{10,11... | collective-permute-start | bytes 49160 | tf_op jit(solution)/shard_map/ppermute | solution.py:450
  18.5 5.8 %collective-permute-start.4 = (bf16[32,256]{1,0:T(8,128)(2,1)S(1)}, bf16[32,256]{1,0:T(8,128)(2,1)S(1)}, u32[]{:S(2)}, u32[]{:S(2)}) collective-permute-start(bf16[32,256]{1,0:T(8,128)(2,1)S(1)} %get-tuple-element.47), channel_id=1, source_target_pairs={{1,2},{2,1},{3,4},{4,3},{5,6},{6,5},{7,0},{0,7},{9,10},{10,9},{11,... | collective-permute-start | bytes 49160 | tf_op jit(solution)/shard_map/ppermute | solution.py:451
  24.4 5.1 %collective-permute-start.5 = (bf16[4,64,256]{2,1,0:T(8,128)(2,1)S(1)}, bf16[4,64,256]{2,1,0:T(8,128)(2,1)S(1)}, u32[]{:S(2)}, u32[]{:S(2)}) collective-permute-start(bf16[4,64,256]{2,1,0:T(8,128)(2,1)S(1)} %get-tuple-element.48), channel_id=1, source_target_pairs={{0,8},{8,0},{1,9},{9,1},{2,10},{10,2},{3,11},{11,3},{4,12},{12,4},... | collective-permute-start | bytes 393224 | tf_op jit(solution)/shard_map/ppermute | solution.py:453
  32.8 1.9 %collective-permute-start.8 = (bf16[16,88,128]{2,1,0:T(8,128)(2,1)S(1)}, bf16[16,88,128]{2,1,0:T(8,128)(2,1)S(1)}, u32[]{:S(2)}, u32[]{:S(2)}) collective-permute-start(bf16[16,88,128]{2,1,0:T(8,128)(2,1)S(1)} %get-tuple-element.64), channel_id=1, source_target_pairs={{0,8},{8,0},{1,9},{9,1},{2,10},{10,2},{3,11},{11,3},{4,12},{12,4},... | collective-permute-start | bytes 1081352 | tf_op jit(solution)/shard_map/ppermute | solution.py:464
  49.4 4.3 %collective-permute-start.9 = (bf16[88,128]{1,0:T(8,128)(2,1)S(1)}, bf16[88,128]{1,0:T(8,128)(2,1)S(1)}, u32[]{:S(2)}, u32[]{:S(2)}) collective-permute-start(bf16[88,128]{1,0:T(8,128)(2,1)S(1)} %shard_map.64.own_ref), channel_id=1, source_target_pairs={{0,2},{2,0},{4,6},{6,4},{1,3},{3,1},{5,7},{7,5},{8,10},{10,8},{12,... | collective-permute-start | bytes 67592 | tf_op jit(solution)/shard_map/ppermute | solution.py:474
  53.6 5.9 %collective-permute-start.10 = (bf16[88,128]{1,0:T(8,128)(2,1)S(1)}, bf16[88,128]{1,0:T(8,128)(2,1)S(1)}, u32[]{:S(2)}, u32[]{:S(2)}) collective-permute-start(bf16[88,128]{1,0:T(8,128)(2,1)S(1)} %shard_map.65.own_ref), channel_id=1, source_target_pairs={{0,6},{2,4},{4,2},{6,0},{1,7},{3,5},{5,3},{7,1},{8,14},{10,12},{12... | collective-permute-start | bytes 67592 | tf_op jit(solution)/shard_map/ppermute | solution.py:478
  71.6 6.5 %collective-permute-start.11 = (bf16[16,80,128]{2,1,0:T(8,128)(2,1)S(1)}, bf16[16,80,128]{2,1,0:T(8,128)(2,1)S(1)}, u32[]{:S(2)}, u32[]{:S(2)}) collective-permute-start(bf16[16,80,128]{2,1,0:T(8,128)(2,1)S(1)} %all_to_all.11.own_ref), channel_id=1, source_target_pairs={{0,8},{8,0},{1,9},{9,1},{2,10},{10,2},{3,11},{11,3},{4,12},{12,4},... | collective-permute-start | bytes 983048 | tf_op jit(solution)/shard_map/ppermute | solution.py:498

commit v15 on v14

--- a/solution.py
+++ b/solution.py
@@ -279,7 +279,7 @@
 
 
 def last_kernel(at_ref, base_ref, own_ref, got_ref, x_ref, proj_in, gram_in, squares_in, *refs):
-    moved_ref, keep_ref, send_ref, proj_ref, gram_ref = refs
+    moved_ref, send_ref, proj_ref, gram_ref, squares_ref = refs
     moved, squares = move(base_ref[...], own_ref, got_ref)
     moved_ref[...] = moved
     squares = squares + squares_in[...]
@@ -292,7 +292,7 @@
     pair = jnp.concatenate([squares[:, 0:128], squares[:, 128:256]], axis=0)
     packed = split_squares(pair, 8).astype(BF16)
     emit(send_ref, 1 - core, proj_ref, gram_ref, packed)
-    emit(keep_ref, core, proj_ref, gram_ref, packed)
+    squares_ref[...] = squares
 
 
 def step_cost(members, cells, frames, width):
@@ -326,17 +326,17 @@
         cost_estimate=step_cost(members, most * cells, frames, width),
     )(place, *args)
     args = [base, owns[most], gots[most], series[most], *carry]
-    tail, keep, send = pl.pallas_call(
+    tail, send, *sums = pl.pallas_call(
         last_kernel,
         in_specs=[SM] + [VM] * len(args),
-        out_specs=[VM] * 3,
+        out_specs=[VM] * 5,
         out_shape=[jax.ShapeDtypeStruct((cells, width), BF16)]
-        + [jax.ShapeDtypeStruct((PARTS, PART_ROWS, 128), BF16)] * 2,
-        scratch_shapes=[pltpu.VMEM(s.shape, F32) for s in sums[:2]],
+        + [jax.ShapeDtypeStruct((PARTS, PART_ROWS, 128), BF16), *sums],
+        input_output_aliases={5: 2, 6: 3, 7: 4},
         compiler_params=PARAMS,
         cost_estimate=step_cost(members, cells, frames, width),
     )(place, *args)
-    return [moved, tail], keep, send
+    return [moved, tail], sums, send
 
 
 def whole_squares(part):
@@ -347,13 +347,21 @@
     return split_squares(whole_squares(total), 8).astype(BF16)
 
 
-def join_kernel(keep_ref, got_ref, out_ref):
-    out_ref[:, 0:SUM_ROWS, :] = (
-        keep_ref[:, 0:SUM_ROWS, :].astype(F32) + got_ref[:, 0:SUM_ROWS, :].astype(F32)
-    ).astype(BF16)
-    tail = keep_ref[0].astype(F32) + got_ref[0].astype(F32)
-    packed = packed_squares(tail)
+def join_kernel(at_ref, proj_ref, gram_ref, squares_ref, got_ref, out_ref):
+    core = core_of(at_ref[0])
+    members, width, _ = proj_ref.shape
+    squares = squares_ref[...]
+    pair = jnp.concatenate([squares[:, 0:128], squares[:, 128:256]], axis=0)
+    packed = split_squares(pair + whole_squares(got_ref[0].astype(F32)), 8).astype(BF16)
     for j in range(PARTS):
+        tb, m, r = j // 8, (j // 4) % members, j % 4
+        got = got_ref[j].astype(F32)
+        at = pl.multiple_of((core * 2 + tb) * 128, 128)
+        block = proj_ref[m, r * PROJ_ROWS : (r + 1) * PROJ_ROWS, pl.ds(at, 128)]
+        out_ref[j, 0:PROJ_ROWS, :] = (block + got[0:PROJ_ROWS, :]).astype(BF16)
+        at = pl.multiple_of(core * 128, 128)
+        block = gram_ref[j * GRAM_ROWS : (j + 1) * GRAM_ROWS, pl.ds(at, 128)]
+        out_ref[j, PROJ_ROWS:SUM_ROWS, :] = (block + got[PROJ_ROWS:SUM_ROWS, :]).astype(BF16)
         out_ref[j, SUM_ROWS:PART_ROWS, :] = packed
 
 
@@ -451,7 +459,7 @@
     zb = lax.ppermute(row_b, SY, both_ways([(i, (i + 1) % n_z) for i in range(1, n_z, 2)]))
     xb, edge_a, za, zb = lax.optimization_barrier((xb, edge_a, za, zb))
     xa = lax.ppermute(edge_a, "c", swap)
-    moved, keep, send = steps(
+    moved, sums, send = steps(
         place,
         modes,
         (xa, xb, za, zb),
@@ -463,8 +471,8 @@
     part_shape = jax.ShapeDtypeStruct((PARTS, PART_ROWS, 128), BF16)
     other = lax.ppermute(send, "c", swap)
     joined = pl.pallas_call(
-        join_kernel, in_specs=[VM, VM], out_specs=VM, out_shape=part_shape, compiler_params=PARAMS
-    )(keep, other)
+        join_kernel, in_specs=[SM] + [VM] * 4, out_specs=VM, out_shape=part_shape, compiler_params=PARAMS
+    )(place, *sums, other)
     parts = lax.all_to_all(joined, GROUP, 0, 0)
     line_shape = jax.ShapeDtypeStruct((PART_ROWS, 128), BF16)
     line = pl.pallas_call(

time: 79.5 us -> 79.5 us (level)
  no operation moved by 1% of the time
where the time goes in v15:
time: 79.5 us; the launch traced here: 79.4 us
  starting transfers between devices  31.1 us (39%)
  blocking collectives  26.3 us (33%)
  Pallas kernels  15.1 us (19%)
  waiting for transfers between devices  6.1 us (8%)
    all_to_all x1, blocking collectives, local(): parts = lax.all_to_all(joined, GROUP, 0, 0)  14.4 us
    all_to_all x1, blocking collectives, local(): half = lax.all_to_all(spread, GROUP, 0, 0)  11.9 us
    ppermute x1, starting transfers between devices, local(): other_half = lax.ppermute(half, 'c', swap)  5.22 us
    ppermute x1, starting transfers between devices, local(): lax.ppermute(row_b, SY, both_ways([(i, (i + 1) % n_z) for i in range(1, n...  4.68 us
    ppermute x1, starting transfers between devices, local(): near = lax.ppermute(line, 'zh', [(i, i ^ 3) for i in range(pairs)])  4.58 us
    ppermute x1, starting transfers between devices, local(): xa = lax.ppermute(edge_a, 'c', swap)  4.13 us
    pallas_call x1, Pallas kernels, rest_grad(): pl.pallas_call(functools.partial(rest_grad_kernel, begin), in_specs=[SM,...  4.1 us
    ppermute x1, starting transfers between devices, local(): near = lax.ppermute(line, 'zh', [(i, i ^ 1) for i in range(pairs)])  3.08 us
  transfers between devices with their start and end apart: 12, of which 6 were waited for; matrix products, arithmetic and copies ran while one was open for 0% of the time, Pallas kernels for 13%

profile of v15, /device:TPU:1, one launch (start us, length us, event | category | flops | bytes accessed | tf_op | source)
XLA Modules:
  0.0 79.4 jit_solution(1610174873297610086)
XLA Ops:
  0.7 2.5 %shard_map.58 = (bf16[512,256]{1,0:T(8,128)(2,1)S(1)}, bf16[2,256,512]{2,1,0:T(8,128)(2,1)S(1)}, bf16[2,512,512]{2,1,0:T(8,128)(2,1)S(1)}, bf16[4,64,256]{2,1,0:T(8,128)(2,1)S(1)}) custom-call(s32[1]{0:T(128)} %bitcast.at_ref, bf16[4,8,64,256]{3,2,1,0:T(8,128)(2,1)} %m_hbm.5, bf16[2,256,512]{2,1,0:T(8,128)(2,1)} %c_hbm.1, bf16[2,4,512,512]{3,2,1,0:T(8,128)(2,1)} %bitcast.3), custom_call_target="tpu_custom_call" | custom-call | flops 536870912 | bytes 2097152 | tf_op jit(solution)/shard_map/pallas_call | solution.py:154
  3.2 2.1 %collective-permute-start.1 = (bf16[512,256]{1,0:T(8,128)(2,1)S(1)}, bf16[512,256]{1,0:T(8,128)(2,1)S(1)}, u32[]{:S(2)}, u32[]{:S(2)}) collective-permute-start(bf16[512,256]{1,0:T(8,128)(2,1)S(1)} %get-tuple-element.45.refs_0_), channel_id=1, source_target_pairs={{0,128},{128,0},{1,129},{129,1},{2,130},{130,2},{3,131},{131,3},{4... | collective-permute-start | bytes 786440 | tf_op jit(solution)/shard_map/ppermute | solution.py:449
  5.3 2.4 %shard_map.59 = (bf16[512,256]{1,0:T(8,128)(2,1)S(1)}, bf16[2,512,512]{2,1,0:T(8,128)(2,1)S(1)}) custom-call(bf16[4,8,64,256]{3,2,1,0:T(8,128)(2,1)} %m_hbm.5, bf16[2,256,512]{2,1,0:T(8,128)(2,1)S(1)} %get-tuple-element.41.c_ref, bf16[2,4,512,512]{3,2,1,0:T(8,128)(2,1)} %bitcast.4), custom_call_target="tpu_custom_call" | custom-call | flops 536870912 | bytes 2097152 | tf_op jit(solution)/shard_map/pallas_call | solution.py:172
  7.7 0.1 collective-permute-start.2
  7.8 2.7 %collective-permute-start = (bf16[4,64,256]{2,1,0:T(8,128)(2,1)S(1)}, bf16[4,64,256]{2,1,0:T(8,128)(2,1)S(1)}, u32[]{:S(2)}, u32[]{:S(2)}) collective-permute-start(bf16[4,64,256]{2,1,0:T(8,128)(2,1)S(1)} %get-tuple-element.43), channel_id=1, source_target_pairs={{8,16},{16,8},{24,32},{32,24},{40,48},{48,40},{56,64},{64,56},{72,... | collective-permute-start | bytes 393224 | tf_op jit(solution)/shard_map/ppermute | solution.py:450
  10.5 4.1 %shard_map.60 = (bf16[512,256]{1,0:T(8,128)(2,1)S(1)}, bf16[512,256]{1,0:T(8,128)(2,1)S(1)}, bf16[4,8,64,256]{3,2,1,0:T(8,128)(2,1)S(1)}, bf16[2,2,512,512]{3,2,...) custom-call(s32[1]{0:T(128)} %bitcast.at_ref, ...), custom_call_target="tpu_custom_call" | custom-call | flops 1073741824 | bytes 3670016 | tf_op jit(solution)/shard_map/pallas_call | solution.py:198
  14.6 1.3 %collective-permute-start.6 = (bf16[512,256]{1,0:T(8,128)(2,1)S(1)}, bf16[512,256]{1,0:T(8,128)(2,1)S(1)}, u32[]{:S(2)}, u32[]{:S(2)}) collective-permute-start(bf16[512,256]{1,0:T(8,128)(2,1)S(1)} %get-tuple-element.54.refs_2_), channel_id=1, source_target_pairs={{0,128},{128,0},{1,129},{129,1},{2,130},{130,2},{3,131},{131,3},{4... | collective-permute-start | bytes 786440 | tf_op jit(solution)/shard_map/ppermute | solution.py:455
  15.9 0.2 collective-permute-start.7
  16.1 0.0 collective-permute-done.1.refs_3_
  16.2 0.0 collective-permute-done.2.refs_4_
  16.2 2.4 %collective-permute-start.3 = (bf16[32,256]{1,0:T(8,128)(2,1)S(1)}, bf16[32,256]{1,0:T(8,128)(2,1)S(1)}, u32[]{:S(2)}, u32[]{:S(2)}) collective-permute-start(bf16[32,256]{1,0:T(8,128)(2,1)S(1)} %get-tuple-element.48), channel_id=1, source_target_pairs={{0,1},{1,0},{2,3},{3,2},{4,5},{5,4},{6,7},{7,6},{8,9},{9,8},{10,11... | collective-permute-start | bytes 49160 | tf_op jit(solution)/shard_map/ppermute | solution.py:458
  18.5 4.7 %collective-permute-start.4 = (bf16[32,256]{1,0:T(8,128)(2,1)S(1)}, bf16[32,256]{1,0:T(8,128)(2,1)S(1)}, u32[]{:S(2)}, u32[]{:S(2)}) collective-permute-start(bf16[32,256]{1,0:T(8,128)(2,1)S(1)} %get-tuple-element.49), channel_id=1, source_target_pairs={{1,2},{2,1},{3,4},{4,3},{5,6},{6,5},{7,0},{0,7},{9,10},{10,9},{11,... | collective-permute-start | bytes 49160 | tf_op jit(solution)/shard_map/ppermute | solution.py:459
  23.2 0.0 collective-permute-done.xb_ref
  23.2 0.0 collective-permute-done.3.za_ref
  23.2 1.1 %collective-permute-done.4.zb_ref = bf16[32,256]{1,0:T(8,128)(2,1)S(1)} collective-permute-done((bf16[32,256]{1,0:T(8,128)(2,1)S(1)}, bf16[32,256]{1,0:T(8,128)(2,1)S(1)}, u32[]{:S(2)}, u32[]{:S(2)}) %collective-permute-start.4) | collective-permute-done | bytes 16416 | tf_op jit(solution)/shard_map/ppermute | solution.py:459
  24.4 4.1 %collective-permute-start.5 = (bf16[4,64,256]{2,1,0:T(8,128)(2,1)S(1)}, bf16[4,64,256]{2,1,0:T(8,128)(2,1)S(1)}, u32[]{:S(2)}, u32[]{:S(2)}) collective-permute-start(bf16[4,64,256]{2,1,0:T(8,128)(2,1)S(1)} %get-tuple-element.50), channel_id=1, source_target_pairs={{0,8},{8,0},{1,9},{9,1},{2,10},{10,2},{3,11},{11,3},{4,12},{12,4},... | collective-permute-start | bytes 393224 | tf_op jit(solution)/shard_map/ppermute | solution.py:461
  28.5 0.0 collective-permute-done.6.refs_5_
  28.5 1.0 %collective-permute-done.5.xa_ref = bf16[4,64,256]{2,1,0:T(8,128)(2,1)S(1)} collective-permute-done((bf16[4,64,256]{2,1,0:T(8,128)(2,1)S(1)}, bf16[4,64,256]{2,1,0:T(8,128)(2,1)S(1)}, u32[]{:S(2)}, u32[]{:S(2)}) %collective-permute-start.5) | collective-permute-done | bytes 131104 | tf_op jit(solution)/shard_map/ppermute | solution.py:461
  29.5 2.4 %shard_map.61 = (f32[512,256]{1,0:T(8,128)S(1)}, bf16[1536,256]{1,0:T(8,128)(2,1)S(1)}, f32[2,256,512]{2,1,0:T(8,128)S(1)}, f32[256,256]{1,0:T(8,128)S(1)}, f32[1,256]{1,0:T(1,128)S(1)}) custom-call(s32[1]{0:T(128)} %bitcast.at_ref, bf16[4,8,64,256]{3,2,1,0:T(8,128)(2,1)S(1)} %get-tuple-element.42.m_ref, ...), custom_call_target="tpu_custom_call" | custom-call | flops 1006632960 | bytes 6291456 | tf_op jit(solution)/shard_map/pallas_call | solution.py:316
  31.9 0.0 collective-permute-done.7.got_ref
  31.9 1.0 %shard_map.62 = (bf16[512,256]{1,0:T(8,128)(2,1)S(1)}, bf16[16,88,128]{2,1,0:T(8,128)(2,1)S(1)}, f32[2,256,512]{2,1,0:T(8,128)S(1)}, f32[256,256]{1,0:T(8,128)S(1)}, f32[1,256]{1,0:T(1,128)S(1)}) custom-call(s32[1]{0:T(128)} %bitcast.at_ref, f32[512,256]{1,0:T(8,128)S(1)} %get-tuple-element.60.base_ref, ...), custom_call_target="tpu_custom_call", output_to_operand_aliasing={{2}: (5, {}), {3}: (6, {}), {4}: (7, {})} | custom-call | flops 335544320 | bytes 2097152 | tf_op jit(solution)/shard_map/pallas_call | solution.py:329
  32.9 0.6 collective-permute-start.8
  33.5 1.3 %collective-permute-done.8.got_ref = bf16[16,88,128]{2,1,0:T(8,128)(2,1)S(1)} collective-permute-done((bf16[16,88,128]{2,1,0:T(8,128)(2,1)S(1)}, bf16[16,88,128]{2,1,0:T(8,128)(2,1)S(1)}, u32[]{:S(2)}, u32[]{:S(2)}) %collective-permute-start.8) | collective-permute-done | bytes 360480 | tf_op jit(solution)/shard_map/ppermute | solution.py:472
  34.8 0.1 shard_map.63
  34.9 14.4 %all_to_all.10.in_ref = bf16[16,88,128]{2,1,0:T(8,128)(2,1)S(1)} all-to-all(bf16[16,88,128]{2,1,0:T(8,128)(2,1)S(1)} %shard_map.63), channel_id=1, replica_groups=mesh['ens'=2,'xh'=2,'y'=4,'c'=2,'zh'=4,'zl'=2] {'xh','y','zl'}, dimensions={0} | all-to-all | bytes 720896 | tf_op jit(solution)/shard_map/all_to_all | solution.py:476
  49.3 0.1 shard_map.64.own_ref
  49.4 3.1 %collective-permute-start.9 = (bf16[88,128]{1,0:T(8,128)(2,1)S(1)}, bf16[88,128]{1,0:T(8,128)(2,1)S(1)}, u32[]{:S(2)}, u32[]{:S(2)}) collective-permute-start(bf16[88,128]{1,0:T(8,128)(2,1)S(1)} %shard_map.64.own_ref), channel_id=1, source_target_pairs={{0,2},{2,0},{4,6},{6,4},{1,3},{3,1},{5,7},{7,5},{8,10},{10,8},{12,... | collective-permute-start | bytes 67592 | tf_op jit(solution)/shard_map/ppermute | solution.py:482
  52.5 1.2 %collective-permute-done.9.got_ref = bf16[88,128]{1,0:T(8,128)(2,1)S(1)} collective-permute-done((bf16[88,128]{1,0:T(8,128)(2,1)S(1)}, bf16[88,128]{1,0:T(8,128)(2,1)S(1)}, u32[]{:S(2)}, u32[]{:S(2)}) %collective-permute-start.9) | collective-permute-done | bytes 22560 | tf_op jit(solution)/shard_map/ppermute | solution.py:482
  53.7 4.6 %collective-permute-start.10 = (bf16[88,128]{1,0:T(8,128)(2,1)S(1)}, bf16[88,128]{1,0:T(8,128)(2,1)S(1)}, u32[]{:S(2)}, u32[]{:S(2)}) collective-permute-start(bf16[88,128]{1,0:T(8,128)(2,1)S(1)} %shard_map.65.own_ref), channel_id=1, source_target_pairs={{0,6},{2,4},{4,2},{6,0},{1,7},{3,5},{5,3},{7,1},{8,14},{10,12},{12... | collective-permute-start | bytes 67592 | tf_op jit(solution)/shard_map/ppermute | solution.py:486
  58.3 1.4 %collective-permute-done.10.got_ref = bf16[88,128]{1,0:T(8,128)(2,1)S(1)} collective-permute-done((bf16[88,128]{1,0:T(8,128)(2,1)S(1)}, bf16[88,128]{1,0:T(8,128)(2,1)S(1)}, u32[]{:S(2)}, u32[]{:S(2)}) %collective-permute-start.10) | collective-permute-done | bytes 22560 | tf_op jit(solution)/shard_map/ppermute | solution.py:486
  59.6 0.1 shard_map.66
  59.8 11.9 %all_to_all.11.own_ref = bf16[16,80,128]{2,1,0:T(8,128)(2,1)S(1)} all-to-all(bf16[16,80,128]{2,1,0:T(8,128)(2,1)S(1)} %get-tuple-element.72), channel_id=1, replica_groups=mesh['ens'=2,'xh'=2,'y'=4,'c'=2,'zh'=4,'zl'=2] {'xh','y','zl'}, dimensions={0} | all-to-all | bytes 655360 | tf_op jit(solution)/shard_map/all_to_all | solution.py:498
  71.7 5.2 %collective-permute-start.11 = (bf16[16,80,128]{2,1,0:T(8,128)(2,1)S(1)}, bf16[16,80,128]{2,1,0:T(8,128)(2,1)S(1)}, u32[]{:S(2)}, u32[]{:S(2)}) collective-permute-start(bf16[16,80,128]{2,1,0:T(8,128)(2,1)S(1)} %all_to_all.11.own_ref), channel_id=1, source_target_pairs={{0,8},{8,0},{1,9},{9,1},{2,10},{10,2},{3,11},{11,3},{4,12},{12,4},... | collective-permute-start | bytes 983048 | tf_op jit(solution)/shard_map/ppermute | solution.py:506
  76.9 1.2 %shard_map.67 = bf16[2048,256]{1,0:T(8,128)(2,1)} custom-call(f32[2,128]{1,0:T(2,128)S(1)} %get-tuple-element.69.shrink_ref, bf16[1536,256]{1,0:T(8,128)(2,1)S(1)} %get-tuple-element.70.refs_0_, bf16[512,256]{1,0:T(8,128)(2,1)S(1)} %get-tuple-element.71.refs_1_), custom_call_target="tpu_custom_call" | custom-call | tf_op jit(solution)/shard_map/pallas_call | solution.py:499
  78.1 0.1 collective-permute-done.11.got_ref
  78.2 1.2 %shard_map.68 = (f32[2,256,512]{2,1,0:T(8,128)}, f32[256,256]{1,0:T(8,128)}) custom-call(s32[1]{0:T(128)} %bitcast.at_ref, bf16[16,80,128]{2,1,0:T(8,128)(2,1)S(1)} %all_to_all.11.own_ref, bf16[16,80,128]{2,1,0:T(8,128)(2,1)S(1)} %collective-permute-done.11.got_ref), custom_call_target="tpu_custom_call" | custom-call | tf_op jit(solution)/shard_map/pallas_call | solution.py:507
  (1 shorter events, 0.0 us)
Async XLA Ops:
  3.2 13.0 %collective-permute-start.1 = (bf16[512,256]{1,0:T(8,128)(2,1)S(1)}, bf16[512,256]{1,0:T(8,128)(2,1)S(1)}, u32[]{:S(2)}, u32[]{:S(2)}) collective-permute-start(bf16[512,256]{1,0:T(8,128)(2,1)S(1)} %get-tuple-element.45.refs_0_), channel_id=1, source_target_pairs={{0,128},{128,0},{1,129},{129,1},{2,130},{130,2},{3,131},{131,3},{4... | collective-permute-start | bytes 786440 | tf_op jit(solution)/shard_map/ppermute | solution.py:449
  7.7 8.4 %collective-permute-start.2 = (bf16[512,256]{1,0:T(8,128)(2,1)S(1)}, bf16[512,256]{1,0:T(8,128)(2,1)S(1)}, u32[]{:S(2)}, u32[]{:S(2)}) collective-permute-start(bf16[512,256]{1,0:T(8,128)(2,1)S(1)} %get-tuple-element.40.refs_1_), channel_id=1, source_target_pairs={{0,128},{128,0},{1,129},{129,1},{2,130},{130,2},{3,131},{131,3},{4... | collective-permute-start | bytes 786440 | tf_op jit(solution)/shard_map/ppermute | solution.py:452
  7.8 15.4 %collective-permute-start = (bf16[4,64,256]{2,1,0:T(8,128)(2,1)S(1)}, bf16[4,64,256]{2,1,0:T(8,128)(2,1)S(1)}, u32[]{:S(2)}, u32[]{:S(2)}) collective-permute-start(bf16[4,64,256]{2,1,0:T(8,128)(2,1)S(1)} %get-tuple-element.43), channel_id=1, source_target_pairs={{8,16},{16,8},{24,32},{32,24},{40,48},{48,40},{56,64},{64,56},{72,... | collective-permute-start | bytes 393224 | tf_op jit(solution)/shard_map/ppermute | solution.py:450
  14.6 13.9 %collective-permute-start.6 = (bf16[512,256]{1,0:T(8,128)(2,1)S(1)}, bf16[512,256]{1,0:T(8,128)(2,1)S(1)}, u32[]{:S(2)}, u32[]{:S(2)}) collective-permute-start(bf16[512,256]{1,0:T(8,128)(2,1)S(1)} %get-tuple-element.54.refs_2_), channel_id=1, source_target_pairs={{0,128},{128,0},{1,129},{129,1},{2,130},{130,2},{3,131},{131,3},{4... | collective-permute-start | bytes 786440 | tf_op jit(solution)/shard_map/ppermute | solution.py:455
  15.9 16.0 %collective-permute-start.7 = (bf16[512,256]{1,0:T(8,128)(2,1)S(1)}, bf16[512,256]{1,0:T(8,128)(2,1)S(1)}, u32[]{:S(2)}, u32[]{:S(2)}) collective-permute-start(bf16[512,256]{1,0:T(8,128)(2,1)S(1)} %get-tuple-element.61.own_ref), channel_id=1, source_target_pairs={{0,128},{128,0},{1,129},{129,1},{2,130},{130,2},{3,131},{131,3},{4... | collective-permute-start | bytes 786440 | tf_op jit(solution)/shard_map/ppermute | solution.py:456
  16.2 7.1 %collective-permute-start.3 = (bf16[32,256]{1,0:T(8,128)(2,1)S(1)}, bf16[32,256]{1,0:T(8,128)(2,1)S(1)}, u32[]{:S(2)}, u32[]{:S(2)}) collective-permute-start(bf16[32,256]{1,0:T(8,128)(2,1)S(1)} %get-tuple-element.48), channel_id=1, source_target_pairs={{0,1},{1,0},{2,3},{3,2},{4,5},{5,4},{6,7},{7,6},{8,9},{9,8},{10,11... | collective-permute-start | bytes 49160 | tf_op jit(solution)/shard_map/ppermute | solution.py:458
  18.5 5.8 %collective-permute-start.4 = (bf16[32,256]{1,0:T(8,128)(2,1)S(1)}, bf16[32,256]{1,0:T(8,128)(2,1)S(1)}, u32[]{:S(2)}, u32[]{:S(2)}) collective-permute-start(bf16[32,256]{1,0:T(8,128)(2,1)S(1)} %get-tuple-element.49), channel_id=1, source_target_pairs={{1,2},{2,1},{3,4},{4,3},{5,6},{6,5},{7,0},{0,7},{9,10},{10,9},{11,... | collective-permute-start | bytes 49160 | tf_op jit(solution)/shard_map/ppermute | solution.py:459
  24.4 5.1 %collective-permute-start.5 = (bf16[4,64,256]{2,1,0:T(8,128)(2,1)S(1)}, bf16[4,64,256]{2,1,0:T(8,128)(2,1)S(1)}, u32[]{:S(2)}, u32[]{:S(2)}) collective-permute-start(bf16[4,64,256]{2,1,0:T(8,128)(2,1)S(1)} %get-tuple-element.50), channel_id=1, source_target_pairs={{0,8},{8,0},{1,9},{9,1},{2,10},{10,2},{3,11},{11,3},{4,12},{12,4},... | collective-permute-start | bytes 393224 | tf_op jit(solution)/shard_map/ppermute | solution.py:461
  32.9 1.9 %collective-permute-start.8 = (bf16[16,88,128]{2,1,0:T(8,128)(2,1)S(1)}, bf16[16,88,128]{2,1,0:T(8,128)(2,1)S(1)}, u32[]{:S(2)}, u32[]{:S(2)}) collective-permute-start(bf16[16,88,128]{2,1,0:T(8,128)(2,1)S(1)} %get-tuple-element.68), channel_id=1, source_target_pairs={{0,8},{8,0},{1,9},{9,1},{2,10},{10,2},{3,11},{11,3},{4,12},{12,4},... | collective-permute-start | bytes 1081352 | tf_op jit(solution)/shard_map/ppermute | solution.py:472
  49.4 4.3 %collective-permute-start.9 = (bf16[88,128]{1,0:T(8,128)(2,1)S(1)}, bf16[88,128]{1,0:T(8,128)(2,1)S(1)}, u32[]{:S(2)}, u32[]{:S(2)}) collective-permute-start(bf16[88,128]{1,0:T(8,128)(2,1)S(1)} %shard_map.64.own_ref), channel_id=1, source_target_pairs={{0,2},{2,0},{4,6},{6,4},{1,3},{3,1},{5,7},{7,5},{8,10},{10,8},{12,... | collective-permute-start | bytes 67592 | tf_op jit(solution)/shard_map/ppermute | solution.py:482
  53.7 5.9 %collective-permute-start.10 = (bf16[88,128]{1,0:T(8,128)(2,1)S(1)}, bf16[88,128]{1,0:T(8,128)(2,1)S(1)}, u32[]{:S(2)}, u32[]{:S(2)}) collective-permute-start(bf16[88,128]{1,0:T(8,128)(2,1)S(1)} %shard_map.65.own_ref), channel_id=1, source_target_pairs={{0,6},{2,4},{4,2},{6,0},{1,7},{3,5},{5,3},{7,1},{8,14},{10,12},{12... | collective-permute-start | bytes 67592 | tf_op jit(solution)/shard_map/ppermute | solution.py:486
  71.7 6.5 %collective-permute-start.11 = (bf16[16,80,128]{2,1,0:T(8,128)(2,1)S(1)}, bf16[16,80,128]{2,1,0:T(8,128)(2,1)S(1)}, u32[]{:S(2)}, u32[]{:S(2)}) collective-permute-start(bf16[16,80,128]{2,1,0:T(8,128)(2,1)S(1)} %all_to_all.11.own_ref), channel_id=1, source_target_pairs={{0,8},{8,0},{1,9},{9,1},{2,10},{10,2},{3,11},{11,3},{4,12},{12,4},... | collective-permute-start | bytes 983048 | tf_op jit(solution)/shard_map/ppermute | solution.py:506
